TPU v7x, 32 devices: a whole 2x2x4 slice. The times are simulated.
32 devices in a mesh: dp: 4 (over x, core), fsdp: 8 (over z, y).
Axes of the slice: x: 2, y: 2, z: 4, core: 2. Of those that a mesh axis runs over, the one named last changes fastest.
Arguments:
- tokens: bfloat16 [4096, 2048], P(('dp', 'fsdp')), may hold values from -6 to 6
- cotangent: bfloat16 [4096, 2048], P(('dp', 'fsdp')), may hold values from -6 to 6
- routes: int32 [4096, 8], P(('dp', 'fsdp')), may hold values from 0 to 15, all different within a row; in each aligned block of 128 rows (0 to 127, 128 to 255, ...) at most 80 rows name the same one
- w_query: bfloat16 [2048, 2048], P(('dp', 'fsdp')), may hold values from -0.125 to 0.125
- w_key: bfloat16 [2048, 2048], P(('dp', 'fsdp')), may hold values from -0.125 to 0.125
- w_value: bfloat16 [2048, 2048], P(('dp', 'fsdp')), may hold values from -0.125 to 0.125
- w_output: bfloat16 [2048, 2048], P(('dp', 'fsdp')), may hold values from -0.5 to 0.5
- w_router: bfloat16 [2048, 16], P(('dp', 'fsdp')), may hold values from -0.0625 to 0.0625
- gain_attn: bfloat16 [2048], P(('dp', 'fsdp')), may hold values from 0.5 to 1.5
- gain_query: bfloat16 [2048], P(('dp', 'fsdp')), may hold values from 0.5 to 1.5
- gain_key: bfloat16 [2048], P(('dp', 'fsdp')), may hold values from 0.5 to 1.5
- gain_ffn: bfloat16 [2048], P(('dp', 'fsdp')), may hold values from 0.5 to 1.5
- expert_gate: bfloat16 [16, 2048, 1024], P('fsdp', None, 'dp'), may hold values from -0.125 to 0.125
- expert_up: bfloat16 [16, 2048, 1024], P('fsdp', None, 'dp'), may hold values from -0.125 to 0.125
- expert_down: bfloat16 [16, 2048, 1024], P('fsdp', None, 'dp'), may hold values from -0.75 to 0.75
Outputs:
- layer_out: bfloat16 [4096, 2048], P(('dp', 'fsdp'))
- grad_tokens: float32 [4096, 2048], P(('dp', 'fsdp'))
- grad_w_query: float32 [2048, 2048], P(('dp', 'fsdp'))
- grad_w_key: float32 [2048, 2048], P(('dp', 'fsdp'))
- grad_w_value: float32 [2048, 2048], P(('dp', 'fsdp'))
- grad_w_output: float32 [2048, 2048], P(('dp', 'fsdp'))
- grad_w_router: float32 [2048, 16], P(('dp', 'fsdp'))
- grad_gain_attn: float32 [2048], P(('dp', 'fsdp'))
- grad_gain_query: float32 [2048], P(('dp', 'fsdp'))
- grad_gain_key: float32 [2048], P(('dp', 'fsdp'))
- grad_gain_ffn: float32 [2048], P(('dp', 'fsdp'))
- grad_expert_gate: float32 [16, 2048, 1024], P('fsdp', None, 'dp')
- grad_expert_up: float32 [16, 2048, 1024], P('fsdp', None, 'dp')
- grad_expert_down: float32 [16, 2048, 1024], P('fsdp', None, 'dp')
Inputs may be any that keep to these rules, and one draw needn't show every extreme that they name: Within the rows of one device no expert is named by more than 80 routes, and in every draw some expert is named by exactly 80 routes of some device; a token's 8 experts differ.
All inputs are finite; a program needn't handle non-finite values.
Results may differ from a plain program's by a relative error of at most 0.024.
Values may be sent and summed in bfloat16 or wider, within the bound.
No kernel may reach another device: no remote copies, remote signals or barrier semaphores. Data moves between devices by JAX's collectives and lax.ppermute only.
A program may use at most 512 MiB of HBM per device.

v0:
```python
import jax
import jax.numpy as jnp
from jax import lax
from jax.sharding import PartitionSpec as P

HEADS = 16
TOPK = 8


epsilon = 1e-05
rope_base = 10000.0
far_low = -1e30


def rms_norm(values, scaling):
    factor = lax.rsqrt(jnp.mean(values * values, axis=-1, keepdims=True) + epsilon)
    return values * factor * scaling


def rotary(values, positions):
    half_dim = values.shape[-1] // 2
    inv_freq = rope_base ** (-(jnp.arange(half_dim, dtype=jnp.float32) * 2.0) / values.shape[-1])
    angles = positions.astype(jnp.float32)[:, None] * inv_freq[None, :]
    cosine = jnp.cos(angles)[:, None, :]
    sine_vals = jnp.sin(angles)[:, None, :]
    first_half = values[..., :half_dim]
    second = values[..., half_dim:]
    return jnp.concatenate(
        [first_half * cosine - second * sine_vals, second * cosine + first_half * sine_vals],
        axis=-1,
    )


def head_prep(values, scaling, positions):
    normed = rms_norm(values, scaling)
    return rotary(normed.reshape(values.shape[0], HEADS, -1), positions)


def swiglu(gate_hid, up_hid):
    return jax.nn.silu(gate_hid) * up_hid


def gating(logits, routes, num_experts):
    prob_vals = jax.nn.softmax(logits, axis=-1)
    pick_table = (
        routes[:, :, None] == jnp.arange(num_experts, dtype=jnp.int32)[None, None, :]
    ).astype(jnp.float32)
    chosen = jnp.sum(pick_table * prob_vals[:, None, :], axis=-1)
    return chosen / jnp.sum(chosen, axis=-1, keepdims=True)


def per_device(
    tokens,
    cotangent,
    routes,
    w_query,
    w_key,
    w_value,
    w_output,
    w_router,
    gain_attn,
    gain_query,
    gain_key,
    gain_ffn,
    expert_gate,
    expert_up,
    expert_down,
):
    row_count = tokens.shape[0]
    model_width = tokens.shape[1]
    head_dim = model_width // HEADS
    score_scale = head_dim ** (-0.5)
    fsdp_size = lax.axis_size("fsdp")
    local_experts = expert_gate.shape[0]
    num_experts = local_experts * fsdp_size
    capacity = max(2, (row_count * TOPK * 5 + 4 * num_experts - 1) // (4 * num_experts))
    positions = lax.axis_index("fsdp") * row_count + jnp.arange(row_count, dtype=jnp.int32)
    first_pos = positions[0]
    last_pos = positions[row_count - 1]
    inputs = tokens.astype(jnp.float32)
    dense_full = (
        lax.all_gather(w_query, ("dp", "fsdp"), axis=0, tiled=True),
        lax.all_gather(w_key, ("dp", "fsdp"), axis=0, tiled=True),
        lax.all_gather(w_value, ("dp", "fsdp"), axis=0, tiled=True),
        lax.all_gather(w_output, ("dp", "fsdp"), axis=0, tiled=True),
        lax.all_gather(w_router, ("dp", "fsdp"), axis=0, tiled=True),
        lax.all_gather(gain_attn, ("dp", "fsdp"), axis=0, tiled=True),
        lax.all_gather(gain_query, ("dp", "fsdp"), axis=0, tiled=True),
        lax.all_gather(gain_key, ("dp", "fsdp"), axis=0, tiled=True),
        lax.all_gather(gain_ffn, ("dp", "fsdp"), axis=0, tiled=True),
    )
    expert_full = (
        lax.all_gather(expert_gate, "dp", axis=2, tiled=True),
        lax.all_gather(expert_up, "dp", axis=2, tiled=True),
        lax.all_gather(expert_down, "dp", axis=2, tiled=True),
    )
    query_full, key_full, value_full, output_full, router_full = dense_full[:5]
    gain_in_full = dense_full[5].astype(jnp.float32)
    gain_q_full = dense_full[6].astype(jnp.float32)
    gain_k_full = dense_full[7].astype(jnp.float32)
    gain_mid_full = dense_full[8].astype(jnp.float32)
    normed_low = rms_norm(inputs, gain_in_full).astype(jnp.bfloat16)
    query_raw = jnp.dot(normed_low, query_full, preferred_element_type=jnp.float32)
    key_raw = jnp.dot(normed_low, key_full, preferred_element_type=jnp.float32)
    value_raw = jnp.dot(normed_low, value_full, preferred_element_type=jnp.float32)
    query_low = head_prep(query_raw, gain_q_full, positions).astype(jnp.bfloat16)
    key_low = head_prep(key_raw, gain_k_full, positions).astype(jnp.bfloat16)
    value_low = value_raw.astype(jnp.bfloat16).reshape(row_count, HEADS, head_dim)
    start_state = (
        jnp.full((HEADS, row_count), far_low, jnp.float32),
        jnp.zeros((HEADS, row_count), jnp.float32),
        jnp.zeros((row_count, HEADS, head_dim), jnp.float32),
    )
    shard_piece = (
        lax.all_gather(key_low, "fsdp", axis=0, tiled=True),
        lax.all_gather(value_low, "fsdp", axis=0, tiled=True),
    )

    def attend_update(state):
        run_max, run_sum, run_acc = state
        key_piece, value_piece = shard_piece
        scores = (
            jnp.einsum("qhd,khd->hqk", query_low, key_piece, preferred_element_type=jnp.float32)
            * score_scale
        )
        key_pos = jnp.arange(key_piece.shape[0], dtype=jnp.int32)
        allowed = (key_pos[None, :] <= positions[:, None])[None]
        new_max = jnp.maximum(run_max, jnp.max(jnp.where(allowed, scores, far_low), axis=-1))
        exp_vals = jnp.where(allowed, jnp.exp(scores - new_max[..., None]), 0.0)
        factor = jnp.exp(run_max - new_max)
        run_sum = jnp.sum(exp_vals, axis=-1)
        run_acc = run_acc * factor.T[:, :, None] + jnp.einsum(
            "hqk,khd->qhd",
            exp_vals.astype(jnp.bfloat16),
            value_piece,
            preferred_element_type=jnp.float32,
        )
        return (new_max, run_sum, run_acc)

    run_max, run_sum, run_acc = lax.cond(
        jnp.int32(0) <= last_pos, attend_update, lambda state: state, start_state
    )
    attn_f32 = run_acc / run_sum.T[:, :, None]
    log_sum = run_max + jnp.log(run_sum)
    attn_low = attn_f32.reshape(row_count, model_width).astype(jnp.bfloat16)
    resid_mid = inputs + jnp.dot(attn_low, output_full, preferred_element_type=jnp.float32)
    mid_low = rms_norm(resid_mid, gain_mid_full).astype(jnp.bfloat16)
    logits = jnp.dot(mid_low, router_full, preferred_element_type=jnp.float32)
    gate_vals, gate_pull = jax.vjp(
        lambda logit_vals: gating(logit_vals, routes, num_experts), logits
    )
    route_flat = routes.reshape(-1)
    pick_table = (route_flat[:, None] == jnp.arange(num_experts, dtype=jnp.int32)[None, :]).astype(
        jnp.int32
    )
    slot_index = jnp.sum(pick_table * (jnp.cumsum(pick_table, axis=0) - 1), axis=1)
    target = route_flat * capacity + slot_index
    spread = jnp.repeat(mid_low, TOPK, axis=0)
    send_rows = (
        jnp.zeros((num_experts * capacity, model_width), jnp.bfloat16).at[target].set(spread)
    )
    send_rows = send_rows.reshape(fsdp_size, local_experts, capacity, model_width)
    arrived = lax.all_to_all(send_rows, "fsdp", split_axis=0, concat_axis=0, tiled=True)
    gate_w, up_w, down_w = expert_full
    gate_hid = jnp.einsum("secd,edh->sech", arrived, gate_w, preferred_element_type=jnp.float32)
    up_hid = jnp.einsum("secd,edh->sech", arrived, up_w, preferred_element_type=jnp.float32)
    act_low = swiglu(gate_hid, up_hid).astype(jnp.bfloat16)
    expert_out = jnp.einsum(
        "sech,edh->secd", act_low, down_w, preferred_element_type=jnp.float32
    ).astype(jnp.bfloat16)
    returned = lax.all_to_all(expert_out, "fsdp", split_axis=0, concat_axis=0, tiled=True).reshape(
        num_experts * capacity, model_width
    )
    picked = returned[target].reshape(row_count, TOPK, model_width).astype(jnp.float32)
    resid_out = resid_mid + jnp.sum(gate_vals[:, :, None] * picked, axis=1)
    layer_out = resid_out.astype(jnp.bfloat16)
    back_dense = (
        lax.all_gather(w_query, ("dp", "fsdp"), axis=0, tiled=True),
        lax.all_gather(w_key, ("dp", "fsdp"), axis=0, tiled=True),
        lax.all_gather(w_value, ("dp", "fsdp"), axis=0, tiled=True),
        lax.all_gather(w_output, ("dp", "fsdp"), axis=0, tiled=True),
        lax.all_gather(w_router, ("dp", "fsdp"), axis=0, tiled=True),
        lax.all_gather(gain_attn, ("dp", "fsdp"), axis=0, tiled=True),
        lax.all_gather(gain_query, ("dp", "fsdp"), axis=0, tiled=True),
        lax.all_gather(gain_key, ("dp", "fsdp"), axis=0, tiled=True),
        lax.all_gather(gain_ffn, ("dp", "fsdp"), axis=0, tiled=True),
    )
    back_experts = (
        lax.all_gather(expert_gate, "dp", axis=2, tiled=True),
        lax.all_gather(expert_up, "dp", axis=2, tiled=True),
        lax.all_gather(expert_down, "dp", axis=2, tiled=True),
    )
    query_back, key_back, value_back, output_back, router_back = back_dense[:5]
    gain_in_back = back_dense[5].astype(jnp.float32)
    gain_q_back = back_dense[6].astype(jnp.float32)
    gain_k_back = back_dense[7].astype(jnp.float32)
    gain_mid_back = back_dense[8].astype(jnp.float32)
    gate_back, up_back, down_back = back_experts
    grad_out = cotangent.astype(jnp.float32)
    grad_gates = jnp.sum(grad_out[:, None, :] * picked, axis=-1)
    grad_routed = (
        (gate_vals[:, :, None] * grad_out[:, None, :]).astype(jnp.bfloat16).reshape(-1, model_width)
    )
    send_grads = (
        jnp.zeros((num_experts * capacity, model_width), jnp.bfloat16).at[target].set(grad_routed)
    )
    send_grads = send_grads.reshape(fsdp_size, local_experts, capacity, model_width)
    grad_arrived = lax.all_to_all(send_grads, "fsdp", split_axis=0, concat_axis=0, tiled=True)
    gate_again = jnp.einsum(
        "secd,edh->sech", arrived, gate_back, preferred_element_type=jnp.float32
    )
    up_again = jnp.einsum("secd,edh->sech", arrived, up_back, preferred_element_type=jnp.float32)
    act_vals, act_pull = jax.vjp(swiglu, gate_again, up_again)
    act_again = act_vals.astype(jnp.bfloat16)
    grad_act = jnp.einsum(
        "secd,edh->sech", grad_arrived, down_back, preferred_element_type=jnp.float32
    )
    grad_down = jnp.einsum(
        "secd,sech->edh", grad_arrived, act_again, preferred_element_type=jnp.float32
    )
    grad_gate_hid, grad_up_hid = act_pull(grad_act)
    grad_gate_low = grad_gate_hid.astype(jnp.bfloat16)
    grad_up_low = grad_up_hid.astype(jnp.bfloat16)
    grad_gate_w = jnp.einsum(
        "secd,sech->edh", arrived, grad_gate_low, preferred_element_type=jnp.float32
    )
    grad_up_w = jnp.einsum(
        "secd,sech->edh", arrived, grad_up_low, preferred_element_type=jnp.float32
    )
    grad_inputs = jnp.einsum(
        "sech,edh->secd", grad_gate_low, gate_back, preferred_element_type=jnp.float32
    ) + jnp.einsum("sech,edh->secd", grad_up_low, up_back, preferred_element_type=jnp.float32)
    grad_returned = lax.all_to_all(
        grad_inputs.astype(jnp.bfloat16), "fsdp", split_axis=0, concat_axis=0, tiled=True
    )
    grad_returned = grad_returned.reshape(num_experts * capacity, model_width)
    grad_mid = jnp.sum(
        grad_returned[target].reshape(row_count, TOPK, model_width).astype(jnp.float32), axis=1
    )
    expert_grads = (
        lax.psum_scatter(
            grad_gate_w.astype(jnp.bfloat16), "dp", scatter_dimension=2, tiled=True
        ).astype(jnp.float32),
        lax.psum_scatter(
            grad_up_w.astype(jnp.bfloat16), "dp", scatter_dimension=2, tiled=True
        ).astype(jnp.float32),
        lax.psum_scatter(
            grad_down.astype(jnp.bfloat16), "dp", scatter_dimension=2, tiled=True
        ).astype(jnp.float32),
    )
    (grad_logits,) = gate_pull(grad_gates)
    grad_logits_low = grad_logits.astype(jnp.bfloat16)
    grad_router = jnp.einsum(
        "td,te->de", mid_low, grad_logits_low, preferred_element_type=jnp.float32
    )
    grad_mid = grad_mid + jnp.einsum(
        "te,de->td", grad_logits_low, router_back, preferred_element_type=jnp.float32
    )
    mid_value, mid_pull = jax.vjp(rms_norm, resid_mid, gain_mid_back)
    grad_resid_part, grad_gain_mid = mid_pull(grad_mid)
    grad_resid = grad_out + grad_resid_part
    grad_attn_out = grad_resid.astype(jnp.bfloat16)
    grad_output_w = jnp.einsum(
        "td,te->de", attn_low, grad_attn_out, preferred_element_type=jnp.float32
    )
    grad_attn = jnp.einsum(
        "te,de->td", grad_attn_out, output_back, preferred_element_type=jnp.float32
    )
    grad_attn = grad_attn.astype(jnp.bfloat16).reshape(row_count, HEADS, head_dim)
    delta_rows = jnp.sum(grad_attn.astype(jnp.float32) * attn_f32, axis=-1).T
    key_all, value_all = (
        lax.all_gather(key_low, "fsdp", axis=0, tiled=True),
        lax.all_gather(value_low, "fsdp", axis=0, tiled=True),
    )

    def probs_block(key_block, value_block, begin_at):
        scores = (
            jnp.einsum("qhd,khd->hqk", query_low, key_block, preferred_element_type=jnp.float32)
            * score_scale
        )
        key_pos = begin_at + jnp.arange(key_block.shape[0], dtype=jnp.int32)
        allowed = (key_pos[None, :] <= positions[:, None])[None]
        prob_vals = jnp.where(allowed, jnp.exp(scores - log_sum[..., None]), 0.0)
        grad_probs = jnp.einsum(
            "qhd,khd->hqk", grad_attn, value_block, preferred_element_type=jnp.float32
        )
        grad_scores = (prob_vals * (grad_probs - delta_rows[..., None])).astype(jnp.bfloat16)
        return (prob_vals, grad_scores)

    block_rows = 8 * row_count
    block_needed = last_pos // block_rows + 1
    zero_query = jnp.zeros((row_count, HEADS, head_dim), jnp.float32)

    def query_step(block_index, accum):
        begin_at = block_index * block_rows
        key_block = lax.dynamic_slice_in_dim(key_all, begin_at, block_rows, 0)
        value_block = lax.dynamic_slice_in_dim(value_all, begin_at, block_rows, 0)
        prob_vals, grad_scores = probs_block(key_block, value_block, begin_at)
        return accum + jnp.einsum(
            "hqk,khd->qhd", grad_scores, key_block, preferred_element_type=jnp.float32
        )

    grad_query_rot = lax.fori_loop(0, block_needed, query_step, zero_query) * score_scale
    stats_all = (
        lax.all_gather(log_sum.T, "fsdp", axis=0, tiled=True),
        lax.all_gather(delta_rows.T, "fsdp", axis=0, tiled=True),
    )
    query_piece = lax.all_gather(query_low, "fsdp", axis=0, tiled=True)
    grad_piece = lax.all_gather(grad_attn, "fsdp", axis=0, tiled=True)
    span = query_piece.shape[0]

    def add_update(state):
        lse_piece = stats_all[0].T
        delta_piece = stats_all[1].T
        scores = (
            jnp.einsum("qhd,khd->hqk", query_piece, key_low, preferred_element_type=jnp.float32)
            * score_scale
        )
        query_pos = jnp.arange(span, dtype=jnp.int32)
        allowed = (positions[None, :] <= query_pos[:, None])[None]
        prob_vals = jnp.where(allowed, jnp.exp(scores - lse_piece[..., None]), 0.0)
        grad_probs = jnp.einsum(
            "qhd,khd->hqk", grad_piece, value_low, preferred_element_type=jnp.float32
        )
        grad_scores = (prob_vals * (grad_probs - delta_piece[..., None])).astype(jnp.bfloat16)
        grad_value_acc = jnp.einsum(
            "hqk,qhd->khd",
            prob_vals.astype(jnp.bfloat16),
            grad_piece,
            preferred_element_type=jnp.float32,
        )
        grad_key_acc = jnp.einsum(
            "hqk,qhd->khd", grad_scores, query_piece, preferred_element_type=jnp.float32
        )
        return (grad_key_acc, grad_value_acc)

    grad_key_sum, grad_value_sum = lax.cond(
        jnp.int32(0) + span > first_pos, add_update, lambda state: state, (zero_query, zero_query)
    )
    grad_key_rot = grad_key_sum * score_scale
    grad_value_low = grad_value_sum.reshape(row_count, model_width).astype(jnp.bfloat16)
    query_value, query_pull = jax.vjp(
        lambda raw_vals, scaling: head_prep(raw_vals, scaling, positions), query_raw, gain_q_back
    )
    grad_query_raw, grad_gain_query = query_pull(grad_query_rot)
    key_value, key_pull = jax.vjp(
        lambda raw_vals, scaling: head_prep(raw_vals, scaling, positions), key_raw, gain_k_back
    )
    grad_key_raw, grad_gain_key = key_pull(grad_key_rot)
    grad_query_low = grad_query_raw.astype(jnp.bfloat16)
    grad_key_low = grad_key_raw.astype(jnp.bfloat16)
    grad_wq = jnp.einsum(
        "td,te->de", normed_low, grad_query_low, preferred_element_type=jnp.float32
    )
    grad_wk = jnp.einsum("td,te->de", normed_low, grad_key_low, preferred_element_type=jnp.float32)
    grad_wv = jnp.einsum(
        "td,te->de", normed_low, grad_value_low, preferred_element_type=jnp.float32
    )
    grad_normed = (
        jnp.einsum("te,de->td", grad_query_low, query_back, preferred_element_type=jnp.float32)
        + jnp.einsum("te,de->td", grad_key_low, key_back, preferred_element_type=jnp.float32)
        + jnp.einsum("te,de->td", grad_value_low, value_back, preferred_element_type=jnp.float32)
    )
    in_value, input_pull = jax.vjp(rms_norm, inputs, gain_in_back)
    grad_input_part, grad_gain_in = input_pull(grad_normed)
    grad_tokens = grad_resid + grad_input_part
    dense_grads = (
        lax.psum_scatter(grad_wq, ("dp", "fsdp"), scatter_dimension=0, tiled=True),
        lax.psum_scatter(grad_wk, ("dp", "fsdp"), scatter_dimension=0, tiled=True),
        lax.psum_scatter(grad_wv, ("dp", "fsdp"), scatter_dimension=0, tiled=True),
        lax.psum_scatter(grad_output_w, ("dp", "fsdp"), scatter_dimension=0, tiled=True),
        lax.psum_scatter(grad_router, ("dp", "fsdp"), scatter_dimension=0, tiled=True),
        lax.psum_scatter(grad_gain_in, ("dp", "fsdp"), scatter_dimension=0, tiled=True),
        lax.psum_scatter(grad_gain_query, ("dp", "fsdp"), scatter_dimension=0, tiled=True),
        lax.psum_scatter(grad_gain_key, ("dp", "fsdp"), scatter_dimension=0, tiled=True),
        lax.psum_scatter(grad_gain_mid, ("dp", "fsdp"), scatter_dimension=0, tiled=True),
    )
    return (
        layer_out,
        grad_tokens,
        dense_grads[0],
        dense_grads[1],
        dense_grads[2],
        dense_grads[3],
        dense_grads[4],
        dense_grads[5],
        dense_grads[6],
        dense_grads[7],
        dense_grads[8],
        expert_grads[0],
        expert_grads[1],
        expert_grads[2],
    )


def solution(mesh):
    in_specs = (
        P(("dp", "fsdp"), None),
        P(("dp", "fsdp"), None),
        P(("dp", "fsdp"), None),
        P(("dp", "fsdp"), None),
        P(("dp", "fsdp"), None),
        P(("dp", "fsdp"), None),
        P(("dp", "fsdp"), None),
        P(("dp", "fsdp"), None),
        P(("dp", "fsdp")),
        P(("dp", "fsdp")),
        P(("dp", "fsdp")),
        P(("dp", "fsdp")),
        P("fsdp", None, "dp"),
        P("fsdp", None, "dp"),
        P("fsdp", None, "dp"),
    )
    out_specs = (
        P(("dp", "fsdp"), None),
        P(("dp", "fsdp"), None),
        P(("dp", "fsdp"), None),
        P(("dp", "fsdp"), None),
        P(("dp", "fsdp"), None),
        P(("dp", "fsdp"), None),
        P(("dp", "fsdp"), None),
        P(("dp", "fsdp")),
        P(("dp", "fsdp")),
        P(("dp", "fsdp")),
        P(("dp", "fsdp")),
        P("fsdp", None, "dp"),
        P("fsdp", None, "dp"),
        P("fsdp", None, "dp"),
    )
    return jax.shard_map(
        per_device, mesh=mesh, in_specs=in_specs, out_specs=out_specs, check_vma=False
    )
```

profile of v0, /device:TPU:0, one launch (start us, length us, event | category | flops | bytes accessed | tf_op | source)
XLA Modules:
  0.0 2969.3 jit_solution(9807492984370496422)
XLA Ops:
  12.9 42.7 %all-reduce.13 = (bf16[2048]{0:T(1024)(128)(2,1)S(1)}, bf16[2048]{0:T(1024)(128)(2,1)S(1)}, bf16[2048]{0:T(1024)(128)(2,1)S(1)}, bf16[2048]{0:T(1024)(128)(2,1)S(1)}) all-reduce(bf16[2048]{0:T(1024)(128)(2,1)S(1)} %dynamic-update-slice, bf16[2048]{0:T(1024)(128)(2,1)S(1)} %dynamic-update-slice.1, ...), channel_id=1, replica_groups=mesh['dp'=4,'fsdp'=8] {'dp','fsdp'}, use_global_device_ids=true, to_apply=%add.4 | all-reduce | flops 8192 | bytes 32768
  57.2 34.4 %all-gather.13.cloned.1.call-done = bf16[2048,2048]{1,0:T(8,128)(2,1)} async-done(((bf16[64,2048]{1,0:T(8,128)(2,1)}), bf16[2048,2048]{1,0:T(8,128)(2,1)}) %all-gather.13.cloned.1.call-update) | async-done | bytes 8388624 | tf_op jit(solution)/shard_map/all_gather | solution.py:82
  91.6 5.0 multiply_reduce_fusion.7
  97.9 72.7 %all-gather.15.cloned.1.call-done = bf16[2048,2048]{1,0:T(8,128)(2,1)} async-done(((bf16[64,2048]{1,0:T(8,128)(2,1)}), bf16[2048,2048]{1,0:T(8,128)(2,1)}) %all-gather.15.cloned.1.call-update) | async-done | bytes 8388624 | tf_op jit(solution)/shard_map/all_gather | solution.py:83
  170.6 4.8 multiply_reduce_fusion.6
  180.0 69.6 %all-gather.19.cloned.1.call-done = bf16[2048,2048]{1,0:T(8,128)(2,1)} async-done(((bf16[64,2048]{1,0:T(8,128)(2,1)}), bf16[2048,2048]{1,0:T(8,128)(2,1)}) %all-gather.19.cloned.1.call-update) | async-done | bytes 8388624 | tf_op jit(solution)/shard_map/all_gather | solution.py:84
  249.6 4.7 fusion.97
  260.2 68.5 %all-gather = bf16[32,64,16]{1,2,0:T(8,128)(2,1)S(1)} all-gather(bf16[1,64,16]{1,2,0:T(8,128)(2,1)S(1)} %bitcast.257), channel_id=1, replica_groups=mesh['dp'=4,'fsdp'=8] {'dp','fsdp'}, dimensions={0}, use_global_device_ids=true | all-gather | bytes 67584 | tf_op jit(solution)/shard_map/all_gather | solution.py:86
  328.9 4.5 reduce-window.6
  335.3 64.9 %all-gather.21.cloned.1.call-done = bf16[1024,16,128]{2,1,0:T(8,128)(2,1)} async-done(((bf16[128,16,128]{2,1,0:T(8,128)(2,1)}), bf16[1024,16,128]{2,1,0:T(8,128)(2,1)}) %all-gather.21.cloned.1.call-update) | async-done | bytes 4194320 | tf_op jit(solution)/shard_map/all_gather | solution.py:116
  400.2 15.5 conditional.2
  405.9 4.5 fusion.16
  416.9 61.8 %all-gather.23.cloned.1.call-done = bf16[2048,2048]{1,0:T(8,128)(2,1)} async-done(((bf16[64,2048]{1,0:T(8,128)(2,1)}), bf16[2048,2048]{1,0:T(8,128)(2,1)}) %all-gather.23.cloned.1.call-update) | async-done | bytes 8388624 | tf_op jit(solution)/shard_map/all_gather | solution.py:85
  478.7 4.8 multiply_reduce_fusion.5
  484.2 10.0 scatter_custom_fusion.1
  494.2 4.7 all-to-all-start.2
  499.6 9.6 scatter_custom_fusion
  509.2 106.0 %all-to-all-done.2 = bf16[8,2,80,2048]{3,2,1,0:T(8,128)(2,1)} async-done(((bf16[8,2,80,2048]{3,2,1,0:T(8,128)(2,1)}), bf16[8,2,80,2048]{3,2,1,0:T(8,128)(2,1)}, u32[]{:S(2)}, u32[]{:S(2)}) %all-to-all-start.2) | async-done | bytes 5242912 | tf_op jit(solution)/shard_map/all_to_all | solution.py:208
  615.3 4.8 all-to-all-start
  620.1 11.5 fusion.62
  631.6 104.0 %all-to-all-done = bf16[8,2,80,2048]{3,2,1,0:T(8,128)(2,1)} async-done(((bf16[8,2,80,2048]{3,2,1,0:T(8,128)(2,1)}), bf16[8,2,80,2048]{3,2,1,0:T(8,128)(2,1)}, u32[]{:S(2)}, u32[]{:S(2)}) %all-to-all-start) | async-done | bytes 5242912 | tf_op jit(solution)/shard_map/all_to_all | solution.py:163
  735.6 11.5 fusion.56
  747.1 15.1 fusion.69
  762.3 10.4 convert_bitcast_fusion
  775.4 5.1 all-to-all-start.1
  780.5 12.3 fusion.54
  792.8 12.3 fusion.70
  805.1 5.7 copy.156
  810.8 84.6 %all-to-all-done.1 = bf16[8,2,80,2048]{3,2,1,0:T(8,128)(2,1)} async-done(((bf16[8,2,80,2048]{3,2,1,0:T(8,128)(2,1)}), bf16[8,2,80,2048]{3,2,1,0:T(8,128)(2,1)}, u32[]{:S(2)}, u32[]{:S(2)}) %all-to-all-start.1) | async-done | bytes 5242912 | tf_op jit(solution)/shard_map/all_to_all | solution.py:171
  895.4 4.6 all-to-all-start.3
  900.7 12.0 gather_fusion
  912.7 6.0 fusion.53
  918.9 146.8 %all-to-all-done.3 = bf16[8,2,80,2048]{3,2,1,0:T(8,128)(2,1)} async-done(((bf16[8,2,80,2048]{3,2,1,0:T(8,128)(2,1)}), bf16[8,2,80,2048]{3,2,1,0:T(8,128)(2,1)}, u32[]{:S(2)}, u32[]{:S(2)}) %all-to-all-start.3) | async-done | bytes 5242912 | tf_op jit(solution)/shard_map/all_to_all | solution.py:233
  1065.6 12.0 gather_fusion.1
  1077.6 5.2 convert_reduce_fusion
  1085.1 6.3 convolution_convert_fusion
  1093.9 11.9 bitcast_convert_fusion
  1105.9 12.1 bitcast_convert_fusion.2
  1118.0 11.9 bitcast_convert_fusion.1
  1130.9 8.1 fusion.108
  1143.2 5.3 copy.160
  1148.5 30.6 %all_gather.83 = f32[1024,16]{0,1:T(8,128)S(1)} all-gather(f32[128,16]{0,1:T(8,128)S(1)} %bitcast.251), channel_id=1, replica_groups=mesh['dp'=4,'fsdp'=8] {'fsdp'}, dimensions={0}, use_global_device_ids=true | all-gather | bytes 73728 | tf_op jit(solution)/shard_map/all_gather | solution.py:305
  1179.8 33.6 %all_gather.85 = f32[1024,16]{1,0:T(8,128)} all-gather(f32[128,16]{1,0:T(8,128)S(1)} %multiply_reduce_fusion.3), channel_id=1, replica_groups=mesh['dp'=4,'fsdp'=8] {'fsdp'}, dimensions={0}, use_global_device_ids=true | all-gather | bytes 73728 | tf_op jit(solution)/shard_map/all_gather | solution.py:306
  1213.7 15.1 while.11
  1213.7 6.9 fusion.196
  1220.8 8.0 fusion.197
  1229.8 31.5 %conditional.3 = (f32[128,16,128]{2,0,1:T(8,128)S(1)}, bf16[128,2048]{0,1:T(8,128)(2,1)S(1)}) conditional(s32[]{:T(128)} %bitcast.38, () %tuple.37, (s32[128]{0:T(128)}, bf16[1024,16,128]{2,0,1:T(8,128)(2,1)}, bf16[128,16,128]{2,0,1:T(8,128)(2,1)S(1)}, f32[1024,16]{0,1:T(8,128)S(1)}, bf16[1024,16,128]{2,1,0:T(8,128)(2,1)}, ...), branch_computations={%region_28.29_spmd, %region_29.30_spmd} | conditional | flops 2168848384 | bytes 56033864 | solution.py:337
  1230.2 6.7 fusion.141
  1237.0 6.7 copy.163
  1244.6 10.6 fusion.34
  1255.2 6.1 fusion.35
  1269.2 8.2 fusion.128
  1283.5 8.2 fusion.130
  1291.7 8.2 fusion.126
  1302.0 6.7 fusion.143
  1308.7 8.3 convolution_add_fusion.2
  1320.1 37.7 %all-reduce.12 = (f32[2048]{0:T(1024)S(1)}, f32[2048]{0:T(1024)S(1)}, f32[2048]{0:T(1024)S(1)}, f32[2048]{0:T(1024)S(1)}) all-reduce(f32[2048]{0:T(1024)S(1)} %get-tuple-element.253, f32[2048]{0:T(1024)S(1)} %get-tuple-element.251, f32[2048]{0:T(1024)S(1)} %get-tuple-element.249, ...), channel_id=7, replica_groups=mesh['dp'=4,'fsdp'=8] {'dp','fsdp'}, use_global_device_ids=true, to_apply=%region_38.39.clone | all-reduce | flops 8192 | bytes 65536
  1361.5 11.4 reduce-scatter.23.cloned.1.call-done
  1376.8 70.1 %reduce-scatter.19.cloned.1.call-done = bf16[2,2048,256]{2,1,0:T(8,128)(2,1)} async-done(((bf16[2,2048,1024]{2,1,0:T(8,128)(2,1)}), bf16[2,2048,256]{2,1,0:T(8,128)(2,1)}) %reduce-scatter.19.cloned.1.call-update) | async-done | bytes 2097168 | tf_op jit(solution)/shard_map/reduce_scatter | solution.py:241
  1450.9 70.4 %reduce-scatter.21.cloned.1.call-done = bf16[2,2048,256]{2,1,0:T(8,128)(2,1)} async-done(((bf16[2,2048,1024]{2,1,0:T(8,128)(2,1)}), bf16[2,2048,256]{2,1,0:T(8,128)(2,1)}) %reduce-scatter.21.cloned.1.call-update) | async-done | bytes 2097168 | tf_op jit(solution)/shard_map/reduce_scatter | solution.py:244
  1525.2 357.0 %reduce-scatter.17.cloned.1.call-done = f32[64,2048]{1,0:T(8,128)} async-done(((f32[2048,2048]{1,0:T(8,128)}), f32[64,2048]{1,0:T(8,128)}) %reduce-scatter.17.cloned.1.call-update) | async-done | bytes 524304 | tf_op jit(solution)/shard_map/reduce_scatter | solution.py:371
  1882.2 360.0 %reduce-scatter.13.cloned.1.call-done = f32[64,2048]{1,0:T(8,128)} async-done(((f32[2048,2048]{1,0:T(8,128)}), f32[64,2048]{1,0:T(8,128)}) %reduce-scatter.13.cloned.1.call-update) | async-done | bytes 524304 | tf_op jit(solution)/shard_map/reduce_scatter | solution.py:369
  2242.2 360.1 %reduce-scatter.11.cloned.1.call-done = f32[64,2048]{1,0:T(8,128)} async-done(((f32[2048,2048]{1,0:T(8,128)}), f32[64,2048]{1,0:T(8,128)}) %reduce-scatter.11.cloned.1.call-update) | async-done | bytes 524304 | tf_op jit(solution)/shard_map/reduce_scatter | solution.py:368
  2602.3 360.2 %reduce-scatter.15.cloned.1.call-done = f32[64,2048]{1,0:T(8,128)} async-done(((f32[2048,2048]{1,0:T(8,128)}), f32[64,2048]{1,0:T(8,128)}) %reduce-scatter.15.cloned.1.call-update) | async-done | bytes 524304 | tf_op jit(solution)/shard_map/reduce_scatter | solution.py:370
  (270 shorter events, 81.1 us)
Async XLA Ops:
  7.2 84.4 %all-gather.13.cloned.1.call-start = ((), (), s32[]{:S(2)}) async-start(), calls=%async_computation.12 | async-start | bytes 8650752 | tf_op jit(solution)/shard_map/all_gather | solution.py:82
  7.9 162.7 %all-gather.15.cloned.1.call-start = ((), (), s32[]{:S(2)}) async-start(), calls=%async_computation.13 | async-start | bytes 8650752 | tf_op jit(solution)/shard_map/all_gather | solution.py:83
  8.7 241.0 %all-gather.19.cloned.1.call-start = ((), (), s32[]{:S(2)}) async-start(), calls=%async_computation.15 | async-start | bytes 8650752 | tf_op jit(solution)/shard_map/all_gather | solution.py:84
  9.4 325.9 %all-gather.17.cloned.1.call-start = ((), (), s32[]{:S(2)}) async-start(), calls=%async_computation.14 | async-start | bytes 4718592 | tf_op jit(solution)/shard_map/all_gather | solution.py:115
  55.5 194.1 %copy-start.19 = (f32[2048]{0:T(1024)}, f32[2048]{0:T(1024)S(1)}, u32[]{:S(2)}) copy-start(f32[2048]{0:T(1024)S(1)} %convert_element_type.171) | copy-start | bytes 24580
  55.6 41.1 %copy-start.31 = (f32[2048]{0:T(1024)}, f32[2048]{0:T(1024)S(1)}, u32[]{:S(2)}) copy-start(f32[2048]{0:T(1024)S(1)} %convert_element_type.173) | copy-start | bytes 24580
  55.6 119.9 %copy-start.33 = (f32[2048]{0:T(1024)}, f32[2048]{0:T(1024)S(1)}, u32[]{:S(2)}) copy-start(f32[2048]{0:T(1024)S(1)} %convert_element_type.175) | copy-start | bytes 24580
  56.8 39.7 %copy-start.46 = (f32[128]{0:T(128)}, f32[128]{0:T(128)S(1)}, u32[]{:S(2)}) copy-start(f32[128]{0:T(128)S(1)} %fusion.104) | copy-start | bytes 1540
  56.9 192.8 %copy-start.35 = (f32[128]{0:T(128)}, f32[128]{0:T(128)S(1)}, u32[]{:S(2)}) copy-start(f32[128]{0:T(128)S(1)} %fusion.121) | copy-start | bytes 1540
  57.2 120.3 %copy-start.25 = (f32[128,64]{1,0:T(8,128)}, f32[128,64]{1,0:T(8,128)S(1)}, u32[]{:S(2)}) copy-start(f32[128,64]{1,0:T(8,128)S(1)} %get-tuple-element.310) | copy-start | bytes 98308
  57.2 120.3 %copy-start.27 = (f32[128,64]{1,0:T(8,128)}, f32[128,64]{1,0:T(8,128)S(1)}, u32[]{:S(2)}) copy-start(f32[128,64]{1,0:T(8,128)S(1)} %get-tuple-element.311) | copy-start | bytes 98308
  57.2 113.4 %copy-start = (bf16[128,2048]{1,0:T(8,128)(2,1)S(1)}, bf16[128,2048]{1,0:T(8,128)(2,1)}, u32[]{:S(2)}) copy-start(bf16[128,2048]{1,0:T(8,128)(2,1)} %param.21) | copy-start | bytes 1572868
  96.6 78.8 %copy-start.48 = (f32[128]{0:T(128)}, f32[128]{0:T(128)S(1)}, u32[]{:S(2)}) copy-start(f32[128]{0:T(128)S(1)} %get-tuple-element.316) | copy-start | bytes 1540
  96.6 78.8 %copy-start.41 = (f32[128]{0:T(128)}, f32[128]{0:T(128)S(1)}, u32[]{:S(2)}) copy-start(f32[128]{0:T(128)S(1)} %fusion.122) | copy-start | bytes 1540
  179.9 220.2 %all-gather.21.cloned.1.call-start = ((), (), s32[]{:S(2)}) async-start(), calls=%async_computation.16 | async-start | bytes 4718592 | tf_op jit(solution)/shard_map/all_gather | solution.py:116
  254.3 3.0 copy-start.37
  254.3 5.8 copy-start.45
  254.4 79.6 %copy-start.21 = (bf16[128,2048]{1,0:T(8,128)(2,1)S(1)}, bf16[128,2048]{1,0:T(8,128)(2,1)}, u32[]{:S(2)}) copy-start(bf16[128,2048]{1,0:T(8,128)(2,1)} %param.22) | copy-start | bytes 1572868
  255.3 223.4 %all-gather.23.cloned.1.call-start = ((), (), s32[]{:S(2)}) async-start(), calls=%async_computation.17 | async-start | bytes 8650752 | tf_op jit(solution)/shard_map/all_gather | solution.py:85
  255.9 364.3 %all-gather.29.cloned.1.call-start = ((), (), s32[]{:S(2)}) async-start(), calls=%async_computation.20 | async-start | bytes 10485760 | tf_op jit(solution)/shard_map/all_gather | solution.py:95
  256.6 375.0 %all-gather.27.cloned.1.call-start = ((), (), s32[]{:S(2)}) async-start(), calls=%async_computation.19 | async-start | bytes 10485760 | tf_op jit(solution)/shard_map/all_gather | solution.py:94
  401.2 4.8 copy-start.16
  415.7 63.0 %copy-start.6 = (f32[128,16,128]{2,1,0:T(8,128)}, f32[128,16,128]{2,1,0:T(8,128)S(1)}, u32[]{:S(2)}) copy-start(f32[128,16,128]{2,1,0:T(8,128)S(1)} %get-tuple-element.244) | copy-start | bytes 3145732
  416.5 66.9 %copy-start.29 = (f32[128,16]{1,0:T(8,128)}, f32[128,16]{1,0:T(8,128)S(1)}, u32[]{:S(2)}) copy-start(f32[128,16]{1,0:T(8,128)S(1)} %copy.142) | copy-start | bytes 24580
  416.9 66.6 %copy-start.8 = (bf16[128,16,128]{2,1,0:T(8,128)(2,1)}, bf16[128,16,128]{2,1,0:T(8,128)(2,1)S(1)}, u32[]{:S(2)}) copy-start(bf16[128,16,128]{2,1,0:T(8,128)(2,1)S(1)} %fusion.113) | copy-start | bytes 1572868
  494.2 121.1 %all-to-all-start.2 = ((bf16[8,2,80,2048]{3,2,1,0:T(8,128)(2,1)}), bf16[8,2,80,2048]{3,2,1,0:T(8,128)(2,1)}, u32[]{:S(2)}, u32[]{:S(2)}) async-start(bf16[8,2,80,2048]{3,2,1,0:T(8,128)(2,1)} %bitcast.235), calls=%async_computation.2 | async-start | bytes 10485760 | tf_op jit(solution)/shard_map/all_to_all | solution.py:208
  498.9 248.2 %all-gather.25.cloned.1.call-start = ((), (), s32[]{:S(2)}) async-start(), calls=%async_computation.18 | async-start | bytes 10485760 | tf_op jit(solution)/shard_map/all_gather | solution.py:93
  615.3 120.4 %all-to-all-start = ((bf16[8,2,80,2048]{3,2,1,0:T(8,128)(2,1)}), bf16[8,2,80,2048]{3,2,1,0:T(8,128)(2,1)}, u32[]{:S(2)}, u32[]{:S(2)}) async-start(bf16[8,2,80,2048]{3,2,1,0:T(8,128)(2,1)} %bitcast.234), calls=%async_computation | async-start | bytes 10485760 | tf_op jit(solution)/shard_map/all_to_all | solution.py:163
  762.3 10.4 copy-start.53
  775.4 120.0 %all-to-all-start.1 = ((bf16[8,2,80,2048]{3,2,1,0:T(8,128)(2,1)}), bf16[8,2,80,2048]{3,2,1,0:T(8,128)(2,1)}, u32[]{:S(2)}, u32[]{:S(2)}) async-start(bf16[8,2,80,2048]{3,2,1,0:T(8,128)(2,1)} %copy.153), calls=%async_computation.1 | async-start | bytes 10485760 | tf_op jit(solution)/shard_map/all_to_all | solution.py:171
  780.5 12.3 copy-start.52
  895.4 170.3 %all-to-all-start.3 = ((bf16[8,2,80,2048]{3,2,1,0:T(8,128)(2,1)}), bf16[8,2,80,2048]{3,2,1,0:T(8,128)(2,1)}, u32[]{:S(2)}, u32[]{:S(2)}) async-start(bf16[8,2,80,2048]{3,2,1,0:T(8,128)(2,1)} %copy.156), calls=%async_computation.3 | async-start | bytes 10485760 | tf_op jit(solution)/shard_map/all_to_all | solution.py:233
  900.0 329.7 %all-gather.31.cloned.1.call-start = ((), (), s32[]{:S(2)}) async-start(), calls=%async_computation.21 | async-start | bytes 4718592 | tf_op jit(solution)/shard_map/all_gather | solution.py:308
  900.6 329.2 %all-gather.33.cloned.1.call-start = ((), (), s32[]{:S(2)}) async-start(), calls=%async_computation.22 | async-start | bytes 4718592 | tf_op jit(solution)/shard_map/all_gather | solution.py:309
  1077.6 6.3 copy-start.17
  1077.6 6.3 copy-start.22
  1092.3 208.3 %reduce-scatter.25.cloned.1.call-start = ((), (), s32[]{:S(2)}) async-start(), calls=%async_computation.30 | async-start | bytes 1081344
  1093.7 279.2 %reduce-scatter.23.cloned.1.call-start = ((), (), s32[]{:S(2)}) async-start(), calls=%async_computation.29 | async-start | bytes 10485760 | tf_op jit(solution)/shard_map/reduce_scatter | solution.py:247
  1105.9 341.1 %reduce-scatter.19.cloned.1.call-start = ((), (), s32[]{:S(2)}) async-start(), calls=%async_computation.27 | async-start | bytes 10485760 | tf_op jit(solution)/shard_map/reduce_scatter | solution.py:241
  1118.0 403.3 %reduce-scatter.21.cloned.1.call-start = ((), (), s32[]{:S(2)}) async-start(), calls=%async_computation.28 | async-start | bytes 10485760 | tf_op jit(solution)/shard_map/reduce_scatter | solution.py:244
  1129.9 752.3 %reduce-scatter.17.cloned.1.call-start = ((), (), s32[]{:S(2)}) async-start(), calls=%async_computation.26 | async-start | bytes 17301504 | tf_op jit(solution)/shard_map/reduce_scatter | solution.py:371
  1139.1 3.5 copy-start.40
  1139.1 40.0 %copy-start.7 = (f32[128,16,128]{2,1,0:T(8,128)S(1)}, f32[128,16,128]{2,1,0:T(8,128)}, u32[]{:S(2)}) copy-start(f32[128,16,128]{2,1,0:T(8,128)} %copy-done.6) | copy-start | bytes 3145732
  1139.1 40.0 %copy-start.13 = (bf16[16,8,16,128]{3,2,1,0:T(8,128)(2,1)S(1)}, bf16[16,8,16,128]{3,2,1,0:T(8,128)(2,1)}, u32[]{:S(2)}) copy-start(bf16[16,8,16,128]{3,2,1,0:T(8,128)(2,1)} %copy.191) | copy-start | bytes 1572868
  1139.1 40.0 %copy-start.30 = (f32[128,16]{1,0:T(8,128)S(1)}, f32[128,16]{1,0:T(8,128)}, u32[]{:S(2)}) copy-start(f32[128,16]{1,0:T(8,128)} %copy-done.29) | copy-start | bytes 24580
  1139.1 1103.1 %reduce-scatter.13.cloned.1.call-start = ((), (), s32[]{:S(2)}) async-start(), calls=%async_computation.24 | async-start | bytes 17301504 | tf_op jit(solution)/shard_map/reduce_scatter | solution.py:369
  1213.6 16.2 copy-start.10
  1229.8 33.9 %copy-start.26 = (f32[128,64]{1,0:T(8,128)S(1)}, f32[128,64]{1,0:T(8,128)}, u32[]{:S(2)}) copy-start(f32[128,64]{1,0:T(8,128)} %copy-done.25) | copy-start | bytes 98308
  1229.8 33.9 %copy-start.28 = (f32[128,64]{1,0:T(8,128)S(1)}, f32[128,64]{1,0:T(8,128)}, u32[]{:S(2)}) copy-start(f32[128,64]{1,0:T(8,128)} %copy-done.27) | copy-start | bytes 98308
  1237.0 7.4 copy-start.23
  1237.0 7.6 copy-start.24
  1262.3 5.1 copy-start.5
  1262.3 5.1 copy-start.34
  1262.3 5.1 copy-start.44
  1263.7 4.2 copy-start.51
  1277.4 3.3 copy-start.49
  1277.4 1324.9 %reduce-scatter.11.cloned.1.call-start = ((), (), s32[]{:S(2)}) async-start(), calls=%async_computation.23 | async-start | bytes 17301504 | tf_op jit(solution)/shard_map/reduce_scatter | solution.py:368
  1291.6 1670.9 %reduce-scatter.15.cloned.1.call-start = ((), (), s32[]{:S(2)}) async-start(), calls=%async_computation.25 | async-start | bytes 17301504 | tf_op jit(solution)/shard_map/reduce_scatter | solution.py:370
  1299.9 2.2 copy-start.12
  1299.9 8.8 copy-start.15
  1302.0 15.0 slice-start
  1308.7 8.3 slice-start.1
  1317.0 3.1 copy-start.38
  1317.0 43.2 %copy-start.47 = (f32[128]{0:T(128)S(1)}, f32[128]{0:T(128)}, u32[]{:S(2)}) copy-start(f32[128]{0:T(128)} %copy-done.46) | copy-start | bytes 1540
  (15 other events, 19.6 us)
Sparse Core Ops, SparseCore 0:
  11.0 80.5 all-gather.12
  94.6 75.9 all-gather.14
  173.6 75.9 all-gather.18
  252.2 73.2 all-gather.16
  328.1 71.9 all-gather.20
  403.0 75.6 all-gather.22
  480.2 57.9 all-gather.28
  539.8 59.3 all-gather.26
  600.8 59.3 all-gather.24
  903.3 152.5 all-gather.30
  1092.4 72.6 all-gather.32
  1167.2 133.3 reduce-scatter.24
  1303.4 69.4 reduce-scatter.22
  1375.3 71.5 reduce-scatter.18
  1449.5 71.7 reduce-scatter.20
  1524.0 358.1 reduce-scatter.16
  1884.9 357.2 reduce-scatter.12
  2245.0 357.3 reduce-scatter.10
  2605.2 357.3 reduce-scatter.14
where the time goes:
time: 2980 us; the launch traced here: 2970 us
  waiting for transfers between devices  2340 us (79%)
  matrix products  235 us (8%)
  blocking collectives  213 us (7%)
  local copies, waits for them, and re-layouts  75.3 us (3%)
  other arithmetic  65.3 us (2%)
    reduce_scatter x1, waiting for transfers between devices, per_device(): lax.psum_scatter(grad_wv, ('dp', 'fsdp'), scatter_dimension=0, tiled=True)  360 us
    reduce_scatter x1, waiting for transfers between devices, per_device(): lax.psum_scatter(grad_wq, ('dp', 'fsdp'), scatter_dimension=0, tiled=True)  360 us
    reduce_scatter x1, waiting for transfers between devices, per_device(): lax.psum_scatter(grad_wk, ('dp', 'fsdp'), scatter_dimension=0, tiled=True)  360 us
    reduce_scatter x1, waiting for transfers between devices, per_device(): lax.psum_scatter(grad_output_w, ('dp', 'fsdp'), scatter_dimension=0, tile...  357 us
    all_to_all x1, waiting for transfers between devices, per_device(): lax.all_to_all(grad_inputs.astype(jnp.bfloat16), 'fsdp', split_axis=0, co...  147 us
    all_to_all x1, waiting for transfers between devices, per_device(): lax.all_to_all(send_grads, 'fsdp', split_axis=0, concat_axis=0, tiled=True)  106 us
    all_to_all x1, waiting for transfers between devices, per_device(): lax.all_to_all(send_rows, 'fsdp', split_axis=0, concat_axis=0, tiled=True)  104 us
    all_to_all x1, waiting for transfers between devices, per_device(): lax.all_to_all(expert_out, 'fsdp', split_axis=0, concat_axis=0, tiled=True)  84.6 us
  transfers between devices with their start and end apart: 23, of which 17 were waited for; matrix products, arithmetic and copies ran while one was open for 11% of the time, Pallas kernels for 0%

commit v1 on v0

--- a/solution.py
+++ b/solution.py
@@ -1,6 +1,10 @@
+import functools
+
 import jax
 import jax.numpy as jnp
 from jax import lax
+from jax.experimental import pallas as pl
+from jax.experimental.pallas import tpu as pltpu
 from jax.sharding import PartitionSpec as P
 
 HEADS = 16
@@ -49,7 +53,7 @@
     return chosen / jnp.sum(chosen, axis=-1, keepdims=True)
 
 
-def per_device(
+def per_device_gathered(
     tokens,
     cotangent,
     routes,
@@ -393,6 +397,526 @@
     )
 
 
+def small_bits(size):
+    return max(size - 1, 0).bit_length()
+
+
+def exchange_pairs(size, bit):
+    return [(i, i ^ bit) for i in range(size)]
+
+
+class Ring:
+    def __init__(self, size):
+        self.size = size
+        self.half = size // 2
+        self.order = list(range(0, size, 2)) + list(range(size - 1, 0, -2))
+        place = [self.order.index(i) for i in range(size)]
+        mine = lax.axis_index("fsdp")
+        rank = jnp.asarray(place, jnp.int32)[mine]
+        self.slot_device = jnp.asarray(self.order, jnp.int32)[
+            (rank + jnp.arange(size, dtype=jnp.int32)) % size
+        ]
+        self.device_slot = (jnp.asarray(place, jnp.int32) - rank) % size
+        self.up = [(self.order[i], self.order[(i + 1) % size]) for i in range(size)]
+        self.down = [(self.order[i], self.order[i - 1]) for i in range(size)]
+
+    def forward(self, values):
+        return lax.ppermute(values, "fsdp", self.up)
+
+    def backward(self, values):
+        return lax.ppermute(values, "fsdp", self.down)
+
+    def sum_rows(self, values):
+        blocks = values.reshape(values.shape[0], self.size, -1)
+        blocks = pair_sum(blocks[:, self.device_slot], "fsdp", self.size)
+        return blocks[:, self.slot_device].reshape(values.shape)
+
+    def gather(self, block):
+        blocks = [None] * self.size
+        blocks[0] = block
+        from_low, from_high = block, block
+        for step in range(1, self.half):
+            from_low = self.forward(from_low)
+            from_high = self.backward(from_high)
+            blocks[-step] = from_low
+            blocks[step] = from_high
+        middle = block.shape[0] // 2
+        blocks[self.half] = jnp.concatenate(
+            [self.forward(from_low[:middle]), self.backward(from_high[middle:])], axis=0
+        )
+        return blocks
+
+    def reduce(self, blocks):
+        middle = blocks[0].shape[0] // 2
+        half = self.half
+        rising = self.forward(blocks[half][:middle])
+        falling = self.backward(blocks[half][middle:])
+        for step in range(half - 1, 0, -1):
+            upper, lower = blocks[step], blocks[-step]
+            if step == half - 1:
+                upper = jnp.concatenate([upper[:middle] + rising, upper[middle:]], axis=0)
+                lower = jnp.concatenate([lower[:middle], lower[middle:] + falling], axis=0)
+            else:
+                upper = upper + rising
+                lower = lower + falling
+            rising = self.forward(upper)
+            falling = self.backward(lower)
+        return (
+            blocks[0].astype(jnp.float32)
+            + rising.astype(jnp.float32)
+            + falling.astype(jnp.float32)
+        )
+
+
+def pair_sum(values, axis, size):
+    bit = 1
+    while bit < size:
+        values = values + lax.ppermute(values, axis, exchange_pairs(size, bit))
+        bit *= 2
+    return values
+
+
+def pair_gather(values, axis, size):
+    mine = lax.axis_index(axis)
+    values = values[None]
+    bit = 1
+    while bit < size:
+        other = lax.ppermute(values, axis, exchange_pairs(size, bit))
+        upper = (mine & bit) != 0
+        values = jnp.where(
+            upper,
+            jnp.concatenate([other, values], axis=0),
+            jnp.concatenate([values, other], axis=0),
+        )
+        bit *= 2
+    return values
+
+
+def pair_scatter(values, axis, size):
+    mine = lax.axis_index(axis)
+    bit = size // 2
+    while bit >= 1:
+        span = values.shape[0] // 2
+        upper = (mine & bit) != 0
+        low_half, high_half = values[:span], values[span:]
+        kept = jnp.where(upper, high_half, low_half)
+        sent = jnp.where(upper, low_half, high_half)
+        values = kept + lax.ppermute(sent, axis, exchange_pairs(size, bit))
+        bit //= 2
+    return values
+
+
+def share_relative(block, size):
+    blocks = [block]
+    bit = size // 2
+    while bit >= 1:
+        blocks = blocks + [
+            lax.ppermute(piece, "dp", exchange_pairs(size, bit)) for piece in blocks
+        ]
+        bit //= 2
+    order = [0]
+    bit = size // 2
+    while bit >= 1:
+        order = order + [i ^ bit for i in order]
+        bit //= 2
+    placed = [None] * size
+    for piece, index in zip(blocks, order):
+        placed[index] = piece
+    return placed
+
+
+def combine_relative(blocks, size):
+    bit = 1
+    held = dict(enumerate(blocks))
+    while bit < size:
+        kept = {}
+        for index in held:
+            if index & bit == 0:
+                other = lax.ppermute(
+                    held[index | bit].astype(jnp.bfloat16), "dp", exchange_pairs(size, bit)
+                )
+                kept[index] = held[index].astype(jnp.float32) + other.astype(jnp.float32)
+        held = kept
+        bit *= 2
+    return held[0]
+
+
+def attend_kernel(scale, chunk, pos_row, pos_col, query, key, value, out, lse):
+    keys, values = key[...], value[...]
+    key_pos = pos_row[...]
+    for begin in range(0, query.shape[0], chunk):
+        rows = pl.ds(begin, chunk)
+        scores = (
+            lax.dot_general(
+                query[rows, :], keys, (((1,), (1,)), ((), ())), preferred_element_type=jnp.float32
+            )
+            * scale
+        )
+        scores = jnp.where(key_pos <= pos_col[rows, :], scores, far_low)
+        top = jnp.max(scores, axis=-1, keepdims=True)
+        weights = jnp.exp(scores - top)
+        total = jnp.sum(weights, axis=-1, keepdims=True)
+        mixed = jnp.dot(weights.astype(jnp.bfloat16), values, preferred_element_type=jnp.float32)
+        out[rows, :] = mixed / total
+        lse[rows, :] = top + jnp.log(total)
+
+
+def attend(query, key, value, positions, head_dim):
+    tokens, width = query.shape
+    heads = width // head_dim
+    whole = pl.BlockSpec((tokens, head_dim), lambda h: (0, h))
+    return pl.pallas_call(
+        functools.partial(attend_kernel, head_dim ** (-0.5), min(256, tokens)),
+        grid=(heads,),
+        in_specs=[
+            pl.BlockSpec((1, tokens), lambda h: (0, 0)),
+            pl.BlockSpec((tokens, 1), lambda h: (0, 0)),
+            whole,
+            whole,
+            whole,
+        ],
+        out_specs=[whole, pl.BlockSpec((None, tokens, 1), lambda h: (h, 0, 0))],
+        out_shape=[
+            jax.ShapeDtypeStruct((tokens, width), jnp.float32),
+            jax.ShapeDtypeStruct((heads, tokens, 1), jnp.float32),
+        ],
+        name="attend",
+    )(positions[None, :], positions[:, None], query, key, value)
+
+
+def attend_back_kernel(
+    scale, chunk, pos_row, pos_col, query, key, value, grad, mixed, lse, d_query, d_key, d_value
+):
+    keys, values = key[...], value[...]
+    key_pos = pos_row[...]
+    rows_first = (((0,), (0,)), ((), ()))
+    for begin in range(0, query.shape[0], chunk):
+        rows = pl.ds(begin, chunk)
+        queries, grads = query[rows, :], grad[rows, :]
+        scores = (
+            lax.dot_general(
+                queries, keys, (((1,), (1,)), ((), ())), preferred_element_type=jnp.float32
+            )
+            * scale
+        )
+        probs = jnp.where(
+            key_pos <= pos_col[rows, :], jnp.exp(scores - lse[rows, :]), 0.0
+        )
+        grad_probs = lax.dot_general(
+            grads, values, (((1,), (1,)), ((), ())), preferred_element_type=jnp.float32
+        )
+        delta = jnp.sum(grads.astype(jnp.float32) * mixed[rows, :], axis=-1, keepdims=True)
+        grad_scores = (probs * (grad_probs - delta)).astype(jnp.bfloat16)
+        d_query[rows, :] = (
+            jnp.dot(grad_scores, keys, preferred_element_type=jnp.float32) * scale
+        )
+        part_key = (
+            lax.dot_general(grad_scores, queries, rows_first, preferred_element_type=jnp.float32)
+            * scale
+        )
+        part_value = lax.dot_general(
+            probs.astype(jnp.bfloat16), grads, rows_first, preferred_element_type=jnp.float32
+        )
+        if begin == 0:
+            d_key[...] = part_key
+            d_value[...] = part_value
+        else:
+            d_key[...] += part_key
+            d_value[...] += part_value
+
+
+def attend_back(query, key, value, grad, mixed, lse, positions, head_dim):
+    tokens, width = query.shape
+    heads = width // head_dim
+    whole = pl.BlockSpec((tokens, head_dim), lambda h: (0, h))
+    result = jax.ShapeDtypeStruct((tokens, width), jnp.float32)
+    return pl.pallas_call(
+        functools.partial(attend_back_kernel, head_dim ** (-0.5), min(256, tokens)),
+        grid=(heads,),
+        in_specs=[
+            pl.BlockSpec((1, tokens), lambda h: (0, 0)),
+            pl.BlockSpec((tokens, 1), lambda h: (0, 0)),
+            whole,
+            whole,
+            whole,
+            whole,
+            whole,
+            pl.BlockSpec((None, tokens, 1), lambda h: (h, 0, 0)),
+        ],
+        out_specs=[whole, whole, whole],
+        out_shape=[result, result, result],
+        name="attend_back",
+    )(positions[None, :], positions[:, None], query, key, value, grad, mixed, lse)
+
+
+def turn(values, cosine, sine, heads):
+    rows, width = values.shape
+    parts = values.reshape(rows, heads, 2, -1)
+    first, second = parts[:, :, 0], parts[:, :, 1]
+    cosine, sine = cosine[:, None, :], sine[:, None, :]
+    return jnp.stack(
+        [first * cosine - second * sine, second * cosine + first * sine], axis=2
+    ).reshape(rows, width)
+
+
+def per_device(
+    tokens,
+    cotangent,
+    routes,
+    w_query,
+    w_key,
+    w_value,
+    w_output,
+    w_router,
+    gain_attn,
+    gain_query,
+    gain_key,
+    gain_ffn,
+    expert_gate,
+    expert_up,
+    expert_down,
+):
+    rows, width = tokens.shape
+    size = lax.axis_size("fsdp")
+    dp_size = lax.axis_size("dp")
+    head_dim = width // HEADS
+    own_heads = HEADS // size
+    part = own_heads * head_dim
+    own_rows = w_query.shape[0]
+    local_experts = expert_gate.shape[0]
+    num_experts = local_experts * size
+    group = part // own_rows
+    span = rows * size
+    f_index = lax.axis_index("fsdp")
+    d_index = lax.axis_index("dp")
+    low, f32 = jnp.bfloat16, jnp.float32
+    ring = Ring(size)
+    positions = (
+        ring.slot_device[:, None] * rows + jnp.arange(rows, dtype=jnp.int32)[None, :]
+    ).reshape(span)
+    dp_flat = ("dp", "fsdp")
+    to_rows = []
+    for d in range(dp_size):
+        for f in range(size):
+            flat = d * size + f
+            to_rows.append((flat, (flat % group) * size + flat // group))
+    from_rows = [(b, a) for a, b in to_rows]
+
+    token_blocks = ring.gather(tokens)
+    x_all = jnp.concatenate(token_blocks, axis=0).astype(f32)
+
+    small = jnp.concatenate(
+        [w_router, gain_attn[:, None], gain_query[:, None], gain_key[:, None], gain_ffn[:, None]],
+        axis=1,
+    )
+    small = pair_gather(pair_gather(small, "fsdp", size), "dp", dp_size)
+    small = small.reshape(width, -1)
+    router = small[:, :num_experts]
+    gains = small[:, num_experts:].astype(f32)
+    gain_in, gain_q, gain_k, gain_mid = (gains[:, i] for i in range(4))
+    gain_q = lax.dynamic_slice_in_dim(gain_q, f_index * part, part)
+    gain_k = lax.dynamic_slice_in_dim(gain_k, f_index * part, part)
+
+    packed = jnp.stack(
+        [w.reshape(own_rows, size, part) for w in (w_query, w_key, w_value)], axis=2
+    ).transpose(1, 0, 2, 3)
+    packed = lax.all_to_all(packed, "fsdp", split_axis=0, concat_axis=0, tiled=True)
+    packed = packed.reshape(size * own_rows, 3 * part)
+    w_in = jnp.zeros((width, 3 * part), low)
+    for index, piece in enumerate(share_relative(packed, dp_size)):
+        w_in = lax.dynamic_update_slice_in_dim(
+            w_in, piece, (d_index ^ index) * packed.shape[0], 0
+        )
+    out_rows = lax.ppermute(w_output, dp_flat, to_rows)
+    w_out = jnp.zeros((part, width), low)
+    for index, piece in enumerate(share_relative(out_rows, dp_size)):
+        w_out = lax.dynamic_update_slice_in_dim(w_out, piece, (d_index ^ index) * own_rows, 0)
+
+    down_w = jnp.concatenate(share_relative(expert_down, dp_size), axis=2)
+    gate_w = jnp.concatenate(share_relative(expert_gate, dp_size), axis=2)
+    up_w = jnp.concatenate(share_relative(expert_up, dp_size), axis=2)
+
+    in_factor = lax.rsqrt(jnp.mean(x_all * x_all, axis=-1, keepdims=True) + epsilon)
+    normed = (x_all * in_factor * gain_in).astype(low)
+    raw = jnp.dot(normed, w_in, preferred_element_type=f32)
+    q_raw, k_raw, v_raw = raw[:, :part], raw[:, part : 2 * part], raw[:, 2 * part :]
+    squares = jnp.stack([jnp.sum(q_raw * q_raw, axis=-1), jnp.sum(k_raw * k_raw, axis=-1)])
+    squares = ring.sum_rows(squares)
+    factors = lax.rsqrt(squares / width + epsilon)
+    q_factor, k_factor = factors[0][:, None], factors[1][:, None]
+    half_dim = head_dim // 2
+    inv_freq = rope_base ** (-(jnp.arange(half_dim, dtype=f32) * 2.0) / head_dim)
+    angles = positions.astype(f32)[:, None] * inv_freq[None, :]
+    cosine, sine = jnp.cos(angles), jnp.sin(angles)
+    q_low = turn(q_raw * q_factor * gain_q, cosine, sine, own_heads).astype(low)
+    k_low = turn(k_raw * k_factor * gain_k, cosine, sine, own_heads).astype(low)
+    v_low = v_raw.astype(low)
+    mixed, lse = attend(q_low, k_low, v_low, positions, head_dim)
+    mixed_low = mixed.astype(low)
+    attn_part = jnp.dot(mixed_low, w_out, preferred_element_type=f32).astype(low)
+    attn_blocks = [attn_part[k * rows : (k + 1) * rows] for k in range(size)]
+    resid_mid = tokens.astype(f32) + ring.reduce(attn_blocks)
+
+    mid_factor = lax.rsqrt(jnp.mean(resid_mid * resid_mid, axis=-1, keepdims=True) + epsilon)
+    mid_low = (resid_mid * mid_factor * gain_mid).astype(low)
+    mid_all = jnp.concatenate(ring.gather(mid_low), axis=0)
+    logits = jnp.dot(mid_low, router, preferred_element_type=f32)
+    chosen_mask = jnp.any(
+        routes[:, :, None] == jnp.arange(num_experts, dtype=jnp.int32)[None, None, :], axis=1
+    )
+    router_probs = jax.nn.softmax(logits, axis=-1)
+    chosen = jnp.where(chosen_mask, router_probs, 0.0)
+    chosen_sum = jnp.sum(chosen, axis=-1, keepdims=True)
+    gates = chosen / chosen_sum
+    gates_all = pair_gather(gates, "fsdp", size)[ring.slot_device]
+    own_gates = lax.dynamic_slice_in_dim(
+        gates_all.reshape(span, num_experts), f_index * local_experts, local_experts, 1
+    ).T[:, :, None]
+    cot_all = jnp.concatenate(ring.gather(cotangent), axis=0)
+    back_act = jnp.einsum("td,edh->eth", cot_all, down_w, preferred_element_type=f32)
+    gate_hid = jnp.einsum("td,edh->eth", mid_all, gate_w, preferred_element_type=f32)
+    up_hid = jnp.einsum("td,edh->eth", mid_all, up_w, preferred_element_type=f32)
+    sig = jax.nn.sigmoid(gate_hid)
+    silu = gate_hid * sig
+    act = (silu * up_hid).astype(low)
+    grad_gates = jnp.sum(act.astype(f32) * back_act, axis=-1)
+    grad_act = own_gates * back_act
+    d_gate = (grad_act * up_hid * (sig * (1.0 + gate_hid * (1.0 - sig)))).astype(low)
+    d_up = (grad_act * silu).astype(low)
+    act_gated = (own_gates * act.astype(f32)).astype(low)
+    grad_in = (
+        jnp.einsum("eth,edh->td", d_gate, gate_w, preferred_element_type=f32)
+        + jnp.einsum("eth,edh->td", d_up, up_w, preferred_element_type=f32)
+    ).astype(low)
+    expert_out = jnp.einsum("eth,edh->etd", act, down_w, preferred_element_type=f32).astype(low)
+    moe_part = jnp.sum(own_gates * expert_out.astype(f32), axis=0).astype(low)
+
+    by_device = grad_gates.reshape(local_experts, size, rows)[:, ring.device_slot]
+    gates_back = pair_gather(by_device, "fsdp", size)
+    gates_back = lax.dynamic_slice_in_dim(gates_back, f_index, 1, 2)
+    gates_back = gates_back.reshape(num_experts, rows).T
+    inner = jnp.sum(jnp.where(chosen_mask, gates_back * gates, 0.0), axis=-1, keepdims=True)
+    grad_probs = jnp.where(chosen_mask, (gates_back - inner) / chosen_sum, 0.0)
+    grad_logits = router_probs * (
+        grad_probs - jnp.sum(router_probs * grad_probs, axis=-1, keepdims=True)
+    )
+    grad_logits_low = grad_logits.astype(low)
+    grad_router = lax.dot_general(
+        mid_low, grad_logits_low, (((0,), (0,)), ((), ())), preferred_element_type=f32
+    )
+    grad_mid = ring.reduce([grad_in[k * rows : (k + 1) * rows] for k in range(size)])
+    grad_mid = grad_mid + lax.dot_general(
+        grad_logits_low, router, (((1,), (1,)), ((), ())), preferred_element_type=f32
+    )
+    grad_out = cotangent.astype(f32)
+    scaled = grad_mid * gain_mid
+    grad_resid = (
+        grad_out
+        + mid_factor * scaled
+        - resid_mid * mid_factor**3 * jnp.mean(scaled * resid_mid, axis=-1, keepdims=True)
+    )
+    grad_gain_mid = jnp.sum(grad_mid * resid_mid * mid_factor, axis=0)
+    grad_attn_out = jnp.concatenate(ring.gather(grad_resid.astype(low)), axis=0)
+    layer_out = (
+        resid_mid + ring.reduce([moe_part[k * rows : (k + 1) * rows] for k in range(size)])
+    ).astype(low)
+
+    def weight_grad(left, right):
+        whole = jnp.einsum("td,eth->edh", left, right, preferred_element_type=f32).astype(low)
+        step = whole.shape[2] // dp_size
+        return combine_relative(
+            [whole[:, :, k * step : (k + 1) * step] for k in range(dp_size)], dp_size
+        )
+
+    grad_down_w = weight_grad(cot_all, act_gated)
+    grad_gate_w = weight_grad(mid_all, d_gate)
+    grad_up_w = weight_grad(mid_all, d_up)
+
+    def to_rows_sum(values, step):
+        pieces = [
+            lax.dynamic_slice_in_dim(values, (d_index ^ k) * step, step, 0) for k in range(dp_size)
+        ]
+        return combine_relative(pieces, dp_size)
+
+    grad_w_out = lax.dot_general(
+        mixed_low, grad_attn_out, (((0,), (0,)), ((), ())), preferred_element_type=f32
+    )
+    grad_w_out = lax.ppermute(
+        to_rows_sum(grad_w_out, own_rows), dp_flat, from_rows
+    )
+    grad_mixed = lax.dot_general(
+        grad_attn_out, w_out, (((1,), (1,)), ((), ())), preferred_element_type=f32
+    ).astype(low)
+    d_query, d_key, d_value = attend_back(
+        q_low, k_low, v_low, grad_mixed, mixed, lse, positions, head_dim
+    )
+    e_query = turn(d_query, cosine, -sine, own_heads)
+    e_key = turn(d_key, cosine, -sine, own_heads)
+    g_query, g_key = e_query * gain_q, e_key * gain_k
+    dots = jnp.stack([jnp.sum(g_query * q_raw, axis=-1), jnp.sum(g_key * k_raw, axis=-1)])
+    dots = ring.sum_rows(dots) / width
+    grad_gain_q = jnp.sum(e_query * q_raw * q_factor, axis=0)
+    grad_gain_k = jnp.sum(e_key * k_raw * k_factor, axis=0)
+    grad_raw = jnp.concatenate(
+        [
+            q_factor * g_query - q_raw * q_factor**3 * dots[0][:, None],
+            k_factor * g_key - k_raw * k_factor**3 * dots[1][:, None],
+            d_value,
+        ],
+        axis=1,
+    ).astype(low)
+    grad_w_in = lax.dot_general(
+        normed, grad_raw, (((0,), (0,)), ((), ())), preferred_element_type=f32
+    )
+    grad_normed_part = lax.dot_general(
+        grad_raw, w_in, (((1,), (1,)), ((), ())), preferred_element_type=f32
+    )
+    grad_gain_in = jnp.sum(grad_normed_part * x_all * in_factor, axis=0)
+    grad_normed_low = grad_normed_part.astype(low)
+    grad_normed = ring.reduce([grad_normed_low[k * rows : (k + 1) * rows] for k in range(size)])
+    own_x = tokens.astype(f32)
+    own_factor = in_factor[:rows]
+    scaled_in = grad_normed * gain_in
+    grad_tokens = (
+        grad_resid
+        + own_factor * scaled_in
+        - own_x * own_factor**3 * jnp.mean(scaled_in * own_x, axis=-1, keepdims=True)
+    )
+    grad_w_in = to_rows_sum(grad_w_in, size * own_rows).astype(low)
+    grad_w_in = grad_w_in.reshape(size, own_rows, 3 * part)
+    grad_w_in = lax.all_to_all(grad_w_in, "fsdp", split_axis=0, concat_axis=0, tiled=True)
+    grad_w_in = grad_w_in.reshape(size, own_rows, 3, part).transpose(2, 1, 0, 3)
+    grad_w_in = grad_w_in.reshape(3, own_rows, width).astype(f32)
+
+    sums = jnp.concatenate([grad_router, grad_gain_mid[:, None], grad_gain_in[:, None]], axis=1)
+    sums = pair_scatter(sums, "fsdp", size)
+    sums = jnp.concatenate([sums, grad_gain_q[:, None], grad_gain_k[:, None]], axis=1)
+    sums = pair_scatter(sums, "dp", dp_size)
+    sums = lax.ppermute(sums, dp_flat, from_rows)
+    return (
+        layer_out,
+        grad_tokens,
+        grad_w_in[0],
+        grad_w_in[1],
+        grad_w_in[2],
+        grad_w_out,
+        sums[:, :num_experts],
+        sums[:, num_experts + 1],
+        sums[:, num_experts + 2],
+        sums[:, num_experts + 3],
+        sums[:, num_experts],
+        grad_gate_w,
+        grad_up_w,
+        grad_down_w,
+    )
+
+
+def splits_evenly(mesh):
+    size, dp_size = mesh.shape["fsdp"], mesh.shape["dp"]
+    powers = size & (size - 1) == 0 and dp_size & (dp_size - 1) == 0
+    return powers and size >= 4 and HEADS % size == 0
+
+
 def solution(mesh):
     in_specs = (
         P(("dp", "fsdp"), None),
@@ -428,5 +952,6 @@
         P("fsdp", None, "dp"),
     )
     return jax.shard_map(
-        per_device, mesh=mesh, in_specs=in_specs, out_specs=out_specs, check_vma=False
-    )
+        per_device if splits_evenly(mesh) else per_device_gathered,
+        mesh=mesh, in_specs=in_specs, out_specs=out_specs, check_vma=False
+    )

time: 2980 us -> 892 us (0.30)
  waiting for transfers between devices: 2340 us -> 373 us
  blocking collectives: 213 us -> 0 us
  starting transfers between devices: 21 us -> 150 us
  matrix products: 235 us -> 160 us
  local copies, waits for them, and re-layouts: 75.3 us -> 114 us
    reduce_scatter x7 -> x0, waiting for transfers between devices: 1590 us -> none  [the longest x1 360 us: per_device(): lax.psum_scatter(grad_wv, ('dp', 'fsdp'), scatter_dimension=0, tiled=True)]
    all_to_all x4 -> x2, waiting for transfers between devices: 441 us -> 0.01 us  [the longest x1 0.01 us: per_device(): lax.all_to_all(packed, 'fsdp', split_axis=0, concat_axis=0, tiled=True)]
    ppermute x0 -> x119, waiting for transfers between devices: none -> 373 us  [the longest x32 130 us: backward(): return lax.ppermute(values, 'fsdp', self.down)]
    all_gather x11 -> x0, waiting for transfers between devices: 303 us -> none  [the longest x1 72.7 us: per_device(): lax.all_gather(w_key, ('dp', 'fsdp'), axis=0, tiled=True)]
    ppermute x0 -> x119, starting transfers between devices: none -> 142 us  [the longest x32 41.2 us: backward(): return lax.ppermute(values, 'fsdp', self.down)]
    all_gather x3 -> x0, blocking collectives: 133 us -> none  [the longest x1 68.5 us: per_device(): lax.all_gather(w_router, ('dp', 'fsdp'), axis=0, tiled=True)]
    unnamed x2 -> x0, blocking collectives: 80.4 us -> none
    dot_general x30 -> x18, matrix products: 233 us -> 160 us  [the longest x3 34.2 us: weight_grad(): jnp.einsum('td,eth->edh', left, right, preferred_element_type=f32)]
  transfers between devices with their start and end apart: 23 -> 121, of which waited for: 17 -> 63; matrix products, arithmetic and copies ran while one was open for 11% -> 28% of each run, Pallas kernels for 0% -> 2%
where the time goes in v1:
time: 892 us; the launch traced here: 886 us
  waiting for transfers between devices  373 us (42%)
  matrix products  160 us (18%)
  starting transfers between devices  150 us (17%)
  local copies, waits for them, and re-layouts  114 us (13%)
  other arithmetic  68.3 us (8%)
  Pallas kernels  16.7 us (2%)
    ppermute x32, waiting for transfers between devices, backward(): return lax.ppermute(values, 'fsdp', self.down)  130 us
    ppermute x32, waiting for transfers between devices, forward(): return lax.ppermute(values, 'fsdp', self.up)  98.9 us
    ppermute x15, waiting for transfers between devices, combine_relative(): lax.ppermute(held[index | bit].astype(jnp.bfloat16), 'dp', exchange_pairs...  63.7 us
    unnamed x210, local copies, waits for them, and re-layouts  63.1 us
    ppermute x32, starting transfers between devices, backward(): return lax.ppermute(values, 'fsdp', self.down)  41.2 us
    ppermute x32, starting transfers between devices, forward(): return lax.ppermute(values, 'fsdp', self.up)  35.7 us
    ppermute x15, waiting for transfers between devices, share_relative(): lax.ppermute(piece, 'dp', exchange_pairs(size, bit))  34.4 us
    dot_general x3, matrix products, weight_grad(): jnp.einsum('td,eth->edh', left, right, preferred_element_type=f32)  34.2 us
  transfers between devices with their start and end apart: 121, of which 63 were waited for; matrix products, arithmetic and copies ran while one was open for 28% of the time, Pallas kernels for 2%

profile of v1, /device:TPU:0, one launch (start us, length us, event | category | flops | bytes accessed | tf_op | source)
XLA Modules:
  0.0 885.8 jit_solution(9185213990299969757)
XLA Ops:
  13.5 4.9 all-to-all-start
  22.9 7.4 collective-permute-done.8
  31.2 8.1 collective-permute-done.9
  58.6 10.9 %collective-permute-start.49 = (bf16[2,2048,256]{2,1,0:T(8,128)(2,1)}, bf16[2,2048,256]{2,1,0:T(8,128)(2,1)}, u32[]{:S(2)}, u32[]{:S(2)}) collective-permute-start(bf16[2,2048,256]{2,1,0:T(8,128)(2,1)} %param.32), channel_id=1, source_target_pairs={{0,16},{8,24},{16,0},{24,8},{1,17},{9,25},{17,1},{25,9},{2,18},{10... | collective-permute-start | bytes 6291464 | tf_op jit(solution)/shard_map/ppermute | solution.py:514
  92.1 4.2 collective-permute-start.7
  100.2 7.7 collective-permute-start.14
  109.1 23.6 %collective-permute-done.14 = bf16[512,768]{1,0:T(8,128)(2,1)S(1)} collective-permute-done((bf16[512,768]{1,0:T(8,128)(2,1)S(1)}, bf16[512,768]{1,0:T(8,128)(2,1)S(1)}, u32[]{:S(2)}, u32[]{:S(2)}) %collective-permute-start.14) | collective-permute-done | bytes 786464 | tf_op jit(solution)/shard_map/ppermute | solution.py:514
  135.5 7.2 collective-permute-done.21
  170.0 7.0 attend.1
  184.5 4.7 collective-permute-done.23
  205.6 15.6 %collective-permute-done.24 = bf16[128,2048]{1,0:T(8,128)(2,1)S(1)} collective-permute-done((bf16[128,2048]{1,0:T(8,128)(2,1)S(1)}, bf16[128,2048]{1,0:T(8,128)(2,1)S(1)}, u32[]{:S(2)}, u32[]{:S(2)}) %collective-permute-start.24) | collective-permute-done | bytes 524320 | tf_op jit(solution)/shard_map/ppermute | solution.py:424
  242.0 9.0 %collective-permute-done.29 = bf16[128,2048]{1,0:T(8,128)(2,1)S(1)} collective-permute-done((bf16[128,2048]{1,0:T(8,128)(2,1)S(1)}, bf16[128,2048]{1,0:T(8,128)(2,1)S(1)}, u32[]{:S(2)}, u32[]{:S(2)}) %collective-permute-start.29) | collective-permute-done | bytes 524320 | tf_op jit(solution)/shard_map/ppermute | solution.py:427
  257.5 6.1 collective-permute-done.30
  273.4 4.9 collective-permute-done.32
  283.5 7.9 collective-permute-done.37
  298.9 4.7 collective-permute-done.38
  305.5 4.1 collective-permute-done.42
  311.2 4.8 collective-permute-done.39
  326.1 14.7 %fusion.24 = f32[2,1024,1024]{2,1,0:T(8,128)} fusion(bf16[1024,2048]{1,0:T(8,128)(2,1)} %constant_dynamic-update-slice_fusion.9, bf16[2,2048,256]{1,2,0:T(8,128)(2,1)} %collective-permute-done.36, bf16[2,2048,256]{1,2,0:T(8,128)(2,1)} %collective-permute-done.35, bf16[2,2048,256]{1,2,0:T(8,128)(2,1)} %collective-permute-done.34, ...), kind=kOutput, calls=%fused_computation.49 | convolution fusion | flops 8623489024 | bytes 20971520 | tf_op jit(solution)/shard_map/td,edh->eth/dot_general | solution.py:777
  342.2 16.7 %fusion.22 = f32[2,1024,1024]{2,1,0:T(8,128)} fusion(bf16[1024,2048]{1,0:T(8,128)(2,1)S(1)} %copy-done.49, bf16[2,2048,256]{1,2,0:T(8,128)(2,1)S(1)} %collective-permute-done.47, bf16[2,2048,256]{1,2,0:T(8,128)(2,1)} %collective-permute-done.46, bf16[2,2048,256]{1,2,0:T(8,128)(2,1)S(1)} %collective-permute-done.45, bf16[2,2048,256]{1,2,0:T(8,128)(2,1)} %copy.227), kind=kOutput, calls=%fused_computation.47 | convolution fusion | flops 8623489024 | bytes 20971520 | tf_op jit(solution)/shard_map/td,edh->eth/dot_general | solution.py:778
  358.9 24.6 %fusion = (f32[2,1024]{1,0:T(2,128)S(1)}, bf16[2,1024,1024]{1,2,0:T(8,128)(2,1)}, bf16[2,1024,1024]{1,2,0:T(8,128)(2,1)}, bf16[2,1024,1024]{1,2,0:T(8,128)(2,1)}) fusion(f32[2,1024,1024]{2,1,0:T(8,128)} %fusion.22, f32[2,1024,1024]{2,1,0:T(8,128)} %fusion.24, f32[2,1024]{1,0:T(2,128)S(1)} %dynamic-slice_bitcast_fusion, ...), kind=kOutput, calls=%fused_computation.13 | convolution fusion | flops 8629778432 | bytes 41959424 | tf_op jit(solution)/shard_map/td,edh->eth/dot_general | solution.py:776
  383.5 13.8 %convert_bitcast_fusion = bf16[2,2048,1024]{1,2,0:T(8,128)(2,1)} fusion(bf16[2,1024,1024]{1,2,0:T(8,128)(2,1)} %get-tuple-element.122, bf16[1024,2048]{1,0:T(8,128)(2,1)} %constant_dynamic-update-slice_fusion.22, f32[2,1024]{1,0:T(2,128)S(1)} %dynamic-slice_bitcast_fusion), kind=kOutput, calls=%fused_computation.38 | convolution fusion | flops 8600420352 | bytes 16785408 | tf_op jit(solution)/shard_map/td,eth->edh/dot_general | solution.py:825
  397.4 18.0 %multiply_reduce_fusion = bf16[1024,2048]{1,0:T(8,128)(2,1)} fusion(f32[2,1024]{1,0:T(2,128)S(1)} %dynamic-slice_bitcast_fusion, bf16[2,1024,1024]{1,2,0:T(8,128)(2,1)} %get-tuple-element.122, bf16[2,2048,1024]{2,1,0:T(8,128)(2,1)} %copy-done.38), kind=kOutput, calls=%fused_computation.7 | convolution fusion | flops 8604614656 | bytes 16785408 | tf_op jit(solution)/shard_map/eth,edh->etd/dot_general | solution.py:791
  415.3 5.1 fusion.66
  421.6 9.4 %convert_bitcast_fusion.1 = bf16[2,2048,1024]{1,2,0:T(8,128)(2,1)S(1)} fusion(bf16[2,1024,1024]{1,2,0:T(8,128)(2,1)S(1)} %copy-done.76, bf16[1024,2048]{1,0:T(8,128)(2,1)S(1)} %copy-done.50), kind=kOutput, calls=%fused_computation.39 | convolution fusion | flops 8594128896 | bytes 16777216 | tf_op jit(solution)/shard_map/td,eth->edh/dot_general | solution.py:825
  436.6 11.0 %convert_bitcast_fusion.2 = bf16[2,2048,1024]{1,2,0:T(8,128)(2,1)} fusion(bf16[2,1024,1024]{1,2,0:T(8,128)(2,1)S(1)} %copy-done.77, bf16[1024,2048]{1,0:T(8,128)(2,1)S(1)} %copy-done.50), kind=kOutput, calls=%fused_computation.40 | convolution fusion | flops 8594128896 | bytes 16777216 | tf_op jit(solution)/shard_map/td,eth->edh/dot_general | solution.py:825
  451.5 15.0 %fusion.27 = f32[1024,2048,1]{1,0,2:T(8,128)} fusion(bf16[2,1024,1024]{1,2,0:T(8,128)(2,1)} %get-tuple-element.127, bf16[2,2048,256]{1,2,0:T(8,128)(2,1)} %collective-permute-done.36, bf16[2,2048,256]{1,2,0:T(8,128)(2,1)} %collective-permute-done.35, bf16[2,2048,256]{1,2,0:T(8,128)(2,1)} %collective-permute-done.34, bf16[2,2048,256]{1,2,0:T(8,128)(2,1)} %copy.224), kind=kOutput, calls=%fused_computation.67 | convolution fusion | flops 8623489024 | bytes 20971520 | tf_op jit(solution)/shard_map/eth,edh->td/dot_general | solution.py:788
  466.5 14.1 %fusion.7 = bf16[1024,2048]{1,0:T(8,128)(2,1)S(1)} fusion(f32[1024,2048,1]{1,0,2:T(8,128)} %fusion.27, bf16[2,1024,1024]{1,2,0:T(8,128)(2,1)} %get-tuple-element.128, bf16[2,2048,256]{1,2,0:T(8,128)(2,1)} %copy-done.74, bf16[2,2048,256]{1,2,0:T(8,128)(2,1)} %collective-permute-done.46, bf16[2,2048,256]{1,2,0:T(8,128)(2,1)} %copy-done.73, ...), kind=kOutput, calls=%fused_computation.23 | convolution fusion | flops 8627683328 | bytes 25165824 | tf_op jit(solution)/shard_map/eth,edh->td/dot_general | solution.py:789
  483.3 4.7 collective-permute-done.67
  490.4 10.9 %collective-permute-done.71 = bf16[64,2048]{1,0:T(8,128)(2,1)S(1)} collective-permute-done((bf16[64,2048]{1,0:T(8,128)(2,1)S(1)}, bf16[64,2048]{1,0:T(8,128)(2,1)S(1)}, u32[]{:S(2)}, u32[]{:S(2)}) %collective-permute-start.71) | collective-permute-done | bytes 262176 | tf_op jit(solution)/shard_map/ppermute | solution.py:427
  503.1 9.6 %collective-permute-done.68 = bf16[128,2048]{1,0:T(8,128)(2,1)S(1)} collective-permute-done((bf16[128,2048]{1,0:T(8,128)(2,1)S(1)}, bf16[128,2048]{1,0:T(8,128)(2,1)S(1)}, u32[]{:S(2)}, u32[]{:S(2)}) %collective-permute-start.68) | collective-permute-done | bytes 524320 | tf_op jit(solution)/shard_map/ppermute | solution.py:424
  516.6 6.8 collective-permute-done.72
  524.4 4.6 collective-permute-done.69
  530.2 6.4 collective-permute-done.53
  542.4 7.6 collective-permute-done.57
  552.8 8.0 collective-permute-done.70
  560.9 4.2 collective-permute-done.74
  565.4 7.7 collective-permute-done.58
  580.8 7.3 collective-permute-done.78
  590.1 4.5 add_convert_fusion
  604.0 6.5 collective-permute-done.83
  612.8 4.2 collective-permute-done.84
  619.4 4.1 convolution_convert_fusion.1.grad
  623.5 9.7 %attend_back.1 = (f32[1024,256]{1,0:T(8,128)}, f32[1024,256]{1,0:T(8,128)}, f32[1024,256]{1,0:T(8,128)}) custom-call(s32[1,1024]{1,0:T(1,128)} %bitcast.246, s32[1024,1]{1,0:T(8,128)} %copy.218.pos_col, bf16[1024,256]{1,0:T(8,128)(2,1)} %copy.219.query, bf16[1024,256]{1,0:T(8,128)(2,1)} %copy.220.key, bf16[1024,256]{1,0:T(8,128)(2,1)} %slice.675.value, ...), custom_call_target="tpu_custom_call" | custom-call | tf_op jit(solution)/shard_map/attend_back/pallas_call | solution.py:633
  650.8 4.5 add_convert_fusion.2
  656.1 9.8 %collective-permute-done.118 = bf16[2,2048,256]{1,2,0:T(8,128)(2,1)} collective-permute-done((bf16[2,2048,256]{1,2,0:T(8,128)(2,1)}, bf16[2,2048,256]{1,2,0:T(8,128)(2,1)}, u32[]{:S(2)}, u32[]{:S(2)}) %collective-permute-start.118) | collective-permute-done | bytes 2097184 | tf_op jit(solution)/shard_map/ppermute | solution.py:535
  667.6 6.1 convert_add_fusion
  674.0 36.8 %collective-permute-done.115 = bf16[2,2048,256]{1,2,0:T(8,128)(2,1)} collective-permute-done((bf16[2,2048,256]{1,2,0:T(8,128)(2,1)}, bf16[2,2048,256]{1,2,0:T(8,128)(2,1)}, u32[]{:S(2)}, u32[]{:S(2)}) %collective-permute-start.115) | collective-permute-done | bytes 2097184 | tf_op jit(solution)/shard_map/ppermute | solution.py:535
  710.8 6.1 convert_add_fusion.1
  721.4 6.1 fusion.6
  739.0 4.0 fusion.28
  744.1 5.6 collective-permute-done.107
  751.6 4.5 collective-permute-done.89
  759.1 6.6 collective-permute-done.93
  767.5 11.3 %collective-permute-done.90 = bf16[128,2048]{1,0:T(8,128)(2,1)S(1)} collective-permute-done((bf16[128,2048]{1,0:T(8,128)(2,1)S(1)}, bf16[128,2048]{1,0:T(8,128)(2,1)S(1)}, u32[]{:S(2)}, u32[]{:S(2)}) %collective-permute-start.90) | collective-permute-done | bytes 524320 | tf_op jit(solution)/shard_map/ppermute | solution.py:424
  782.8 8.3 collective-permute-done.94
  794.6 5.7 collective-permute-done.102
  803.5 10.1 %collective-permute-done.99 = bf16[512,768]{1,0:T(8,128)(2,1)S(1)} collective-permute-done((bf16[512,768]{1,0:T(8,128)(2,1)S(1)}, bf16[512,768]{1,0:T(8,128)(2,1)S(1)}, u32[]{:S(2)}, u32[]{:S(2)}) %collective-permute-start.99) | collective-permute-done | bytes 786464 | tf_op jit(solution)/shard_map/ppermute | solution.py:535
  813.6 5.4 collective-permute-start.103
  827.7 6.1 convert_add_fusion.2
  833.8 5.5 copy.248
  839.3 5.3 copy.247
  844.6 5.5 copy.246
  851.2 22.3 %collective-permute-done.96 = bf16[128,2048]{1,0:T(8,128)(2,1)S(1)} collective-permute-done((bf16[128,2048]{1,0:T(8,128)(2,1)}, bf16[128,2048]{1,0:T(8,128)(2,1)S(1)}, u32[]{:S(2)}, u32[]{:S(2)}) %collective-permute-start.96) | collective-permute-done | bytes 524320 | tf_op jit(solution)/shard_map/ppermute | solution.py:427
  (592 shorter events, 315.5 us)
Async XLA Ops:
  0.7 55.7 %collective-permute-start = (bf16[128,2048]{1,0:T(8,128)(2,1)}, bf16[128,2048]{1,0:T(8,128)(2,1)S(1)}, u32[]{:S(2)}, u32[]{:S(2)}) collective-permute-start(bf16[128,2048]{1,0:T(8,128)(2,1)} %param.18), channel_id=1, source_target_pairs={{0,1},{2,0},{4,2},{6,4},{7,6},{5,7},{3,5},{1,3},{8,9},{10,8},{12,1... | collective-permute-start | bytes 1572872 | tf_op jit(solution)/shard_map/ppermute | solution.py:427
  3.7 53.9 %collective-permute-start.3 = (bf16[128,2048]{1,0:T(8,128)(2,1)}, bf16[128,2048]{1,0:T(8,128)(2,1)S(1)}, u32[]{:S(2)}, u32[]{:S(2)}) collective-permute-start(bf16[128,2048]{1,0:T(8,128)(2,1)} %param.18), channel_id=1, source_target_pairs={{0,2},{2,4},{4,6},{6,7},{7,5},{5,3},{3,1},{1,0},{8,10},{10,12},{12... | collective-permute-start | bytes 1572872 | tf_op jit(solution)/shard_map/ppermute | solution.py:424
  3.8 178.7 %collective-permute-start.59 = (bf16[128,2048]{1,0:T(8,128)(2,1)}, bf16[128,2048]{1,0:T(8,128)(2,1)}, u32[]{:S(2)}, u32[]{:S(2)}) collective-permute-start(bf16[128,2048]{1,0:T(8,128)(2,1)} %param.19), channel_id=1, source_target_pairs={{0,1},{2,0},{4,2},{6,4},{7,6},{5,7},{3,5},{1,3},{8,9},{10,8},{12,1... | collective-permute-start | bytes 1572872 | tf_op jit(solution)/shard_map/ppermute | solution.py:427
  5.7 178.0 %collective-permute-start.62 = (bf16[128,2048]{1,0:T(8,128)(2,1)}, bf16[128,2048]{1,0:T(8,128)(2,1)}, u32[]{:S(2)}, u32[]{:S(2)}) collective-permute-start(bf16[128,2048]{1,0:T(8,128)(2,1)} %param.19), channel_id=1, source_target_pairs={{0,2},{2,4},{4,6},{6,7},{7,5},{5,3},{3,1},{1,0},{8,10},{10,12},{12... | collective-permute-start | bytes 1572872 | tf_op jit(solution)/shard_map/ppermute | solution.py:424
  7.3 23.0 %collective-permute-start.8 = (bf16[1,64,20]{1,2,0:T(8,128)(2,1)S(1)}, bf16[1,64,20]{1,2,0:T(8,128)(2,1)S(1)}, u32[]{:S(2)}, u32[]{:S(2)}) collective-permute-start(bf16[1,64,20]{1,2,0:T(8,128)(2,1)S(1)} %bitcast.252), channel_id=1, source_target_pairs={{0,1},{1,0},{2,3},{3,2},{4,5},{5,4},{6,7},{7,6},{8,9},{9,8},{10,11... | collective-permute-start | bytes 7688 | tf_op jit(solution)/shard_map/ppermute | solution.py:484
  13.5 71.0 %all-to-all-start = ((bf16[8,64,3,256]{3,1,2,0:T(8,128)(2,1)}), bf16[8,64,3,256]{3,1,2,0:T(8,128)(2,1)S(1)}, u32[]{:S(2)}, u32[]{:S(2)}) async-start(bf16[8,64,3,256]{3,1,2,0:T(8,128)(2,1)} %copy.211), calls=%async_computation | async-start | bytes 1572864 | tf_op jit(solution)/shard_map/all_to_all | solution.py:723
  56.4 21.4 %collective-permute-start.1 = (bf16[128,2048]{1,0:T(8,128)(2,1)S(1)}, bf16[128,2048]{1,0:T(8,128)(2,1)}, u32[]{:S(2)}, u32[]{:S(2)}) collective-permute-start(bf16[128,2048]{1,0:T(8,128)(2,1)S(1)} %collective-permute-done), channel_id=1, source_target_pairs={{0,1},{2,0},{4,2},{6,4},{7,6},{5,7},{3,5},{1,3},{8,9},{10,8},{12,1... | collective-permute-start | bytes 1572872 | tf_op jit(solution)/shard_map/ppermute | solution.py:427
  57.6 15.5 %collective-permute-start.4 = (bf16[128,2048]{1,0:T(8,128)(2,1)S(1)}, bf16[128,2048]{1,0:T(8,128)(2,1)}, u32[]{:S(2)}, u32[]{:S(2)}) collective-permute-start(bf16[128,2048]{1,0:T(8,128)(2,1)S(1)} %collective-permute-done.3), channel_id=1, source_target_pairs={{0,2},{2,4},{4,6},{6,7},{7,5},{5,3},{3,1},{1,0},{8,10},{10,12},{12... | collective-permute-start | bytes 1572872 | tf_op jit(solution)/shard_map/ppermute | solution.py:424
  58.6 198.2 %collective-permute-start.49 = (bf16[2,2048,256]{2,1,0:T(8,128)(2,1)}, bf16[2,2048,256]{2,1,0:T(8,128)(2,1)}, u32[]{:S(2)}, u32[]{:S(2)}) collective-permute-start(bf16[2,2048,256]{2,1,0:T(8,128)(2,1)} %param.32), channel_id=1, source_target_pairs={{0,16},{8,24},{16,0},{24,8},{1,17},{9,25},{17,1},{25,9},{2,18},{10... | collective-permute-start | bytes 6291464 | tf_op jit(solution)/shard_map/ppermute | solution.py:514
  73.1 15.8 %collective-permute-start.5 = (bf16[128,2048]{1,0:T(8,128)(2,1)}, bf16[128,2048]{1,0:T(8,128)(2,1)S(1)}, u32[]{:S(2)}, u32[]{:S(2)}) collective-permute-start(bf16[128,2048]{1,0:T(8,128)(2,1)} %collective-permute-done.4), channel_id=1, source_target_pairs={{0,2},{2,4},{4,6},{6,7},{7,5},{5,3},{3,1},{1,0},{8,10},{10,12},{12... | collective-permute-start | bytes 1572872 | tf_op jit(solution)/shard_map/ppermute | solution.py:424
  77.8 14.3 %collective-permute-start.2 = (bf16[128,2048]{1,0:T(8,128)(2,1)}, bf16[128,2048]{1,0:T(8,128)(2,1)S(1)}, u32[]{:S(2)}, u32[]{:S(2)}) collective-permute-start(bf16[128,2048]{1,0:T(8,128)(2,1)} %collective-permute-done.1), channel_id=1, source_target_pairs={{0,1},{2,0},{4,2},{6,4},{7,6},{5,7},{3,5},{1,3},{8,9},{10,8},{12,1... | collective-permute-start | bytes 1572872 | tf_op jit(solution)/shard_map/ppermute | solution.py:427
  98.6 35.0 %collective-permute-start.13 = (bf16[512,768]{1,0:T(8,128)(2,1)S(1)}, bf16[512,768]{1,0:T(8,128)(2,1)S(1)}, u32[]{:S(2)}, u32[]{:S(2)}) collective-permute-start(bf16[512,768]{1,0:T(8,128)(2,1)S(1)} %bitcast.206), channel_id=1, source_target_pairs={{0,8},{8,0},{16,24},{24,16},{1,9},{9,1},{17,25},{25,17},{2,10},{10... | collective-permute-start | bytes 2359304 | tf_op jit(solution)/shard_map/ppermute | solution.py:514
  100.2 32.5 %collective-permute-start.14 = (bf16[512,768]{1,0:T(8,128)(2,1)S(1)}, bf16[512,768]{1,0:T(8,128)(2,1)S(1)}, u32[]{:S(2)}, u32[]{:S(2)}) collective-permute-start(bf16[512,768]{1,0:T(8,128)(2,1)S(1)} %bitcast.207), channel_id=1, source_target_pairs={{0,16},{8,24},{16,0},{24,8},{1,17},{9,25},{17,1},{25,9},{2,18},{10... | collective-permute-start | bytes 2359304 | tf_op jit(solution)/shard_map/ppermute | solution.py:514
  142.7 14.8 %collective-permute-start.22 = (bf16[64,2048]{1,0:T(8,128)(2,1)}, bf16[64,2048]{1,0:T(8,128)(2,1)}, u32[]{:S(2)}, u32[]{:S(2)}) collective-permute-start(bf16[64,2048]{1,0:T(8,128)(2,1)} %collective-permute-done.21), channel_id=1, source_target_pairs={{0,8},{8,0},{16,24},{24,16},{1,9},{9,1},{17,25},{25,17},{2,10},{10... | collective-permute-start | bytes 786440 | tf_op jit(solution)/shard_map/ppermute | solution.py:514
  182.5 15.3 %collective-permute-start.60 = (bf16[128,2048]{1,0:T(8,128)(2,1)}, bf16[128,2048]{1,0:T(8,128)(2,1)}, u32[]{:S(2)}, u32[]{:S(2)}) collective-permute-start(bf16[128,2048]{1,0:T(8,128)(2,1)} %collective-permute-done.59), channel_id=1, source_target_pairs={{0,1},{2,0},{4,2},{6,4},{7,6},{5,7},{3,5},{1,3},{8,9},{10,8},{12,1... | collective-permute-start | bytes 1572872 | tf_op jit(solution)/shard_map/ppermute | solution.py:427
  183.7 15.2 %collective-permute-start.63 = (bf16[128,2048]{1,0:T(8,128)(2,1)}, bf16[128,2048]{1,0:T(8,128)(2,1)}, u32[]{:S(2)}, u32[]{:S(2)}) collective-permute-start(bf16[128,2048]{1,0:T(8,128)(2,1)} %collective-permute-done.62), channel_id=1, source_target_pairs={{0,2},{2,4},{4,6},{6,7},{7,5},{5,3},{3,1},{1,0},{8,10},{10,12},{12... | collective-permute-start | bytes 1572872 | tf_op jit(solution)/shard_map/ppermute | solution.py:424
  197.8 29.4 %collective-permute-start.61 = (bf16[128,2048]{1,0:T(8,128)(2,1)}, bf16[128,2048]{1,0:T(8,128)(2,1)S(1)}, u32[]{:S(2)}, u32[]{:S(2)}) collective-permute-start(bf16[128,2048]{1,0:T(8,128)(2,1)} %collective-permute-done.60), channel_id=1, source_target_pairs={{0,1},{2,0},{4,2},{6,4},{7,6},{5,7},{3,5},{1,3},{8,9},{10,8},{12,1... | collective-permute-start | bytes 1572872 | tf_op jit(solution)/shard_map/ppermute | solution.py:427
  198.9 28.3 %collective-permute-start.64 = (bf16[128,2048]{1,0:T(8,128)(2,1)}, bf16[128,2048]{1,0:T(8,128)(2,1)S(1)}, u32[]{:S(2)}, u32[]{:S(2)}) collective-permute-start(bf16[128,2048]{1,0:T(8,128)(2,1)} %collective-permute-done.63), channel_id=1, source_target_pairs={{0,2},{2,4},{4,6},{6,7},{7,5},{5,3},{3,1},{1,0},{8,10},{10,12},{12... | collective-permute-start | bytes 1572872 | tf_op jit(solution)/shard_map/ppermute | solution.py:424
  199.9 21.4 %collective-permute-start.24 = (bf16[128,2048]{1,0:T(8,128)(2,1)S(1)}, bf16[128,2048]{1,0:T(8,128)(2,1)S(1)}, u32[]{:S(2)}, u32[]{:S(2)}) collective-permute-start(bf16[128,2048]{1,0:T(8,128)(2,1)S(1)} %pad_maximum_fusion.13), channel_id=1, source_target_pairs={{0,2},{2,4},{4,6},{6,7},{7,5},{5,3},{3,1},{1,0},{8,10},{10,12},{12... | collective-permute-start | bytes 1572872 | tf_op jit(solution)/shard_map/ppermute | solution.py:424
  204.4 24.9 %collective-permute-start.28 = (bf16[128,2048]{1,0:T(8,128)(2,1)S(1)}, bf16[128,2048]{1,0:T(8,128)(2,1)S(1)}, u32[]{:S(2)}, u32[]{:S(2)}) collective-permute-start(bf16[128,2048]{1,0:T(8,128)(2,1)S(1)} %pad_maximum_fusion.14), channel_id=1, source_target_pairs={{0,1},{2,0},{4,2},{6,4},{7,6},{5,7},{3,5},{1,3},{8,9},{10,8},{12,1... | collective-permute-start | bytes 1572872 | tf_op jit(solution)/shard_map/ppermute | solution.py:427
  227.2 40.8 %collective-permute-start.48 = (bf16[2,2048,256]{2,1,0:T(8,128)(2,1)S(1)}, bf16[2,2048,256]{2,1,0:T(8,128)(2,1)S(1)}, u32[]{:S(2)}, u32[]{:S(2)}) collective-permute-start(bf16[2,2048,256]{2,1,0:T(8,128)(2,1)S(1)} %copy-done.27), channel_id=1, source_target_pairs={{0,8},{8,0},{16,24},{24,16},{1,9},{9,1},{17,25},{25,17},{2,10},{10... | collective-permute-start | bytes 6291464 | tf_op jit(solution)/shard_map/ppermute | solution.py:514
  227.2 65.8 %collective-permute-start.35 = (bf16[2,2048,256]{1,2,0:T(8,128)(2,1)}, bf16[2,2048,256]{1,2,0:T(8,128)(2,1)}, u32[]{:S(2)}, u32[]{:S(2)}) collective-permute-start(bf16[2,2048,256]{1,2,0:T(8,128)(2,1)} %copy.224), channel_id=1, source_target_pairs={{0,16},{8,24},{16,0},{24,8},{1,17},{9,25},{17,1},{25,9},{2,18},{10... | collective-permute-start | bytes 6291464 | tf_op jit(solution)/shard_map/ppermute | solution.py:514
  241.3 16.3 %collective-permute-start.26 = (bf16[128,2048]{1,0:T(8,128)(2,1)S(1)}, bf16[128,2048]{1,0:T(8,128)(2,1)S(1)}, u32[]{:S(2)}, u32[]{:S(2)}) collective-permute-start(bf16[128,2048]{1,0:T(8,128)(2,1)S(1)} %get-tuple-element.159), channel_id=1, source_target_pairs={{0,2},{2,4},{4,6},{6,7},{7,5},{5,3},{3,1},{1,0},{8,10},{10,12},{12... | collective-permute-start | bytes 1572872 | tf_op jit(solution)/shard_map/ppermute | solution.py:424
  256.8 63.8 %collective-permute-start.46 = (bf16[2,2048,256]{1,2,0:T(8,128)(2,1)}, bf16[2,2048,256]{1,2,0:T(8,128)(2,1)}, u32[]{:S(2)}, u32[]{:S(2)}) collective-permute-start(bf16[2,2048,256]{1,2,0:T(8,128)(2,1)} %copy.227), channel_id=1, source_target_pairs={{0,16},{8,24},{16,0},{24,8},{1,17},{9,25},{17,1},{25,9},{2,18},{10... | collective-permute-start | bytes 6291464 | tf_op jit(solution)/shard_map/ppermute | solution.py:514
  257.5 24.4 %collective-permute-start.50 = (bf16[2,2048,256]{2,1,0:T(8,128)(2,1)}, bf16[2,2048,256]{2,1,0:T(8,128)(2,1)S(1)}, u32[]{:S(2)}, u32[]{:S(2)}) collective-permute-start(bf16[2,2048,256]{2,1,0:T(8,128)(2,1)} %collective-permute-done.49), channel_id=1, source_target_pairs={{0,8},{8,0},{16,24},{24,16},{1,9},{9,1},{17,25},{25,17},{2,10},{10... | collective-permute-start | bytes 6291464 | tf_op jit(solution)/shard_map/ppermute | solution.py:514
  281.3 15.7 %collective-permute-start.41 = (bf16[128,2048]{1,0:T(8,128)(2,1)S(1)}, bf16[128,2048]{1,0:T(8,128)(2,1)S(1)}, u32[]{:S(2)}, u32[]{:S(2)}) collective-permute-start(bf16[128,2048]{1,0:T(8,128)(2,1)S(1)} %collective-permute-done.40), channel_id=1, source_target_pairs={{0,2},{2,4},{4,6},{6,7},{7,5},{5,3},{3,1},{1,0},{8,10},{10,12},{12... | collective-permute-start | bytes 1572872 | tf_op jit(solution)/shard_map/ppermute | solution.py:424
  293.0 33.1 %collective-permute-start.34 = (bf16[2,2048,256]{1,2,0:T(8,128)(2,1)}, bf16[2,2048,256]{1,2,0:T(8,128)(2,1)}, u32[]{:S(2)}, u32[]{:S(2)}) collective-permute-start(bf16[2,2048,256]{1,2,0:T(8,128)(2,1)} %copy.224), channel_id=1, source_target_pairs={{0,8},{8,0},{16,24},{24,16},{1,9},{9,1},{17,25},{25,17},{2,10},{10... | collective-permute-start | bytes 6291464 | tf_op jit(solution)/shard_map/ppermute | solution.py:514
  294.7 31.5 %collective-permute-start.36 = (bf16[2,2048,256]{1,2,0:T(8,128)(2,1)}, bf16[2,2048,256]{1,2,0:T(8,128)(2,1)}, u32[]{:S(2)}, u32[]{:S(2)}) collective-permute-start(bf16[2,2048,256]{1,2,0:T(8,128)(2,1)} %collective-permute-done.35), channel_id=1, source_target_pairs={{0,8},{8,0},{16,24},{24,16},{1,9},{9,1},{17,25},{25,17},{2,10},{10... | collective-permute-start | bytes 6291464 | tf_op jit(solution)/shard_map/ppermute | solution.py:514
  320.6 20.2 %collective-permute-start.45 = (bf16[2,2048,256]{1,2,0:T(8,128)(2,1)}, bf16[2,2048,256]{1,2,0:T(8,128)(2,1)S(1)}, u32[]{:S(2)}, u32[]{:S(2)}) collective-permute-start(bf16[2,2048,256]{1,2,0:T(8,128)(2,1)} %copy.227), channel_id=1, source_target_pairs={{0,8},{8,0},{16,24},{24,16},{1,9},{9,1},{17,25},{25,17},{2,10},{10... | collective-permute-start | bytes 6291464 | tf_op jit(solution)/shard_map/ppermute | solution.py:514
  320.6 20.2 %collective-permute-start.47 = (bf16[2,2048,256]{1,2,0:T(8,128)(2,1)}, bf16[2,2048,256]{1,2,0:T(8,128)(2,1)S(1)}, u32[]{:S(2)}, u32[]{:S(2)}) collective-permute-start(bf16[2,2048,256]{1,2,0:T(8,128)(2,1)} %collective-permute-done.46), channel_id=1, source_target_pairs={{0,8},{8,0},{16,24},{24,16},{1,9},{9,1},{17,25},{25,17},{2,10},{10... | collective-permute-start | bytes 6291464 | tf_op jit(solution)/shard_map/ppermute | solution.py:514
  420.4 160.3 %collective-permute-start.117 = (bf16[2,2048,256]{1,2,0:T(8,128)(2,1)}, bf16[2,2048,256]{1,2,0:T(8,128)(2,1)}, u32[]{:S(2)}, u32[]{:S(2)}) collective-permute-start(bf16[2,2048,256]{1,2,0:T(8,128)(2,1)} %get-tuple-element.130), channel_id=1, source_target_pairs={{0,8},{8,0},{16,24},{24,16},{1,9},{9,1},{17,25},{25,17},{2,10},{10... | collective-permute-start | bytes 6291464 | tf_op jit(solution)/shard_map/ppermute | solution.py:535
  448.2 66.7 %collective-permute-start.75 = (f32[1,2,8,128]{3,1,2,0:T(2,128)S(1)}, f32[1,2,8,128]{3,1,2,0:T(2,128)S(1)}, u32[]{:S(2)}, u32[]{:S(2)}) collective-permute-start(f32[1,2,8,128]{3,1,2,0:T(2,128)S(1)} %bitcast.250), channel_id=1, source_target_pairs={{0,1},{1,0},{2,3},{3,2},{4,5},{5,4},{6,7},{7,6},{8,9},{9,8},{10,11... | collective-permute-start | bytes 24584 | tf_op jit(solution)/shard_map/ppermute | solution.py:484
  449.4 33.7 %collective-permute-start.51 = (bf16[64,2048]{1,0:T(8,128)(2,1)S(1)}, bf16[64,2048]{1,0:T(8,128)(2,1)S(1)}, u32[]{:S(2)}, u32[]{:S(2)}) collective-permute-start(bf16[64,2048]{1,0:T(8,128)(2,1)S(1)} %get-tuple-element.157), channel_id=1, source_target_pairs={{0,2},{2,4},{4,6},{6,7},{7,5},{5,3},{3,1},{1,0},{8,10},{10,12},{12... | collective-permute-start | bytes 786440 | tf_op jit(solution)/shard_map/ppermute | solution.py:424
  451.5 31.6 %collective-permute-start.55 = (bf16[64,2048]{1,0:T(8,128)(2,1)S(1)}, bf16[64,2048]{1,0:T(8,128)(2,1)S(1)}, u32[]{:S(2)}, u32[]{:S(2)}) collective-permute-start(bf16[64,2048]{1,0:T(8,128)(2,1)S(1)} %get-tuple-element.158), channel_id=1, source_target_pairs={{0,1},{2,0},{4,2},{6,4},{7,6},{5,7},{3,5},{1,3},{8,9},{10,8},{12,1... | collective-permute-start | bytes 786440 | tf_op jit(solution)/shard_map/ppermute | solution.py:427
  483.2 47.0 %collective-permute-start.56 = (bf16[128,2048]{1,0:T(8,128)(2,1)S(1)}, bf16[128,2048]{1,0:T(8,128)(2,1)S(1)}, u32[]{:S(2)}, u32[]{:S(2)}) collective-permute-start(bf16[128,2048]{1,0:T(8,128)(2,1)S(1)} %pad_maximum_fusion.16), channel_id=1, source_target_pairs={{0,1},{2,0},{4,2},{6,4},{7,6},{5,7},{3,5},{1,3},{8,9},{10,8},{12,1... | collective-permute-start | bytes 1572872 | tf_op jit(solution)/shard_map/ppermute | solution.py:427
  489.9 24.2 %collective-permute-start.52 = (bf16[128,2048]{1,0:T(8,128)(2,1)S(1)}, bf16[128,2048]{1,0:T(8,128)(2,1)S(1)}, u32[]{:S(2)}, u32[]{:S(2)}) collective-permute-start(bf16[128,2048]{1,0:T(8,128)(2,1)S(1)} %pad_maximum_fusion.15), channel_id=1, source_target_pairs={{0,2},{2,4},{4,6},{6,7},{7,5},{5,3},{3,1},{1,0},{8,10},{10,12},{12... | collective-permute-start | bytes 1572872 | tf_op jit(solution)/shard_map/ppermute | solution.py:424
  514.1 14.9 %collective-permute-start.69 = (bf16[128,2048]{1,0:T(8,128)(2,1)S(1)}, bf16[128,2048]{1,0:T(8,128)(2,1)S(1)}, u32[]{:S(2)}, u32[]{:S(2)}) collective-permute-start(bf16[128,2048]{1,0:T(8,128)(2,1)S(1)} %slice_add_fusion.6), channel_id=1, source_target_pairs={{0,2},{2,4},{4,6},{6,7},{7,5},{5,3},{3,1},{1,0},{8,10},{10,12},{12... | collective-permute-start | bytes 1572872 | tf_op jit(solution)/shard_map/ppermute | solution.py:424
  515.0 21.7 %collective-permute-start.53 = (bf16[128,2048]{1,0:T(8,128)(2,1)S(1)}, bf16[128,2048]{1,0:T(8,128)(2,1)S(1)}, u32[]{:S(2)}, u32[]{:S(2)}) collective-permute-start(bf16[128,2048]{1,0:T(8,128)(2,1)S(1)} %slice_add_fusion.10), channel_id=1, source_target_pairs={{0,2},{2,4},{4,6},{6,7},{7,5},{5,3},{3,1},{1,0},{8,10},{10,12},{12... | collective-permute-start | bytes 1572872 | tf_op jit(solution)/shard_map/ppermute | solution.py:424
  523.4 14.3 %collective-permute-start.76 = (f32[2,2,8,128]{3,1,2,0:T(2,128)S(1)}, f32[2,2,8,128]{3,1,2,0:T(2,128)S(1)}, u32[]{:S(2)}, u32[]{:S(2)}) collective-permute-start(f32[2,2,8,128]{3,1,2,0:T(2,128)S(1)} %maximum_select_fusion.8), channel_id=1, source_target_pairs={{0,2},{1,3},{2,0},{3,1},{4,6},{5,7},{6,4},{7,5},{8,10},{9,11},{10,... | collective-permute-start | bytes 49160 | tf_op jit(solution)/shard_map/ppermute | solution.py:484
  537.7 15.0 %collective-permute-start.77 = (f32[4,2,8,128]{3,1,2,0:T(2,128)S(1)}, f32[4,2,8,128]{3,1,2,0:T(2,128)S(1)}, u32[]{:S(2)}, u32[]{:S(2)}) collective-permute-start(f32[4,2,8,128]{3,1,2,0:T(2,128)S(1)} %maximum_select_fusion.5), channel_id=1, source_target_pairs={{0,4},{1,5},{2,6},{3,7},{4,0},{5,1},{6,2},{7,3},{8,12},{9,13},{10,... | collective-permute-start | bytes 98312 | tf_op jit(solution)/shard_map/ppermute | solution.py:484
  538.9 26.6 %collective-permute-start.54 = (bf16[128,2048]{1,0:T(8,128)(2,1)S(1)}, bf16[128,2048]{1,0:T(8,128)(2,1)S(1)}, u32[]{:S(2)}, u32[]{:S(2)}) collective-permute-start(bf16[128,2048]{1,0:T(8,128)(2,1)S(1)} %get-tuple-element.151), channel_id=1, source_target_pairs={{0,2},{2,4},{4,6},{6,7},{7,5},{5,3},{3,1},{1,0},{8,10},{10,12},{12... | collective-permute-start | bytes 1572872 | tf_op jit(solution)/shard_map/ppermute | solution.py:424
  540.8 20.1 %collective-permute-start.70 = (bf16[128,2048]{1,0:T(8,128)(2,1)S(1)}, bf16[128,2048]{1,0:T(8,128)(2,1)S(1)}, u32[]{:S(2)}, u32[]{:S(2)}) collective-permute-start(bf16[128,2048]{1,0:T(8,128)(2,1)S(1)} %get-tuple-element.145), channel_id=1, source_target_pairs={{0,2},{2,4},{4,6},{6,7},{7,5},{5,3},{3,1},{1,0},{8,10},{10,12},{12... | collective-permute-start | bytes 1572872 | tf_op jit(solution)/shard_map/ppermute | solution.py:424
  550.0 15.1 %collective-permute-start.74 = (bf16[128,2048]{1,0:T(8,128)(2,1)S(1)}, bf16[128,2048]{1,0:T(8,128)(2,1)S(1)}, u32[]{:S(2)}, u32[]{:S(2)}) collective-permute-start(bf16[128,2048]{1,0:T(8,128)(2,1)S(1)} %slice_add_fusion.5), channel_id=1, source_target_pairs={{0,1},{2,0},{4,2},{6,4},{7,6},{5,7},{3,5},{1,3},{8,9},{10,8},{12,1... | collective-permute-start | bytes 1572872 | tf_op jit(solution)/shard_map/ppermute | solution.py:427
  552.7 20.4 %collective-permute-start.58 = (bf16[128,2048]{1,0:T(8,128)(2,1)S(1)}, bf16[128,2048]{1,0:T(8,128)(2,1)S(1)}, u32[]{:S(2)}, u32[]{:S(2)}) collective-permute-start(bf16[128,2048]{1,0:T(8,128)(2,1)S(1)} %slice_add_fusion.9), channel_id=1, source_target_pairs={{0,1},{2,0},{4,2},{6,4},{7,6},{5,7},{3,5},{1,3},{8,9},{10,8},{12,1... | collective-permute-start | bytes 1572872 | tf_op jit(solution)/shard_map/ppermute | solution.py:427
  560.9 94.4 %collective-permute-start.116 = (bf16[2,2048,256]{1,2,0:T(8,128)(2,1)}, bf16[2,2048,256]{1,2,0:T(8,128)(2,1)}, u32[]{:S(2)}, u32[]{:S(2)}) collective-permute-start(bf16[2,2048,256]{1,2,0:T(8,128)(2,1)} %get-tuple-element.129), channel_id=1, source_target_pairs={{0,8},{8,0},{16,24},{24,16},{1,9},{9,1},{17,25},{25,17},{2,10},{10... | collective-permute-start | bytes 6291464 | tf_op jit(solution)/shard_map/ppermute | solution.py:535
  565.1 29.5 %collective-permute-start.114 = (bf16[2,2048,256]{1,2,0:T(8,128)(2,1)S(1)}, bf16[2,2048,256]{1,2,0:T(8,128)(2,1)S(1)}, u32[]{:S(2)}, u32[]{:S(2)}) collective-permute-start(bf16[2,2048,256]{1,2,0:T(8,128)(2,1)S(1)} %copy-done.28), channel_id=1, source_target_pairs={{0,8},{8,0},{16,24},{24,16},{1,9},{9,1},{17,25},{25,17},{2,10},{10... | collective-permute-start | bytes 6291464 | tf_op jit(solution)/shard_map/ppermute | solution.py:535
  580.7 93.3 %collective-permute-start.113 = (bf16[2,2048,256]{1,2,0:T(8,128)(2,1)}, bf16[2,2048,256]{1,2,0:T(8,128)(2,1)}, u32[]{:S(2)}, u32[]{:S(2)}) collective-permute-start(bf16[2,2048,256]{1,2,0:T(8,128)(2,1)} %get-tuple-element.131), channel_id=1, source_target_pairs={{0,8},{8,0},{16,24},{24,16},{1,9},{9,1},{17,25},{25,17},{2,10},{10... | collective-permute-start | bytes 6291464 | tf_op jit(solution)/shard_map/ppermute | solution.py:535
  594.6 54.7 %collective-permute-start.111 = (bf16[2,2048,256]{1,2,0:T(8,128)(2,1)}, bf16[2,2048,256]{1,2,0:T(8,128)(2,1)}, u32[]{:S(2)}, u32[]{:S(2)}) collective-permute-start(bf16[2,2048,256]{1,2,0:T(8,128)(2,1)} %get-tuple-element.134), channel_id=1, source_target_pairs={{0,8},{8,0},{16,24},{24,16},{1,9},{9,1},{17,25},{25,17},{2,10},{10... | collective-permute-start | bytes 6291464 | tf_op jit(solution)/shard_map/ppermute | solution.py:535
  598.2 14.2 %collective-permute-start.80 = (bf16[128,2048]{1,0:T(8,128)(2,1)S(1)}, bf16[128,2048]{1,0:T(8,128)(2,1)S(1)}, u32[]{:S(2)}, u32[]{:S(2)}) collective-permute-start(bf16[128,2048]{1,0:T(8,128)(2,1)S(1)} %collective-permute-done.79), channel_id=1, source_target_pairs={{0,1},{2,0},{4,2},{6,4},{7,6},{5,7},{3,5},{1,3},{8,9},{10,8},{12,1... | collective-permute-start | bytes 1572872 | tf_op jit(solution)/shard_map/ppermute | solution.py:427
  617.0 48.9 %collective-permute-start.118 = (bf16[2,2048,256]{1,2,0:T(8,128)(2,1)}, bf16[2,2048,256]{1,2,0:T(8,128)(2,1)}, u32[]{:S(2)}, u32[]{:S(2)}) collective-permute-start(bf16[2,2048,256]{1,2,0:T(8,128)(2,1)} %add_convert_fusion), channel_id=1, source_target_pairs={{0,16},{8,24},{16,0},{24,8},{1,17},{9,25},{17,1},{25,9},{2,18},{10... | collective-permute-start | bytes 6291464 | tf_op jit(solution)/shard_map/ppermute | solution.py:535
  618.8 92.0 %collective-permute-start.115 = (bf16[2,2048,256]{1,2,0:T(8,128)(2,1)}, bf16[2,2048,256]{1,2,0:T(8,128)(2,1)}, u32[]{:S(2)}, u32[]{:S(2)}) collective-permute-start(bf16[2,2048,256]{1,2,0:T(8,128)(2,1)} %add_convert_fusion.1), channel_id=1, source_target_pairs={{0,16},{8,24},{16,0},{24,8},{1,17},{9,25},{17,1},{25,9},{2,18},{10... | collective-permute-start | bytes 6291464 | tf_op jit(solution)/shard_map/ppermute | solution.py:535
  655.3 172.3 %collective-permute-start.110 = (bf16[2,2048,256]{1,2,0:T(8,128)(2,1)}, bf16[2,2048,256]{1,2,0:T(8,128)(2,1)}, u32[]{:S(2)}, u32[]{:S(2)}) collective-permute-start(bf16[2,2048,256]{1,2,0:T(8,128)(2,1)} %get-tuple-element.133), channel_id=1, source_target_pairs={{0,8},{8,0},{16,24},{24,16},{1,9},{9,1},{17,25},{25,17},{2,10},{10... | collective-permute-start | bytes 6291464 | tf_op jit(solution)/shard_map/ppermute | solution.py:535
  655.3 172.4 %collective-permute-start.112 = (bf16[2,2048,256]{1,2,0:T(8,128)(2,1)}, bf16[2,2048,256]{1,2,0:T(8,128)(2,1)}, u32[]{:S(2)}, u32[]{:S(2)}) collective-permute-start(bf16[2,2048,256]{1,2,0:T(8,128)(2,1)} %add_convert_fusion.2), channel_id=1, source_target_pairs={{0,16},{8,24},{16,0},{24,8},{1,17},{9,25},{17,1},{25,9},{2,18},{10... | collective-permute-start | bytes 6291464 | tf_op jit(solution)/shard_map/ppermute | solution.py:535
  673.7 44.0 %collective-permute-start.88 = (f32[2,8,128]{2,0,1:T(2,128)S(1)}, f32[2,8,128]{2,0,1:T(2,128)S(1)}, u32[]{:S(2)}, u32[]{:S(2)}) collective-permute-start(f32[2,8,128]{2,0,1:T(2,128)S(1)} %add.460), channel_id=1, source_target_pairs={{0,4},{1,5},{2,6},{3,7},{4,0},{5,1},{6,2},{7,3},{8,12},{9,13},{10,... | collective-permute-start | bytes 24584 | tf_op jit(solution)/shard_map/ppermute | solution.py:474
  735.0 45.6 %collective-permute-start.101 = (bf16[64,2048]{1,0:T(8,128)(2,1)S(1)}, bf16[64,2048]{1,0:T(8,128)(2,1)S(1)}, u32[]{:S(2)}, u32[]{:S(2)}) collective-permute-start(bf16[64,2048]{1,0:T(8,128)(2,1)S(1)} %get-tuple-element.170), channel_id=1, source_target_pairs={{0,8},{8,0},{16,24},{24,16},{1,9},{9,1},{17,25},{25,17},{2,10},{10... | collective-permute-start | bytes 786440 | tf_op jit(solution)/shard_map/ppermute | solution.py:535
  744.0 37.0 %collective-permute-start.98 = (bf16[512,768]{1,0:T(8,128)(2,1)S(1)}, bf16[512,768]{1,0:T(8,128)(2,1)S(1)}, u32[]{:S(2)}, u32[]{:S(2)}) collective-permute-start(bf16[512,768]{1,0:T(8,128)(2,1)S(1)} %get-tuple-element.138), channel_id=1, source_target_pairs={{0,8},{8,0},{16,24},{24,16},{1,9},{9,1},{17,25},{25,17},{2,10},{10... | collective-permute-start | bytes 2359304 | tf_op jit(solution)/shard_map/ppermute | solution.py:535
  782.6 20.2 %collective-permute-start.97 = (bf16[512,768]{1,0:T(8,128)(2,1)S(1)}, bf16[512,768]{1,0:T(8,128)(2,1)S(1)}, u32[]{:S(2)}, u32[]{:S(2)}) collective-permute-start(bf16[512,768]{1,0:T(8,128)(2,1)S(1)} %get-tuple-element.137), channel_id=1, source_target_pairs={{0,8},{8,0},{16,24},{24,16},{1,9},{9,1},{17,25},{25,17},{2,10},{10... | collective-permute-start | bytes 2359304 | tf_op jit(solution)/shard_map/ppermute | solution.py:535
  792.6 21.0 %collective-permute-start.99 = (bf16[512,768]{1,0:T(8,128)(2,1)S(1)}, bf16[512,768]{1,0:T(8,128)(2,1)S(1)}, u32[]{:S(2)}, u32[]{:S(2)}) collective-permute-start(bf16[512,768]{1,0:T(8,128)(2,1)S(1)} %add_convert_fusion.4), channel_id=1, source_target_pairs={{0,16},{8,24},{16,0},{24,8},{1,17},{9,25},{17,1},{25,9},{2,18},{10... | collective-permute-start | bytes 2359304 | tf_op jit(solution)/shard_map/ppermute | solution.py:535
  800.3 23.4 %collective-permute-start.95 = (bf16[128,2048]{1,0:T(8,128)(2,1)S(1)}, bf16[128,2048]{1,0:T(8,128)(2,1)S(1)}, u32[]{:S(2)}, u32[]{:S(2)}) collective-permute-start(bf16[128,2048]{1,0:T(8,128)(2,1)S(1)} %get-tuple-element.140), channel_id=1, source_target_pairs={{0,1},{2,0},{4,2},{6,4},{7,6},{5,7},{3,5},{1,3},{8,9},{10,8},{12,1... | collective-permute-start | bytes 1572872 | tf_op jit(solution)/shard_map/ppermute | solution.py:427
  802.9 47.2 %collective-permute-start.109 = (f32[64,20]{0,1:T(8,128)S(1)}, f32[64,20]{0,1:T(8,128)S(1)}, u32[]{:S(2)}, u32[]{:S(2)}) collective-permute-start(f32[64,20]{0,1:T(8,128)S(1)} %select_add_fusion.3), channel_id=1, source_target_pairs={{0,0},{8,1},{16,2},{24,3},{1,4},{9,5},{17,6},{25,7},{2,8},{10,9},{... | collective-permute-start | bytes 15368 | tf_op jit(solution)/shard_map/ppermute | solution.py:895
  813.6 37.6 %collective-permute-start.103 = (f32[64,2048]{1,0:T(8,128)}, f32[64,2048]{1,0:T(8,128)}, u32[]{:S(2)}, u32[]{:S(2)}) collective-permute-start(f32[64,2048]{1,0:T(8,128)} %convert_add_fusion.4), channel_id=1, source_target_pairs={{0,0},{8,1},{16,2},{24,3},{1,4},{9,5},{17,6},{25,7},{2,8},{10,9},{... | collective-permute-start | bytes 1572872 | tf_op jit(solution)/shard_map/ppermute | solution.py:844
  820.2 57.4 %all-to-all-start.1 = ((bf16[8,64,768]{2,1,0:T(8,128)(2,1)}), bf16[8,64,768]{2,1,0:T(8,128)(2,1)S(1)}, u32[]{:S(2)}, u32[]{:S(2)}) async-start(bf16[8,64,768]{2,1,0:T(8,128)(2,1)} %bitcast.57), calls=%async_computation.1 | async-start | bytes 1572864 | tf_op jit(solution)/shard_map/all_to_all | solution.py:887
  823.7 27.5 %collective-permute-start.92 = (bf16[128,2048]{1,0:T(8,128)(2,1)}, bf16[128,2048]{1,0:T(8,128)(2,1)S(1)}, u32[]{:S(2)}, u32[]{:S(2)}) collective-permute-start(bf16[128,2048]{1,0:T(8,128)(2,1)} %get-tuple-element.139), channel_id=1, source_target_pairs={{0,2},{2,4},{4,6},{6,7},{7,5},{5,3},{3,1},{1,0},{8,10},{10,12},{12... | collective-permute-start | bytes 1572872 | tf_op jit(solution)/shard_map/ppermute | solution.py:424
  827.5 46.1 %collective-permute-start.96 = (bf16[128,2048]{1,0:T(8,128)(2,1)}, bf16[128,2048]{1,0:T(8,128)(2,1)S(1)}, u32[]{:S(2)}, u32[]{:S(2)}) collective-permute-start(bf16[128,2048]{1,0:T(8,128)(2,1)} %slice_add_fusion.1), channel_id=1, source_target_pairs={{0,1},{2,0},{4,2},{6,4},{7,6},{5,7},{3,5},{1,3},{8,9},{10,8},{12,1... | collective-permute-start | bytes 1572872 | tf_op jit(solution)/shard_map/ppermute | solution.py:427
  (140 other events, 3668.1 us)

commit v2 on v0

--- a/solution.py
+++ b/solution.py
@@ -1,6 +1,10 @@
+import functools
+
 import jax
 import jax.numpy as jnp
 from jax import lax
+from jax.experimental import pallas as pl
+from jax.experimental.pallas import tpu as pltpu
 from jax.sharding import PartitionSpec as P
 
 HEADS = 16
@@ -9,6 +13,8 @@
 
 epsilon = 1e-05
 rope_base = 10000.0
+hidden_parts = 4
+dp_axes = ("x", "core")
 far_low = -1e30
 
 
@@ -49,7 +55,7 @@
     return chosen / jnp.sum(chosen, axis=-1, keepdims=True)
 
 
-def per_device(
+def per_device_gathered(
     tokens,
     cotangent,
     routes,
@@ -393,40 +399,1317 @@
     )
 
 
+def after(values, ties):
+    if callable(ties):
+        ties = ties(values)
+    if ties is None:
+        return values
+    return lax.optimization_barrier((values, ties))[0]
+
+
+class Ring:
+    def __init__(self, size, rows):
+        self.size = size
+        self.half = size // 2
+        self.rows = rows
+        middle = rows // 2
+        self.pieces = [(k, 0, rows) for k in range(self.half)]
+        self.pieces += [(self.half, 0, middle), (self.half, middle, middle)]
+        self.pieces += [(k, 0, rows) for k in range(self.half + 1, size)]
+        self.order = list(range(0, size, 2)) + list(range(size - 1, 0, -2))
+        place = [self.order.index(i) for i in range(size)]
+        rank = jnp.asarray(place, jnp.int32)[lax.axis_index("fsdp")]
+        self.slot_device = jnp.asarray(self.order, jnp.int32)[
+            (rank + jnp.arange(size, dtype=jnp.int32)) % size
+        ]
+        self.device_slot = (jnp.asarray(place, jnp.int32) - rank) % size
+        self.up = [(self.order[i], self.order[(i + 1) % size]) for i in range(size)]
+        self.down = [(self.order[i], self.order[i - 1]) for i in range(size)]
+
+    def forward(self, values):
+        return lax.ppermute(values, "fsdp", self.up)
+
+    def backward(self, values):
+        return lax.ppermute(values, "fsdp", self.down)
+
+    def gather(self, block, halves=True):
+        return Gather(self, block, halves)
+
+    def reduce(self, pieces):
+        return Reduce(self, pieces)
+
+
+class Gather:
+    def __init__(self, ring, block, halves=True):
+        self.ring, self.halves = ring, halves
+        self.low, self.high, self.opposite = [block], [block], None
+
+    def step(self, ties=None):
+        ring, middle = self.ring, self.ring.rows // 2
+        from_low, from_high = after((self.low[-1], self.high[-1]), ties)
+        if len(self.low) < ring.half:
+            self.low.append(ring.forward(from_low))
+            self.high.append(ring.backward(from_high))
+            return self.low[-1], self.high[-1]
+        if self.halves:
+            self.opposite = [ring.forward(from_low[:middle]), ring.backward(from_high[middle:])]
+        else:
+            self.opposite = [ring.forward(from_low)]
+        return tuple(self.opposite)
+
+    def stacked(self):
+        return jnp.stack(self.blocks())[self.ring.device_slot]
+
+    def blocks(self):
+        return self.high + self.opposite + self.low[:0:-1]
+
+
+class Reduce:
+    def __init__(self, ring, pieces):
+        self.ring, self.pieces, self.arrived, self.left = ring, pieces, None, ring.half
+
+    def step(self, ties=None):
+        ring, pieces, middle = self.ring, self.pieces, self.ring.rows // 2
+        if self.arrived is None:
+            upper, lower = pieces[ring.half], pieces[ring.half + 1]
+        else:
+            rising, falling = self.arrived
+            upper, lower = pieces[self.left], pieces[-self.left]
+            if self.left == ring.half - 1:
+                upper = jnp.concatenate([upper[:middle] + rising, upper[middle:]], axis=0)
+                lower = jnp.concatenate([lower[:middle], lower[middle:] + falling], axis=0)
+            else:
+                upper, lower = upper + rising, lower + falling
+        upper, lower = after((upper, lower), ties)
+        self.arrived = (ring.forward(upper), ring.backward(lower))
+        self.left -= 1
+        return self.arrived
+
+    def total(self):
+        rising, falling = self.arrived
+        return (
+            self.pieces[0].astype(jnp.float32)
+            + rising.astype(jnp.float32)
+            + falling.astype(jnp.float32)
+        )
+
+
+def exchange_pairs(size, bit):
+    return [(i, i ^ bit) for i in range(size)]
+
+
+def pair_sum(values, axis, size):
+    bit = 1
+    while bit < size:
+        values = values + lax.ppermute(values, axis, exchange_pairs(size, bit))
+        bit *= 2
+    return values
+
+
+def pair_gather(values, axis, size, ties=()):
+    ties = dict(ties)
+    mine = lax.axis_index(axis)
+    values = values[None]
+    bit = 1
+    while bit < size:
+        values = after(values, ties.get(bit))
+        other = lax.ppermute(values, axis, exchange_pairs(size, bit))
+        upper = (mine & bit) != 0
+        values = jnp.where(
+            upper,
+            jnp.concatenate([other, values], axis=0),
+            jnp.concatenate([values, other], axis=0),
+        )
+        bit *= 2
+    return values
+
+
+def pair_scatter(values, axis, size, ties=()):
+    ties = dict(ties)
+    mine = lax.axis_index(axis)
+    bit = size // 2
+    while bit >= 1:
+        span = values.shape[1] // 2
+        upper = (mine & bit) != 0
+        low_half, high_half = values[:, :span], values[:, span:]
+        kept = jnp.where(upper, high_half, low_half)
+        sent = after(jnp.where(upper, low_half, high_half), ties.get(bit))
+        values = kept + lax.ppermute(sent, axis, exchange_pairs(size, bit))
+        bit //= 2
+    return values
+
+
+def share_relative(block, size, ties=(), second=()):
+    block = after(block, ties)
+    held = {0: block}
+    bit = size // 2
+    while bit >= 1:
+        for index in list(held):
+            sent = held[index] if index == 0 else after(held[index], second)
+            held[index ^ bit] = lax.ppermute(sent, dp_axes, exchange_pairs(size, bit))
+        bit //= 2
+    return [held[index] for index in range(size)]
+
+
+def combine_relative(blocks, ties=(None, None)):
+    half = blocks.shape[0] // 2
+    far = lax.ppermute(after(blocks[:half], ties[0]), dp_axes, exchange_pairs(4, 1))
+    sums = blocks[half:].astype(jnp.float32) + far.astype(jnp.float32)
+    other = after(sums[half // 2 :].astype(jnp.bfloat16), ties[1])
+    other = lax.ppermute(other, dp_axes, exchange_pairs(4, 2))
+    return sums[: half // 2] + other.astype(jnp.float32)
+
+
+anywhere = pl.BlockSpec(memory_space=pl.ANY)
+rows_first = (((0,), (0,)), ((), ()))
+columns_last = (((1,), (1,)), ((), ()))
+
+
+def dot(left, right, dims=(((1,), (0,)), ((), ()))):
+    return lax.dot_general(left, right, dims, preferred_element_type=jnp.float32)
+
+
+def row_sums(*columns):
+    total = None
+    for i, values in enumerate(columns):
+        place = lax.broadcasted_iota(jnp.int32, (8, values.shape[1]), 0) == i
+        sums = lax.dot_general(
+            place.astype(jnp.float32),
+            values,
+            columns_last,
+            precision=lax.Precision.HIGHEST,
+            preferred_element_type=jnp.float32,
+        )
+        total = sums if total is None else total + sums
+    return total
+
+
+def as_columns(rows):
+    same = lax.broadcasted_iota(jnp.int32, (8, 8), 0) == lax.broadcasted_iota(jnp.int32, (8, 8), 1)
+    return lax.dot_general(
+        rows,
+        same.astype(jnp.float32),
+        rows_first,
+        precision=lax.Precision.HIGHEST,
+        preferred_element_type=jnp.float32,
+    )
+
+
+def whole_block(shape):
+    return pl.BlockSpec(shape, lambda *_: (0,) * len(shape))
+
+
+def piece_copies(pieces, scalars, blocks, target, sems):
+    rows = pieces[0][2]
+    copies = []
+    for i, (slot, first, count) in enumerate(pieces):
+        begin = pl.multiple_of(scalars[slot] * rows + first, count)
+        copies.append(
+            pltpu.make_async_copy(blocks[i], target.at[pl.ds(begin, count), :], sems.at[i])
+        )
+    return copies
+
+
+def piece_results(pieces, scalars, source, blocks, sems):
+    rows = pieces[0][2]
+    copies = []
+    for i, (slot, first, count) in enumerate(pieces):
+        begin = pl.multiple_of(scalars[slot] * rows + first, count)
+        copies.append(
+            pltpu.make_async_copy(source.at[pl.ds(begin, count), :], blocks[i], sems.at[i])
+        )
+    return copies
+
+
+def row_copies(scalars, which, blocks, target, sems):
+    own = scalars[which]
+    count = blocks[0].shape[0]
+    return [
+        pltpu.make_async_copy(
+            block, target.at[pl.ds(pl.multiple_of((own ^ i) * count, count), count), :], sems.at[i]
+        )
+        for i, block in enumerate(blocks)
+    ]
+
+
+def run_copies(copies):
+    for copy in copies:
+        copy.start()
+    for copy in copies:
+        copy.wait()
+
+
+def piece_shapes(pieces, width):
+    return [jax.ShapeDtypeStruct((count, width), jnp.bfloat16) for _, _, count in pieces]
+
+
+def project_kernel(pieces, parts, chunk, scalars, *refs):
+    n = len(pieces)
+    blocks, weights, gain = refs[:n], refs[n : n + parts], refs[n + parts]
+    normed, raw, factor, squares, kept, tokens, weight, sems, w_sems, k_sem = refs[n + parts + 1 :]
+    step = pl.program_id(0)
+
+    @pl.when(step == 0)
+    def _():
+        run_copies(
+            piece_copies(pieces, scalars, blocks, tokens, sems)
+            + row_copies(scalars, len(scalars) - 1, weights, weight, w_sems)
+        )
+        pltpu.make_async_copy(tokens, kept, k_sem).start()
+
+    rows = pl.ds(pl.multiple_of(step * chunk, chunk), chunk)
+    values = tokens[rows, :].astype(jnp.float32)
+    scale = lax.rsqrt(jnp.mean(values * values, axis=-1, keepdims=True) + epsilon)
+    low = (values * scale * gain[...]).astype(jnp.bfloat16)
+    normed[...] = low
+    factor[...] = scale
+    product = dot(low, weight[...])
+    raw[...] = product
+    part = product.shape[1] // 3
+    squares[...] = row_sums(product[:, :part] ** 2, product[:, part : 2 * part] ** 2)
+
+    @pl.when(step == pl.num_programs(0) - 1)
+    def _():
+        pltpu.make_async_copy(tokens, kept, k_sem).wait()
+
+
+def project(ring, scalars, blocks, weights, gain):
+    width = blocks[0].shape[1]
+    span = ring.rows * ring.size
+    columns = weights[0].shape[1]
+    chunk = min(256, span)
+    n = len(ring.pieces)
+    by_rows = lambda i, s: (i, 0)
+    return pl.pallas_call(
+        functools.partial(project_kernel, ring.pieces, len(weights), chunk),
+        grid_spec=pltpu.PrefetchScalarGridSpec(
+            num_scalar_prefetch=1,
+            grid=(span // chunk,),
+            in_specs=[anywhere] * (n + len(weights)) + [whole_block((1, width))],
+            out_specs=[
+                pl.BlockSpec((chunk, width), by_rows),
+                pl.BlockSpec((chunk, columns), by_rows),
+                pl.BlockSpec((chunk, 1), by_rows),
+                pl.BlockSpec((8, chunk), lambda i, s: (0, i)),
+                anywhere,
+            ],
+            scratch_shapes=[
+                pltpu.VMEM((span, width), jnp.bfloat16),
+                pltpu.VMEM((width, columns), jnp.bfloat16),
+                pltpu.SemaphoreType.DMA((n,)),
+                pltpu.SemaphoreType.DMA((len(weights),)),
+                pltpu.SemaphoreType.DMA,
+            ],
+        ),
+        out_shape=[
+            jax.ShapeDtypeStruct((span, width), jnp.bfloat16),
+            jax.ShapeDtypeStruct((span, columns), jnp.float32),
+            jax.ShapeDtypeStruct((span, 1), jnp.float32),
+            jax.ShapeDtypeStruct((8, span), jnp.float32),
+            jax.ShapeDtypeStruct((span, width), jnp.bfloat16),
+        ],
+        name="project",
+    )(scalars, *blocks, *weights, gain)
+
+
+def turned(values, cosine, sine):
+    return values * cosine + pltpu.roll(values, values.shape[-1] // 2, 1) * sine
+
+
+def attend_kernel(pieces, parts, chunk, scale, scalars, *refs):
+    q_raw, k_raw, v_raw, factors, gain_q, gain_k, cosine, sine = refs[:8]
+    weights = refs[8 : 8 + parts]
+    query, key, value, mixed, lse = refs[8 + parts : 13 + parts]
+    n = len(pieces)
+    results = refs[13 + parts : 13 + parts + n]
+    weight, total, summed, w_sems, sems = refs[13 + parts + n :]
+    head = pl.program_id(0)
+    last = pl.num_programs(0) - 1
+    tokens, head_dim = query.shape
+
+    @pl.when(head == 0)
+    def _():
+        run_copies(row_copies(scalars, len(scalars) - 1, weights, weight, w_sems))
+
+    columns = as_columns(factors[...])
+    query[...] = turned(
+        q_raw[...] * columns[:, 0:1] * gain_q[...], cosine[...], sine[...]
+    ).astype(jnp.bfloat16)
+    key[...] = turned(
+        k_raw[...] * columns[:, 1:2] * gain_k[...], cosine[...], sine[...]
+    ).astype(jnp.bfloat16)
+    value[...] = v_raw[...].astype(jnp.bfloat16)
+    own_rows = weight[pl.ds(pl.multiple_of(head * head_dim, head_dim), head_dim), :]
+    for begin in range(0, tokens, chunk):
+        rows, seen = pl.ds(begin, chunk), pl.ds(0, begin + chunk)
+        scores = dot(query[rows, :], key[seen, :], columns_last) * scale
+        shape = scores.shape
+        allowed = lax.broadcasted_iota(jnp.int32, shape, 1) <= begin + lax.broadcasted_iota(
+            jnp.int32, shape, 0
+        )
+        scores = jnp.where(allowed, scores, far_low)
+        top = jnp.max(scores, axis=-1, keepdims=True)
+        weights_now = jnp.exp(scores - top)
+        sums = jnp.sum(weights_now, axis=-1, keepdims=True)
+        out = dot(weights_now.astype(jnp.bfloat16), value[seen, :]) / sums
+        mixed[rows, :] = out
+        lse[rows, :] = top + jnp.log(sums)
+        product = dot(out.astype(jnp.bfloat16), own_rows)
+
+        @pl.when(head == 0)
+        def _():
+            total[rows, :] = product
+
+        @pl.when(jnp.logical_and(head > 0, head < last))
+        def _():
+            total[rows, :] += product
+
+        @pl.when(jnp.logical_and(head > 0, head == last))
+        def _():
+            summed[rows, :] = (total[rows, :] + product).astype(jnp.bfloat16)
+
+        @pl.when(jnp.logical_and(head == 0, head == last))
+        def _():
+            summed[rows, :] = product.astype(jnp.bfloat16)
+
+    @pl.when(head == last)
+    def _():
+        run_copies(piece_results(pieces, scalars, summed, results, sems))
+
+
+def attend(ring, scalars, raw, factors, gain_q, gain_k, cosine, sine, weights, head_dim):
+    tokens = raw.shape[0]
+    part = raw.shape[1] // 3
+    heads = part // head_dim
+    width = weights[0].shape[1]
+    n = len(ring.pieces)
+    column = lambda first: pl.BlockSpec((tokens, head_dim), lambda h, s: (0, first + h))
+    gain = pl.BlockSpec((1, head_dim), lambda h, s: (0, h))
+    table = whole_block((tokens, head_dim))
+    low = jax.ShapeDtypeStruct((tokens, part), jnp.bfloat16)
+    out = pl.pallas_call(
+        functools.partial(
+            attend_kernel, ring.pieces, len(weights), min(256, tokens), head_dim ** (-0.5)
+        ),
+        grid_spec=pltpu.PrefetchScalarGridSpec(
+            num_scalar_prefetch=1,
+            grid=(heads,),
+            in_specs=[column(0), column(heads), column(2 * heads), whole_block((8, tokens))]
+            + [gain, gain, table, table]
+            + [anywhere] * len(weights),
+            out_specs=[column(0)] * 4
+            + [pl.BlockSpec((None, tokens, 1), lambda h, s: (h, 0, 0))]
+            + [anywhere] * n,
+            scratch_shapes=[
+                pltpu.VMEM((part, width), jnp.bfloat16),
+                pltpu.VMEM((tokens, width), jnp.float32),
+                pltpu.VMEM((tokens, width), jnp.bfloat16),
+                pltpu.SemaphoreType.DMA((len(weights),)),
+                pltpu.SemaphoreType.DMA((n,)),
+            ],
+        ),
+        out_shape=[low, low, low, jax.ShapeDtypeStruct((tokens, part), jnp.float32)]
+        + [jax.ShapeDtypeStruct((heads, tokens, 1), jnp.float32)]
+        + piece_shapes(ring.pieces, width),
+        name="attend",
+    )(scalars, raw, raw, raw, factors, gain_q, gain_k, cosine, sine, *weights)
+    return out[:5], out[5:]
+
+
+def attend_back_kernel(pieces, parts, chunk, scale, head, scalars, *refs):
+    query, key, value, mixed, lse, q_raw, k_raw, factors, gain_q, gain_k, cosine, sine = refs[:12]
+    n = len(pieces)
+    weights = refs[12 : 12 + parts]
+    blocks = refs[12 + parts : 12 + parts + n]
+    outs = refs[12 + parts + n :]
+    turn_q, turn_k, d_value, dots, sum_q, sum_k = outs[:6]
+    kept = outs[6] if head == 0 else None
+    weight, grads, d_key, d_val, d_query, w_sems, sems, k_sem = outs[-8:]
+    tokens, head_dim = query.shape
+    run_copies(
+        row_copies(scalars, len(scalars) - 1, weights, weight, w_sems)
+        + piece_copies(pieces, scalars, blocks, grads, sems)
+    )
+    if kept is not None:
+        pltpu.make_async_copy(grads, kept, k_sem).start()
+    own_rows = weight[pl.ds(head * head_dim, head_dim), :]
+    for begin in range(0, tokens, chunk):
+        rows, seen = pl.ds(begin, chunk), pl.ds(0, begin + chunk)
+        grad = dot(grads[rows, :], own_rows, columns_last).astype(jnp.bfloat16)
+        queries = query[rows, :]
+        scores = dot(queries, key[seen, :], columns_last) * scale
+        shape = scores.shape
+        allowed = lax.broadcasted_iota(jnp.int32, shape, 1) <= begin + lax.broadcasted_iota(
+            jnp.int32, shape, 0
+        )
+        probs = jnp.where(allowed, jnp.exp(scores - lse[rows, :]), 0.0)
+        delta = jnp.sum(grad.astype(jnp.float32) * mixed[rows, :], axis=-1, keepdims=True)
+        grad_probs = dot(grad, value[seen, :], columns_last)
+        grad_scores = (probs * (grad_probs - delta)).astype(jnp.bfloat16)
+        d_query[rows, :] = dot(grad_scores, key[seen, :]) * scale
+        part_key = dot(grad_scores, queries, rows_first) * scale
+        part_value = dot(probs.astype(jnp.bfloat16), grad, rows_first)
+        if begin > 0:
+            before = pl.ds(0, begin)
+            d_key[before, :] += part_key[:begin]
+            d_val[before, :] += part_value[:begin]
+        d_key[rows, :] = part_key[begin:]
+        d_val[rows, :] = part_value[begin:]
+    d_value[...] = d_val[...].astype(jnp.bfloat16)
+    back_q = turned(d_query[...], cosine[...], -sine[...])
+    back_k = turned(d_key[...], cosine[...], -sine[...])
+    turn_q[...] = back_q
+    turn_k[...] = back_k
+    with_q, with_k = back_q * q_raw[...], back_k * k_raw[...]
+    columns = as_columns(factors[...])
+    sum_q[...] = jnp.sum(with_q * columns[:, 0:1], axis=0, keepdims=True)
+    sum_k[...] = jnp.sum(with_k * columns[:, 1:2], axis=0, keepdims=True)
+    dots[...] = row_sums(with_q * gain_q[...], with_k * gain_k[...])
+    if kept is not None:
+        pltpu.make_async_copy(grads, kept, k_sem).wait()
+
+
+def attend_back(
+    ring, scalars, saved, raw, factors, gain_q, gain_k, cosine, sine, weights, blocks, head_dim,
+    head,
+):
+    query, key, value, mixed, lse = saved
+    tokens, part = query.shape
+    heads = part // head_dim
+    width = weights[0].shape[1]
+    n = len(ring.pieces)
+    column = lambda first: pl.BlockSpec((tokens, head_dim), lambda i, s: (0, first + head))
+    gain = pl.BlockSpec((1, head_dim), lambda i, s: (0, head))
+    table = whole_block((tokens, head_dim))
+    result = jax.ShapeDtypeStruct((tokens, head_dim), jnp.float32)
+    sums = jax.ShapeDtypeStruct((1, head_dim), jnp.float32)
+    kept = [anywhere] if head == 0 else []
+    accumulate = pltpu.VMEM((tokens, head_dim), jnp.float32)
+    return pl.pallas_call(
+        functools.partial(
+            attend_back_kernel, ring.pieces, len(weights), min(256, tokens), head_dim ** (-0.5),
+            head,
+        ),
+        grid_spec=pltpu.PrefetchScalarGridSpec(
+            num_scalar_prefetch=1,
+            grid=(1,),
+            in_specs=[column(0)] * 4
+            + [pl.BlockSpec((None, tokens, 1), lambda i, s: (head, 0, 0))]
+            + [column(0), column(heads), whole_block((8, tokens)), gain, gain, table, table]
+            + [anywhere] * (len(weights) + n),
+            out_specs=[table] * 3
+            + [whole_block((8, tokens))]
+            + [whole_block((1, head_dim))] * 2
+            + kept,
+            scratch_shapes=[
+                pltpu.VMEM((part, width), jnp.bfloat16),
+                pltpu.VMEM((tokens, width), jnp.bfloat16),
+                accumulate,
+                accumulate,
+                accumulate,
+                pltpu.SemaphoreType.DMA((len(weights),)),
+                pltpu.SemaphoreType.DMA((n,)),
+                pltpu.SemaphoreType.DMA,
+            ],
+        ),
+        out_shape=[
+            result,
+            result,
+            jax.ShapeDtypeStruct((tokens, head_dim), jnp.bfloat16),
+            jax.ShapeDtypeStruct((8, tokens), jnp.float32),
+            sums,
+            sums,
+        ]
+        + [jax.ShapeDtypeStruct((tokens, width), jnp.bfloat16)] * len(kept),
+        name="attend_back",
+    )(
+        scalars, query, key, value, mixed, lse, raw, raw, factors, gain_q, gain_k, cosine, sine,
+        *weights, *blocks,
+    )
+
+
+def project_back_kernel(pieces, parts, chunk, heads, scalars, *refs):
+    turns, refs = refs[: 3 * heads], refs[3 * heads :]
+    raw, factors, dots, gain_q, gain_k, tokens, in_factor = refs[:7]
+    n = len(pieces)
+    weights = refs[7 : 7 + parts]
+    grad_raw, sum_in = refs[7 + parts : 9 + parts]
+    results = refs[9 + parts : 9 + parts + n]
+    weight, summed, w_sems, sems = refs[9 + parts + n :]
+    step = pl.program_id(0)
+    head_dim = turns[0].shape[1]
+    part = heads * head_dim
+
+    @pl.when(step == 0)
+    def _():
+        run_copies(row_copies(scalars, len(scalars) - 1, weights, weight, w_sems))
+        sum_in[...] = jnp.zeros_like(sum_in)
+
+    factor_columns, dot_columns = as_columns(factors[...]), as_columns(dots[...])
+    for i, gain in enumerate((gain_q, gain_k)):
+        factor = factor_columns[:, i : i + 1]
+        cubed = factor * factor * factor * dot_columns[:, i : i + 1]
+        for head in range(heads):
+            columns = pl.ds(i * part + head * head_dim, head_dim)
+            turn = turns[3 * head + i][...] * gain[:, head * head_dim : (head + 1) * head_dim]
+            grad_raw[:, columns] = (factor * turn - raw[:, columns] * cubed).astype(jnp.bfloat16)
+    for head in range(heads):
+        grad_raw[:, pl.ds(2 * part + head * head_dim, head_dim)] = turns[3 * head + 2][...]
+    normed = dot(grad_raw[...], weight[...], columns_last)
+    sum_in[...] += jnp.sum(
+        normed * (tokens[...].astype(jnp.float32) * in_factor[...]), axis=0, keepdims=True
+    )
+    summed[pl.ds(pl.multiple_of(step * chunk, chunk), chunk), :] = normed.astype(jnp.bfloat16)
+
+    @pl.when(step == pl.num_programs(0) - 1)
+    def _():
+        run_copies(piece_results(pieces, scalars, summed, results, sems))
+
+
+def project_back(
+    ring, scalars, turns, raw, factors, dots, gain_q, gain_k, tokens, in_factor, weights
+):
+    span, width = tokens.shape
+    heads, head_dim = len(turns) // 3, turns[0].shape[1]
+    part = heads * head_dim
+    columns = weights[0].shape[1]
+    chunk = min(256, span)
+    n = len(ring.pieces)
+    by_rows = lambda wide: pl.BlockSpec((chunk, wide), lambda i, s: (i, 0))
+    out = pl.pallas_call(
+        functools.partial(project_back_kernel, ring.pieces, len(weights), chunk, heads),
+        grid_spec=pltpu.PrefetchScalarGridSpec(
+            num_scalar_prefetch=1,
+            grid=(span // chunk,),
+            in_specs=[by_rows(head_dim)] * (3 * heads)
+            + [by_rows(columns)]
+            + [pl.BlockSpec((8, chunk), lambda i, s: (0, i))] * 2
+            + [whole_block((1, part))] * 2
+            + [by_rows(width), by_rows(1)]
+            + [anywhere] * len(weights),
+            out_specs=[by_rows(columns), whole_block((1, width))] + [anywhere] * n,
+            scratch_shapes=[
+                pltpu.VMEM((width, columns), jnp.bfloat16),
+                pltpu.VMEM((span, width), jnp.bfloat16),
+                pltpu.SemaphoreType.DMA((len(weights),)),
+                pltpu.SemaphoreType.DMA((n,)),
+            ],
+        ),
+        out_shape=[
+            jax.ShapeDtypeStruct((span, columns), jnp.bfloat16),
+            jax.ShapeDtypeStruct((1, width), jnp.float32),
+        ]
+        + piece_shapes(ring.pieces, width),
+        name="project_back",
+    )(
+        scalars, *turns, raw, factors, dots, gain_q, gain_k, tokens, in_factor, *weights
+    )
+    return out[0], out[1], out[2:]
+
+
+def expert_column(scalars, part, parts, wide):
+    half = parts // 2
+    relative = 2 * (part % half) + jnp.where(part < half, 1, 0)
+    return pl.multiple_of((scalars[len(scalars) - 1] ^ relative) * wide, wide)
+
+
+def weight_copies(groups, scalars, buffers, sems, step, parts):
+    expert, part, place = step // parts, step % parts, step % 2
+    wide = buffers.shape[3]
+    columns = pl.ds(expert_column(scalars, part, parts, wide), wide)
+    return [
+        pltpu.make_async_copy(
+            group.at[expert, :, columns], buffers.at[place, g], sems.at[place, g]
+        )
+        for g, group in enumerate(groups)
+    ]
+
+
+def stream(groups, scalars, buffers, sems, parts):
+    step = pl.program_id(0)
+
+    @pl.when(step == 0)
+    def _():
+        for copy in weight_copies(groups, scalars, buffers, sems, step, parts):
+            copy.start()
+
+    @pl.when(step + 1 < pl.num_programs(0))
+    def _():
+        for copy in weight_copies(groups, scalars, buffers, sems, step + 1, parts):
+            copy.start()
+
+    for copy in weight_copies(groups, scalars, buffers, sems, step, parts):
+        copy.wait()
+    return buffers.at[step % 2]
+
+
+def expert_first_kernel(pieces, parts, chunk, scalars, *refs):
+    n = len(pieces)
+    blocks, down = refs[:n], refs[n]
+    product, kept, rows_all, buffers, sems, w_sems, k_sem = refs[n + 1 :]
+    step = pl.program_id(0)
+
+    @pl.when(step == 0)
+    def _():
+        copies = piece_copies(pieces, scalars, blocks, rows_all, sems)
+        for copy in copies:
+            copy.start()
+
+    weight = stream([down], scalars, buffers, w_sems, parts)
+
+    @pl.when(step == 0)
+    def _():
+        for copy in piece_copies(pieces, scalars, blocks, rows_all, sems):
+            copy.wait()
+        pltpu.make_async_copy(rows_all, kept, k_sem).start()
+
+    for begin in range(0, rows_all.shape[0], chunk):
+        rows = pl.ds(begin, chunk)
+        product[rows, :] = dot(rows_all[rows, :], weight[0])
+
+    @pl.when(step == pl.num_programs(0) - 1)
+    def _():
+        pltpu.make_async_copy(rows_all, kept, k_sem).wait()
+
+
+def expert_first(ring, scalars, blocks, down):
+    experts, width, hidden = down.shape
+    parts = hidden_parts
+    step_hidden = hidden // parts
+    span = ring.rows * ring.size
+    n = len(ring.pieces)
+    return pl.pallas_call(
+        functools.partial(expert_first_kernel, ring.pieces, parts, min(256, span)),
+        grid_spec=pltpu.PrefetchScalarGridSpec(
+            num_scalar_prefetch=1,
+            grid=(experts * parts,),
+            in_specs=[anywhere] * (n + 1),
+            out_specs=[
+                pl.BlockSpec((None, span, step_hidden), lambda i, s: (i // parts, 0, i % parts)),
+                anywhere,
+            ],
+            scratch_shapes=[
+                pltpu.VMEM((span, width), jnp.bfloat16),
+                pltpu.VMEM((2, 1, width, step_hidden), jnp.bfloat16),
+                pltpu.SemaphoreType.DMA((n,)),
+                pltpu.SemaphoreType.DMA((2, 1)),
+                pltpu.SemaphoreType.DMA,
+            ],
+        ),
+        out_shape=[
+            jax.ShapeDtypeStruct((experts, span, parts * step_hidden), jnp.float32),
+            jax.ShapeDtypeStruct((span, width), jnp.bfloat16),
+        ],
+        name="expert_first",
+    )(scalars, *blocks, down)
+
+
+def expert_hidden_kernel(pieces, parts, chunk, scalars, *refs):
+    n = len(pieces)
+    blocks, gate, up = refs[:n], refs[n], refs[n + 1]
+    product, gates = refs[n + 2 : n + 4]
+    act, gated, d_gate, d_up, grad_gates, kept = refs[n + 4 : n + 10]
+    rows_all, buffers, sems, w_sems, k_sem = refs[n + 10 :]
+    step = pl.program_id(0)
+
+    @pl.when(step == 0)
+    def _():
+        copies = piece_copies(pieces, scalars, blocks, rows_all, sems)
+        for copy in copies:
+            copy.start()
+
+    weight = stream([gate, up], scalars, buffers, w_sems, parts)
+
+    @pl.when(step == 0)
+    def _():
+        for copy in piece_copies(pieces, scalars, blocks, rows_all, sems):
+            copy.wait()
+        pltpu.make_async_copy(rows_all, kept, k_sem).start()
+
+    @pl.when(step % parts == 0)
+    def _():
+        grad_gates[...] = jnp.zeros_like(grad_gates)
+
+    for begin in range(0, rows_all.shape[0], chunk):
+        rows = pl.ds(begin, chunk)
+        gate_hid = dot(rows_all[rows, :], weight[0])
+        up_hid = dot(rows_all[rows, :], weight[1])
+        own_gate = gates[rows, :]
+        back = product[rows, :]
+        sig = 1.0 / (1.0 + jnp.exp(-gate_hid))
+        silu = gate_hid * sig
+        act_low = (silu * up_hid).astype(jnp.bfloat16)
+        act_now = act_low.astype(jnp.float32)
+        act[rows, :] = act_low
+        gated[rows, :] = (own_gate * act_now).astype(jnp.bfloat16)
+        grad_gates[rows, :] += jnp.sum(act_now * back, axis=-1, keepdims=True)
+        grad_act = own_gate * back
+        d_gate[rows, :] = (grad_act * up_hid * (sig * (1.0 + gate_hid * (1.0 - sig)))).astype(
+            jnp.bfloat16
+        )
+        d_up[rows, :] = (grad_act * silu).astype(jnp.bfloat16)
+
+    @pl.when(step == pl.num_programs(0) - 1)
+    def _():
+        pltpu.make_async_copy(rows_all, kept, k_sem).wait()
+
+
+def hidden_place(parts, experts):
+    half = parts // 2
+    return lambda i: ((i % parts) // half * experts + i // parts) * half + (i % parts) % half
+
+
+def expert_hidden(ring, scalars, blocks, gate, up, product, gates):
+    experts, width, hidden_units = gate.shape
+    parts = hidden_parts
+    step_hidden = hidden_units // parts
+    span = ring.rows * ring.size
+    n = len(ring.pieces)
+    place = hidden_place(parts, experts)
+    relative = pl.BlockSpec((None, span, step_hidden), lambda i, s: (i // parts, 0, i % parts))
+    placed = pl.BlockSpec((span, step_hidden), lambda i, s: (0, place(i)))
+    column = pl.BlockSpec((None, span, 1), lambda i, s: (i // parts, 0, 0))
+    hidden = jax.ShapeDtypeStruct((span, experts * parts * step_hidden), jnp.bfloat16)
+    return pl.pallas_call(
+        functools.partial(expert_hidden_kernel, ring.pieces, parts, min(256, span)),
+        grid_spec=pltpu.PrefetchScalarGridSpec(
+            num_scalar_prefetch=1,
+            grid=(experts * parts,),
+            in_specs=[anywhere] * (n + 2) + [relative, column],
+            out_specs=[placed] * 4 + [column, anywhere],
+            scratch_shapes=[
+                pltpu.VMEM((span, width), jnp.bfloat16),
+                pltpu.VMEM((2, 2, width, step_hidden), jnp.bfloat16),
+                pltpu.SemaphoreType.DMA((n,)),
+                pltpu.SemaphoreType.DMA((2, 2)),
+                pltpu.SemaphoreType.DMA,
+            ],
+        ),
+        out_shape=[
+            hidden,
+            hidden,
+            hidden,
+            hidden,
+            jax.ShapeDtypeStruct((experts, span, 1), jnp.float32),
+            jax.ShapeDtypeStruct((span, width), jnp.bfloat16),
+        ],
+        name="expert_hidden",
+    )(scalars, *blocks, gate, up, product, gates)
+
+
+def pack_weights(scalars, weights, packed, parts):
+    experts, _, hidden = weights.shape
+    wide = hidden // parts
+    place = hidden_place(parts, experts)
+    for expert in range(experts):
+        for part in range(parts):
+            column = place(expert * parts + part) * wide
+            relative = 2 * (part % (parts // 2)) + (1 if part < parts // 2 else 0)
+            source = pl.multiple_of((scalars[len(scalars) - 1] ^ relative) * wide, wide)
+            packed[:, column : column + wide] = weights[expert, :, pl.ds(source, wide)]
+
+
+def store_pieces(pieces, scalars, source, results):
+    rows = pieces[0][2]
+    for (slot, first, count), result in zip(pieces, results):
+        begin = pl.multiple_of(scalars[slot] * rows + first, count)
+        result[...] = source[pl.ds(begin, count), :]
+
+
+def expert_inputs_kernel(pieces, parts, scalars, *refs):
+    d_gate, d_up = refs[:2]
+    gate, up = refs[2:4]
+    n = len(pieces)
+    results = refs[4 : 4 + n]
+    packed, summed = refs[4 + n :]
+    pack_weights(scalars, gate, packed.at[0], parts)
+    pack_weights(scalars, up, packed.at[1], parts)
+    total = dot(d_gate[...], packed[0], columns_last) + dot(d_up[...], packed[1], columns_last)
+    summed[...] = total.astype(jnp.bfloat16)
+    store_pieces(pieces, scalars, summed, results)
+
+
+def expert_inputs(ring, scalars, d_gate, d_up, gate, up):
+    experts, width, hidden_units = gate.shape
+    parts = hidden_parts
+    span, hidden = d_gate.shape
+    wide = min(256, width)
+    whole = pl.BlockSpec((span, hidden), lambda i, s: (0, 0), pipeline_mode=pl.Buffered(1))
+    weight = pl.BlockSpec((experts, wide, hidden_units), lambda i, s: (0, i, 0))
+    return pl.pallas_call(
+        functools.partial(expert_inputs_kernel, ring.pieces, parts),
+        grid_spec=pltpu.PrefetchScalarGridSpec(
+            num_scalar_prefetch=1,
+            grid=(width // wide,),
+            in_specs=[whole] * 2 + [weight] * 2,
+            out_specs=[
+                pl.BlockSpec((count, wide), lambda i, s: (0, i)) for _, _, count in ring.pieces
+            ],
+            scratch_shapes=[
+                pltpu.VMEM((2, wide, hidden), jnp.bfloat16),
+                pltpu.VMEM((span, wide), jnp.bfloat16),
+            ],
+        ),
+        out_shape=piece_shapes(ring.pieces, width),
+        name="expert_inputs",
+    )(scalars, d_gate, d_up, gate, up)
+
+
+def expert_outputs_kernel(pieces, parts, scalars, *refs):
+    act, gates = refs[:2]
+    down = refs[2]
+    n = len(pieces)
+    results = refs[3 : 3 + n]
+    packed, summed = refs[3 + n :]
+    experts, _, hidden_units = down.shape
+    pack_weights(scalars, down, packed, parts)
+    half = hidden_units // 2
+    total = None
+    for expert in range(experts):
+        first = pl.ds(expert * half, half)
+        second = pl.ds((experts + expert) * half, half)
+        out = dot(act[:, first], packed[:, first], columns_last)
+        out = out + dot(act[:, second], packed[:, second], columns_last)
+        out = gates[expert] * out.astype(jnp.bfloat16).astype(jnp.float32)
+        total = out if total is None else total + out
+    summed[...] = total.astype(jnp.bfloat16)
+    store_pieces(pieces, scalars, summed, results)
+
+
+def expert_outputs(ring, scalars, act, gates, down):
+    experts, width, hidden_units = down.shape
+    parts = hidden_parts
+    span, hidden = act.shape
+    wide = min(256, width)
+    whole = pl.BlockSpec((span, hidden), lambda i, s: (0, 0), pipeline_mode=pl.Buffered(1))
+    return pl.pallas_call(
+        functools.partial(expert_outputs_kernel, ring.pieces, parts),
+        grid_spec=pltpu.PrefetchScalarGridSpec(
+            num_scalar_prefetch=1,
+            grid=(width // wide,),
+            in_specs=[whole, whole_block((experts, span, 1))]
+            + [pl.BlockSpec((experts, wide, hidden_units), lambda i, s: (0, i, 0))],
+            out_specs=[
+                pl.BlockSpec((count, wide), lambda i, s: (0, i)) for _, _, count in ring.pieces
+            ],
+            scratch_shapes=[
+                pltpu.VMEM((wide, hidden), jnp.bfloat16),
+                pltpu.VMEM((span, wide), jnp.bfloat16),
+            ],
+        ),
+        out_shape=piece_shapes(ring.pieces, width),
+        name="expert_outputs",
+    )(scalars, act, gates, down)
+
+
+def weight_far_kernel(left, right, result):
+    result[...] = dot(left[...], right[...], rows_first).astype(jnp.bfloat16)
+
+
+def weight_far(left, right):
+    span, width = left.shape
+    split = right.shape[1] // 2
+    wide = min(256, width)
+    return pl.pallas_call(
+        weight_far_kernel,
+        grid=(width // wide,),
+        in_specs=[
+            pl.BlockSpec((span, wide), lambda i: (0, i)),
+            pl.BlockSpec((span, split), lambda i: (0, 0), pipeline_mode=pl.Buffered(1)),
+        ],
+        out_specs=pl.BlockSpec((wide, split), lambda i: (i, 0)),
+        out_shape=jax.ShapeDtypeStruct((width, split), jnp.bfloat16),
+        name="weight_far",
+    )(left, right)
+
+
+def weight_near_kernel(scalars, left, right, arrived, result):
+    total = dot(left[...], right[...], rows_first) + arrived[...].astype(jnp.float32)
+    experts, step_hidden = result.shape[0] // 2, result.shape[2]
+    own = scalars[len(scalars) - 1] // 2
+    for expert in range(experts):
+        for other in range(2):
+            column = (2 * expert + other) * step_hidden
+            result[(own ^ other) * experts + expert] = total[
+                :, column : column + step_hidden
+            ].astype(jnp.bfloat16)
+
+
+def weight_near(scalars, left, right, arrived, experts):
+    span, width = left.shape
+    split = right.shape[1] // 2
+    step_hidden = split // (2 * experts)
+    wide = min(256, width)
+    return pl.pallas_call(
+        weight_near_kernel,
+        grid_spec=pltpu.PrefetchScalarGridSpec(
+            num_scalar_prefetch=1,
+            grid=(width // wide,),
+            in_specs=[
+                pl.BlockSpec((span, wide), lambda i, s: (0, i)),
+                pl.BlockSpec((span, split), lambda i, s: (0, 1), pipeline_mode=pl.Buffered(1)),
+                pl.BlockSpec((wide, split), lambda i, s: (i, 0)),
+            ],
+            out_specs=pl.BlockSpec((2 * experts, wide, step_hidden), lambda i, s: (0, i, 0)),
+        ),
+        out_shape=jax.ShapeDtypeStruct((2 * experts, width, step_hidden), jnp.bfloat16),
+        name="weight_near",
+    )(scalars, left, right, arrived)
+
+
+def weight_rows_kernel(scalars, left, right, result):
+    result[...] = dot(left[...], right[...], rows_first).astype(jnp.bfloat16)
+
+
+def weight_rows(scalars, left, right, parts):
+    span, width = left.shape
+    columns = right.shape[1]
+    count = width // parts
+    own = scalars.shape[0] - 1
+    relative = lambda i: 2 * (i % 2) + jnp.where(i < 2, 1, 0)
+    return pl.pallas_call(
+        weight_rows_kernel,
+        grid_spec=pltpu.PrefetchScalarGridSpec(
+            num_scalar_prefetch=1,
+            grid=(parts,),
+            in_specs=[
+                pl.BlockSpec((span, count), lambda i, s: (0, s[own] ^ relative(i))),
+                whole_block((span, columns)),
+            ],
+            out_specs=pl.BlockSpec((None, count, columns), lambda i, s: (i, 0, 0)),
+        ),
+        out_shape=jax.ShapeDtypeStruct((parts, count, columns), jnp.bfloat16),
+        name="weight_rows",
+    )(scalars, left, right)
+
+
+def per_device(
+    tokens,
+    cotangent,
+    routes,
+    w_query,
+    w_key,
+    w_value,
+    w_output,
+    w_router,
+    gain_attn,
+    gain_query,
+    gain_key,
+    gain_ffn,
+    expert_gate,
+    expert_up,
+    expert_down,
+):
+    rows, width = tokens.shape
+    size = lax.axis_size("fsdp")
+    dp_size = lax.axis_size("x") * lax.axis_size("core")
+    head_dim = width // HEADS
+    own_heads = HEADS // size
+    part = own_heads * head_dim
+    own_rows = w_query.shape[0]
+    local_experts = expert_gate.shape[0]
+    num_experts = local_experts * size
+    group = part // own_rows
+    span = rows * size
+    f_index = lax.axis_index("fsdp")
+    d_index = lax.axis_index(dp_axes)
+    low, f32 = jnp.bfloat16, jnp.float32
+    ring = Ring(size, rows)
+    half = ring.half
+    scalars = jnp.concatenate([ring.slot_device, d_index[None].astype(jnp.int32)])
+    dp_flat = (*dp_axes, "fsdp")
+    to_rows = []
+    for flat in range(dp_size * size):
+        to_rows.append((flat, (flat % group) * size + flat // group))
+    from_rows = [(b, a) for a, b in to_rows]
+
+    packed = jnp.concatenate(
+        [w.reshape(own_rows, size, part) for w in (w_query, w_key, w_value)], axis=2
+    ).transpose(1, 0, 2)
+    packed = lax.all_to_all(packed, "fsdp", split_axis=0, concat_axis=0, tiled=True)
+    packed = packed.reshape(size * own_rows, 3 * part)
+
+    small = jnp.concatenate(
+        [w_router.T, gain_attn[None], gain_query[None], gain_key[None], gain_ffn[None]], axis=0
+    )
+    small = pair_gather(small, dp_axes, dp_size)
+
+    token_ring, small_ring = ring.gather(tokens), ring.gather(small, False)
+    token_steps, small_steps = [token_ring.step()], [small_ring.step()]
+    out_rows = lax.ppermute(after(w_output, token_steps[0]), dp_flat, to_rows)
+    for k in range(1, half):
+        ties = {1: packed, half - 1: (token_steps[-1], out_rows)}.get(k, token_steps[-1])
+        small_steps.append(small_ring.step(ties))
+        token_steps.append(token_ring.step((ties, small_steps[k - 1])))
+    token_blocks = token_ring.blocks()
+    w_in = share_relative(packed, dp_size, None, token_steps[2])
+    small = small_ring.stacked().transpose(2, 1, 0, 3).reshape(-1, width)
+    router = small[:num_experts]
+    gains = small[num_experts:].astype(f32)
+    gain_in, gain_q, gain_k, gain_mid = (gains[i][None, :] for i in range(4))
+    gain_q = lax.dynamic_slice_in_dim(gain_q, f_index * part, part, 1)
+    gain_k = lax.dynamic_slice_in_dim(gain_k, f_index * part, part, 1)
+    half_dim = head_dim // 2
+    inv_freq = rope_base ** (-(jnp.arange(half_dim, dtype=f32) * 2.0) / head_dim)
+    angles = jnp.arange(span, dtype=jnp.int32).astype(f32)[:, None] * inv_freq[None, :]
+    cosine, sine = jnp.cos(angles), jnp.sin(angles)
+    cosine = jnp.concatenate([cosine, cosine], axis=1)
+    sine = jnp.concatenate([-sine, sine], axis=1)
+    w_out = share_relative(out_rows, dp_size, token_steps[2], token_steps[3])
+
+    down_w = lax.all_gather(expert_down, dp_axes, axis=2, tiled=True)
+    gate_w = lax.all_gather(expert_gate, dp_axes, axis=2, tiled=True)
+    up_w = lax.all_gather(expert_up, dp_axes, axis=2, tiled=True)
+
+    cot_ring = ring.gather(cotangent)
+    cot_step = cot_ring.step(token_steps[3])
+    normed, raw, in_factor, squares, x_all = project(
+        ring, scalars, token_blocks, w_in, gain_in
+    )
+    squares = pair_sum(after(squares, (cot_step, w_out)), "fsdp", size)
+    cot_step = cot_ring.step(squares)
+    factors = lax.rsqrt(squares / width + epsilon)
+    saved, attn_pieces = attend(
+        ring, scalars, raw, factors, gain_q, gain_k, cosine, sine, w_out, head_dim
+    )
+    attn_ring = ring.reduce(after(attn_pieces, cot_step))
+    attn_ring.step()
+    cot_step = cot_ring.step(attn_pieces[0])
+    attn_step = attn_ring.step(cot_step)
+    cot_step = cot_ring.step(attn_step)
+    attn_ring.step(cot_step)
+    attn_ring.step()
+    resid_mid = tokens.astype(f32) + attn_ring.total()
+
+    mid_factor = lax.rsqrt(jnp.mean(resid_mid * resid_mid, axis=-1, keepdims=True) + epsilon)
+    mid_low = (resid_mid * mid_factor * gain_mid).astype(low)
+    mid_ring = ring.gather(mid_low)
+    mid_steps = [mid_ring.step()]
+    logits = dot(mid_low, router, columns_last)
+    chosen_mask = jnp.any(
+        routes[:, :, None] == jnp.arange(num_experts, dtype=jnp.int32)[None, None, :], axis=1
+    )
+    router_probs = jax.nn.softmax(logits, axis=-1)
+    chosen = jnp.where(chosen_mask, router_probs, 0.0)
+    chosen_sum = jnp.sum(chosen, axis=-1, keepdims=True)
+    gates = chosen / chosen_sum
+    gate_ring = ring.gather(gates.T, False)
+    gate_steps = [gate_ring.step(mid_steps[0])]
+    mid_steps.append(mid_ring.step())
+    back_act, cot_all = expert_first(
+        ring, after(scalars, mid_steps[0]), cot_ring.blocks(), down_w
+    )
+    gate_steps.append(gate_ring.step((mid_steps[1], back_act)))
+    mid_steps.append(mid_ring.step((back_act, gate_steps[0])))
+    gate_steps.append(gate_ring.step(mid_steps[2]))
+    mid_steps.append(mid_ring.step(gate_steps[1]))
+    gate_steps.append(gate_ring.step(mid_steps[2]))
+    mid_blocks = mid_ring.blocks()
+    gates_all = gate_ring.stacked()
+    own_gates = lax.dynamic_slice_in_dim(gates_all, f_index * local_experts, local_experts, 1)
+    own_gates = own_gates.transpose(1, 0, 2).reshape(local_experts, span)[:, :, None]
+    act, act_gated, d_gate, d_up, grad_gates, mid_all = expert_hidden(
+        ring, scalars, mid_blocks, gate_w, up_w, back_act, own_gates
+    )
+    grad_in = expert_inputs(ring, scalars, d_gate, d_up, gate_w, up_w)
+
+    def far_part(left, right, ties):
+        return weight_far(after(left, ties), right)
+
+    def near_part(left, right, far, ties):
+        far = lax.ppermute(after(far, ties), dp_axes, exchange_pairs(dp_size, 1))
+        return weight_near(scalars, after(left, ties), right, far, local_experts)
+
+    def finish(near):
+        return lax.psum_scatter(near, "x", scatter_dimension=0, tiled=True).astype(f32)
+
+    by_device = grad_gates.reshape(local_experts, size, rows)
+    grad_ring, route_ring = ring.reduce(grad_in), ring.gather(by_device, False)
+    route_steps = [route_ring.step(grad_in)]
+    grad_steps = [grad_ring.step()]
+    gate_far = far_part(mid_all, d_gate, grad_in)
+    route_steps.append(route_ring.step(grad_steps[0]))
+    grad_steps.append(grad_ring.step((gate_far, route_steps[0])))
+    up_far = far_part(mid_all, d_up, grad_steps[0])
+    route_steps.append(route_ring.step(grad_steps[1]))
+    grad_steps.append(grad_ring.step((up_far, route_steps[1])))
+    gate_near = near_part(mid_all, d_gate, gate_far, grad_steps[1])
+    route_steps.append(route_ring.step(grad_steps[2]))
+    grad_steps.append(grad_ring.step((gate_near, route_steps[2])))
+    up_near = near_part(mid_all, d_up, up_far, grad_steps[2])
+    grad_mid = after(grad_ring.total(), up_near)
+
+    gates_back = route_ring.stacked()
+    gates_back = lax.dynamic_slice_in_dim(gates_back, f_index, 1, 2)
+    gates_back = gates_back.reshape(num_experts, rows).T
+    inner = jnp.sum(jnp.where(chosen_mask, gates_back * gates, 0.0), axis=-1, keepdims=True)
+    grad_probs = jnp.where(chosen_mask, (gates_back - inner) / chosen_sum, 0.0)
+    grad_logits = router_probs * (
+        grad_probs - jnp.sum(router_probs * grad_probs, axis=-1, keepdims=True)
+    )
+    grad_logits_low = grad_logits.astype(low)
+    grad_router = dot(grad_logits_low, mid_low, rows_first)
+    grad_mid = grad_mid + dot(grad_logits_low, router)
+    grad_out = cotangent.astype(f32)
+    scaled = grad_mid * gain_mid
+    grad_resid = (
+        grad_out
+        + mid_factor * scaled
+        - resid_mid * mid_factor**3 * jnp.mean(scaled * resid_mid, axis=-1, keepdims=True)
+    )
+    grad_gain_mid = jnp.sum(grad_mid * resid_mid * mid_factor, axis=0)
+    grad_low = grad_resid.astype(low)
+
+    back_ring = ring.gather(grad_low)
+    back_steps = [back_ring.step()]
+    down_far = far_part(cot_all, act_gated, grad_low)
+    back_steps.append(back_ring.step(down_far))
+    moe_pieces = expert_outputs(ring, after(scalars, back_steps[0]), act, own_gates, down_w)
+    back_steps.append(back_ring.step(moe_pieces[0]))
+    down_near = near_part(cot_all, act_gated, down_far, back_steps[1])
+    back_steps.append(back_ring.step(down_near))
+    grad_blocks = back_ring.blocks()
+
+    def head_back(head, ties):
+        return attend_back(
+            ring, after(scalars, ties), saved, raw, factors, gain_q, gain_k, cosine, sine, w_out,
+            grad_blocks, head_dim, head,
+        )
+
+    moe_ring = ring.reduce(after(moe_pieces, back_steps[3]))
+    moe_step = moe_ring.step()
+    backs = [head_back(0, back_steps[3])]
+    for head in range(1, own_heads):
+        if moe_ring.left > 2:
+            moe_step = moe_ring.step(backs[-1])
+        backs.append(head_back(head, backs[-1][0]))
+    grad_attn_out = backs[0][6]
+    dots = after(sum(back[3] for back in backs), moe_step)
+    grad_gain_q = jnp.concatenate([back[4] for back in backs], axis=1)
+    grad_gain_k = jnp.concatenate([back[5] for back in backs], axis=1)
+    grad_w_out = dot(saved[3].astype(low), after(grad_attn_out, dots), rows_first)
+    dots = pair_sum(dots, "fsdp", size) / width
+    grad_w_out = jnp.concatenate(
+        [
+            lax.dynamic_slice_in_dim(grad_w_out, (d_index ^ k) * own_rows, own_rows, 0)[None]
+            for k in (1, 3, 0, 2)
+        ],
+        axis=0,
+    ).astype(low)
+    while moe_ring.left > 1:
+        moe_step = moe_ring.step(dots)
+    grad_raw, grad_gain_in, normed_pieces = project_back(
+        ring, scalars, [value for back in backs for value in back[:3]], raw, factors,
+        after(dots, grad_w_out), gain_q, gain_k, x_all, in_factor, w_in,
+    )
+    grad_w_out = combine_relative(grad_w_out)[0].astype(low)
+    grad_w_out = lax.ppermute(grad_w_out, dp_flat, from_rows).astype(f32)
+    normed_pieces = after(normed_pieces, moe_step)
+    moe_step = moe_ring.step(normed_pieces)
+    layer_out = (resid_mid + moe_ring.total()).astype(low)
+
+    in_ring = ring.reduce(normed_pieces)
+    in_steps = [in_ring.step()]
+    grad_w_in = weight_rows(scalars, after(normed, normed_pieces), grad_raw, dp_size)
+    grad_gains = lax.dynamic_update_slice(
+        jnp.zeros((2, width), f32),
+        jnp.concatenate([grad_gain_q, grad_gain_k], axis=0),
+        (0, f_index * part),
+    )
+    sums = jnp.concatenate([grad_router, grad_gain_mid[None], grad_gain_in, grad_gains], axis=0)
+    sums = pair_scatter(after(sums, normed_pieces), dp_axes, dp_size)
+    in_steps.append(in_ring.step((grad_w_in, moe_step)))
+    grad_w_in = combine_relative(grad_w_in, (in_steps[0], in_steps[0]))[0].astype(low)
+    sums = pair_scatter(sums, "fsdp", size, {4: in_steps[0], 2: in_steps[1]})
+    in_steps.append(in_ring.step())
+    in_steps.append(in_ring.step(grad_w_in))
+    grad_normed = in_ring.total()
+    grad_gate_w, grad_up_w, grad_down_w = (
+        finish(near) for near in (gate_near, up_near, down_near)
+    )
+    grad_w_in = grad_w_in.reshape(size, own_rows, 3 * part)
+    grad_w_in = lax.all_to_all(grad_w_in, "fsdp", split_axis=0, concat_axis=0, tiled=True)
+    grad_w_in = [
+        grad_w_in[:, :, i * part : (i + 1) * part].transpose(1, 0, 2).reshape(own_rows, width)
+        for i in range(3)
+    ]
+    grad_w_in = [values.astype(f32) for values in grad_w_in]
+    own_x = tokens.astype(f32)
+    own_factor = lax.rsqrt(jnp.mean(own_x * own_x, axis=-1, keepdims=True) + epsilon)
+    scaled_in = grad_normed * gain_in
+    grad_tokens = (
+        grad_resid
+        + own_factor * scaled_in
+        - own_x * own_factor**3 * jnp.mean(scaled_in * own_x, axis=-1, keepdims=True)
+    )
+    return (
+        layer_out,
+        grad_tokens,
+        grad_w_in[0],
+        grad_w_in[1],
+        grad_w_in[2],
+        grad_w_out,
+        sums[:num_experts].T,
+        sums[num_experts + 1],
+        sums[num_experts + 2],
+        sums[num_experts + 3],
+        sums[num_experts],
+        grad_gate_w,
+        grad_up_w,
+        grad_down_w,
+    )
+
+
+def splits_evenly(mesh):
+    size, dp_size = mesh.shape["fsdp"], mesh.shape["dp"]
+    powers = size & (size - 1) == 0 and dp_size & (dp_size - 1) == 0
+    return powers and dp_size == 4 and size == 8 and HEADS % size == 0
+
+
 def solution(mesh):
+    split = splits_evenly(mesh)
+    dp = "dp"
+    if split:
+        devices = mesh.devices.reshape(2, 2, mesh.shape["fsdp"])
+        mesh, dp = jax.sharding.Mesh(devices, (*dp_axes, "fsdp")), dp_axes
+    flat = (*dp_axes, "fsdp") if split else ("dp", "fsdp")
     in_specs = (
-        P(("dp", "fsdp"), None),
-        P(("dp", "fsdp"), None),
-        P(("dp", "fsdp"), None),
-        P(("dp", "fsdp"), None),
-        P(("dp", "fsdp"), None),
-        P(("dp", "fsdp"), None),
-        P(("dp", "fsdp"), None),
-        P(("dp", "fsdp"), None),
-        P(("dp", "fsdp")),
-        P(("dp", "fsdp")),
-        P(("dp", "fsdp")),
-        P(("dp", "fsdp")),
-        P("fsdp", None, "dp"),
-        P("fsdp", None, "dp"),
-        P("fsdp", None, "dp"),
+        P(flat, None),
+        P(flat, None),
+        P(flat, None),
+        P(flat, None),
+        P(flat, None),
+        P(flat, None),
+        P(flat, None),
+        P(flat, None),
+        P(flat),
+        P(flat),
+        P(flat),
+        P(flat),
+        P("fsdp", None, dp),
+        P("fsdp", None, dp),
+        P("fsdp", None, dp),
     )
     out_specs = (
-        P(("dp", "fsdp"), None),
-        P(("dp", "fsdp"), None),
-        P(("dp", "fsdp"), None),
-        P(("dp", "fsdp"), None),
-        P(("dp", "fsdp"), None),
-        P(("dp", "fsdp"), None),
-        P(("dp", "fsdp"), None),
-        P(("dp", "fsdp")),
-        P(("dp", "fsdp")),
-        P(("dp", "fsdp")),
-        P(("dp", "fsdp")),
-        P("fsdp", None, "dp"),
-        P("fsdp", None, "dp"),
-        P("fsdp", None, "dp"),
+        P(flat, None),
+        P(flat, None),
+        P(flat, None),
+        P(flat, None),
+        P(flat, None),
+        P(flat, None),
+        P(flat, None),
+        P(flat),
+        P(flat),
+        P(flat),
+        P(flat),
+        P("fsdp", None, dp),
+        P("fsdp", None, dp),
+        P("fsdp", None, dp),
     )
     return jax.shard_map(
-        per_device, mesh=mesh, in_specs=in_specs, out_specs=out_specs, check_vma=False
-    )
+        per_device if split else per_device_gathered,
+        mesh=mesh,
+        in_specs=in_specs,
+        out_specs=out_specs,
+        check_vma=False,
+    )

time: 2980 us -> 733 us (0.25)
  waiting for transfers between devices: 2340 us -> 239 us
  Pallas kernels: 0 us -> 232 us
  matrix products: 235 us -> 5.37 us
  blocking collectives: 213 us -> 0 us
  starting transfers between devices: 21 us -> 134 us
  local copies, waits for them, and re-layouts: 75.3 us -> 27.2 us
    reduce_scatter x7 -> x3, waiting for transfers between devices: 1590 us -> 0.01 us  [finish(): lax.psum_scatter(near, 'x', scatter_dimension=0, tiled=True).astype(f32)]
    all_to_all x4 -> x2, waiting for transfers between devices: 441 us -> 12 us  [the longest x1 11.9 us: per_device(): lax.all_to_all(grad_w_in, 'fsdp', split_axis=0, concat_axis=0, tiled=True)]
    all_gather x11 -> x3, waiting for transfers between devices: 303 us -> 0.01 us  [the longest x1 0.01 us: per_device(): down_w = lax.all_gather(expert_down, dp_axes, axis=2, tiled=True)]
    pallas_call x0 -> x16, Pallas kernels: none -> 232 us  [the longest x3 35.1 us: weight_near(): pl.pallas_call(weight_near_kernel, grid_spec=pltpu.PrefetchScalarGridSpec...]
    dot_general x30 -> x4, matrix products: 233 us -> 5.37 us  [dot(): lax.dot_general(left, right, dims, preferred_element_type=jnp.float32)]
    ppermute x0 -> x113, waiting for transfers between devices: none -> 224 us  [the longest x44 127 us: forward(): return lax.ppermute(values, 'fsdp', self.up)]
    all_gather x3 -> x0, blocking collectives: 133 us -> none  [the longest x1 68.5 us: per_device(): lax.all_gather(w_router, ('dp', 'fsdp'), axis=0, tiled=True)]
    ppermute x0 -> x113, starting transfers between devices: none -> 123 us  [the longest x44 73.4 us: forward(): return lax.ppermute(values, 'fsdp', self.up)]
  transfers between devices with their start and end apart: 23 -> 121, of which waited for: 17 -> 51; matrix products, arithmetic and copies ran while one was open for 11% -> 13% of each run, Pallas kernels for 0% -> 23%
where the time goes in v2:
time: 733 us; the launch traced here: 725 us
  waiting for transfers between devices  239 us (33%)
  Pallas kernels  232 us (32%)
  starting transfers between devices  134 us (18%)
  other arithmetic  71.9 us (10%)
  local copies, waits for them, and re-layouts  27.2 us (4%)
  between operations  16 us (2%)
    ppermute x44, waiting for transfers between devices, forward(): return lax.ppermute(values, 'fsdp', self.up)  127 us
    ppermute x44, starting transfers between devices, forward(): return lax.ppermute(values, 'fsdp', self.up)  73.4 us
    ppermute x41, waiting for transfers between devices, backward(): return lax.ppermute(values, 'fsdp', self.down)  59.2 us
    pallas_call x3, Pallas kernels, weight_near(): pl.pallas_call(weight_near_kernel, grid_spec=pltpu.PrefetchScalarGridSpec...  35.1 us
    pallas_call x3, Pallas kernels, weight_far(): pl.pallas_call(weight_far_kernel, grid=(width // wide,), in_specs=[pl.Blo...  31.3 us
    ppermute x41, starting transfers between devices, backward(): return lax.ppermute(values, 'fsdp', self.down)  30.9 us
    pallas_call x1, Pallas kernels, expert_hidden(): pl.pallas_call(functools.partial(expert_hidden_kernel, ring.pieces, parts...  30.8 us
    pallas_call x1, Pallas kernels, expert_inputs(): pl.pallas_call(functools.partial(expert_inputs_kernel, ring.pieces, parts...  25.5 us
  transfers between devices with their start and end apart: 121, of which 51 were waited for; matrix products, arithmetic and copies ran while one was open for 13% of the time, Pallas kernels for 23%

profile of v2, /device:TPU:0, one launch (start us, length us, event | category | flops | bytes accessed | tf_op | source)
XLA Modules:
  0.0 725.3 jit_solution(14759275527724954375)
XLA Ops:
  9.8 7.3 %all-to-all-start = ((bf16[8,64,768]{2,1,0:T(8,128)(2,1)}), bf16[8,64,768]{2,1,0:T(8,128)(2,1)S(1)}, u32[]{:S(2)}, u32[]{:S(2)}) async-start(bf16[8,64,768]{2,1,0:T(8,128)(2,1)} %maximum_bitcast_fusion), calls=%async_computation | async-start | bytes 1572864 | tf_op jit(solution)/shard_map/all_to_all | solution.py:1429
  28.0 13.7 %collective-permute-done.4 = bf16[4,20,64]{2,1,0:T(8,128)(2,1)S(1)} collective-permute-done((bf16[4,20,64]{2,1,0:T(8,128)(2,1)S(1)}, bf16[4,20,64]{2,1,0:T(8,128)(2,1)S(1)}, u32[]{:S(2)}, u32[]{:S(2)}) %collective-permute-start.4) | collective-permute-done | bytes 10272 | tf_op jit(solution)/shard_map/ppermute | solution.py:430
  45.4 4.3 collective-permute-start.7
  53.8 9.1 %collective-permute-done.8 = bf16[4,20,64]{2,1,0:T(8,128)(2,1)S(1)} collective-permute-done((bf16[4,20,64]{2,1,0:T(8,128)(2,1)S(1)}, bf16[4,20,64]{2,1,0:T(8,128)(2,1)S(1)}, u32[]{:S(2)}, u32[]{:S(2)}) %collective-permute-start.8) | collective-permute-done | bytes 10272 | tf_op jit(solution)/shard_map/ppermute | solution.py:430
  66.1 5.8 collective-permute-start.11
  73.2 2.6 collective-permute-start.13
  77.7 2.7 collective-permute-done.13
  81.9 4.1 collective-permute-start.20
  86.6 2.8 collective-permute-done.18.refs_11_.refs_15_
  91.6 2.5 collective-permute-start.24
  96.0 2.3 collective-permute-done.15.refs_4_
  98.3 3.2 collective-permute-done.16.refs_5_
  109.3 13.3 %project.1 = (bf16[1024,2048]{1,0:T(8,128)(2,1)}, f32[1024,768]{1,0:T(8,128)}, f32[1024,1]{1,0:T(8,128)}, f32[8,1024]{1,0:T(8,128)}, bf16[1024,2048]{1,0:T(8,128)(2,1)}) custom-call(s32[9]{0:T(128)} %pad_add_fusion.scalars, bf16[128,2048]{1,0:T(8,128)(2,1)} %refs_0_.2, bf16[128,2048]{1,0:T(8,128)(2,1)} %copy-done.41, bf16[128,2048]{1,0:T(8,128)(2,1)} %copy-done.49, ...), custom_call_target="tpu_custom_call" | custom-call | tf_op jit(solution)/shard_map/project/pallas_call | solution.py:683
  122.8 4.1 collective-permute-done.26
  131.6 2.6 collective-permute-start.28
  144.1 19.1 %attend.1 = (bf16[1024,256]{1,0:T(8,128)(2,1)}, bf16[1024,256]{1,0:T(8,128)(2,1)}, bf16[1024,256]{1,0:T(8,128)(2,1)}, f32[1024,256]{1,0:T(8,128)}, f32[2,1024,1]...) custom-call(s32[9]{0:T(128)} %pad_add_fusion.scalars, ...), custom_call_target="tpu_custom_call" | custom-call | tf_op jit(solution)/shard_map/attend/pallas_call | solution.py:790
  167.3 5.4 collective-permute-done.32
  173.8 6.6 collective-permute-done.31
  183.8 9.9 %collective-permute-done.35 = bf16[128,2048]{1,0:T(8,128)(2,1)S(1)} collective-permute-done((bf16[128,2048]{1,0:T(8,128)(2,1)S(1)}, bf16[128,2048]{1,0:T(8,128)(2,1)S(1)}, u32[]{:S(2)}, u32[]{:S(2)}) %collective-permute-start.35) | collective-permute-done | bytes 524320 | tf_op jit(solution)/shard_map/ppermute | solution.py:430
  196.3 6.5 collective-permute-done.37.refs_4_
  206.8 12.2 %collective-permute-done.39 = bf16[128,2048]{1,0:T(8,128)(2,1)S(1)} collective-permute-done((bf16[128,2048]{1,0:T(8,128)(2,1)S(1)}, bf16[128,2048]{1,0:T(8,128)(2,1)S(1)}, u32[]{:S(2)}, u32[]{:S(2)}) %collective-permute-start.39) | collective-permute-done | bytes 524320 | tf_op jit(solution)/shard_map/ppermute | solution.py:430
  221.5 9.2 %collective-permute-done.40 = bf16[128,2048]{1,0:T(8,128)(2,1)} collective-permute-done((bf16[128,2048]{1,0:T(8,128)(2,1)S(1)}, bf16[128,2048]{1,0:T(8,128)(2,1)}, u32[]{:S(2)}, u32[]{:S(2)}) %collective-permute-start.40) | collective-permute-done | bytes 524320 | tf_op jit(solution)/shard_map/ppermute | solution.py:430
  230.8 4.6 collective-permute-done.42
  237.3 2.6 collective-permute-start.45
  240.2 10.1 %collective-permute-done.43.refs_1_ = bf16[128,2048]{1,0:T(8,128)(2,1)S(1)} collective-permute-done((bf16[128,2048]{1,0:T(8,128)(2,1)S(1)}, bf16[128,2048]{1,0:T(8,128)(2,1)S(1)}, u32[]{:S(2)}, u32[]{:S(2)}) %collective-permute-start.43) | collective-permute-done | bytes 524320 | tf_op jit(solution)/shard_map/ppermute | solution.py:433
  254.8 15.7 %expert_first.1 = (f32[2,1024,1024]{2,1,0:T(8,128)}, bf16[1024,2048]{1,0:T(8,128)(2,1)}) custom-call(s32[9]{0:T(128)} %pad_add_fusion.scalars, bf16[128,2048]{1,0:T(8,128)(2,1)} %refs_0_.3, bf16[128,2048]{1,0:T(8,128)(2,1)} %collective-permute-done.22.refs_1_, bf16[128,2048]{1,0:T(8,128)(2,1)} %copy-done.43, bf16[128,2048]{1,0:T(8,128)(2,1)} %copy-done.29, ...), custom_call_target="tpu_custom_call" | custom-call | tf_op jit(solution)/shard_map/expert_first/pallas_call | solution.py:1081
  274.8 5.4 collective-permute-done.51
  294.3 30.8 %expert_hidden.1 = (bf16[1024,2048]{1,0:T(8,128)(2,1)}, bf16[1024,2048]{1,0:T(8,128)(2,1)}, bf16[1024,2048]{1,0:T(8,128)(2,1)}, bf16[1024,2048]{1,0:T(8,128)(2,1...) custom-call(s32[9]{0:T(128)} %pad_add_fusion.scalars, bf16[128,2048]{1,0:T(8,128)(2,1)} %copy-done.4, ...), custom_call_target="tpu_custom_call" | custom-call | tf_op jit(solution)/shard_map/expert_hidden/pallas_call | solution.py:1173
  325.1 25.5 %expert_inputs.1 = (bf16[128,2048]{1,0:T(8,128)(2,1)}, bf16[128,2048]{1,0:T(8,128)(2,1)}, bf16[128,2048]{1,0:T(8,128)(2,1)}, bf16[128,2048]{1,0:T(8,128)(2,1)}, ...) custom-call(s32[9]{0:T(128)} %pad_add_fusion.scalars, ...), custom_call_target="tpu_custom_call" | custom-call | tf_op jit(solution)/shard_map/expert_inputs/pallas_call | solution.py:1239
  355.1 10.2 %weight_far.3 = bf16[2048,1024]{1,0:T(8,128)(2,1)} custom-call(bf16[1024,2048]{1,0:T(8,128)(2,1)} %get-tuple-element.290.left, bf16[1024,2048]{1,0:T(8,128)(2,1)} %get-tuple-element.261.refs_0_.right), custom_call_target="tpu_custom_call" | custom-call | tf_op jit(solution)/shard_map/weight_far/pallas_call | solution.py:1313
  367.7 7.2 collective-permute-done.62
  376.5 7.3 %collective-permute-done.68.arrived = bf16[2048,1024]{1,0:T(8,128)(2,1)} collective-permute-done((bf16[2048,1024]{1,0:T(8,128)(2,1)S(1)}, bf16[2048,1024]{1,0:T(8,128)(2,1)}, u32[]{:S(2)}, u32[]{:S(2)}) %collective-permute-start.68) | collective-permute-done | bytes 4194336 | tf_op jit(solution)/shard_map/ppermute | solution.py:1520
  383.8 11.7 %weight_near.3 = bf16[4,2048,256]{2,1,0:T(8,128)(2,1)} custom-call(s32[9]{0:T(128)} %pad_add_fusion.scalars, bf16[1024,2048]{1,0:T(8,128)(2,1)} %get-tuple-element.290.left, bf16[1024,2048]{1,0:T(8,128)(2,1)} %get-tuple-element.261.refs_0_.right, bf16[2048,1024]{1,0:T(8,128)(2,1)} %collective-permute-done.68.arrived), custom_call_target="tpu_custom_call" | custom-call | tf_op jit(solution)/shard_map/weight_near/pallas_call | solution.py:1343
  397.7 10.7 %weight_far.4 = bf16[2048,1024]{1,0:T(8,128)(2,1)} custom-call(bf16[1024,2048]{1,0:T(8,128)(2,1)} %get-tuple-element.290.left, bf16[1024,2048]{1,0:T(8,128)(2,1)} %get-tuple-element.262.refs_1_.right), custom_call_target="tpu_custom_call" | custom-call | tf_op jit(solution)/shard_map/weight_far/pallas_call | solution.py:1313
  413.1 10.9 %collective-permute-done.66 = bf16[128,2048]{1,0:T(8,128)(2,1)S(1)} collective-permute-done((bf16[128,2048]{1,0:T(8,128)(2,1)S(1)}, bf16[128,2048]{1,0:T(8,128)(2,1)S(1)}, u32[]{:S(2)}, u32[]{:S(2)}) %collective-permute-start.66) | collective-permute-done | bytes 524320 | tf_op jit(solution)/shard_map/ppermute | solution.py:430
  429.8 3.0 collective-permute-done.74
  435.7 11.8 %weight_near.4 = bf16[4,2048,256]{2,1,0:T(8,128)(2,1)} custom-call(s32[9]{0:T(128)} %pad_add_fusion.scalars, bf16[1024,2048]{1,0:T(8,128)(2,1)} %get-tuple-element.290.left, bf16[1024,2048]{1,0:T(8,128)(2,1)} %get-tuple-element.262.refs_1_.right, bf16[2048,1024]{1,0:T(8,128)(2,1)} %collective-permute-done.73.arrived), custom_call_target="tpu_custom_call" | custom-call | tf_op jit(solution)/shard_map/weight_near/pallas_call | solution.py:1343
  450.5 2.6 fusion.22
  455.1 10.3 %weight_far.5 = bf16[2048,1024]{1,0:T(8,128)(2,1)} custom-call(bf16[1024,2048]{1,0:T(8,128)(2,1)} %get-tuple-element.312.left, bf16[1024,2048]{1,0:T(8,128)(2,1)} %get-tuple-element.307.right), custom_call_target="tpu_custom_call" | custom-call | tf_op jit(solution)/shard_map/weight_far/pallas_call | solution.py:1313
  467.6 9.4 %collective-permute-done.77.refs_23_ = bf16[128,2048]{1,0:T(8,128)(2,1)S(1)} collective-permute-done((bf16[128,2048]{1,0:T(8,128)(2,1)S(1)}, bf16[128,2048]{1,0:T(8,128)(2,1)S(1)}, u32[]{:S(2)}, u32[]{:S(2)}) %collective-permute-start.77) | collective-permute-done | bytes 524320 | tf_op jit(solution)/shard_map/ppermute | solution.py:430
  477.1 15.3 %expert_outputs.1 = (bf16[128,2048]{1,0:T(8,128)(2,1)}, bf16[128,2048]{1,0:T(8,128)(2,1)}, bf16[128,2048]{1,0:T(8,128)(2,1)}, bf16[128,2048]{1,0:T(8,128)(2,1)},...) custom-call(s32[9]{0:T(128)} %pad_add_fusion.scalars, ...), custom_call_target="tpu_custom_call" | custom-call | tf_op jit(solution)/shard_map/expert_outputs/pallas_call | solution.py:1285
  494.5 11.7 %weight_near.5 = bf16[4,2048,256]{2,1,0:T(8,128)(2,1)} custom-call(s32[9]{0:T(128)} %pad_add_fusion.scalars, bf16[1024,2048]{1,0:T(8,128)(2,1)} %get-tuple-element.312.left, bf16[1024,2048]{1,0:T(8,128)(2,1)} %get-tuple-element.307.right, bf16[2048,1024]{1,0:T(8,128)(2,1)} %collective-permute-done.81.arrived), custom_call_target="tpu_custom_call" | custom-call | tf_op jit(solution)/shard_map/weight_near/pallas_call | solution.py:1343
  509.3 5.7 collective-permute-done.82.refs_20_
  517.8 12.1 %attend_back.2 = (f32[1024,128]{1,0:T(8,128)}, f32[1024,128]{1,0:T(8,128)}, bf16[1024,128]{1,0:T(8,128)(2,1)}, f32[8,1024]{1,0:T(8,128)}, f32[1,128]{1,0:T(1,128...) custom-call(s32[9]{0:T(128)} %pad_add_fusion.scalars, bf16[1024,256]{1,0:T(8,128)(2,1)} %get-tuple-element.324.refs_0_, ...), custom_call_target="tpu_custom_call" | custom-call | tf_op jit(solution)/shard_map/attend_back/pallas_call | solution.py:888
  535.3 11.5 %attend_back.3 = (f32[1024,128]{1,0:T(8,128)}, f32[1024,128]{1,0:T(8,128)}, bf16[1024,128]{1,0:T(8,128)(2,1)}, f32[8,1024]{1,0:T(8,128)}, f32[1,128]{1,0:T(1,128)}, /*index=5*/f32[1,128]{1,0:T(1,128)}) custom-call(s32[9]{0:T(128)} %pad_add_fusion.scalars, bf16[1024,256]{1,0:T(8,128)(2,1)} %get-tuple-element.324.refs_0_, ...), custom_call_target="tpu_custom_call" | custom-call | tf_op jit(solution)/shard_map/attend_back/pallas_call | solution.py:888
  548.8 2.8 collective-permute-done.88
  555.6 2.8 collective-permute-start.90
  565.1 3.5 fusion.6
  568.7 14.0 %project_back.1 = (bf16[1024,768]{1,0:T(8,128)(2,1)}, f32[1,2048]{1,0:T(1,128)}, bf16[128,2048]{1,0:T(8,128)(2,1)}, bf16[128,2048]{1,0:T(8,128)(2,1)}, bf16[128,...) custom-call(s32[9]{0:T(128)} %pad_add_fusion.scalars, ...), custom_call_target="tpu_custom_call" | custom-call | tf_op jit(solution)/shard_map/project_back/pallas_call | solution.py:979
  584.4 5.8 collective-permute-done.108
  600.9 8.0 %weight_rows.1 = bf16[4,512,768]{2,1,0:T(8,128)(2,1)} custom-call(s32[9]{0:T(128)} %pad_add_fusion.scalars, bf16[1024,2048]{1,0:T(8,128)(2,1)} %get-tuple-element.371.left, bf16[1024,768]{1,0:T(8,128)(2,1)} %get-tuple-element.372.right), custom_call_target="tpu_custom_call" | custom-call | tf_op jit(solution)/shard_map/weight_rows/pallas_call | solution.py:1370
  609.0 2.7 slice.255
  615.8 9.8 %collective-permute-done.94 = bf16[128,2048]{1,0:T(8,128)(2,1)S(1)} collective-permute-done((bf16[128,2048]{1,0:T(8,128)(2,1)}, bf16[128,2048]{1,0:T(8,128)(2,1)S(1)}, u32[]{:S(2)}, u32[]{:S(2)}) %collective-permute-start.94) | collective-permute-done | bytes 524320 | tf_op jit(solution)/shard_map/ppermute | solution.py:433
  629.4 8.7 %collective-permute-done.97 = bf16[128,2048]{1,0:T(8,128)(2,1)} collective-permute-done((bf16[128,2048]{1,0:T(8,128)(2,1)S(1)}, bf16[128,2048]{1,0:T(8,128)(2,1)}, u32[]{:S(2)}, u32[]{:S(2)}) %collective-permute-start.97) | collective-permute-done | bytes 524320 | tf_op jit(solution)/shard_map/ppermute | solution.py:430
  638.1 14.4 %collective-permute-done.99 = bf16[128,2048]{1,0:T(8,128)(2,1)} collective-permute-done((bf16[128,2048]{1,0:T(8,128)(2,1)S(1)}, bf16[128,2048]{1,0:T(8,128)(2,1)}, u32[]{:S(2)}, u32[]{:S(2)}) %collective-permute-start.99) | collective-permute-done | bytes 524320 | tf_op jit(solution)/shard_map/ppermute | solution.py:433
  653.4 2.3 add.323
  666.5 4.1 convert_element_type.189
  676.5 2.7 collective-permute-start.101
  679.1 5.4 collective-permute-done.104
  686.7 4.0 all-to-all-start.1
  691.3 4.0 convert_element_type.190
  697.0 2.6 fusion.3
  699.7 11.9 %all-to-all-done.1 = bf16[8,64,768]{2,1,0:T(8,128)(2,1)S(1)} async-done(((bf16[8,64,768]{2,1,0:T(8,128)(2,1)}), bf16[8,64,768]{2,1,0:T(8,128)(2,1)S(1)}, u32[]{:S(2)}, u32[]{:S(2)}) %all-to-all-start.1) | async-done | bytes 786464 | tf_op jit(solution)/shard_map/all_to_all | solution.py:1631
  714.3 3.9 convert_element_type.191
  (543 shorter events, 200.1 us)
Async XLA Ops:
  7.2 247.6 %all-gather.4.cloned.1.call-start = ((), (), s32[]{:S(2)}) async-start(), calls=%async_computation.5 | async-start | bytes 10485760 | tf_op jit(solution)/shard_map/all_gather | solution.py:1460
  8.0 284.8 %all-gather.6.cloned.1.call-start = ((), (), s32[]{:S(2)}) async-start(), calls=%async_computation.6 | async-start | bytes 10485760 | tf_op jit(solution)/shard_map/all_gather | solution.py:1461
  9.8 34.1 %all-to-all-start = ((bf16[8,64,768]{2,1,0:T(8,128)(2,1)}), bf16[8,64,768]{2,1,0:T(8,128)(2,1)S(1)}, u32[]{:S(2)}, u32[]{:S(2)}) async-start(bf16[8,64,768]{2,1,0:T(8,128)(2,1)} %maximum_bitcast_fusion), calls=%async_computation | async-start | bytes 1572864 | tf_op jit(solution)/shard_map/all_to_all | solution.py:1429
  17.1 275.7 %all-gather.8.cloned.1.call-start = ((), (), s32[]{:S(2)}) async-start(), calls=%async_computation.7 | async-start | bytes 10485760 | tf_op jit(solution)/shard_map/all_gather | solution.py:1462
  17.9 648.7 %reduce-scatter.4.cloned.1.call-start = ((), (), s32[]{:S(2)}) async-start(), calls=%async_computation.8 | async-start | bytes 6291456 | tf_op jit(solution)/shard_map/reduce_scatter | solution.py:1524
  17.9 26.0 %collective-permute-start = (bf16[128,2048]{1,0:T(8,128)(2,1)S(1)}, bf16[128,2048]{1,0:T(8,128)(2,1)S(1)}, u32[]{:S(2)}, u32[]{:S(2)}) collective-permute-start(bf16[128,2048]{1,0:T(8,128)(2,1)S(1)} %copy-done.6), channel_id=1, source_target_pairs={{0,1},{2,0},{4,2},{6,4},{7,6},{5,7},{3,5},{1,3},{8,9},{10,8},{12,1... | collective-permute-start | bytes 1572872 | tf_op jit(solution)/shard_map/ppermute | solution.py:433
  20.0 24.0 %collective-permute-start.1 = (bf16[128,2048]{1,0:T(8,128)(2,1)S(1)}, bf16[128,2048]{1,0:T(8,128)(2,1)}, u32[]{:S(2)}, u32[]{:S(2)}) collective-permute-start(bf16[128,2048]{1,0:T(8,128)(2,1)S(1)} %copy-done.6), channel_id=1, source_target_pairs={{0,2},{2,4},{4,6},{6,7},{7,5},{5,3},{3,1},{1,0},{8,10},{10,12},{12... | collective-permute-start | bytes 1572872 | tf_op jit(solution)/shard_map/ppermute | solution.py:430
  25.1 16.6 %collective-permute-start.4 = (bf16[4,20,64]{2,1,0:T(8,128)(2,1)S(1)}, bf16[4,20,64]{2,1,0:T(8,128)(2,1)S(1)}, u32[]{:S(2)}, u32[]{:S(2)}) collective-permute-start(bf16[4,20,64]{2,1,0:T(8,128)(2,1)S(1)} %maximum_select_fusion), channel_id=1, source_target_pairs={{0,2},{2,4},{4,6},{6,7},{7,5},{5,3},{3,1},{1,0},{8,10},{10,12},{12... | collective-permute-start | bytes 30728 | tf_op jit(solution)/shard_map/ppermute | solution.py:430
  27.2 16.7 %collective-permute-start.5 = (bf16[4,20,64]{2,1,0:T(8,128)(2,1)S(1)}, bf16[4,20,64]{2,1,0:T(8,128)(2,1)S(1)}, u32[]{:S(2)}, u32[]{:S(2)}) collective-permute-start(bf16[4,20,64]{2,1,0:T(8,128)(2,1)S(1)} %maximum_select_fusion), channel_id=1, source_target_pairs={{0,1},{2,0},{4,2},{6,4},{7,6},{5,7},{3,5},{1,3},{8,9},{10,8},{12,1... | collective-permute-start | bytes 30728 | tf_op jit(solution)/shard_map/ppermute | solution.py:433
  44.0 20.4 %collective-permute-start.6 = (bf16[128,2048]{1,0:T(8,128)(2,1)S(1)}, bf16[128,2048]{1,0:T(8,128)(2,1)S(1)}, u32[]{:S(2)}, u32[]{:S(2)}) collective-permute-start(bf16[128,2048]{1,0:T(8,128)(2,1)S(1)} %collective-permute-done.refs_1_), channel_id=1, source_target_pairs={{0,1},{2,0},{4,2},{6,4},{7,6},{5,7},{3,5},{1,3},{8,9},{10,8},{12,1... | collective-permute-start | bytes 1572872 | tf_op jit(solution)/shard_map/ppermute | solution.py:433
  45.4 19.0 %collective-permute-start.7 = (bf16[128,2048]{1,0:T(8,128)(2,1)}, bf16[128,2048]{1,0:T(8,128)(2,1)S(1)}, u32[]{:S(2)}, u32[]{:S(2)}) collective-permute-start(bf16[128,2048]{1,0:T(8,128)(2,1)} %collective-permute-done.1.refs_8_), channel_id=1, source_target_pairs={{0,2},{2,4},{4,6},{6,7},{7,5},{5,3},{3,1},{1,0},{8,10},{10,12},{12... | collective-permute-start | bytes 1572872 | tf_op jit(solution)/shard_map/ppermute | solution.py:430
  53.1 22.7 %collective-permute-start.12 = (bf16[64,2048]{1,0:T(8,128)(2,1)S(1)}, bf16[64,2048]{1,0:T(8,128)(2,1)S(1)}, u32[]{:S(2)}, u32[]{:S(2)}) collective-permute-start(bf16[64,2048]{1,0:T(8,128)(2,1)S(1)} %copy-done.87), channel_id=1, source_target_pairs={{0,0},{1,8},{2,16},{3,24},{4,1},{5,9},{6,17},{7,25},{8,2},{9,10},{... | collective-permute-start | bytes 786440 | tf_op jit(solution)/shard_map/ppermute | solution.py:1439
  62.9 26.5 %collective-permute-start.18 = (bf16[512,768]{1,0:T(8,128)(2,1)S(1)}, bf16[512,768]{1,0:T(8,128)(2,1)S(1)}, u32[]{:S(2)}, u32[]{:S(2)}) collective-permute-start(bf16[512,768]{1,0:T(8,128)(2,1)S(1)} %bitcast.146), channel_id=1, source_target_pairs={{0,16},{8,24},{16,0},{24,8},{1,17},{9,25},{17,1},{25,9},{2,18},{10... | collective-permute-start | bytes 2359304 | tf_op jit(solution)/shard_map/ppermute | solution.py:549
  64.4 17.5 %collective-permute-start.10 = (bf16[128,2048]{1,0:T(8,128)(2,1)S(1)}, bf16[128,2048]{1,0:T(8,128)(2,1)S(1)}, u32[]{:S(2)}, u32[]{:S(2)}) collective-permute-start(bf16[128,2048]{1,0:T(8,128)(2,1)S(1)} %collective-permute-done.6.refs_2_), channel_id=1, source_target_pairs={{0,1},{2,0},{4,2},{6,4},{7,6},{5,7},{3,5},{1,3},{8,9},{10,8},{12,1... | collective-permute-start | bytes 1572872 | tf_op jit(solution)/shard_map/ppermute | solution.py:433
  66.1 15.8 %collective-permute-start.11 = (bf16[128,2048]{1,0:T(8,128)(2,1)S(1)}, bf16[128,2048]{1,0:T(8,128)(2,1)S(1)}, u32[]{:S(2)}, u32[]{:S(2)}) collective-permute-start(bf16[128,2048]{1,0:T(8,128)(2,1)S(1)} %collective-permute-done.7.refs_7_), channel_id=1, source_target_pairs={{0,2},{2,4},{4,6},{6,7},{7,5},{5,3},{3,1},{1,0},{8,10},{10,12},{12... | collective-permute-start | bytes 1572872 | tf_op jit(solution)/shard_map/ppermute | solution.py:430
  80.4 25.9 %collective-permute-start.17 = (bf16[512,768]{1,0:T(8,128)(2,1)S(1)}, bf16[512,768]{1,0:T(8,128)(2,1)S(1)}, u32[]{:S(2)}, u32[]{:S(2)}) collective-permute-start(bf16[512,768]{1,0:T(8,128)(2,1)S(1)} %bitcast.147), channel_id=1, source_target_pairs={{0,8},{8,0},{16,24},{24,16},{1,9},{9,1},{17,25},{25,17},{2,10},{10... | collective-permute-start | bytes 2359304 | tf_op jit(solution)/shard_map/ppermute | solution.py:549
  89.4 19.0 %collective-permute-start.19 = (bf16[512,768]{1,0:T(8,128)(2,1)S(1)}, bf16[512,768]{1,0:T(8,128)(2,1)S(1)}, u32[]{:S(2)}, u32[]{:S(2)}) collective-permute-start(bf16[512,768]{1,0:T(8,128)(2,1)S(1)} %collective-permute-done.18.refs_11_.refs_15_), channel_id=1, source_target_pairs={{0,8},{8,0},{16,24},{24,16},{1,9},{9,1},{17,25},{25,17},{2,10},{10... | collective-permute-start | bytes 2359304 | tf_op jit(solution)/shard_map/ppermute | solution.py:549
  91.6 14.7 %collective-permute-start.24 = (bf16[64,2048]{1,0:T(8,128)(2,1)S(1)}, bf16[64,2048]{1,0:T(8,128)(2,1)}, u32[]{:S(2)}, u32[]{:S(2)}) collective-permute-start(bf16[64,2048]{1,0:T(8,128)(2,1)S(1)} %collective-permute-done.12.refs_8_.refs_12_), channel_id=1, source_target_pairs={{0,16},{8,24},{16,0},{24,8},{1,17},{9,25},{17,1},{25,9},{2,18},{10... | collective-permute-start | bytes 786440 | tf_op jit(solution)/shard_map/ppermute | solution.py:549
  101.5 21.2 %collective-permute-start.21 = (bf16[128,2048]{1,0:T(8,128)(2,1)}, bf16[128,2048]{1,0:T(8,128)(2,1)}, u32[]{:S(2)}, u32[]{:S(2)}) collective-permute-start(bf16[128,2048]{1,0:T(8,128)(2,1)} %refs_0_.3), channel_id=1, source_target_pairs={{0,2},{2,4},{4,6},{6,7},{7,5},{5,3},{3,1},{1,0},{8,10},{10,12},{12... | collective-permute-start | bytes 1572872 | tf_op jit(solution)/shard_map/ppermute | solution.py:430
  103.2 19.5 %collective-permute-start.22 = (bf16[128,2048]{1,0:T(8,128)(2,1)}, bf16[128,2048]{1,0:T(8,128)(2,1)}, u32[]{:S(2)}, u32[]{:S(2)}) collective-permute-start(bf16[128,2048]{1,0:T(8,128)(2,1)} %refs_0_.3), channel_id=1, source_target_pairs={{0,1},{2,0},{4,2},{6,4},{7,6},{5,7},{3,5},{1,3},{8,9},{10,8},{12,1... | collective-permute-start | bytes 1572872 | tf_op jit(solution)/shard_map/ppermute | solution.py:433
  106.3 16.3 %collective-permute-start.23 = (bf16[64,2048]{1,0:T(8,128)(2,1)S(1)}, bf16[64,2048]{1,0:T(8,128)(2,1)}, u32[]{:S(2)}, u32[]{:S(2)}) collective-permute-start(bf16[64,2048]{1,0:T(8,128)(2,1)S(1)} %collective-permute-done.12.refs_8_.refs_12_), channel_id=1, source_target_pairs={{0,8},{8,0},{16,24},{24,16},{1,9},{9,1},{17,25},{25,17},{2,10},{10... | collective-permute-start | bytes 786440 | tf_op jit(solution)/shard_map/ppermute | solution.py:549
  106.3 16.3 %collective-permute-start.25 = (bf16[64,2048]{1,0:T(8,128)(2,1)}, bf16[64,2048]{1,0:T(8,128)(2,1)}, u32[]{:S(2)}, u32[]{:S(2)}) collective-permute-start(bf16[64,2048]{1,0:T(8,128)(2,1)} %collective-permute-done.24.refs_10_.refs_14_), channel_id=1, source_target_pairs={{0,8},{8,0},{16,24},{24,16},{1,9},{9,1},{17,25},{25,17},{2,10},{10... | collective-permute-start | bytes 786440 | tf_op jit(solution)/shard_map/ppermute | solution.py:549
  137.0 26.2 %collective-permute-start.29 = (bf16[128,2048]{1,0:T(8,128)(2,1)}, bf16[128,2048]{1,0:T(8,128)(2,1)S(1)}, u32[]{:S(2)}, u32[]{:S(2)}) collective-permute-start(bf16[128,2048]{1,0:T(8,128)(2,1)} %collective-permute-done.21.refs_8_), channel_id=1, source_target_pairs={{0,2},{2,4},{4,6},{6,7},{7,5},{5,3},{3,1},{1,0},{8,10},{10,12},{12... | collective-permute-start | bytes 1572872 | tf_op jit(solution)/shard_map/ppermute | solution.py:430
  138.7 24.5 %collective-permute-start.30 = (bf16[128,2048]{1,0:T(8,128)(2,1)}, bf16[128,2048]{1,0:T(8,128)(2,1)S(1)}, u32[]{:S(2)}, u32[]{:S(2)}) collective-permute-start(bf16[128,2048]{1,0:T(8,128)(2,1)} %collective-permute-done.22.refs_1_), channel_id=1, source_target_pairs={{0,1},{2,0},{4,2},{6,4},{7,6},{5,7},{3,5},{1,3},{8,9},{10,8},{12,1... | collective-permute-start | bytes 1572872 | tf_op jit(solution)/shard_map/ppermute | solution.py:433
  164.1 17.5 %collective-permute-start.33 = (bf16[128,2048]{1,0:T(8,128)(2,1)S(1)}, bf16[128,2048]{1,0:T(8,128)(2,1)S(1)}, u32[]{:S(2)}, u32[]{:S(2)}) collective-permute-start(bf16[128,2048]{1,0:T(8,128)(2,1)S(1)} %collective-permute-done.29.refs_7_), channel_id=1, source_target_pairs={{0,2},{2,4},{4,6},{6,7},{7,5},{5,3},{3,1},{1,0},{8,10},{10,12},{12... | collective-permute-start | bytes 1572872 | tf_op jit(solution)/shard_map/ppermute | solution.py:430
  165.3 16.3 %collective-permute-start.34 = (bf16[128,2048]{1,0:T(8,128)(2,1)S(1)}, bf16[128,2048]{1,0:T(8,128)(2,1)S(1)}, u32[]{:S(2)}, u32[]{:S(2)}) collective-permute-start(bf16[128,2048]{1,0:T(8,128)(2,1)S(1)} %collective-permute-done.30.refs_2_), channel_id=1, source_target_pairs={{0,1},{2,0},{4,2},{6,4},{7,6},{5,7},{3,5},{1,3},{8,9},{10,8},{12,1... | collective-permute-start | bytes 1572872 | tf_op jit(solution)/shard_map/ppermute | solution.py:433
  166.2 14.3 %collective-permute-start.31 = (bf16[64,2048]{1,0:T(8,128)(2,1)}, bf16[64,2048]{1,0:T(8,128)(2,1)S(1)}, u32[]{:S(2)}, u32[]{:S(2)}) collective-permute-start(bf16[64,2048]{1,0:T(8,128)(2,1)} %get-tuple-element.235), channel_id=1, source_target_pairs={{0,2},{2,4},{4,6},{6,7},{7,5},{5,3},{3,1},{1,0},{8,10},{10,12},{12... | collective-permute-start | bytes 786440 | tf_op jit(solution)/shard_map/ppermute | solution.py:430
  204.7 14.3 %collective-permute-start.39 = (bf16[128,2048]{1,0:T(8,128)(2,1)S(1)}, bf16[128,2048]{1,0:T(8,128)(2,1)S(1)}, u32[]{:S(2)}, u32[]{:S(2)}) collective-permute-start(bf16[128,2048]{1,0:T(8,128)(2,1)S(1)} %add.286), channel_id=1, source_target_pairs={{0,2},{2,4},{4,6},{6,7},{7,5},{5,3},{3,1},{1,0},{8,10},{10,12},{12... | collective-permute-start | bytes 1572872 | tf_op jit(solution)/shard_map/ppermute | solution.py:430
  206.6 14.7 %collective-permute-start.41 = (bf16[128,2048]{1,0:T(8,128)(2,1)S(1)}, bf16[128,2048]{1,0:T(8,128)(2,1)S(1)}, u32[]{:S(2)}, u32[]{:S(2)}) collective-permute-start(bf16[128,2048]{1,0:T(8,128)(2,1)S(1)} %add.287), channel_id=1, source_target_pairs={{0,1},{2,0},{4,2},{6,4},{7,6},{5,7},{3,5},{1,3},{8,9},{10,8},{12,1... | collective-permute-start | bytes 1572872 | tf_op jit(solution)/shard_map/ppermute | solution.py:433
  250.3 20.3 %collective-permute-start.44 = (bf16[128,2048]{1,0:T(8,128)(2,1)S(1)}, bf16[128,2048]{1,0:T(8,128)(2,1)S(1)}, u32[]{:S(2)}, u32[]{:S(2)}) collective-permute-start(bf16[128,2048]{1,0:T(8,128)(2,1)S(1)} %collective-permute-done.43.refs_1_), channel_id=1, source_target_pairs={{0,1},{2,0},{4,2},{6,4},{7,6},{5,7},{3,5},{1,3},{8,9},{10,8},{12,1... | collective-permute-start | bytes 1572872 | tf_op jit(solution)/shard_map/ppermute | solution.py:433
  250.4 20.3 %collective-permute-start.46 = (bf16[128,2048]{1,0:T(8,128)(2,1)}, bf16[128,2048]{1,0:T(8,128)(2,1)}, u32[]{:S(2)}, u32[]{:S(2)}) collective-permute-start(bf16[128,2048]{1,0:T(8,128)(2,1)} %collective-permute-done.45.refs_8_), channel_id=1, source_target_pairs={{0,2},{2,4},{4,6},{6,7},{7,5},{5,3},{3,1},{1,0},{8,10},{10,12},{12... | collective-permute-start | bytes 1572872 | tf_op jit(solution)/shard_map/ppermute | solution.py:430
  252.7 17.8 %collective-permute-start.47 = (f32[16,128]{1,0:T(8,128)S(1)}, f32[16,128]{1,0:T(8,128)S(1)}, u32[]{:S(2)}, u32[]{:S(2)}) collective-permute-start(f32[16,128]{1,0:T(8,128)S(1)} %fusion.21), channel_id=1, source_target_pairs={{0,2},{2,4},{4,6},{6,7},{7,5},{5,3},{3,1},{1,0},{8,10},{10,12},{12... | collective-permute-start | bytes 24584 | tf_op jit(solution)/shard_map/ppermute | solution.py:430
  254.5 16.1 %collective-permute-start.48 = (f32[16,128]{1,0:T(8,128)S(1)}, f32[16,128]{1,0:T(8,128)S(1)}, u32[]{:S(2)}, u32[]{:S(2)}) collective-permute-start(f32[16,128]{1,0:T(8,128)S(1)} %fusion.21), channel_id=1, source_target_pairs={{0,1},{2,0},{4,2},{6,4},{7,6},{5,7},{3,5},{1,3},{8,9},{10,8},{12,1... | collective-permute-start | bytes 24584 | tf_op jit(solution)/shard_map/ppermute | solution.py:433
  350.6 14.8 %collective-permute-start.59 = (bf16[64,2048]{1,0:T(8,128)(2,1)}, bf16[64,2048]{1,0:T(8,128)(2,1)S(1)}, u32[]{:S(2)}, u32[]{:S(2)}) collective-permute-start(bf16[64,2048]{1,0:T(8,128)(2,1)} %get-tuple-element.269), channel_id=1, source_target_pairs={{0,1},{2,0},{4,2},{6,4},{7,6},{5,7},{3,5},{1,3},{8,9},{10,8},{12,1... | collective-permute-start | bytes 786440 | tf_op jit(solution)/shard_map/ppermute | solution.py:433
  351.0 14.5 %collective-permute-start.58 = (bf16[64,2048]{1,0:T(8,128)(2,1)}, bf16[64,2048]{1,0:T(8,128)(2,1)S(1)}, u32[]{:S(2)}, u32[]{:S(2)}) collective-permute-start(bf16[64,2048]{1,0:T(8,128)(2,1)} %get-tuple-element.267), channel_id=1, source_target_pairs={{0,2},{2,4},{4,6},{6,7},{7,5},{5,3},{3,1},{1,0},{8,10},{10,12},{12... | collective-permute-start | bytes 786440 | tf_op jit(solution)/shard_map/ppermute | solution.py:430
  395.5 295.8 %reduce-scatter.6.cloned.1.call-start = ((), (), s32[]{:S(2)}) async-start(), calls=%async_computation.9 | async-start | bytes 6291456 | tf_op jit(solution)/shard_map/reduce_scatter | solution.py:1524
  395.6 15.4 %collective-permute-start.64 = (f32[2,8,128]{2,1,0:T(8,128)S(1)}, f32[2,8,128]{2,1,0:T(8,128)S(1)}, u32[]{:S(2)}, u32[]{:S(2)}) collective-permute-start(f32[2,8,128]{2,1,0:T(8,128)S(1)} %collective-permute-done.60), channel_id=1, source_target_pairs={{0,2},{2,4},{4,6},{6,7},{7,5},{5,3},{3,1},{1,0},{8,10},{10,12},{12... | collective-permute-start | bytes 24584 | tf_op jit(solution)/shard_map/ppermute | solution.py:430
  396.5 14.4 %collective-permute-start.65 = (f32[2,8,128]{2,1,0:T(8,128)S(1)}, f32[2,8,128]{2,1,0:T(8,128)S(1)}, u32[]{:S(2)}, u32[]{:S(2)}) collective-permute-start(f32[2,8,128]{2,1,0:T(8,128)S(1)} %collective-permute-done.61), channel_id=1, source_target_pairs={{0,1},{2,0},{4,2},{6,4},{7,6},{5,7},{3,5},{1,3},{8,9},{10,8},{12,1... | collective-permute-start | bytes 24584 | tf_op jit(solution)/shard_map/ppermute | solution.py:433
  432.8 14.7 %collective-permute-start.71 = (bf16[128,2048]{1,0:T(8,128)(2,1)S(1)}, bf16[128,2048]{1,0:T(8,128)(2,1)}, u32[]{:S(2)}, u32[]{:S(2)}) collective-permute-start(bf16[128,2048]{1,0:T(8,128)(2,1)S(1)} %add.299), channel_id=1, source_target_pairs={{0,2},{2,4},{4,6},{6,7},{7,5},{5,3},{3,1},{1,0},{8,10},{10,12},{12... | collective-permute-start | bytes 1572872 | tf_op jit(solution)/shard_map/ppermute | solution.py:430
  433.4 14.1 %collective-permute-start.72 = (bf16[128,2048]{1,0:T(8,128)(2,1)S(1)}, bf16[128,2048]{1,0:T(8,128)(2,1)}, u32[]{:S(2)}, u32[]{:S(2)}) collective-permute-start(bf16[128,2048]{1,0:T(8,128)(2,1)S(1)} %add.300), channel_id=1, source_target_pairs={{0,1},{2,0},{4,2},{6,4},{7,6},{5,7},{3,5},{1,3},{8,9},{10,8},{12,1... | collective-permute-start | bytes 1572872 | tf_op jit(solution)/shard_map/ppermute | solution.py:433
  450.4 263.9 %reduce-scatter.8.cloned.1.call-start = ((), (), s32[]{:S(2)}) async-start(), calls=%async_computation.10 | async-start | bytes 6291456 | tf_op jit(solution)/shard_map/reduce_scatter | solution.py:1524
  477.1 17.4 %collective-permute-start.81 = (bf16[2048,1024]{1,0:T(8,128)(2,1)}, bf16[2048,1024]{1,0:T(8,128)(2,1)}, u32[]{:S(2)}, u32[]{:S(2)}) collective-permute-start(bf16[2048,1024]{1,0:T(8,128)(2,1)} %weight_far.5), channel_id=1, source_target_pairs={{0,8},{8,0},{16,24},{24,16},{1,9},{9,1},{17,25},{25,17},{2,10},{10... | collective-permute-start | bytes 12582920 | tf_op jit(solution)/shard_map/ppermute | solution.py:1520
  492.4 14.4 %collective-permute-start.79 = (bf16[128,2048]{1,0:T(8,128)(2,1)S(1)}, bf16[128,2048]{1,0:T(8,128)(2,1)S(1)}, u32[]{:S(2)}, u32[]{:S(2)}) collective-permute-start(bf16[128,2048]{1,0:T(8,128)(2,1)S(1)} %collective-permute-done.77.refs_23_), channel_id=1, source_target_pairs={{0,2},{2,4},{4,6},{6,7},{7,5},{5,3},{3,1},{1,0},{8,10},{10,12},{12... | collective-permute-start | bytes 1572872 | tf_op jit(solution)/shard_map/ppermute | solution.py:430
  492.8 14.2 %collective-permute-start.80 = (bf16[128,2048]{1,0:T(8,128)(2,1)}, bf16[128,2048]{1,0:T(8,128)(2,1)S(1)}, u32[]{:S(2)}, u32[]{:S(2)}) collective-permute-start(bf16[128,2048]{1,0:T(8,128)(2,1)} %copy-done.24), channel_id=1, source_target_pairs={{0,1},{2,0},{4,2},{6,4},{7,6},{5,7},{3,5},{1,3},{8,9},{10,8},{12,1... | collective-permute-start | bytes 1572872 | tf_op jit(solution)/shard_map/ppermute | solution.py:433
  515.7 14.2 %collective-permute-start.85 = (bf16[64,2048]{1,0:T(8,128)(2,1)}, bf16[64,2048]{1,0:T(8,128)(2,1)}, u32[]{:S(2)}, u32[]{:S(2)}) collective-permute-start(bf16[64,2048]{1,0:T(8,128)(2,1)} %get-tuple-element.322), channel_id=1, source_target_pairs={{0,1},{2,0},{4,2},{6,4},{7,6},{5,7},{3,5},{1,3},{8,9},{10,8},{12,1... | collective-permute-start | bytes 786440 | tf_op jit(solution)/shard_map/ppermute | solution.py:433
  516.8 15.1 %collective-permute-start.84 = (bf16[64,2048]{1,0:T(8,128)(2,1)}, bf16[64,2048]{1,0:T(8,128)(2,1)S(1)}, u32[]{:S(2)}, u32[]{:S(2)}) collective-permute-start(bf16[64,2048]{1,0:T(8,128)(2,1)} %get-tuple-element.320), channel_id=1, source_target_pairs={{0,2},{2,4},{4,6},{6,7},{7,5},{5,3},{3,1},{1,0},{8,10},{10,12},{12... | collective-permute-start | bytes 786440 | tf_op jit(solution)/shard_map/ppermute | solution.py:430
  532.9 14.8 %collective-permute-start.86 = (bf16[128,2048]{1,0:T(8,128)(2,1)}, bf16[128,2048]{1,0:T(8,128)(2,1)}, u32[]{:S(2)}, u32[]{:S(2)}) collective-permute-start(bf16[128,2048]{1,0:T(8,128)(2,1)} %pad_maximum_fusion.6), channel_id=1, source_target_pairs={{0,2},{2,4},{4,6},{6,7},{7,5},{5,3},{3,1},{1,0},{8,10},{10,12},{12... | collective-permute-start | bytes 1572872 | tf_op jit(solution)/shard_map/ppermute | solution.py:430
  563.1 20.4 %collective-permute-start.91 = (bf16[128,2048]{1,0:T(8,128)(2,1)}, bf16[128,2048]{1,0:T(8,128)(2,1)}, u32[]{:S(2)}, u32[]{:S(2)}) collective-permute-start(bf16[128,2048]{1,0:T(8,128)(2,1)} %add.307), channel_id=1, source_target_pairs={{0,2},{2,4},{4,6},{6,7},{7,5},{5,3},{3,1},{1,0},{8,10},{10,12},{12... | collective-permute-start | bytes 1572872 | tf_op jit(solution)/shard_map/ppermute | solution.py:430
  564.2 19.2 %collective-permute-start.92 = (bf16[128,2048]{1,0:T(8,128)(2,1)}, bf16[128,2048]{1,0:T(8,128)(2,1)}, u32[]{:S(2)}, u32[]{:S(2)}) collective-permute-start(bf16[128,2048]{1,0:T(8,128)(2,1)} %add.308), channel_id=1, source_target_pairs={{0,1},{2,0},{4,2},{6,4},{7,6},{5,7},{3,5},{1,3},{8,9},{10,8},{12,1... | collective-permute-start | bytes 1572872 | tf_op jit(solution)/shard_map/ppermute | solution.py:433
  590.9 20.8 %collective-permute-start.109 = (f32[20,512]{1,0:T(8,128)}, f32[20,512]{1,0:T(8,128)}, u32[]{:S(2)}, u32[]{:S(2)}) collective-permute-start(f32[20,512]{1,0:T(8,128)} %slice_select_fusion.1), channel_id=1, source_target_pairs={{0,8},{8,0},{16,24},{24,16},{1,9},{9,1},{17,25},{25,17},{2,10},{10... | collective-permute-start | bytes 122888 | tf_op jit(solution)/shard_map/ppermute | solution.py:537
  593.6 34.0 %collective-permute-start.106 = (bf16[1,64,2048]{2,1,0:T(8,128)(2,1)}, bf16[1,64,2048]{2,1,0:T(8,128)(2,1)}, u32[]{:S(2)}, u32[]{:S(2)}) collective-permute-start(bf16[1,64,2048]{2,1,0:T(8,128)(2,1)} %slice.325), channel_id=1, source_target_pairs={{0,16},{8,24},{16,0},{24,8},{1,17},{9,25},{17,1},{25,9},{2,18},{10... | collective-permute-start | bytes 786440 | tf_op jit(solution)/shard_map/ppermute | solution.py:559
  593.6 19.8 %collective-permute-start.95 = (bf16[64,2048]{1,0:T(8,128)(2,1)}, bf16[64,2048]{1,0:T(8,128)(2,1)S(1)}, u32[]{:S(2)}, u32[]{:S(2)}) collective-permute-start(bf16[64,2048]{1,0:T(8,128)(2,1)} %get-tuple-element.363), channel_id=1, source_target_pairs={{0,2},{2,4},{4,6},{6,7},{7,5},{5,3},{3,1},{1,0},{8,10},{10,12},{12... | collective-permute-start | bytes 786440 | tf_op jit(solution)/shard_map/ppermute | solution.py:430
  594.8 18.6 %collective-permute-start.96 = (bf16[64,2048]{1,0:T(8,128)(2,1)}, bf16[64,2048]{1,0:T(8,128)(2,1)}, u32[]{:S(2)}, u32[]{:S(2)}) collective-permute-start(bf16[64,2048]{1,0:T(8,128)(2,1)} %get-tuple-element.364), channel_id=1, source_target_pairs={{0,1},{2,0},{4,2},{6,4},{7,6},{5,7},{3,5},{1,3},{8,9},{10,8},{12,1... | collective-permute-start | bytes 786440 | tf_op jit(solution)/shard_map/ppermute | solution.py:433
  599.7 16.1 %collective-permute-start.93 = (bf16[128,2048]{1,0:T(8,128)(2,1)}, bf16[128,2048]{1,0:T(8,128)(2,1)}, u32[]{:S(2)}, u32[]{:S(2)}) collective-permute-start(bf16[128,2048]{1,0:T(8,128)(2,1)} %add.313), channel_id=1, source_target_pairs={{0,2},{2,4},{4,6},{6,7},{7,5},{5,3},{3,1},{1,0},{8,10},{10,12},{12... | collective-permute-start | bytes 1572872 | tf_op jit(solution)/shard_map/ppermute | solution.py:430
  613.4 15.9 %collective-permute-start.110 = (f32[20,256]{1,0:T(8,128)S(1)}, f32[20,256]{1,0:T(8,128)S(1)}, u32[]{:S(2)}, u32[]{:S(2)}) collective-permute-start(f32[20,256]{1,0:T(8,128)S(1)} %slice_select_fusion.2), channel_id=1, source_target_pairs={{0,4},{1,5},{2,6},{3,7},{4,0},{5,1},{6,2},{7,3},{8,12},{9,13},{10,... | collective-permute-start | bytes 61448 | tf_op jit(solution)/shard_map/ppermute | solution.py:537
  614.5 45.4 %collective-permute-start.103 = (bf16[2,512,768]{2,1,0:T(8,128)(2,1)}, bf16[2,512,768]{2,1,0:T(8,128)(2,1)}, u32[]{:S(2)}, u32[]{:S(2)}) collective-permute-start(bf16[2,512,768]{2,1,0:T(8,128)(2,1)} %slice.255), channel_id=1, source_target_pairs={{0,8},{8,0},{16,24},{24,16},{1,9},{9,1},{17,25},{25,17},{2,10},{10... | collective-permute-start | bytes 4718600 | tf_op jit(solution)/shard_map/ppermute | solution.py:556
  626.4 26.1 %collective-permute-start.99 = (bf16[128,2048]{1,0:T(8,128)(2,1)S(1)}, bf16[128,2048]{1,0:T(8,128)(2,1)}, u32[]{:S(2)}, u32[]{:S(2)}) collective-permute-start(bf16[128,2048]{1,0:T(8,128)(2,1)S(1)} %pad_maximum_fusion.9), channel_id=1, source_target_pairs={{0,1},{2,0},{4,2},{6,4},{7,6},{5,7},{3,5},{1,3},{8,9},{10,8},{12,1... | collective-permute-start | bytes 1572872 | tf_op jit(solution)/shard_map/ppermute | solution.py:433
  628.7 23.9 %collective-permute-start.107 = (bf16[64,2048]{1,0:T(8,128)(2,1)S(1)}, bf16[64,2048]{1,0:T(8,128)(2,1)S(1)}, u32[]{:S(2)}, u32[]{:S(2)}) collective-permute-start(bf16[64,2048]{1,0:T(8,128)(2,1)S(1)} %fusion.12), channel_id=1, source_target_pairs={{0,0},{8,1},{16,2},{24,3},{1,4},{9,5},{17,6},{25,7},{2,8},{10,9},{... | collective-permute-start | bytes 786440 | tf_op jit(solution)/shard_map/ppermute | solution.py:1606
  655.6 16.9 %collective-permute-start.100 = (bf16[128,2048]{1,0:T(8,128)(2,1)}, bf16[128,2048]{1,0:T(8,128)(2,1)}, u32[]{:S(2)}, u32[]{:S(2)}) collective-permute-start(bf16[128,2048]{1,0:T(8,128)(2,1)} %add.323), channel_id=1, source_target_pairs={{0,1},{2,0},{4,2},{6,4},{7,6},{5,7},{3,5},{1,3},{8,9},{10,8},{12,1... | collective-permute-start | bytes 1572872 | tf_op jit(solution)/shard_map/ppermute | solution.py:433
  657.6 16.9 %collective-permute-start.98 = (bf16[128,2048]{1,0:T(8,128)(2,1)}, bf16[128,2048]{1,0:T(8,128)(2,1)}, u32[]{:S(2)}, u32[]{:S(2)}) collective-permute-start(bf16[128,2048]{1,0:T(8,128)(2,1)} %add.321), channel_id=1, source_target_pairs={{0,2},{2,4},{4,6},{6,7},{7,5},{5,3},{3,1},{1,0},{8,10},{10,12},{12... | collective-permute-start | bytes 1572872 | tf_op jit(solution)/shard_map/ppermute | solution.py:430
  664.4 20.2 %collective-permute-start.104 = (bf16[1,512,768]{2,1,0:T(8,128)(2,1)}, bf16[1,512,768]{2,1,0:T(8,128)(2,1)}, u32[]{:S(2)}, u32[]{:S(2)}) collective-permute-start(bf16[1,512,768]{2,1,0:T(8,128)(2,1)} %slice.324), channel_id=1, source_target_pairs={{0,16},{8,24},{16,0},{24,8},{1,17},{9,25},{17,1},{25,9},{2,18},{10... | collective-permute-start | bytes 2359304 | tf_op jit(solution)/shard_map/ppermute | solution.py:559
  676.5 18.8 %collective-permute-start.101 = (bf16[128,2048]{1,0:T(8,128)(2,1)}, bf16[128,2048]{1,0:T(8,128)(2,1)}, u32[]{:S(2)}, u32[]{:S(2)}) collective-permute-start(bf16[128,2048]{1,0:T(8,128)(2,1)} %add.322), channel_id=1, source_target_pairs={{0,2},{2,4},{4,6},{6,7},{7,5},{5,3},{3,1},{1,0},{8,10},{10,12},{12... | collective-permute-start | bytes 1572872 | tf_op jit(solution)/shard_map/ppermute | solution.py:430
  679.1 16.2 %collective-permute-start.102 = (bf16[128,2048]{1,0:T(8,128)(2,1)}, bf16[128,2048]{1,0:T(8,128)(2,1)}, u32[]{:S(2)}, u32[]{:S(2)}) collective-permute-start(bf16[128,2048]{1,0:T(8,128)(2,1)} %add.324), channel_id=1, source_target_pairs={{0,1},{2,0},{4,2},{6,4},{7,6},{5,7},{3,5},{1,3},{8,9},{10,8},{12,1... | collective-permute-start | bytes 1572872 | tf_op jit(solution)/shard_map/ppermute | solution.py:433
  686.7 24.9 %all-to-all-start.1 = ((bf16[8,64,768]{2,1,0:T(8,128)(2,1)}), bf16[8,64,768]{2,1,0:T(8,128)(2,1)S(1)}, u32[]{:S(2)}, u32[]{:S(2)}) async-start(bf16[8,64,768]{2,1,0:T(8,128)(2,1)} %bitcast.150), calls=%async_computation.1 | async-start | bytes 1572864 | tf_op jit(solution)/shard_map/all_to_all | solution.py:1631
  (146 other events, 2211.3 us)
Sparse Core Ops, SparseCore 0:
  9.6 69.3 all-gather.3
  80.6 67.7 all-gather.5
  150.0 60.8 all-gather.7
  395.6 51.2 reduce-scatter.3
  450.5 52.9 reduce-scatter.5
  553.6 60.9 reduce-scatter.7

commit v3 on v2

--- a/solution.py
+++ b/solution.py
@@ -14,6 +14,9 @@
 epsilon = 1e-05
 rope_base = 10000.0
 hidden_parts = 4
+rest_column = 128
+gate_columns = 64
+sum_columns = 128
 dp_axes = ("x", "core")
 far_low = -1e30
 
@@ -439,6 +442,22 @@
         return Reduce(self, pieces)
 
 
+def add_pair_kernel(upper, rising, lower, falling, first, second):
+    count, arrived = upper.shape[0], rising.shape[0]
+    first[:arrived, :] = upper[:arrived, :] + rising[...]
+    second[count - arrived :, :] = lower[count - arrived :, :] + falling[...]
+    if arrived < count:
+        first[arrived:, :] = upper[arrived:, :]
+        second[: count - arrived, :] = lower[: count - arrived, :]
+
+
+def add_pair(upper, rising, lower, falling):
+    shape = jax.ShapeDtypeStruct(upper.shape, upper.dtype)
+    return pl.pallas_call(add_pair_kernel, out_shape=[shape, shape], name="add_pair")(
+        upper, rising, lower, falling
+    )
+
+
 class Gather:
     def __init__(self, ring, block, halves=True):
         self.ring, self.halves = ring, halves
@@ -468,25 +487,24 @@
     def __init__(self, ring, pieces):
         self.ring, self.pieces, self.arrived, self.left = ring, pieces, None, ring.half
 
-    def step(self, ties=None):
-        ring, pieces, middle = self.ring, self.pieces, self.ring.rows // 2
+    def step(self, ties=None, early=None):
+        ring, pieces = self.ring, self.pieces
         if self.arrived is None:
             upper, lower = pieces[ring.half], pieces[ring.half + 1]
         else:
-            rising, falling = self.arrived
+            rising, falling = after(self.arrived, early)
             upper, lower = pieces[self.left], pieces[-self.left]
-            if self.left == ring.half - 1:
-                upper = jnp.concatenate([upper[:middle] + rising, upper[middle:]], axis=0)
-                lower = jnp.concatenate([lower[:middle], lower[middle:] + falling], axis=0)
-            else:
-                upper, lower = upper + rising, lower + falling
+            upper, lower = add_pair(upper, rising, lower, falling)
         upper, lower = after((upper, lower), ties)
         self.arrived = (ring.forward(upper), ring.backward(lower))
         self.left -= 1
         return self.arrived
 
-    def total(self):
-        rising, falling = self.arrived
+    def last(self):
+        return self.pieces[0], *self.arrived
+
+    def total(self, early=None):
+        rising, falling = after(self.arrived, early)
         return (
             self.pieces[0].astype(jnp.float32)
             + rising.astype(jnp.float32)
@@ -524,21 +542,6 @@
     return values
 
 
-def pair_scatter(values, axis, size, ties=()):
-    ties = dict(ties)
-    mine = lax.axis_index(axis)
-    bit = size // 2
-    while bit >= 1:
-        span = values.shape[1] // 2
-        upper = (mine & bit) != 0
-        low_half, high_half = values[:, :span], values[:, span:]
-        kept = jnp.where(upper, high_half, low_half)
-        sent = after(jnp.where(upper, low_half, high_half), ties.get(bit))
-        values = kept + lax.ppermute(sent, axis, exchange_pairs(size, bit))
-        bit //= 2
-    return values
-
-
 def share_relative(block, size, ties=(), second=()):
     block = after(block, ties)
     held = {0: block}
@@ -551,13 +554,12 @@
     return [held[index] for index in range(size)]
 
 
-def combine_relative(blocks, ties=(None, None)):
-    half = blocks.shape[0] // 2
-    far = lax.ppermute(after(blocks[:half], ties[0]), dp_axes, exchange_pairs(4, 1))
-    sums = blocks[half:].astype(jnp.float32) + far.astype(jnp.float32)
-    other = after(sums[half // 2 :].astype(jnp.bfloat16), ties[1])
+def combine_relative(far, near, ties=(None, None)):
+    far = lax.ppermute(after(far, ties[0]), dp_axes, exchange_pairs(4, 1))
+    other = near[1] + far[1].astype(jnp.float32)
+    other = after(other.astype(jnp.bfloat16), ties[1])
     other = lax.ppermute(other, dp_axes, exchange_pairs(4, 2))
-    return sums[: half // 2] + other.astype(jnp.float32)
+    return near[0] + far[0].astype(jnp.float32) + other.astype(jnp.float32)
 
 
 anywhere = pl.BlockSpec(memory_space=pl.ANY)
@@ -585,7 +587,12 @@
 
 
 def as_columns(rows):
-    same = lax.broadcasted_iota(jnp.int32, (8, 8), 0) == lax.broadcasted_iota(jnp.int32, (8, 8), 1)
+    return rows_as_columns(rows, 8)
+
+
+def rows_as_columns(rows, columns):
+    shape = (rows.shape[0], columns)
+    same = lax.broadcasted_iota(jnp.int32, shape, 0) == lax.broadcasted_iota(jnp.int32, shape, 1)
     return lax.dot_general(
         rows,
         same.astype(jnp.float32),
@@ -599,13 +606,16 @@
     return pl.BlockSpec(shape, lambda *_: (0,) * len(shape))
 
 
-def piece_copies(pieces, scalars, blocks, target, sems):
+def piece_copies(pieces, scalars, blocks, target, sems, first_column=0):
     rows = pieces[0][2]
+    columns = pl.ds(first_column, target.shape[1])
     copies = []
     for i, (slot, first, count) in enumerate(pieces):
         begin = pl.multiple_of(scalars[slot] * rows + first, count)
         copies.append(
-            pltpu.make_async_copy(blocks[i], target.at[pl.ds(begin, count), :], sems.at[i])
+            pltpu.make_async_copy(
+                blocks[i].at[:, columns], target.at[pl.ds(begin, count), :], sems.at[i]
+            )
         )
     return copies
 
@@ -1043,6 +1053,104 @@
     return buffers.at[step % 2]
 
 
+def middle_kernel(experts, tokens, first, rising, falling, gain, router, routes, *refs):
+    resid, factor, block, gates, probs, mask, total = refs
+    width = tokens.shape[1]
+    values = tokens[...].astype(jnp.float32) + (
+        first[...].astype(jnp.float32)
+        + rising[...].astype(jnp.float32)
+        + falling[...].astype(jnp.float32)
+    )
+    resid[...] = values
+    scale = lax.rsqrt(jnp.mean(values * values, axis=-1, keepdims=True) + epsilon)
+    factor[...] = scale
+    low = (values * scale * gain[...]).astype(jnp.bfloat16)
+    block[:, :width] = low
+    logits = dot(low, router[...], columns_last)
+    column = lax.broadcasted_iota(jnp.int32, logits.shape, 1)
+    real = column < experts
+    top = jnp.max(jnp.where(real, logits, far_low), axis=-1, keepdims=True)
+    weights = jnp.where(real, jnp.exp(logits - top), 0.0)
+    prob_vals = weights / jnp.sum(weights, axis=-1, keepdims=True)
+    chosen_mask = jnp.zeros(logits.shape, jnp.float32)
+    for j in range(routes.shape[1]):
+        chosen_mask = jnp.where(column == routes[:, j : j + 1], 1.0, chosen_mask)
+    chosen = chosen_mask * prob_vals
+    chosen_sum = jnp.sum(chosen, axis=-1, keepdims=True)
+    gate_vals = chosen / chosen_sum
+    gates[...], probs[...], mask[...], total[...] = gate_vals, prob_vals, chosen_mask, chosen_sum
+    high = gate_vals.astype(jnp.bfloat16).astype(jnp.float32)
+    rest = pltpu.roll(gate_vals - high, gate_columns, 1)
+    block[:, width:] = (high + rest).astype(jnp.bfloat16)
+
+
+def middle(tokens, sums, gain, router, routes, experts):
+    rows, width = tokens.shape
+    lanes = 2 * gate_columns
+    table = jax.ShapeDtypeStruct((rows, lanes), jnp.float32)
+    column = jax.ShapeDtypeStruct((rows, 1), jnp.float32)
+    return pl.pallas_call(
+        functools.partial(middle_kernel, experts),
+        out_shape=[
+            jax.ShapeDtypeStruct((rows, width), jnp.float32),
+            column,
+            jax.ShapeDtypeStruct((rows, width + lanes), jnp.bfloat16),
+            table,
+            table,
+            table,
+            column,
+        ],
+        name="middle",
+    )(tokens, *sums, gain, router, routes)
+
+
+def middle_back_kernel(first, rising, falling, cotangent, resid, factor, block, *refs):
+    gates, probs, mask, total, gain, router = refs[:6]
+    grad_resid, grad_low, sum_gain, grad_router = refs[6:]
+    width = resid.shape[1]
+    summed = (
+        first[...].astype(jnp.float32)
+        + rising[...].astype(jnp.float32)
+        + falling[...].astype(jnp.float32)
+    )
+    lanes = 2 * gate_columns
+    gates_back = summed[:, width : width + lanes]
+    gates_back = gates_back + summed[:, width + rest_column : width + rest_column + lanes]
+    inner = jnp.sum(gates_back * gates[...], axis=-1, keepdims=True)
+    grad_probs = mask[...] * ((gates_back - inner) / total[...])
+    grad_logits = probs[...] * (
+        grad_probs - jnp.sum(probs[...] * grad_probs, axis=-1, keepdims=True)
+    )
+    logits_low = grad_logits.astype(jnp.bfloat16)
+    grad_router[...] = dot(logits_low, block[:, :width], rows_first)
+    grad_mid = summed[:, :width] + dot(logits_low, router[...])
+    scale, values = factor[...], resid[...]
+    scaled = grad_mid * gain[...]
+    sum_gain[...] = jnp.sum(grad_mid * values * scale, axis=0, keepdims=True)
+    mean = jnp.mean(scaled * values, axis=-1, keepdims=True)
+    result = (
+        cotangent[...].astype(jnp.float32)
+        + scale * scaled
+        - values * (scale * scale * scale * mean)
+    )
+    grad_resid[...] = result
+    grad_low[...] = result.astype(jnp.bfloat16)
+
+
+def middle_back(sums, cotangent, resid, factor, block, gates, probs, mask, total, gain, router):
+    rows, width = resid.shape
+    return pl.pallas_call(
+        middle_back_kernel,
+        out_shape=[
+            jax.ShapeDtypeStruct((rows, width), jnp.float32),
+            jax.ShapeDtypeStruct((rows, width), jnp.bfloat16),
+            jax.ShapeDtypeStruct((1, width), jnp.float32),
+            jax.ShapeDtypeStruct((2 * gate_columns, width), jnp.float32),
+        ],
+        name="middle_back",
+    )(*sums, cotangent, resid, factor, block, gates, probs, mask, total, gain, router)
+
+
 def expert_first_kernel(pieces, parts, chunk, scalars, *refs):
     n = len(pieces)
     blocks, down = refs[:n], refs[n]
@@ -1107,24 +1215,32 @@
 def expert_hidden_kernel(pieces, parts, chunk, scalars, *refs):
     n = len(pieces)
     blocks, gate, up = refs[:n], refs[n], refs[n + 1]
-    product, gates = refs[n + 2 : n + 4]
-    act, gated, d_gate, d_up, grad_gates, kept = refs[n + 4 : n + 10]
-    rows_all, buffers, sems, w_sems, k_sem = refs[n + 10 :]
+    product = refs[n + 2]
+    act, gated, d_gate, d_up, grad_gates, gates, kept = refs[n + 3 : n + 10]
+    rows_all, gates_all, buffers, sems, g_sems, w_sems, k_sem = refs[n + 10 :]
     step = pl.program_id(0)
+    experts = gates.shape[0]
+    g_copies = piece_copies(pieces, scalars, blocks, gates_all, g_sems, rows_all.shape[1])
 
     @pl.when(step == 0)
     def _():
-        copies = piece_copies(pieces, scalars, blocks, rows_all, sems)
-        for copy in copies:
+        for copy in piece_copies(pieces, scalars, blocks, rows_all, sems) + g_copies:
             copy.start()
 
     weight = stream([gate, up], scalars, buffers, w_sems, parts)
 
     @pl.when(step == 0)
     def _():
-        for copy in piece_copies(pieces, scalars, blocks, rows_all, sems):
+        for copy in piece_copies(pieces, scalars, blocks, rows_all, sems) + g_copies:
             copy.wait()
         pltpu.make_async_copy(rows_all, kept, k_sem).start()
+        values = gates_all[...].astype(jnp.float32)
+        column = lax.broadcasted_iota(jnp.int32, values.shape, 1) % gate_columns
+        for expert in range(experts):
+            own = scalars[0] * experts + expert
+            gates[expert] = jnp.sum(
+                jnp.where(column == own, values, 0.0), axis=-1, keepdims=True
+            )
 
     @pl.when(step % parts == 0)
     def _():
@@ -1134,7 +1250,7 @@
         rows = pl.ds(begin, chunk)
         gate_hid = dot(rows_all[rows, :], weight[0])
         up_hid = dot(rows_all[rows, :], weight[1])
-        own_gate = gates[rows, :]
+        own_gate = gates[step // parts, rows, :]
         back = product[rows, :]
         sig = 1.0 / (1.0 + jnp.exp(-gate_hid))
         silu = gate_hid * sig
@@ -1159,7 +1275,7 @@
     return lambda i: ((i % parts) // half * experts + i // parts) * half + (i % parts) % half
 
 
-def expert_hidden(ring, scalars, blocks, gate, up, product, gates):
+def expert_hidden(ring, scalars, blocks, gate, up, product):
     experts, width, hidden_units = gate.shape
     parts = hidden_parts
     step_hidden = hidden_units // parts
@@ -1175,11 +1291,13 @@
         grid_spec=pltpu.PrefetchScalarGridSpec(
             num_scalar_prefetch=1,
             grid=(experts * parts,),
-            in_specs=[anywhere] * (n + 2) + [relative, column],
-            out_specs=[placed] * 4 + [column, anywhere],
+            in_specs=[anywhere] * (n + 2) + [relative],
+            out_specs=[placed] * 4 + [column, whole_block((experts, span, 1)), anywhere],
             scratch_shapes=[
                 pltpu.VMEM((span, width), jnp.bfloat16),
+                pltpu.VMEM((span, 2 * gate_columns), jnp.bfloat16),
                 pltpu.VMEM((2, 2, width, step_hidden), jnp.bfloat16),
+                pltpu.SemaphoreType.DMA((n,)),
                 pltpu.SemaphoreType.DMA((n,)),
                 pltpu.SemaphoreType.DMA((2, 2)),
                 pltpu.SemaphoreType.DMA,
@@ -1191,10 +1309,11 @@
             hidden,
             hidden,
             jax.ShapeDtypeStruct((experts, span, 1), jnp.float32),
+            jax.ShapeDtypeStruct((experts, span, 1), jnp.float32),
             jax.ShapeDtypeStruct((span, width), jnp.bfloat16),
         ],
         name="expert_hidden",
-    )(scalars, *blocks, gate, up, product, gates)
+    )(scalars, *blocks, gate, up, product)
 
 
 def pack_weights(scalars, weights, packed, parts):
@@ -1217,31 +1336,52 @@
 
 
 def expert_inputs_kernel(pieces, parts, scalars, *refs):
-    d_gate, d_up = refs[:2]
-    gate, up = refs[2:4]
+    d_gate, d_up, gate, up, grad_gates = refs[:5]
     n = len(pieces)
-    results = refs[4 : 4 + n]
-    packed, summed = refs[4 + n :]
-    pack_weights(scalars, gate, packed.at[0], parts)
-    pack_weights(scalars, up, packed.at[1], parts)
-    total = dot(d_gate[...], packed[0], columns_last) + dot(d_up[...], packed[1], columns_last)
-    summed[...] = total.astype(jnp.bfloat16)
+    results = refs[5 : 5 + n]
+    packed, summed = refs[5 + n :]
+    step = pl.program_id(0)
+    last = pl.num_programs(0) - 1
+
+    @pl.when(step < last)
+    def _():
+        pack_weights(scalars, gate, packed.at[0], parts)
+        pack_weights(scalars, up, packed.at[1], parts)
+        total = dot(d_gate[...], packed[0], columns_last) + dot(d_up[...], packed[1], columns_last)
+        summed[...] = total.astype(jnp.bfloat16)
+
+    @pl.when(step == last)
+    def _():
+        experts = grad_gates.shape[0]
+        column = lax.broadcasted_iota(jnp.int32, summed.shape, 1)
+        placed = jnp.zeros(summed.shape, jnp.float32)
+        for expert in range(experts):
+            value = grad_gates[expert]
+            high = value.astype(jnp.bfloat16).astype(jnp.float32)
+            own = scalars[0] * experts + expert
+            placed = jnp.where(column == own, high, placed)
+            placed = jnp.where(column == own + rest_column, value - high, placed)
+        summed[...] = placed.astype(jnp.bfloat16)
+
     store_pieces(pieces, scalars, summed, results)
 
 
-def expert_inputs(ring, scalars, d_gate, d_up, gate, up):
+def expert_inputs(ring, scalars, d_gate, d_up, gate, up, grad_gates):
     experts, width, hidden_units = gate.shape
     parts = hidden_parts
     span, hidden = d_gate.shape
     wide = min(256, width)
+    steps = width // wide
     whole = pl.BlockSpec((span, hidden), lambda i, s: (0, 0), pipeline_mode=pl.Buffered(1))
-    weight = pl.BlockSpec((experts, wide, hidden_units), lambda i, s: (0, i, 0))
+    weight = pl.BlockSpec(
+        (experts, wide, hidden_units), lambda i, s: (0, jnp.minimum(i, steps - 1), 0)
+    )
     return pl.pallas_call(
         functools.partial(expert_inputs_kernel, ring.pieces, parts),
         grid_spec=pltpu.PrefetchScalarGridSpec(
             num_scalar_prefetch=1,
-            grid=(width // wide,),
-            in_specs=[whole] * 2 + [weight] * 2,
+            grid=(steps + 1,),
+            in_specs=[whole] * 2 + [weight] * 2 + [whole_block((experts, span, 1))],
             out_specs=[
                 pl.BlockSpec((count, wide), lambda i, s: (0, i)) for _, _, count in ring.pieces
             ],
@@ -1250,9 +1390,9 @@
                 pltpu.VMEM((span, wide), jnp.bfloat16),
             ],
         ),
-        out_shape=piece_shapes(ring.pieces, width),
+        out_shape=piece_shapes(ring.pieces, width + wide),
         name="expert_inputs",
-    )(scalars, d_gate, d_up, gate, up)
+    )(scalars, d_gate, d_up, gate, up, grad_gates)
 
 
 def expert_outputs_kernel(pieces, parts, scalars, *refs):
@@ -1357,16 +1497,31 @@
     )(scalars, left, right, arrived)
 
 
-def weight_rows_kernel(scalars, left, right, result):
-    result[...] = dot(left[...], right[...], rows_first).astype(jnp.bfloat16)
-
-
-def weight_rows(scalars, left, right, parts):
+def weight_rows_kernel(scalars, left, right, sums, far, near):
+    columns = right.shape[1]
+    value = dot(left[...], right[...], rows_first)
+    beside = rows_as_columns(sums[...], far.shape[1] - columns)
+    half = pl.num_programs(0) // 2
+
+    @pl.when(pl.program_id(0) < half)
+    def _():
+        far[:, :columns] = value.astype(jnp.bfloat16)
+        far[:, columns:] = beside.astype(jnp.bfloat16)
+
+    @pl.when(pl.program_id(0) >= half)
+    def _():
+        near[:, :columns] = value
+        near[:, columns:] = beside
+
+
+def weight_rows(scalars, left, right, sums, parts):
     span, width = left.shape
     columns = right.shape[1]
     count = width // parts
+    half = parts // 2
     own = scalars.shape[0] - 1
-    relative = lambda i: 2 * (i % 2) + jnp.where(i < 2, 1, 0)
+    relative = lambda i: 2 * (i % half) + jnp.where(i < half, 1, 0)
+    wide = columns + sum_columns
     return pl.pallas_call(
         weight_rows_kernel,
         grid_spec=pltpu.PrefetchScalarGridSpec(
@@ -1375,12 +1530,19 @@
             in_specs=[
                 pl.BlockSpec((span, count), lambda i, s: (0, s[own] ^ relative(i))),
                 whole_block((span, columns)),
+                pl.BlockSpec((sums.shape[0], count), lambda i, s: (0, s[own] ^ relative(i))),
             ],
-            out_specs=pl.BlockSpec((None, count, columns), lambda i, s: (i, 0, 0)),
+            out_specs=[
+                pl.BlockSpec((None, count, wide), lambda i, s: (jnp.minimum(i, half - 1), 0, 0)),
+                pl.BlockSpec((None, count, wide), lambda i, s: (jnp.maximum(i - half, 0), 0, 0)),
+            ],
         ),
-        out_shape=jax.ShapeDtypeStruct((parts, count, columns), jnp.bfloat16),
+        out_shape=[
+            jax.ShapeDtypeStruct((half, count, wide), jnp.bfloat16),
+            jax.ShapeDtypeStruct((half, count, wide), jnp.float32),
+        ],
         name="weight_rows",
-    )(scalars, left, right)
+    )(scalars, left, right, sums)
 
 
 def per_device(
@@ -1440,11 +1602,11 @@
     for k in range(1, half):
         ties = {1: packed, half - 1: (token_steps[-1], out_rows)}.get(k, token_steps[-1])
         small_steps.append(small_ring.step(ties))
-        token_steps.append(token_ring.step((ties, small_steps[k - 1])))
+        token_steps.append(token_ring.step(ties))
     token_blocks = token_ring.blocks()
     w_in = share_relative(packed, dp_size, None, token_steps[2])
     small = small_ring.stacked().transpose(2, 1, 0, 3).reshape(-1, width)
-    router = small[:num_experts]
+    router = jnp.pad(small[:num_experts], ((0, 2 * gate_columns - num_experts), (0, 0)))
     gains = small[num_experts:].astype(f32)
     gain_in, gain_q, gain_k, gain_mid = (gains[i][None, :] for i in range(4))
     gain_q = lax.dynamic_slice_in_dim(gain_q, f_index * part, part, 1)
@@ -1473,101 +1635,67 @@
         ring, scalars, raw, factors, gain_q, gain_k, cosine, sine, w_out, head_dim
     )
     attn_ring = ring.reduce(after(attn_pieces, cot_step))
+    attn_step = attn_ring.step()
+    cot_step = cot_ring.step(attn_step)
     attn_ring.step()
-    cot_step = cot_ring.step(attn_pieces[0])
-    attn_step = attn_ring.step(cot_step)
-    cot_step = cot_ring.step(attn_step)
+    last_cot = cot_ring.step()
     attn_ring.step(cot_step)
-    attn_ring.step()
-    resid_mid = tokens.astype(f32) + attn_ring.total()
-
-    mid_factor = lax.rsqrt(jnp.mean(resid_mid * resid_mid, axis=-1, keepdims=True) + epsilon)
-    mid_low = (resid_mid * mid_factor * gain_mid).astype(low)
-    mid_ring = ring.gather(mid_low)
+    attn_ring.step(last_cot)
+    resid_mid, mid_factor, mid_block, *routing = middle(
+        tokens, attn_ring.last(), gain_mid, router, routes, num_experts
+    )
+
+    mid_ring = ring.gather(mid_block)
     mid_steps = [mid_ring.step()]
-    logits = dot(mid_low, router, columns_last)
-    chosen_mask = jnp.any(
-        routes[:, :, None] == jnp.arange(num_experts, dtype=jnp.int32)[None, None, :], axis=1
-    )
-    router_probs = jax.nn.softmax(logits, axis=-1)
-    chosen = jnp.where(chosen_mask, router_probs, 0.0)
-    chosen_sum = jnp.sum(chosen, axis=-1, keepdims=True)
-    gates = chosen / chosen_sum
-    gate_ring = ring.gather(gates.T, False)
-    gate_steps = [gate_ring.step(mid_steps[0])]
     mid_steps.append(mid_ring.step())
     back_act, cot_all = expert_first(
         ring, after(scalars, mid_steps[0]), cot_ring.blocks(), down_w
     )
-    gate_steps.append(gate_ring.step((mid_steps[1], back_act)))
-    mid_steps.append(mid_ring.step((back_act, gate_steps[0])))
-    gate_steps.append(gate_ring.step(mid_steps[2]))
-    mid_steps.append(mid_ring.step(gate_steps[1]))
-    gate_steps.append(gate_ring.step(mid_steps[2]))
-    mid_blocks = mid_ring.blocks()
-    gates_all = gate_ring.stacked()
-    own_gates = lax.dynamic_slice_in_dim(gates_all, f_index * local_experts, local_experts, 1)
-    own_gates = own_gates.transpose(1, 0, 2).reshape(local_experts, span)[:, :, None]
-    act, act_gated, d_gate, d_up, grad_gates, mid_all = expert_hidden(
-        ring, scalars, mid_blocks, gate_w, up_w, back_act, own_gates
-    )
-    grad_in = expert_inputs(ring, scalars, d_gate, d_up, gate_w, up_w)
+    mid_ring.step(back_act)
+    mid_ring.step()
+    act, act_gated, d_gate, d_up, grad_gates, own_gates, mid_all = expert_hidden(
+        ring, scalars, mid_ring.blocks(), gate_w, up_w, back_act
+    )
+    grad_in = expert_inputs(ring, scalars, d_gate, d_up, gate_w, up_w, grad_gates)
 
     def far_part(left, right, ties):
         return weight_far(after(left, ties), right)
 
+    def cross(far, ties):
+        return lax.ppermute(after(far, ties), dp_axes, exchange_pairs(dp_size, 1))
+
     def near_part(left, right, far, ties):
-        far = lax.ppermute(after(far, ties), dp_axes, exchange_pairs(dp_size, 1))
         return weight_near(scalars, after(left, ties), right, far, local_experts)
 
-    def finish(near):
+    def finish(near, ties):
+        near = after(near, ties)
         return lax.psum_scatter(near, "x", scatter_dimension=0, tiled=True).astype(f32)
 
-    by_device = grad_gates.reshape(local_experts, size, rows)
-    grad_ring, route_ring = ring.reduce(grad_in), ring.gather(by_device, False)
-    route_steps = [route_ring.step(grad_in)]
+    grad_ring = ring.reduce(grad_in)
     grad_steps = [grad_ring.step()]
     gate_far = far_part(mid_all, d_gate, grad_in)
-    route_steps.append(route_ring.step(grad_steps[0]))
-    grad_steps.append(grad_ring.step((gate_far, route_steps[0])))
+    grad_steps.append(grad_ring.step(gate_far))
+    gate_cross = cross(gate_far, grad_steps[0])
     up_far = far_part(mid_all, d_up, grad_steps[0])
-    route_steps.append(route_ring.step(grad_steps[1]))
-    grad_steps.append(grad_ring.step((up_far, route_steps[1])))
-    gate_near = near_part(mid_all, d_gate, gate_far, grad_steps[1])
-    route_steps.append(route_ring.step(grad_steps[2]))
-    grad_steps.append(grad_ring.step((gate_near, route_steps[2])))
-    up_near = near_part(mid_all, d_up, up_far, grad_steps[2])
-    grad_mid = after(grad_ring.total(), up_near)
-
-    gates_back = route_ring.stacked()
-    gates_back = lax.dynamic_slice_in_dim(gates_back, f_index, 1, 2)
-    gates_back = gates_back.reshape(num_experts, rows).T
-    inner = jnp.sum(jnp.where(chosen_mask, gates_back * gates, 0.0), axis=-1, keepdims=True)
-    grad_probs = jnp.where(chosen_mask, (gates_back - inner) / chosen_sum, 0.0)
-    grad_logits = router_probs * (
-        grad_probs - jnp.sum(router_probs * grad_probs, axis=-1, keepdims=True)
-    )
-    grad_logits_low = grad_logits.astype(low)
-    grad_router = dot(grad_logits_low, mid_low, rows_first)
-    grad_mid = grad_mid + dot(grad_logits_low, router)
-    grad_out = cotangent.astype(f32)
-    scaled = grad_mid * gain_mid
-    grad_resid = (
-        grad_out
-        + mid_factor * scaled
-        - resid_mid * mid_factor**3 * jnp.mean(scaled * resid_mid, axis=-1, keepdims=True)
-    )
-    grad_gain_mid = jnp.sum(grad_mid * resid_mid * mid_factor, axis=0)
-    grad_low = grad_resid.astype(low)
+    grad_steps.append(grad_ring.step(up_far))
+    up_cross = cross(up_far, grad_steps[1])
+    down_far = far_part(cot_all, act_gated, grad_steps[1])
+    grad_steps.append(grad_ring.step((down_far, gate_cross)))
+    down_cross = cross(down_far, grad_steps[2])
+    gate_near = near_part(mid_all, d_gate, gate_cross, grad_steps[2])
+    grad_resid, grad_low, grad_gain_mid, grad_router = middle_back(
+        after(grad_ring.last(), (gate_near, up_cross)), cotangent, resid_mid, mid_factor,
+        mid_block, *routing, gain_mid, router,
+    )
 
     back_ring = ring.gather(grad_low)
     back_steps = [back_ring.step()]
-    down_far = far_part(cot_all, act_gated, grad_low)
-    back_steps.append(back_ring.step(down_far))
-    moe_pieces = expert_outputs(ring, after(scalars, back_steps[0]), act, own_gates, down_w)
+    up_near = near_part(mid_all, d_up, up_cross, grad_low)
+    back_steps.append(back_ring.step((up_near, down_cross)))
+    down_near = near_part(cot_all, act_gated, down_cross, back_steps[0])
+    back_steps.append(back_ring.step(down_near))
+    moe_pieces = expert_outputs(ring, after(scalars, back_steps[1]), act, own_gates, down_w)
     back_steps.append(back_ring.step(moe_pieces[0]))
-    down_near = near_part(cot_all, act_gated, down_far, back_steps[1])
-    back_steps.append(back_ring.step(down_near))
     grad_blocks = back_ring.blocks()
 
     def head_back(head, ties):
@@ -1576,64 +1704,64 @@
             grad_blocks, head_dim, head,
         )
 
-    moe_ring = ring.reduce(after(moe_pieces, back_steps[3]))
+    moe_ring = ring.reduce(moe_pieces)
     moe_step = moe_ring.step()
-    backs = [head_back(0, back_steps[3])]
+    backs = [head_back(0, (back_steps[3], moe_step))]
+    moe_step = moe_ring.step()
     for head in range(1, own_heads):
-        if moe_ring.left > 2:
-            moe_step = moe_ring.step(backs[-1])
-        backs.append(head_back(head, backs[-1][0]))
+        backs.append(head_back(head, moe_step))
+        if moe_ring.left > 1:
+            moe_step = moe_ring.step(early=backs[head - 1][0])
     grad_attn_out = backs[0][6]
     dots = after(sum(back[3] for back in backs), moe_step)
     grad_gain_q = jnp.concatenate([back[4] for back in backs], axis=1)
     grad_gain_k = jnp.concatenate([back[5] for back in backs], axis=1)
     grad_w_out = dot(saved[3].astype(low), after(grad_attn_out, dots), rows_first)
     dots = pair_sum(dots, "fsdp", size) / width
-    grad_w_out = jnp.concatenate(
-        [
-            lax.dynamic_slice_in_dim(grad_w_out, (d_index ^ k) * own_rows, own_rows, 0)[None]
-            for k in (1, 3, 0, 2)
-        ],
-        axis=0,
-    ).astype(low)
-    while moe_ring.left > 1:
-        moe_step = moe_ring.step(dots)
+    out_blocks = [
+        lax.dynamic_slice_in_dim(grad_w_out, (d_index ^ k) * own_rows, own_rows, 0)
+        for k in range(dp_size)
+    ]
+    out_far = jnp.stack([out_blocks[1], out_blocks[3]]).astype(low)
+    while moe_ring.left > 0:
+        moe_step = moe_ring.step(dots, backs[-1][0])
+    layer_out = (resid_mid + moe_ring.total()).astype(low)
     grad_raw, grad_gain_in, normed_pieces = project_back(
         ring, scalars, [value for back in backs for value in back[:3]], raw, factors,
-        after(dots, grad_w_out), gain_q, gain_k, x_all, in_factor, w_in,
-    )
-    grad_w_out = combine_relative(grad_w_out)[0].astype(low)
-    grad_w_out = lax.ppermute(grad_w_out, dp_flat, from_rows).astype(f32)
-    normed_pieces = after(normed_pieces, moe_step)
-    moe_step = moe_ring.step(normed_pieces)
-    layer_out = (resid_mid + moe_ring.total()).astype(low)
+        after(dots, out_far), gain_q, gain_k, x_all, in_factor, w_in,
+    )
+    grad_w_out = combine_relative(out_far, [out_blocks[0], out_blocks[2]]).astype(low)
+    normed_pieces = after(normed_pieces, (moe_step, grad_w_out))
 
     in_ring = ring.reduce(normed_pieces)
     in_steps = [in_ring.step()]
-    grad_w_in = weight_rows(scalars, after(normed, normed_pieces), grad_raw, dp_size)
     grad_gains = lax.dynamic_update_slice(
         jnp.zeros((2, width), f32),
         jnp.concatenate([grad_gain_q, grad_gain_k], axis=0),
         (0, f_index * part),
     )
-    sums = jnp.concatenate([grad_router, grad_gain_mid[None], grad_gain_in, grad_gains], axis=0)
-    sums = pair_scatter(after(sums, normed_pieces), dp_axes, dp_size)
-    in_steps.append(in_ring.step((grad_w_in, moe_step)))
-    grad_w_in = combine_relative(grad_w_in, (in_steps[0], in_steps[0]))[0].astype(low)
-    sums = pair_scatter(sums, "fsdp", size, {4: in_steps[0], 2: in_steps[1]})
-    in_steps.append(in_ring.step())
-    in_steps.append(in_ring.step(grad_w_in))
+    sums = [grad_router[:num_experts], grad_gain_mid, grad_gain_in, grad_gains]
+    sums.append(jnp.zeros((-(num_experts + 4) % 8, width), f32))
+    grad_w_in = weight_rows(
+        scalars, after(normed, normed_pieces), grad_raw, jnp.concatenate(sums, axis=0), dp_size
+    )
+    grad_gate_w = finish(gate_near, grad_low)
+    grad_up_w = finish(up_near, back_steps[3])
+    grad_down_w = finish(down_near, back_steps[3])
+    in_steps.append(in_ring.step(early=grad_w_in))
+    grad_w_in = combine_relative(*grad_w_in, (in_steps[0], in_steps[0])).astype(low)
+    in_steps.append(in_ring.step(early=grad_gate_w))
+    in_steps.append(in_ring.step(early=(grad_w_in, grad_up_w, grad_down_w)))
     grad_normed = in_ring.total()
-    grad_gate_w, grad_up_w, grad_down_w = (
-        finish(near) for near in (gate_near, up_near, down_near)
-    )
-    grad_w_in = grad_w_in.reshape(size, own_rows, 3 * part)
+    grad_w_in = after(grad_w_in, in_steps[2]).reshape(size, own_rows, -1)
     grad_w_in = lax.all_to_all(grad_w_in, "fsdp", split_axis=0, concat_axis=0, tiled=True)
+    sums = jnp.sum(grad_w_in[:, :, 3 * part :].astype(f32), axis=0)
     grad_w_in = [
         grad_w_in[:, :, i * part : (i + 1) * part].transpose(1, 0, 2).reshape(own_rows, width)
         for i in range(3)
     ]
     grad_w_in = [values.astype(f32) for values in grad_w_in]
+    grad_w_out = lax.ppermute(after(grad_w_out, in_steps[2]), dp_flat, from_rows).astype(f32)
     own_x = tokens.astype(f32)
     own_factor = lax.rsqrt(jnp.mean(own_x * own_x, axis=-1, keepdims=True) + epsilon)
     scaled_in = grad_normed * gain_in
@@ -1649,11 +1777,11 @@
         grad_w_in[1],
         grad_w_in[2],
         grad_w_out,
-        sums[:num_experts].T,
-        sums[num_experts + 1],
-        sums[num_experts + 2],
-        sums[num_experts + 3],
-        sums[num_experts],
+        sums[:, :num_experts],
+        sums[:, num_experts + 1],
+        sums[:, num_experts + 2],
+        sums[:, num_experts + 3],
+        sums[:, num_experts],
         grad_gate_w,
         grad_up_w,
         grad_down_w,

time: 733 us -> 676 us (0.922)
  waiting for transfers between devices: 239 us -> 189 us
  Pallas kernels: 232 us -> 273 us
  other arithmetic: 71.9 us -> 36.1 us
  starting transfers between devices: 134 us -> 114 us
  local copies, waits for them, and re-layouts: 27.2 us -> 36.1 us
    ppermute x44 -> x36, waiting for transfers between devices: 127 us -> 80.2 us  [forward(): return lax.ppermute(values, 'fsdp', self.up)]
    pallas_call x0 -> x14, Pallas kernels: none -> 39 us  [the longest x12 30.7 us: add_pair(): pl.pallas_call(add_pair_kernel, out_shape=[shape, shape], name='add_pair')]
    ppermute x44 -> x36, starting transfers between devices: 73.4 us -> 35 us  [forward(): return lax.ppermute(values, 'fsdp', self.up)]
    add x28 -> x0, other arithmetic: 26.1 us -> none  [the longest x16 19.6 us: step(): upper, lower = (upper + rising, lower + falling)]
    ppermute x41 -> x35, starting transfers between devices: 30.9 us -> 52.5 us  [backward(): return lax.ppermute(values, 'fsdp', self.down)]
    unnamed x197 -> x174, local copies, waits for them, and re-layouts: 8.42 us -> 20.2 us
    ppermute x11 -> x6, waiting for transfers between devices: 14.4 us -> 4.01 us  [the longest x2 4 us: combine_relative(): far = lax.ppermute(after(far, ties[0]), dp_axes, exchange_pairs(4, 1))]
    ppermute x41 -> x35, waiting for transfers between devices: 59.2 us -> 67.7 us  [backward(): return lax.ppermute(values, 'fsdp', self.down)]
  transfers between devices with their start and end apart: 121 -> 102, of which waited for: 51 -> 50; matrix products, arithmetic and copies ran while one was open for 13% -> 9% of each run, Pallas kernels for 23% -> 31%
where the time goes in v3:
time: 676 us; the launch traced here: 668 us
  Pallas kernels  273 us (40%)
  waiting for transfers between devices  189 us (28%)
  starting transfers between devices  114 us (17%)
  local copies, waits for them, and re-layouts  36.1 us (5%)
  other arithmetic  36.1 us (5%)
  between operations  15.8 us (2%)
    ppermute x36, waiting for transfers between devices, forward(): return lax.ppermute(values, 'fsdp', self.up)  80.2 us
    ppermute x35, waiting for transfers between devices, backward(): return lax.ppermute(values, 'fsdp', self.down)  67.7 us
    ppermute x35, starting transfers between devices, backward(): return lax.ppermute(values, 'fsdp', self.down)  52.5 us
    pallas_call x3, Pallas kernels, weight_near(): pl.pallas_call(weight_near_kernel, grid_spec=pltpu.PrefetchScalarGridSpec...  35.5 us
    ppermute x36, starting transfers between devices, forward(): return lax.ppermute(values, 'fsdp', self.up)  35 us
    pallas_call x1, Pallas kernels, expert_hidden(): pl.pallas_call(functools.partial(expert_hidden_kernel, ring.pieces, parts...  31.4 us
    pallas_call x12, Pallas kernels, add_pair(): pl.pallas_call(add_pair_kernel, out_shape=[shape, shape], name='add_pair')  30.7 us
    pallas_call x3, Pallas kernels, weight_far(): pl.pallas_call(weight_far_kernel, grid=(width // wide,), in_specs=[pl.Blo...  30.4 us
  transfers between devices with their start and end apart: 102, of which 50 were waited for; matrix products, arithmetic and copies ran while one was open for 9% of the time, Pallas kernels for 31%

profile of v3, /device:TPU:0, one launch (start us, length us, event | category | flops | bytes accessed | tf_op | source)
XLA Modules:
  0.0 668.1 jit_solution(5066685092753705859)
XLA Ops:
  10.6 7.3 %all-to-all-start = ((bf16[8,64,768]{2,1,0:T(8,128)(2,1)}), bf16[8,64,768]{2,1,0:T(8,128)(2,1)S(1)}, u32[]{:S(2)}, u32[]{:S(2)}) async-start(bf16[8,64,768]{2,1,0:T(8,128)(2,1)} %maximum_bitcast_fusion), calls=%async_computation | async-start | bytes 1572864 | tf_op jit(solution)/shard_map/all_to_all | solution.py:1591
  22.1 22.0 %collective-permute-done.refs_1_ = bf16[128,2048]{1,0:T(8,128)(2,1)S(1)} collective-permute-done((bf16[128,2048]{1,0:T(8,128)(2,1)S(1)}, bf16[128,2048]{1,0:T(8,128)(2,1)S(1)}, u32[]{:S(2)}, u32[]{:S(2)}) %collective-permute-start) | collective-permute-done | bytes 524320 | tf_op jit(solution)/shard_map/ppermute | solution.py:436
  45.6 4.4 collective-permute-start.3
  58.4 3.0 collective-permute-done.14
  62.8 2.8 collective-permute-start.16
  65.7 7.2 %collective-permute-start.4 = (bf16[128,2048]{1,0:T(8,128)(2,1)S(1)}, bf16[128,2048]{1,0:T(8,128)(2,1)S(1)}, u32[]{:S(2)}, u32[]{:S(2)}) collective-permute-start(bf16[128,2048]{1,0:T(8,128)(2,1)S(1)} %collective-permute-done.2.refs_2_), channel_id=1, source_target_pairs={{0,1},{2,0},{4,2},{6,4},{7,6},{5,7},{3,5},{1,3},{8,9},{10,8},{12,1... | collective-permute-start | bytes 1572872 | tf_op jit(solution)/shard_map/ppermute | solution.py:436
  73.5 2.9 collective-permute-start.17
  77.0 5.6 collective-permute-done.17
  82.6 3.1 collective-permute-start.18
  87.2 3.7 collective-permute-done.19
  96.7 4.3 collective-permute-done.7.refs_4_
  111.2 13.3 %project.1 = (bf16[1024,2048]{1,0:T(8,128)(2,1)}, f32[1024,768]{1,0:T(8,128)}, f32[1024,1]{1,0:T(8,128)}, f32[8,1024]{1,0:T(8,128)}, bf16[1024,2048]{1,0:T(8,128)(2,1)}) custom-call(s32[9]{0:T(128)} %pad_add_fusion.scalars, bf16[128,2048]{1,0:T(8,128)(2,1)} %tokens.1, bf16[128,2048]{1,0:T(8,128)(2,1)} %copy-done.37, bf16[128,2048]{1,0:T(8,128)(2,1)} %copy-done.39, ...), custom_call_target="tpu_custom_call" | custom-call | tf_op jit(solution)/shard_map/project/pallas_call | solution.py:693
  134.4 3.9 collective-permute-done.28
  145.9 18.8 %attend.1 = (bf16[1024,256]{1,0:T(8,128)(2,1)}, bf16[1024,256]{1,0:T(8,128)(2,1)}, bf16[1024,256]{1,0:T(8,128)(2,1)}, f32[1024,256]{1,0:T(8,128)}, f32[2,1024,1]...) custom-call(s32[9]{0:T(128)} %pad_add_fusion.scalars, ...), custom_call_target="tpu_custom_call" | custom-call | tf_op jit(solution)/shard_map/attend/pallas_call | solution.py:800
  166.8 4.6 collective-permute-done.31.rising
  180.3 11.0 %collective-permute-done.33.rising = bf16[128,2048]{1,0:T(8,128)(2,1)S(1)} collective-permute-done((bf16[128,2048]{1,0:T(8,128)(2,1)}, bf16[128,2048]{1,0:T(8,128)(2,1)S(1)}, u32[]{:S(2)}, u32[]{:S(2)}) %collective-permute-start.33) | collective-permute-done | bytes 524320 | tf_op jit(solution)/shard_map/ppermute | solution.py:433
  192.9 2.6 add_pair.13
  195.5 3.2 collective-permute-done.35.refs_6_
  205.3 6.3 collective-permute-done.37.rising
  213.3 2.6 add_pair.14
  222.3 4.8 collective-permute-done.41.rising
  228.7 3.5 middle.1
  234.4 13.3 %collective-permute-done.43.refs_1_ = bf16[128,2176]{1,0:T(8,128)(2,1)S(1)} collective-permute-done((bf16[128,2176]{1,0:T(8,128)(2,1)}, bf16[128,2176]{1,0:T(8,128)(2,1)S(1)}, u32[]{:S(2)}, u32[]{:S(2)}) %collective-permute-start.43) | collective-permute-done | bytes 557088 | tf_op jit(solution)/shard_map/ppermute | solution.py:436
  250.1 15.7 %expert_first.1 = (f32[2,1024,1024]{2,1,0:T(8,128)}, bf16[1024,2048]{1,0:T(8,128)(2,1)}) custom-call(s32[9]{0:T(128)} %pad_add_fusion.scalars, bf16[128,2048]{1,0:T(8,128)(2,1)} %cotangent.1, bf16[128,2048]{1,0:T(8,128)(2,1)} %collective-permute-done.22.refs_1_, bf16[128,2048]{1,0:T(8,128)(2,1)} %copy-done.41, bf16[128,2048]{1,0:T(8,128)(2,1)} %copy-done.23, ...), custom_call_target="tpu_custom_call" | custom-call | tf_op jit(solution)/shard_map/expert_first/pallas_call | solution.py:1189
  268.0 8.2 %collective-permute-done.48.refs_6_ = bf16[128,2176]{1,0:T(8,128)(2,1)S(1)} collective-permute-done((bf16[128,2176]{1,0:T(8,128)(2,1)S(1)}, bf16[128,2176]{1,0:T(8,128)(2,1)S(1)}, u32[]{:S(2)}, u32[]{:S(2)}) %collective-permute-start.48) | collective-permute-done | bytes 557088 | tf_op jit(solution)/shard_map/ppermute | solution.py:433
  278.4 4.4 collective-permute-done.49.refs_4_
  284.5 31.4 %expert_hidden.1 = (bf16[1024,2048]{1,0:T(8,128)(2,1)}, bf16[1024,2048]{1,0:T(8,128)(2,1)}, bf16[1024,2048]{1,0:T(8,128)(2,1)}, bf16[1024,2048]{1,0:T(8,128)(2,1...) custom-call(s32[9]{0:T(128)} %pad_add_fusion.scalars, ...), custom_call_target="tpu_custom_call" | custom-call | tf_op jit(solution)/shard_map/expert_hidden/pallas_call | solution.py:1289
  315.9 26.3 %expert_inputs.1 = (bf16[128,2304]{1,0:T(8,128)(2,1)}, bf16[128,2304]{1,0:T(8,128)(2,1)}, bf16[128,2304]{1,0:T(8,128)(2,1)}, bf16[128,2304]{1,0:T(8,128)(2,1)}, ...) custom-call(s32[9]{0:T(128)} %pad_add_fusion.scalars, ...), custom_call_target="tpu_custom_call" | custom-call | tf_op jit(solution)/shard_map/expert_inputs/pallas_call | solution.py:1379
  344.2 10.1 %weight_far.3 = bf16[2048,1024]{1,0:T(8,128)(2,1)} custom-call(bf16[1024,2048]{1,0:T(8,128)(2,1)} %get-tuple-element.318.left, bf16[1024,2048]{1,0:T(8,128)(2,1)} %get-tuple-element.276.refs_0_.right), custom_call_target="tpu_custom_call" | custom-call | tf_op jit(solution)/shard_map/weight_far/pallas_call | solution.py:1453
  355.8 2.5 add_pair.15
  360.4 10.1 %weight_far.4 = bf16[2048,1024]{1,0:T(8,128)(2,1)} custom-call(bf16[1024,2048]{1,0:T(8,128)(2,1)} %get-tuple-element.318.left, bf16[1024,2048]{1,0:T(8,128)(2,1)} %get-tuple-element.277.refs_1_.right), custom_call_target="tpu_custom_call" | custom-call | tf_op jit(solution)/shard_map/weight_far/pallas_call | solution.py:1453
  370.6 5.1 collective-permute-done.54.falling
  376.5 2.7 add_pair.16
  381.2 10.2 %weight_far.5 = bf16[2048,1024]{1,0:T(8,128)(2,1)} custom-call(bf16[1024,2048]{1,0:T(8,128)(2,1)} %get-tuple-element.334.left, bf16[1024,2048]{1,0:T(8,128)(2,1)} %get-tuple-element.303.right), custom_call_target="tpu_custom_call" | custom-call | tf_op jit(solution)/shard_map/weight_far/pallas_call | solution.py:1453
  391.4 3.0 collective-permute-done.55.rising
  396.1 2.7 add_pair.17
  400.8 11.7 %weight_near.3 = bf16[4,2048,256]{2,1,0:T(8,128)(2,1)} custom-call(s32[9]{0:T(128)} %pad_add_fusion.scalars, bf16[1024,2048]{1,0:T(8,128)(2,1)} %get-tuple-element.318.left, bf16[1024,2048]{1,0:T(8,128)(2,1)} %get-tuple-element.276.refs_0_.right, bf16[2048,1024]{1,0:T(8,128)(2,1)} %collective-permute-done.57.arrived), custom_call_target="tpu_custom_call" | custom-call | tf_op jit(solution)/shard_map/weight_near/pallas_call | solution.py:1483
  414.9 4.7 middle_back.1
  422.9 12.1 %weight_near.4 = bf16[4,2048,256]{2,1,0:T(8,128)(2,1)} custom-call(s32[9]{0:T(128)} %pad_add_fusion.scalars, bf16[1024,2048]{1,0:T(8,128)(2,1)} %get-tuple-element.318.left, bf16[1024,2048]{1,0:T(8,128)(2,1)} %get-tuple-element.277.refs_1_.right, bf16[2048,1024]{1,0:T(8,128)(2,1)} %collective-permute-done.60.arrived), custom_call_target="tpu_custom_call" | custom-call | tf_op jit(solution)/shard_map/weight_near/pallas_call | solution.py:1483
  437.5 11.8 %weight_near.5 = bf16[4,2048,256]{2,1,0:T(8,128)(2,1)} custom-call(s32[9]{0:T(128)} %pad_add_fusion.scalars, bf16[1024,2048]{1,0:T(8,128)(2,1)} %get-tuple-element.334.left, bf16[1024,2048]{1,0:T(8,128)(2,1)} %get-tuple-element.303.right, bf16[2048,1024]{1,0:T(8,128)(2,1)} %collective-permute-done.63.arrived), custom_call_target="tpu_custom_call" | custom-call | tf_op jit(solution)/shard_map/weight_near/pallas_call | solution.py:1483
  451.4 15.2 %expert_outputs.1 = (bf16[128,2048]{1,0:T(8,128)(2,1)}, bf16[128,2048]{1,0:T(8,128)(2,1)}, bf16[128,2048]{1,0:T(8,128)(2,1)}, bf16[128,2048]{1,0:T(8,128)(2,1)},...) custom-call(s32[9]{0:T(128)} %pad_add_fusion.scalars, ...), custom_call_target="tpu_custom_call" | custom-call | tf_op jit(solution)/shard_map/expert_outputs/pallas_call | solution.py:1425
  468.9 4.3 collective-permute-done.72.refs_20_
  476.9 4.3 collective-permute-done.66.rising
  488.3 12.2 %attend_back.2 = (f32[1024,128]{1,0:T(8,128)}, f32[1024,128]{1,0:T(8,128)}, bf16[1024,128]{1,0:T(8,128)(2,1)}, f32[8,1024]{1,0:T(8,128)}, f32[1,128]{1,0:T(1,128...) custom-call(s32[9]{0:T(128)} %pad_add_fusion.scalars, bf16[1024,256]{1,0:T(8,128)(2,1)} %get-tuple-element.340.refs_0_, ...), custom_call_target="tpu_custom_call" | custom-call | tf_op jit(solution)/shard_map/attend_back/pallas_call | solution.py:898
  501.5 2.7 add_pair.19
  506.4 11.6 %attend_back.3 = (f32[1024,128]{1,0:T(8,128)}, f32[1024,128]{1,0:T(8,128)}, bf16[1024,128]{1,0:T(8,128)(2,1)}, f32[8,1024]{1,0:T(8,128)}, f32[1,128]{1,0:T(1,128)}, /*index=5*/f32[1,128]{1,0:T(1,128)}) custom-call(s32[9]{0:T(128)} %pad_add_fusion.scalars, bf16[1024,256]{1,0:T(8,128)(2,1)} %get-tuple-element.340.refs_0_, ...), custom_call_target="tpu_custom_call" | custom-call | tf_op jit(solution)/shard_map/attend_back/pallas_call | solution.py:898
  520.4 3.5 fusion.9
  524.6 3.4 collective-permute-done.76
  528.4 2.6 add_pair.20
  533.8 3.3 collective-permute-done.78
  539.8 14.4 %project_back.1 = (bf16[1024,768]{1,0:T(8,128)(2,1)}, f32[1,2048]{1,0:T(1,128)}, bf16[128,2048]{1,0:T(8,128)(2,1)}, bf16[128,2048]{1,0:T(8,128)(2,1)}, bf16[128,...) custom-call(s32[9]{0:T(128)} %pad_add_fusion.scalars, ...), custom_call_target="tpu_custom_call" | custom-call | tf_op jit(solution)/shard_map/project_back/pallas_call | solution.py:989
  560.1 9.6 %weight_rows.1 = (bf16[2,512,896]{2,1,0:T(8,128)(2,1)}, f32[2,512,896]{2,1,0:T(8,128)}) custom-call(s32[9]{0:T(128)} %pad_add_fusion.scalars, bf16[1024,2048]{1,0:T(8,128)(2,1)} %get-tuple-element.392.left, bf16[1024,768]{1,0:T(8,128)(2,1)} %get-tuple-element.393.right, f32[24,2048]{1,0:T(8,128)} %concatenate.95.sums), custom_call_target="tpu_custom_call" | custom-call | tf_op jit(solution)/shard_map/weight_rows/pallas_call | solution.py:1525
  570.5 4.0 collective-permute-done.89
  580.7 3.9 convert_element_type.146
  584.7 8.2 %collective-permute-done.85.rising = bf16[128,2048]{1,0:T(8,128)(2,1)S(1)} collective-permute-done((bf16[128,2048]{1,0:T(8,128)(2,1)}, bf16[128,2048]{1,0:T(8,128)(2,1)S(1)}, u32[]{:S(2)}, u32[]{:S(2)}) %collective-permute-start.85) | collective-permute-done | bytes 524320 | tf_op jit(solution)/shard_map/ppermute | solution.py:433
  598.2 6.4 collective-permute-done.90
  604.6 3.0 fusion
  610.0 3.6 all-to-all-start.1
  613.7 3.9 collective-permute-start.93
  617.6 3.9 convert_element_type.154
  621.5 4.1 convert_element_type.153
  634.9 8.5 %all-to-all-done.1 = bf16[8,64,896]{2,1,0:T(8,128)(2,1)S(1)} async-done(((bf16[8,64,896]{2,1,0:T(8,128)(2,1)}), bf16[8,64,896]{2,1,0:T(8,128)(2,1)S(1)}, u32[]{:S(2)}, u32[]{:S(2)}) %all-to-all-start.1) | async-done | bytes 917536 | tf_op jit(solution)/shard_map/all_to_all | solution.py:1757
  647.5 10.2 %collective-permute-done.92 = bf16[128,2048]{1,0:T(8,128)(2,1)S(1)} collective-permute-done((bf16[128,2048]{1,0:T(8,128)(2,1)}, bf16[128,2048]{1,0:T(8,128)(2,1)S(1)}, u32[]{:S(2)}, u32[]{:S(2)}) %collective-permute-start.92) | collective-permute-done | bytes 524320 | tf_op jit(solution)/shard_map/ppermute | solution.py:436
  658.2 2.6 fusion.3
  (430 shorter events, 176.2 us)
Async XLA Ops:
  7.2 242.9 %all-gather.4.cloned.1.call-start = ((), (), s32[]{:S(2)}) async-start(), calls=%async_computation.5 | async-start | bytes 10485760 | tf_op jit(solution)/shard_map/all_gather | solution.py:1622
  7.9 270.4 %all-gather.6.cloned.1.call-start = ((), (), s32[]{:S(2)}) async-start(), calls=%async_computation.6 | async-start | bytes 10485760 | tf_op jit(solution)/shard_map/all_gather | solution.py:1623
  8.8 269.6 %all-gather.8.cloned.1.call-start = ((), (), s32[]{:S(2)}) async-start(), calls=%async_computation.7 | async-start | bytes 10485760 | tf_op jit(solution)/shard_map/all_gather | solution.py:1624
  10.6 33.6 %all-to-all-start = ((bf16[8,64,768]{2,1,0:T(8,128)(2,1)}), bf16[8,64,768]{2,1,0:T(8,128)(2,1)S(1)}, u32[]{:S(2)}, u32[]{:S(2)}) async-start(bf16[8,64,768]{2,1,0:T(8,128)(2,1)} %maximum_bitcast_fusion), calls=%async_computation | async-start | bytes 1572864 | tf_op jit(solution)/shard_map/all_to_all | solution.py:1591
  17.8 562.9 %reduce-scatter.4.cloned.1.call-start = ((), (), s32[]{:S(2)}) async-start(), calls=%async_computation.8 | async-start | bytes 6291456 | tf_op jit(solution)/shard_map/reduce_scatter | solution.py:1672
  17.9 26.2 %collective-permute-start = (bf16[128,2048]{1,0:T(8,128)(2,1)S(1)}, bf16[128,2048]{1,0:T(8,128)(2,1)S(1)}, u32[]{:S(2)}, u32[]{:S(2)}) collective-permute-start(bf16[128,2048]{1,0:T(8,128)(2,1)S(1)} %copy-done.2), channel_id=1, source_target_pairs={{0,1},{2,0},{4,2},{6,4},{7,6},{5,7},{3,5},{1,3},{8,9},{10,8},{12,1... | collective-permute-start | bytes 1572872 | tf_op jit(solution)/shard_map/ppermute | solution.py:436
  19.9 24.2 %collective-permute-start.1 = (bf16[128,2048]{1,0:T(8,128)(2,1)S(1)}, bf16[128,2048]{1,0:T(8,128)(2,1)S(1)}, u32[]{:S(2)}, u32[]{:S(2)}) collective-permute-start(bf16[128,2048]{1,0:T(8,128)(2,1)S(1)} %copy-done.2), channel_id=1, source_target_pairs={{0,2},{2,4},{4,6},{6,7},{7,5},{5,3},{3,1},{1,0},{8,10},{10,12},{12... | collective-permute-start | bytes 1572872 | tf_op jit(solution)/shard_map/ppermute | solution.py:433
  20.1 30.6 %collective-permute-start.12 = (bf16[1,20,64]{2,1,0:T(8,128)(2,1)S(1)}, bf16[1,20,64]{2,1,0:T(8,128)(2,1)S(1)}, u32[]{:S(2)}, u32[]{:S(2)}) collective-permute-start(bf16[1,20,64]{2,1,0:T(8,128)(2,1)S(1)} %bitcast.102), channel_id=1, source_target_pairs={{0,8},{8,0},{16,24},{24,16},{1,9},{9,1},{17,25},{25,17},{2,10},{10... | collective-permute-start | bytes 7688 | tf_op jit(solution)/shard_map/ppermute | solution.py:534
  44.1 21.5 %collective-permute-start.2 = (bf16[128,2048]{1,0:T(8,128)(2,1)S(1)}, bf16[128,2048]{1,0:T(8,128)(2,1)S(1)}, u32[]{:S(2)}, u32[]{:S(2)}) collective-permute-start(bf16[128,2048]{1,0:T(8,128)(2,1)S(1)} %collective-permute-done.refs_1_), channel_id=1, source_target_pairs={{0,1},{2,0},{4,2},{6,4},{7,6},{5,7},{3,5},{1,3},{8,9},{10,8},{12,1... | collective-permute-start | bytes 1572872 | tf_op jit(solution)/shard_map/ppermute | solution.py:436
  45.6 20.1 %collective-permute-start.3 = (bf16[128,2048]{1,0:T(8,128)(2,1)S(1)}, bf16[128,2048]{1,0:T(8,128)(2,1)}, u32[]{:S(2)}, u32[]{:S(2)}) collective-permute-start(bf16[128,2048]{1,0:T(8,128)(2,1)S(1)} %collective-permute-done.1.refs_8_), channel_id=1, source_target_pairs={{0,2},{2,4},{4,6},{6,7},{7,5},{5,3},{3,1},{1,0},{8,10},{10,12},{12... | collective-permute-start | bytes 1572872 | tf_op jit(solution)/shard_map/ppermute | solution.py:433
  56.8 29.0 %collective-permute-start.6 = (bf16[64,2048]{1,0:T(8,128)(2,1)}, bf16[64,2048]{1,0:T(8,128)(2,1)S(1)}, u32[]{:S(2)}, u32[]{:S(2)}) collective-permute-start(bf16[64,2048]{1,0:T(8,128)(2,1)} %param.24), channel_id=1, source_target_pairs={{0,0},{1,8},{2,16},{3,24},{4,1},{5,9},{6,17},{7,25},{8,2},{9,10},{... | collective-permute-start | bytes 786440 | tf_op jit(solution)/shard_map/ppermute | solution.py:1601
  61.3 30.4 %collective-permute-start.10 = (bf16[512,768]{1,0:T(8,128)(2,1)S(1)}, bf16[512,768]{1,0:T(8,128)(2,1)S(1)}, u32[]{:S(2)}, u32[]{:S(2)}) collective-permute-start(bf16[512,768]{1,0:T(8,128)(2,1)S(1)} %bitcast.88), channel_id=1, source_target_pairs={{0,16},{8,24},{16,0},{24,8},{1,17},{9,25},{17,1},{25,9},{2,18},{10... | collective-permute-start | bytes 2359304 | tf_op jit(solution)/shard_map/ppermute | solution.py:552
  65.7 25.2 %collective-permute-start.4 = (bf16[128,2048]{1,0:T(8,128)(2,1)S(1)}, bf16[128,2048]{1,0:T(8,128)(2,1)S(1)}, u32[]{:S(2)}, u32[]{:S(2)}) collective-permute-start(bf16[128,2048]{1,0:T(8,128)(2,1)S(1)} %collective-permute-done.2.refs_2_), channel_id=1, source_target_pairs={{0,1},{2,0},{4,2},{6,4},{7,6},{5,7},{3,5},{1,3},{8,9},{10,8},{12,1... | collective-permute-start | bytes 1572872 | tf_op jit(solution)/shard_map/ppermute | solution.py:436
  72.9 18.0 %collective-permute-start.5 = (bf16[128,2048]{1,0:T(8,128)(2,1)}, bf16[128,2048]{1,0:T(8,128)(2,1)S(1)}, u32[]{:S(2)}, u32[]{:S(2)}) collective-permute-start(bf16[128,2048]{1,0:T(8,128)(2,1)} %collective-permute-done.3.refs_7_), channel_id=1, source_target_pairs={{0,2},{2,4},{4,6},{6,7},{7,5},{5,3},{3,1},{1,0},{8,10},{10,12},{12... | collective-permute-start | bytes 1572872 | tf_op jit(solution)/shard_map/ppermute | solution.py:433
  87.2 21.0 %collective-permute-start.9 = (bf16[512,768]{1,0:T(8,128)(2,1)S(1)}, bf16[512,768]{1,0:T(8,128)(2,1)S(1)}, u32[]{:S(2)}, u32[]{:S(2)}) collective-permute-start(bf16[512,768]{1,0:T(8,128)(2,1)S(1)} %bitcast.89), channel_id=1, source_target_pairs={{0,8},{8,0},{16,24},{24,16},{1,9},{9,1},{17,25},{25,17},{2,10},{10... | collective-permute-start | bytes 2359304 | tf_op jit(solution)/shard_map/ppermute | solution.py:552
  91.7 18.6 %collective-permute-start.11 = (bf16[512,768]{1,0:T(8,128)(2,1)S(1)}, bf16[512,768]{1,0:T(8,128)(2,1)S(1)}, u32[]{:S(2)}, u32[]{:S(2)}) collective-permute-start(bf16[512,768]{1,0:T(8,128)(2,1)S(1)} %collective-permute-done.10.refs_11_.refs_15_), channel_id=1, source_target_pairs={{0,8},{8,0},{16,24},{24,16},{1,9},{9,1},{17,25},{25,17},{2,10},{10... | collective-permute-start | bytes 2359304 | tf_op jit(solution)/shard_map/ppermute | solution.py:552
  94.8 13.4 %collective-permute-start.24 = (bf16[64,2048]{1,0:T(8,128)(2,1)S(1)}, bf16[64,2048]{1,0:T(8,128)(2,1)}, u32[]{:S(2)}, u32[]{:S(2)}) collective-permute-start(bf16[64,2048]{1,0:T(8,128)(2,1)S(1)} %collective-permute-done.6.refs_8_.refs_12_), channel_id=1, source_target_pairs={{0,16},{8,24},{16,0},{24,8},{1,17},{9,25},{17,1},{25,9},{2,18},{10... | collective-permute-start | bytes 786440 | tf_op jit(solution)/shard_map/ppermute | solution.py:552
  101.5 23.1 %collective-permute-start.21 = (bf16[128,2048]{1,0:T(8,128)(2,1)}, bf16[128,2048]{1,0:T(8,128)(2,1)}, u32[]{:S(2)}, u32[]{:S(2)}) collective-permute-start(bf16[128,2048]{1,0:T(8,128)(2,1)} %cotangent.1), channel_id=1, source_target_pairs={{0,2},{2,4},{4,6},{6,7},{7,5},{5,3},{3,1},{1,0},{8,10},{10,12},{12... | collective-permute-start | bytes 1572872 | tf_op jit(solution)/shard_map/ppermute | solution.py:433
  103.2 21.4 %collective-permute-start.22 = (bf16[128,2048]{1,0:T(8,128)(2,1)}, bf16[128,2048]{1,0:T(8,128)(2,1)}, u32[]{:S(2)}, u32[]{:S(2)}) collective-permute-start(bf16[128,2048]{1,0:T(8,128)(2,1)} %cotangent.1), channel_id=1, source_target_pairs={{0,1},{2,0},{4,2},{6,4},{7,6},{5,7},{3,5},{1,3},{8,9},{10,8},{12,1... | collective-permute-start | bytes 1572872 | tf_op jit(solution)/shard_map/ppermute | solution.py:436
  108.2 16.3 %collective-permute-start.23 = (bf16[64,2048]{1,0:T(8,128)(2,1)S(1)}, bf16[64,2048]{1,0:T(8,128)(2,1)}, u32[]{:S(2)}, u32[]{:S(2)}) collective-permute-start(bf16[64,2048]{1,0:T(8,128)(2,1)S(1)} %collective-permute-done.6.refs_8_.refs_12_), channel_id=1, source_target_pairs={{0,8},{8,0},{16,24},{24,16},{1,9},{9,1},{17,25},{25,17},{2,10},{10... | collective-permute-start | bytes 786440 | tf_op jit(solution)/shard_map/ppermute | solution.py:552
  108.2 16.3 %collective-permute-start.25 = (bf16[64,2048]{1,0:T(8,128)(2,1)}, bf16[64,2048]{1,0:T(8,128)(2,1)}, u32[]{:S(2)}, u32[]{:S(2)}) collective-permute-start(bf16[64,2048]{1,0:T(8,128)(2,1)} %collective-permute-done.24.refs_10_.refs_14_), channel_id=1, source_target_pairs={{0,8},{8,0},{16,24},{24,16},{1,9},{9,1},{17,25},{25,17},{2,10},{10... | collective-permute-start | bytes 786440 | tf_op jit(solution)/shard_map/ppermute | solution.py:552
  138.9 25.8 %collective-permute-start.29 = (bf16[128,2048]{1,0:T(8,128)(2,1)}, bf16[128,2048]{1,0:T(8,128)(2,1)S(1)}, u32[]{:S(2)}, u32[]{:S(2)}) collective-permute-start(bf16[128,2048]{1,0:T(8,128)(2,1)} %collective-permute-done.21.refs_8_), channel_id=1, source_target_pairs={{0,2},{2,4},{4,6},{6,7},{7,5},{5,3},{3,1},{1,0},{8,10},{10,12},{12... | collective-permute-start | bytes 1572872 | tf_op jit(solution)/shard_map/ppermute | solution.py:433
  140.5 24.2 %collective-permute-start.30 = (bf16[128,2048]{1,0:T(8,128)(2,1)}, bf16[128,2048]{1,0:T(8,128)(2,1)S(1)}, u32[]{:S(2)}, u32[]{:S(2)}) collective-permute-start(bf16[128,2048]{1,0:T(8,128)(2,1)} %collective-permute-done.22.refs_1_), channel_id=1, source_target_pairs={{0,1},{2,0},{4,2},{6,4},{7,6},{5,7},{3,5},{1,3},{8,9},{10,8},{12,1... | collective-permute-start | bytes 1572872 | tf_op jit(solution)/shard_map/ppermute | solution.py:436
  176.2 15.1 %collective-permute-start.33 = (bf16[128,2048]{1,0:T(8,128)(2,1)}, bf16[128,2048]{1,0:T(8,128)(2,1)S(1)}, u32[]{:S(2)}, u32[]{:S(2)}) collective-permute-start(bf16[128,2048]{1,0:T(8,128)(2,1)} %get-tuple-element.256), channel_id=1, source_target_pairs={{0,2},{2,4},{4,6},{6,7},{7,5},{5,3},{3,1},{1,0},{8,10},{10,12},{12... | collective-permute-start | bytes 1572872 | tf_op jit(solution)/shard_map/ppermute | solution.py:433
  176.9 15.1 %collective-permute-start.34 = (bf16[128,2048]{1,0:T(8,128)(2,1)}, bf16[128,2048]{1,0:T(8,128)(2,1)S(1)}, u32[]{:S(2)}, u32[]{:S(2)}) collective-permute-start(bf16[128,2048]{1,0:T(8,128)(2,1)} %get-tuple-element.258), channel_id=1, source_target_pairs={{0,1},{2,0},{4,2},{6,4},{7,6},{5,7},{3,5},{1,3},{8,9},{10,8},{12,1... | collective-permute-start | bytes 1572872 | tf_op jit(solution)/shard_map/ppermute | solution.py:436
  178.3 20.5 %collective-permute-start.35 = (bf16[128,2048]{1,0:T(8,128)(2,1)S(1)}, bf16[128,2048]{1,0:T(8,128)(2,1)S(1)}, u32[]{:S(2)}, u32[]{:S(2)}) collective-permute-start(bf16[128,2048]{1,0:T(8,128)(2,1)S(1)} %collective-permute-done.29.refs_7_), channel_id=1, source_target_pairs={{0,2},{2,4},{4,6},{6,7},{7,5},{5,3},{3,1},{1,0},{8,10},{10,12},{12... | collective-permute-start | bytes 1572872 | tf_op jit(solution)/shard_map/ppermute | solution.py:433
  179.0 20.9 %collective-permute-start.36 = (bf16[128,2048]{1,0:T(8,128)(2,1)S(1)}, bf16[128,2048]{1,0:T(8,128)(2,1)S(1)}, u32[]{:S(2)}, u32[]{:S(2)}) collective-permute-start(bf16[128,2048]{1,0:T(8,128)(2,1)S(1)} %collective-permute-done.30.refs_2_), channel_id=1, source_target_pairs={{0,1},{2,0},{4,2},{6,4},{7,6},{5,7},{3,5},{1,3},{8,9},{10,8},{12,1... | collective-permute-start | bytes 1572872 | tf_op jit(solution)/shard_map/ppermute | solution.py:436
  202.6 14.0 %collective-permute-start.39 = (bf16[64,2048]{1,0:T(8,128)(2,1)}, bf16[64,2048]{1,0:T(8,128)(2,1)}, u32[]{:S(2)}, u32[]{:S(2)}) collective-permute-start(bf16[64,2048]{1,0:T(8,128)(2,1)} %slice.149), channel_id=1, source_target_pairs={{0,2},{2,4},{4,6},{6,7},{7,5},{5,3},{3,1},{1,0},{8,10},{10,12},{12... | collective-permute-start | bytes 786440 | tf_op jit(solution)/shard_map/ppermute | solution.py:433
  203.7 14.0 %collective-permute-start.40 = (bf16[64,2048]{1,0:T(8,128)(2,1)}, bf16[64,2048]{1,0:T(8,128)(2,1)}, u32[]{:S(2)}, u32[]{:S(2)}) collective-permute-start(bf16[64,2048]{1,0:T(8,128)(2,1)} %slice.150), channel_id=1, source_target_pairs={{0,1},{2,0},{4,2},{6,4},{7,6},{5,7},{3,5},{1,3},{8,9},{10,8},{12,1... | collective-permute-start | bytes 786440 | tf_op jit(solution)/shard_map/ppermute | solution.py:436
  232.3 15.5 %collective-permute-start.43 = (bf16[128,2176]{1,0:T(8,128)(2,1)}, bf16[128,2176]{1,0:T(8,128)(2,1)S(1)}, u32[]{:S(2)}, u32[]{:S(2)}) collective-permute-start(bf16[128,2176]{1,0:T(8,128)(2,1)} %get-tuple-element.271.refs_0_.block), channel_id=1, source_target_pairs={{0,1},{2,0},{4,2},{6,4},{7,6},{5,7},{3,5},{1,3},{8,9},{10,8},{12,1... | collective-permute-start | bytes 1671176 | tf_op jit(solution)/shard_map/ppermute | solution.py:436
  233.6 15.6 %collective-permute-start.45 = (bf16[128,2176]{1,0:T(8,128)(2,1)}, bf16[128,2176]{1,0:T(8,128)(2,1)S(1)}, u32[]{:S(2)}, u32[]{:S(2)}) collective-permute-start(bf16[128,2176]{1,0:T(8,128)(2,1)} %get-tuple-element.271.refs_0_.block), channel_id=1, source_target_pairs={{0,2},{2,4},{4,6},{6,7},{7,5},{5,3},{3,1},{1,0},{8,10},{10,12},{12... | collective-permute-start | bytes 1671176 | tf_op jit(solution)/shard_map/ppermute | solution.py:433
  247.7 18.1 %collective-permute-start.44 = (bf16[128,2176]{1,0:T(8,128)(2,1)S(1)}, bf16[128,2176]{1,0:T(8,128)(2,1)S(1)}, u32[]{:S(2)}, u32[]{:S(2)}) collective-permute-start(bf16[128,2176]{1,0:T(8,128)(2,1)S(1)} %collective-permute-done.43.refs_1_), channel_id=1, source_target_pairs={{0,1},{2,0},{4,2},{6,4},{7,6},{5,7},{3,5},{1,3},{8,9},{10,8},{12,1... | collective-permute-start | bytes 1671176 | tf_op jit(solution)/shard_map/ppermute | solution.py:436
  249.2 16.6 %collective-permute-start.46 = (bf16[128,2176]{1,0:T(8,128)(2,1)S(1)}, bf16[128,2176]{1,0:T(8,128)(2,1)S(1)}, u32[]{:S(2)}, u32[]{:S(2)}) collective-permute-start(bf16[128,2176]{1,0:T(8,128)(2,1)S(1)} %collective-permute-done.45.refs_8_), channel_id=1, source_target_pairs={{0,2},{2,4},{4,6},{6,7},{7,5},{5,3},{3,1},{1,0},{8,10},{10,12},{12... | collective-permute-start | bytes 1671176 | tf_op jit(solution)/shard_map/ppermute | solution.py:433
  359.7 39.1 %collective-permute-start.57 = (bf16[2048,1024]{1,0:T(8,128)(2,1)}, bf16[2048,1024]{1,0:T(8,128)(2,1)}, u32[]{:S(2)}, u32[]{:S(2)}) collective-permute-start(bf16[2048,1024]{1,0:T(8,128)(2,1)} %weight_far.3), channel_id=1, source_target_pairs={{0,8},{8,0},{16,24},{24,16},{1,9},{9,1},{17,25},{25,17},{2,10},{10... | collective-permute-start | bytes 12582920 | tf_op jit(solution)/shard_map/ppermute | solution.py:1665
  359.7 16.0 %collective-permute-start.54 = (bf16[128,2304]{1,0:T(8,128)(2,1)}, bf16[128,2304]{1,0:T(8,128)(2,1)S(1)}, u32[]{:S(2)}, u32[]{:S(2)}) collective-permute-start(bf16[128,2304]{1,0:T(8,128)(2,1)} %get-tuple-element.293), channel_id=1, source_target_pairs={{0,1},{2,0},{4,2},{6,4},{7,6},{5,7},{3,5},{1,3},{8,9},{10,8},{12,1... | collective-permute-start | bytes 1769480 | tf_op jit(solution)/shard_map/ppermute | solution.py:436
  375.6 36.8 %collective-permute-start.60 = (bf16[2048,1024]{1,0:T(8,128)(2,1)}, bf16[2048,1024]{1,0:T(8,128)(2,1)}, u32[]{:S(2)}, u32[]{:S(2)}) collective-permute-start(bf16[2048,1024]{1,0:T(8,128)(2,1)} %weight_far.4), channel_id=1, source_target_pairs={{0,8},{8,0},{16,24},{24,16},{1,9},{9,1},{17,25},{25,17},{2,10},{10... | collective-permute-start | bytes 12582920 | tf_op jit(solution)/shard_map/ppermute | solution.py:1665
  379.2 15.2 %collective-permute-start.55 = (bf16[128,2304]{1,0:T(8,128)(2,1)}, bf16[128,2304]{1,0:T(8,128)(2,1)S(1)}, u32[]{:S(2)}, u32[]{:S(2)}) collective-permute-start(bf16[128,2304]{1,0:T(8,128)(2,1)} %get-tuple-element.297), channel_id=1, source_target_pairs={{0,2},{2,4},{4,6},{6,7},{7,5},{5,3},{3,1},{1,0},{8,10},{10,12},{12... | collective-permute-start | bytes 1769480 | tf_op jit(solution)/shard_map/ppermute | solution.py:433
  380.3 14.9 %collective-permute-start.56 = (bf16[128,2304]{1,0:T(8,128)(2,1)}, bf16[128,2304]{1,0:T(8,128)(2,1)S(1)}, u32[]{:S(2)}, u32[]{:S(2)}) collective-permute-start(bf16[128,2304]{1,0:T(8,128)(2,1)} %get-tuple-element.298), channel_id=1, source_target_pairs={{0,1},{2,0},{4,2},{6,4},{7,6},{5,7},{3,5},{1,3},{8,9},{10,8},{12,1... | collective-permute-start | bytes 1769480 | tf_op jit(solution)/shard_map/ppermute | solution.py:436
  398.8 14.2 %collective-permute-start.58 = (bf16[128,2304]{1,0:T(8,128)(2,1)}, bf16[128,2304]{1,0:T(8,128)(2,1)S(1)}, u32[]{:S(2)}, u32[]{:S(2)}) collective-permute-start(bf16[128,2304]{1,0:T(8,128)(2,1)} %get-tuple-element.305), channel_id=1, source_target_pairs={{0,2},{2,4},{4,6},{6,7},{7,5},{5,3},{3,1},{1,0},{8,10},{10,12},{12... | collective-permute-start | bytes 1769480 | tf_op jit(solution)/shard_map/ppermute | solution.py:433
  400.4 13.7 %collective-permute-start.59 = (bf16[128,2304]{1,0:T(8,128)(2,1)}, bf16[128,2304]{1,0:T(8,128)(2,1)S(1)}, u32[]{:S(2)}, u32[]{:S(2)}) collective-permute-start(bf16[128,2304]{1,0:T(8,128)(2,1)} %get-tuple-element.306), channel_id=1, source_target_pairs={{0,1},{2,0},{4,2},{6,4},{7,6},{5,7},{3,5},{1,3},{8,9},{10,8},{12,1... | collective-permute-start | bytes 1769480 | tf_op jit(solution)/shard_map/ppermute | solution.py:436
  419.7 197.9 %reduce-scatter.8.cloned.1.call-start = ((), (), s32[]{:S(2)}) async-start(), calls=%async_computation.10 | async-start | bytes 6291456 | tf_op jit(solution)/shard_map/reduce_scatter | solution.py:1672
  419.7 15.8 %collective-permute-start.63 = (bf16[2048,1024]{1,0:T(8,128)(2,1)}, bf16[2048,1024]{1,0:T(8,128)(2,1)}, u32[]{:S(2)}, u32[]{:S(2)}) collective-permute-start(bf16[2048,1024]{1,0:T(8,128)(2,1)} %weight_far.5), channel_id=1, source_target_pairs={{0,8},{8,0},{16,24},{24,16},{1,9},{9,1},{17,25},{25,17},{2,10},{10... | collective-permute-start | bytes 12582920 | tf_op jit(solution)/shard_map/ppermute | solution.py:1665
  420.7 14.3 %collective-permute-start.61 = (bf16[128,2048]{1,0:T(8,128)(2,1)S(1)}, bf16[128,2048]{1,0:T(8,128)(2,1)S(1)}, u32[]{:S(2)}, u32[]{:S(2)}) collective-permute-start(bf16[128,2048]{1,0:T(8,128)(2,1)S(1)} %copy-done.12), channel_id=1, source_target_pairs={{0,2},{2,4},{4,6},{6,7},{7,5},{5,3},{3,1},{1,0},{8,10},{10,12},{12... | collective-permute-start | bytes 1572872 | tf_op jit(solution)/shard_map/ppermute | solution.py:433
  435.5 13.9 %collective-permute-start.64 = (bf16[128,2048]{1,0:T(8,128)(2,1)S(1)}, bf16[128,2048]{1,0:T(8,128)(2,1)S(1)}, u32[]{:S(2)}, u32[]{:S(2)}) collective-permute-start(bf16[128,2048]{1,0:T(8,128)(2,1)S(1)} %collective-permute-done.61.refs_24_), channel_id=1, source_target_pairs={{0,2},{2,4},{4,6},{6,7},{7,5},{5,3},{3,1},{1,0},{8,10},{10,12},{12... | collective-permute-start | bytes 1572872 | tf_op jit(solution)/shard_map/ppermute | solution.py:433
  449.4 17.4 %collective-permute-start.70 = (bf16[128,2048]{1,0:T(8,128)(2,1)S(1)}, bf16[128,2048]{1,0:T(8,128)(2,1)S(1)}, u32[]{:S(2)}, u32[]{:S(2)}) collective-permute-start(bf16[128,2048]{1,0:T(8,128)(2,1)S(1)} %collective-permute-done.64.refs_23_), channel_id=1, source_target_pairs={{0,2},{2,4},{4,6},{6,7},{7,5},{5,3},{3,1},{1,0},{8,10},{10,12},{12... | collective-permute-start | bytes 1572872 | tf_op jit(solution)/shard_map/ppermute | solution.py:433
  450.9 15.9 %collective-permute-start.71 = (bf16[128,2048]{1,0:T(8,128)(2,1)S(1)}, bf16[128,2048]{1,0:T(8,128)(2,1)S(1)}, u32[]{:S(2)}, u32[]{:S(2)}) collective-permute-start(bf16[128,2048]{1,0:T(8,128)(2,1)S(1)} %collective-permute-done.65.refs_18_), channel_id=1, source_target_pairs={{0,1},{2,0},{4,2},{6,4},{7,6},{5,7},{3,5},{1,3},{8,9},{10,8},{12,1... | collective-permute-start | bytes 1572872 | tf_op jit(solution)/shard_map/ppermute | solution.py:436
  474.8 146.7 %reduce-scatter.6.cloned.1.call-start = ((), (), s32[]{:S(2)}) async-start(), calls=%async_computation.9 | async-start | bytes 6291456 | tf_op jit(solution)/shard_map/reduce_scatter | solution.py:1672
  486.2 14.3 %collective-permute-start.68 = (bf16[128,2048]{1,0:T(8,128)(2,1)}, bf16[128,2048]{1,0:T(8,128)(2,1)S(1)}, u32[]{:S(2)}, u32[]{:S(2)}) collective-permute-start(bf16[128,2048]{1,0:T(8,128)(2,1)} %get-tuple-element.332), channel_id=1, source_target_pairs={{0,2},{2,4},{4,6},{6,7},{7,5},{5,3},{3,1},{1,0},{8,10},{10,12},{12... | collective-permute-start | bytes 1572872 | tf_op jit(solution)/shard_map/ppermute | solution.py:433
  486.3 14.2 %collective-permute-start.69 = (bf16[128,2048]{1,0:T(8,128)(2,1)}, bf16[128,2048]{1,0:T(8,128)(2,1)S(1)}, u32[]{:S(2)}, u32[]{:S(2)}) collective-permute-start(bf16[128,2048]{1,0:T(8,128)(2,1)} %get-tuple-element.333), channel_id=1, source_target_pairs={{0,1},{2,0},{4,2},{6,4},{7,6},{5,7},{3,5},{1,3},{8,9},{10,8},{12,1... | collective-permute-start | bytes 1572872 | tf_op jit(solution)/shard_map/ppermute | solution.py:436
  504.1 14.7 %collective-permute-start.74 = (bf16[128,2048]{1,0:T(8,128)(2,1)}, bf16[128,2048]{1,0:T(8,128)(2,1)S(1)}, u32[]{:S(2)}, u32[]{:S(2)}) collective-permute-start(bf16[128,2048]{1,0:T(8,128)(2,1)} %get-tuple-element.349), channel_id=1, source_target_pairs={{0,2},{2,4},{4,6},{6,7},{7,5},{5,3},{3,1},{1,0},{8,10},{10,12},{12... | collective-permute-start | bytes 1572872 | tf_op jit(solution)/shard_map/ppermute | solution.py:433
  504.3 14.5 %collective-permute-start.75 = (bf16[128,2048]{1,0:T(8,128)(2,1)}, bf16[128,2048]{1,0:T(8,128)(2,1)S(1)}, u32[]{:S(2)}, u32[]{:S(2)}) collective-permute-start(bf16[128,2048]{1,0:T(8,128)(2,1)} %get-tuple-element.350), channel_id=1, source_target_pairs={{0,1},{2,0},{4,2},{6,4},{7,6},{5,7},{3,5},{1,3},{8,9},{10,8},{12,1... | collective-permute-start | bytes 1572872 | tf_op jit(solution)/shard_map/ppermute | solution.py:436
  532.8 21.4 %collective-permute-start.82 = (bf16[64,2048]{1,0:T(8,128)(2,1)}, bf16[64,2048]{1,0:T(8,128)(2,1)S(1)}, u32[]{:S(2)}, u32[]{:S(2)}) collective-permute-start(bf16[64,2048]{1,0:T(8,128)(2,1)} %fusion.6), channel_id=1, source_target_pairs={{0,16},{8,24},{16,0},{24,8},{1,17},{9,25},{17,1},{25,9},{2,18},{10... | collective-permute-start | bytes 786440 | tf_op jit(solution)/shard_map/ppermute | solution.py:561
  537.8 17.2 %collective-permute-start.79 = (bf16[128,2048]{1,0:T(8,128)(2,1)}, bf16[128,2048]{1,0:T(8,128)(2,1)S(1)}, u32[]{:S(2)}, u32[]{:S(2)}) collective-permute-start(bf16[128,2048]{1,0:T(8,128)(2,1)} %get-tuple-element.361), channel_id=1, source_target_pairs={{0,2},{2,4},{4,6},{6,7},{7,5},{5,3},{3,1},{1,0},{8,10},{10,12},{12... | collective-permute-start | bytes 1572872 | tf_op jit(solution)/shard_map/ppermute | solution.py:433
  538.2 16.8 %collective-permute-start.80 = (bf16[128,2048]{1,0:T(8,128)(2,1)}, bf16[128,2048]{1,0:T(8,128)(2,1)}, u32[]{:S(2)}, u32[]{:S(2)}) collective-permute-start(bf16[128,2048]{1,0:T(8,128)(2,1)} %get-tuple-element.362), channel_id=1, source_target_pairs={{0,1},{2,0},{4,2},{6,4},{7,6},{5,7},{3,5},{1,3},{8,9},{10,8},{12,1... | collective-permute-start | bytes 1572872 | tf_op jit(solution)/shard_map/ppermute | solution.py:436
  555.0 14.8 %collective-permute-start.83 = (bf16[64,2048]{1,0:T(8,128)(2,1)}, bf16[64,2048]{1,0:T(8,128)(2,1)S(1)}, u32[]{:S(2)}, u32[]{:S(2)}) collective-permute-start(bf16[64,2048]{1,0:T(8,128)(2,1)} %get-tuple-element.386), channel_id=1, source_target_pairs={{0,2},{2,4},{4,6},{6,7},{7,5},{5,3},{3,1},{1,0},{8,10},{10,12},{12... | collective-permute-start | bytes 786440 | tf_op jit(solution)/shard_map/ppermute | solution.py:433
  555.4 14.4 %collective-permute-start.84 = (bf16[64,2048]{1,0:T(8,128)(2,1)}, bf16[64,2048]{1,0:T(8,128)(2,1)S(1)}, u32[]{:S(2)}, u32[]{:S(2)}) collective-permute-start(bf16[64,2048]{1,0:T(8,128)(2,1)} %get-tuple-element.387), channel_id=1, source_target_pairs={{0,1},{2,0},{4,2},{6,4},{7,6},{5,7},{3,5},{1,3},{8,9},{10,8},{12,1... | collective-permute-start | bytes 786440 | tf_op jit(solution)/shard_map/ppermute | solution.py:436
  576.2 28.4 %collective-permute-start.90 = (bf16[512,896]{1,0:T(8,128)(2,1)S(1)}, bf16[512,896]{1,0:T(8,128)(2,1)}, u32[]{:S(2)}, u32[]{:S(2)}) collective-permute-start(bf16[512,896]{1,0:T(8,128)(2,1)S(1)} %fusion.5), channel_id=1, source_target_pairs={{0,16},{8,24},{16,0},{24,8},{1,17},{9,25},{17,1},{25,9},{2,18},{10... | collective-permute-start | bytes 2752520 | tf_op jit(solution)/shard_map/ppermute | solution.py:561
  578.7 14.2 %collective-permute-start.85 = (bf16[128,2048]{1,0:T(8,128)(2,1)}, bf16[128,2048]{1,0:T(8,128)(2,1)S(1)}, u32[]{:S(2)}, u32[]{:S(2)}) collective-permute-start(bf16[128,2048]{1,0:T(8,128)(2,1)} %get-tuple-element.405), channel_id=1, source_target_pairs={{0,2},{2,4},{4,6},{6,7},{7,5},{5,3},{3,1},{1,0},{8,10},{10,12},{12... | collective-permute-start | bytes 1572872 | tf_op jit(solution)/shard_map/ppermute | solution.py:433
  579.2 14.0 %collective-permute-start.86 = (bf16[128,2048]{1,0:T(8,128)(2,1)}, bf16[128,2048]{1,0:T(8,128)(2,1)}, u32[]{:S(2)}, u32[]{:S(2)}) collective-permute-start(bf16[128,2048]{1,0:T(8,128)(2,1)} %get-tuple-element.406), channel_id=1, source_target_pairs={{0,1},{2,0},{4,2},{6,4},{7,6},{5,7},{3,5},{1,3},{8,9},{10,8},{12,1... | collective-permute-start | bytes 1572872 | tf_op jit(solution)/shard_map/ppermute | solution.py:436
  596.2 13.5 %collective-permute-start.87 = (bf16[128,2048]{1,0:T(8,128)(2,1)}, bf16[128,2048]{1,0:T(8,128)(2,1)}, u32[]{:S(2)}, u32[]{:S(2)}) collective-permute-start(bf16[128,2048]{1,0:T(8,128)(2,1)} %get-tuple-element.410), channel_id=1, source_target_pairs={{0,2},{2,4},{4,6},{6,7},{7,5},{5,3},{3,1},{1,0},{8,10},{10,12},{12... | collective-permute-start | bytes 1572872 | tf_op jit(solution)/shard_map/ppermute | solution.py:433
  610.0 33.3 %all-to-all-start.1 = ((bf16[8,64,896]{2,1,0:T(8,128)(2,1)}), bf16[8,64,896]{2,1,0:T(8,128)(2,1)S(1)}, u32[]{:S(2)}, u32[]{:S(2)}) async-start(bf16[8,64,896]{2,1,0:T(8,128)(2,1)} %bitcast.27), calls=%async_computation.4 | async-start | bytes 1835008 | tf_op jit(solution)/shard_map/all_to_all | solution.py:1757
  613.7 19.3 %collective-permute-start.93 = (bf16[64,2048]{1,0:T(8,128)(2,1)}, bf16[64,2048]{1,0:T(8,128)(2,1)}, u32[]{:S(2)}, u32[]{:S(2)}) collective-permute-start(bf16[64,2048]{1,0:T(8,128)(2,1)} %fusion.8), channel_id=1, source_target_pairs={{0,0},{8,1},{16,2},{24,3},{1,4},{9,5},{17,6},{25,7},{2,8},{10,9},{... | collective-permute-start | bytes 786440 | tf_op jit(solution)/shard_map/ppermute | solution.py:1764
  628.1 19.4 %collective-permute-start.91 = (bf16[128,2048]{1,0:T(8,128)(2,1)}, bf16[128,2048]{1,0:T(8,128)(2,1)S(1)}, u32[]{:S(2)}, u32[]{:S(2)}) collective-permute-start(bf16[128,2048]{1,0:T(8,128)(2,1)} %get-tuple-element.418), channel_id=1, source_target_pairs={{0,2},{2,4},{4,6},{6,7},{7,5},{5,3},{3,1},{1,0},{8,10},{10,12},{12... | collective-permute-start | bytes 1572872 | tf_op jit(solution)/shard_map/ppermute | solution.py:433
  628.4 29.3 %collective-permute-start.92 = (bf16[128,2048]{1,0:T(8,128)(2,1)}, bf16[128,2048]{1,0:T(8,128)(2,1)S(1)}, u32[]{:S(2)}, u32[]{:S(2)}) collective-permute-start(bf16[128,2048]{1,0:T(8,128)(2,1)} %get-tuple-element.419), channel_id=1, source_target_pairs={{0,1},{2,0},{4,2},{6,4},{7,6},{5,7},{3,5},{1,3},{8,9},{10,8},{12,1... | collective-permute-start | bytes 1572872 | tf_op jit(solution)/shard_map/ppermute | solution.py:436
  (121 other events, 1467.1 us)
Sparse Core Ops, SparseCore 0:
  9.6 68.0 all-gather.3
  79.2 71.1 all-gather.5
  151.9 58.8 all-gather.7
  419.8 52.3 reduce-scatter.3
  474.9 53.8 reduce-scatter.7
  530.9 60.8 reduce-scatter.5

commit v4 on v3

--- a/solution.py
+++ b/solution.py
@@ -496,6 +496,7 @@
             upper, lower = pieces[self.left], pieces[-self.left]
             upper, lower = add_pair(upper, rising, lower, falling)
         upper, lower = after((upper, lower), ties)
+        self.sent = (upper, lower)
         self.arrived = (ring.forward(upper), ring.backward(lower))
         self.left -= 1
         return self.arrived
@@ -1025,11 +1026,13 @@
 
 def weight_copies(groups, scalars, buffers, sems, step, parts):
     expert, part, place = step // parts, step % parts, step % 2
-    wide = buffers.shape[3]
+    wide = buffers.shape[2] // len(groups)
     columns = pl.ds(expert_column(scalars, part, parts, wide), wide)
     return [
         pltpu.make_async_copy(
-            group.at[expert, :, columns], buffers.at[place, g], sems.at[place, g]
+            group.at[expert, :, columns],
+            buffers.at[place, :, pl.ds(g * wide, wide)],
+            sems.at[place, g],
         )
         for g, group in enumerate(groups)
     ]
@@ -1151,10 +1154,16 @@
     )(*sums, cotangent, resid, factor, block, gates, probs, mask, total, gain, router)
 
 
+def turn_columns(rows_all, result):
+    wide = result.shape[0]
+    columns = pl.ds(pl.multiple_of(pl.program_id(0) * wide, wide), wide)
+    result[...] = rows_all[:, columns].T
+
+
 def expert_first_kernel(pieces, parts, chunk, scalars, *refs):
     n = len(pieces)
     blocks, down = refs[:n], refs[n]
-    product, kept, rows_all, buffers, sems, w_sems, k_sem = refs[n + 1 :]
+    product, turned_rows, rows_all, buffers, sems, w_sems = refs[n + 1 :]
     step = pl.program_id(0)
 
     @pl.when(step == 0)
@@ -1169,15 +1178,11 @@
     def _():
         for copy in piece_copies(pieces, scalars, blocks, rows_all, sems):
             copy.wait()
-        pltpu.make_async_copy(rows_all, kept, k_sem).start()
 
     for begin in range(0, rows_all.shape[0], chunk):
         rows = pl.ds(begin, chunk)
-        product[rows, :] = dot(rows_all[rows, :], weight[0])
-
-    @pl.when(step == pl.num_programs(0) - 1)
-    def _():
-        pltpu.make_async_copy(rows_all, kept, k_sem).wait()
+        product[rows, :] = dot(rows_all[rows, :], weight[...])
+    turn_columns(rows_all, turned_rows)
 
 
 def expert_first(ring, scalars, blocks, down):
@@ -1194,19 +1199,18 @@
             in_specs=[anywhere] * (n + 1),
             out_specs=[
                 pl.BlockSpec((None, span, step_hidden), lambda i, s: (i // parts, 0, i % parts)),
-                anywhere,
+                pl.BlockSpec((width // (experts * parts), span), lambda i, s: (i, 0)),
             ],
             scratch_shapes=[
                 pltpu.VMEM((span, width), jnp.bfloat16),
-                pltpu.VMEM((2, 1, width, step_hidden), jnp.bfloat16),
+                pltpu.VMEM((2, width, step_hidden), jnp.bfloat16),
                 pltpu.SemaphoreType.DMA((n,)),
                 pltpu.SemaphoreType.DMA((2, 1)),
-                pltpu.SemaphoreType.DMA,
             ],
         ),
         out_shape=[
             jax.ShapeDtypeStruct((experts, span, parts * step_hidden), jnp.float32),
-            jax.ShapeDtypeStruct((span, width), jnp.bfloat16),
+            jax.ShapeDtypeStruct((width, span), jnp.bfloat16),
         ],
         name="expert_first",
     )(scalars, *blocks, down)
@@ -1216,8 +1220,8 @@
     n = len(pieces)
     blocks, gate, up = refs[:n], refs[n], refs[n + 1]
     product = refs[n + 2]
-    act, gated, d_gate, d_up, grad_gates, gates, kept = refs[n + 3 : n + 10]
-    rows_all, gates_all, buffers, sems, g_sems, w_sems, k_sem = refs[n + 10 :]
+    act, gated, d_gate, d_up, grad_gates, gates, turned_rows = refs[n + 3 : n + 10]
+    rows_all, gates_all, buffers, sems, g_sems, w_sems = refs[n + 10 :]
     step = pl.program_id(0)
     experts = gates.shape[0]
     g_copies = piece_copies(pieces, scalars, blocks, gates_all, g_sems, rows_all.shape[1])
@@ -1233,7 +1237,6 @@
     def _():
         for copy in piece_copies(pieces, scalars, blocks, rows_all, sems) + g_copies:
             copy.wait()
-        pltpu.make_async_copy(rows_all, kept, k_sem).start()
         values = gates_all[...].astype(jnp.float32)
         column = lax.broadcasted_iota(jnp.int32, values.shape, 1) % gate_columns
         for expert in range(experts):
@@ -1248,11 +1251,11 @@
 
     for begin in range(0, rows_all.shape[0], chunk):
         rows = pl.ds(begin, chunk)
-        gate_hid = dot(rows_all[rows, :], weight[0])
-        up_hid = dot(rows_all[rows, :], weight[1])
+        both = dot(rows_all[rows, :], weight[...])
+        gate_hid, up_hid = both[:, : act.shape[1]], both[:, act.shape[1] :]
         own_gate = gates[step // parts, rows, :]
         back = product[rows, :]
-        sig = 1.0 / (1.0 + jnp.exp(-gate_hid))
+        sig = 0.5 + 0.5 * jnp.tanh(0.5 * gate_hid)
         silu = gate_hid * sig
         act_low = (silu * up_hid).astype(jnp.bfloat16)
         act_now = act_low.astype(jnp.float32)
@@ -1265,9 +1268,7 @@
         )
         d_up[rows, :] = (grad_act * silu).astype(jnp.bfloat16)
 
-    @pl.when(step == pl.num_programs(0) - 1)
-    def _():
-        pltpu.make_async_copy(rows_all, kept, k_sem).wait()
+    turn_columns(rows_all, turned_rows)
 
 
 def hidden_place(parts, experts):
@@ -1292,15 +1293,16 @@
             num_scalar_prefetch=1,
             grid=(experts * parts,),
             in_specs=[anywhere] * (n + 2) + [relative],
-            out_specs=[placed] * 4 + [column, whole_block((experts, span, 1)), anywhere],
+            out_specs=[placed] * 4
+            + [column, whole_block((experts, span, 1))]
+            + [pl.BlockSpec((width // (experts * parts), span), lambda i, s: (i, 0))],
             scratch_shapes=[
                 pltpu.VMEM((span, width), jnp.bfloat16),
                 pltpu.VMEM((span, 2 * gate_columns), jnp.bfloat16),
-                pltpu.VMEM((2, 2, width, step_hidden), jnp.bfloat16),
+                pltpu.VMEM((2, width, 2 * step_hidden), jnp.bfloat16),
                 pltpu.SemaphoreType.DMA((n,)),
                 pltpu.SemaphoreType.DMA((n,)),
                 pltpu.SemaphoreType.DMA((2, 2)),
-                pltpu.SemaphoreType.DMA,
             ],
         ),
         out_shape=[
@@ -1310,7 +1312,7 @@
             hidden,
             jax.ShapeDtypeStruct((experts, span, 1), jnp.float32),
             jax.ShapeDtypeStruct((experts, span, 1), jnp.float32),
-            jax.ShapeDtypeStruct((span, width), jnp.bfloat16),
+            jax.ShapeDtypeStruct((width, span), jnp.bfloat16),
         ],
         name="expert_hidden",
     )(scalars, *blocks, gate, up, product)
@@ -1443,18 +1445,18 @@
 
 
 def weight_far_kernel(left, right, result):
-    result[...] = dot(left[...], right[...], rows_first).astype(jnp.bfloat16)
+    result[...] = dot(left[...], right[...]).astype(jnp.bfloat16)
 
 
 def weight_far(left, right):
-    span, width = left.shape
+    width, span = left.shape
     split = right.shape[1] // 2
-    wide = min(256, width)
+    wide = min(512, width)
     return pl.pallas_call(
         weight_far_kernel,
         grid=(width // wide,),
         in_specs=[
-            pl.BlockSpec((span, wide), lambda i: (0, i)),
+            pl.BlockSpec((wide, span), lambda i: (i, 0)),
             pl.BlockSpec((span, split), lambda i: (0, 0), pipeline_mode=pl.Buffered(1)),
         ],
         out_specs=pl.BlockSpec((wide, split), lambda i: (i, 0)),
@@ -1464,7 +1466,7 @@
 
 
 def weight_near_kernel(scalars, left, right, arrived, result):
-    total = dot(left[...], right[...], rows_first) + arrived[...].astype(jnp.float32)
+    total = dot(left[...], right[...]) + arrived[...].astype(jnp.float32)
     experts, step_hidden = result.shape[0] // 2, result.shape[2]
     own = scalars[len(scalars) - 1] // 2
     for expert in range(experts):
@@ -1476,17 +1478,17 @@
 
 
 def weight_near(scalars, left, right, arrived, experts):
-    span, width = left.shape
+    width, span = left.shape
     split = right.shape[1] // 2
     step_hidden = split // (2 * experts)
-    wide = min(256, width)
+    wide = min(512, width)
     return pl.pallas_call(
         weight_near_kernel,
         grid_spec=pltpu.PrefetchScalarGridSpec(
             num_scalar_prefetch=1,
             grid=(width // wide,),
             in_specs=[
-                pl.BlockSpec((span, wide), lambda i, s: (0, i)),
+                pl.BlockSpec((wide, span), lambda i, s: (i, 0)),
                 pl.BlockSpec((span, split), lambda i, s: (0, 1), pipeline_mode=pl.Buffered(1)),
                 pl.BlockSpec((wide, split), lambda i, s: (i, 0)),
             ],
@@ -1597,14 +1599,9 @@
     small = pair_gather(small, dp_axes, dp_size)
 
     token_ring, small_ring = ring.gather(tokens), ring.gather(small, False)
-    token_steps, small_steps = [token_ring.step()], [small_ring.step()]
-    out_rows = lax.ppermute(after(w_output, token_steps[0]), dp_flat, to_rows)
-    for k in range(1, half):
-        ties = {1: packed, half - 1: (token_steps[-1], out_rows)}.get(k, token_steps[-1])
-        small_steps.append(small_ring.step(ties))
-        token_steps.append(token_ring.step(ties))
-    token_blocks = token_ring.blocks()
-    w_in = share_relative(packed, dp_size, None, token_steps[2])
+    token_steps = [token_ring.step()]
+    for k in range(half):
+        small_ring.step(token_steps[0] if k > 1 else None)
     small = small_ring.stacked().transpose(2, 1, 0, 3).reshape(-1, width)
     router = jnp.pad(small[:num_experts], ((0, 2 * gate_columns - num_experts), (0, 0)))
     gains = small[num_experts:].astype(f32)
@@ -1617,6 +1614,14 @@
     cosine, sine = jnp.cos(angles), jnp.sin(angles)
     cosine = jnp.concatenate([cosine, cosine], axis=1)
     sine = jnp.concatenate([-sine, sine], axis=1)
+    out_rows = lax.ppermute(after(w_output, token_steps[0]), dp_flat, to_rows)
+    token_steps.append(token_ring.step(packed))
+    token_steps.append(token_ring.step())
+    token_steps.append(
+        token_ring.step((out_rows, router, gain_in, gain_q, gain_k, gain_mid, cosine, sine))
+    )
+    token_blocks = token_ring.blocks()
+    w_in = share_relative(packed, dp_size, None, token_steps[2])
     w_out = share_relative(out_rows, dp_size, token_steps[2], token_steps[3])
 
     down_w = lax.all_gather(expert_down, dp_axes, axis=2, tiled=True)
@@ -1677,25 +1682,25 @@
     grad_steps.append(grad_ring.step(gate_far))
     gate_cross = cross(gate_far, grad_steps[0])
     up_far = far_part(mid_all, d_up, grad_steps[0])
-    grad_steps.append(grad_ring.step(up_far))
+    grad_steps.append(grad_ring.step((up_far, gate_cross)))
     up_cross = cross(up_far, grad_steps[1])
-    down_far = far_part(cot_all, act_gated, grad_steps[1])
-    grad_steps.append(grad_ring.step((down_far, gate_cross)))
-    down_cross = cross(down_far, grad_steps[2])
-    gate_near = near_part(mid_all, d_gate, gate_cross, grad_steps[2])
+    gate_near = near_part(mid_all, d_gate, gate_cross, grad_steps[1])
+    grad_steps.append(grad_ring.step((gate_near, up_cross)))
+    up_near = near_part(mid_all, d_up, up_cross, grad_steps[2])
     grad_resid, grad_low, grad_gain_mid, grad_router = middle_back(
-        after(grad_ring.last(), (gate_near, up_cross)), cotangent, resid_mid, mid_factor,
+        after(grad_ring.last(), up_near), cotangent, resid_mid, mid_factor,
         mid_block, *routing, gain_mid, router,
     )
 
     back_ring = ring.gather(grad_low)
     back_steps = [back_ring.step()]
-    up_near = near_part(mid_all, d_up, up_cross, grad_low)
-    back_steps.append(back_ring.step((up_near, down_cross)))
-    down_near = near_part(cot_all, act_gated, down_cross, back_steps[0])
+    down_far = far_part(cot_all, act_gated, grad_low)
+    back_steps.append(back_ring.step(down_far))
+    down_cross = cross(down_far, back_steps[0])
+    moe_pieces = expert_outputs(ring, after(scalars, back_steps[0]), act, own_gates, down_w)
+    back_steps.append(back_ring.step((moe_pieces[0], down_cross)))
+    down_near = near_part(cot_all, act_gated, down_cross, back_steps[1])
     back_steps.append(back_ring.step(down_near))
-    moe_pieces = expert_outputs(ring, after(scalars, back_steps[1]), act, own_gates, down_w)
-    back_steps.append(back_ring.step(moe_pieces[0]))
     grad_blocks = back_ring.blocks()
 
     def head_back(head, ties):
@@ -1705,7 +1710,7 @@
         )
 
     moe_ring = ring.reduce(moe_pieces)
-    moe_step = moe_ring.step()
+    moe_step = moe_ring.step(back_steps[3])
     backs = [head_back(0, (back_steps[3], moe_step))]
     moe_step = moe_ring.step()
     for head in range(1, own_heads):
@@ -1745,14 +1750,14 @@
     grad_w_in = weight_rows(
         scalars, after(normed, normed_pieces), grad_raw, jnp.concatenate(sums, axis=0), dp_size
     )
-    grad_gate_w = finish(gate_near, grad_low)
-    grad_up_w = finish(up_near, back_steps[3])
+    grad_gate_w = finish(gate_near, grad_ring.sent)
+    grad_up_w = finish(up_near, grad_low)
     grad_down_w = finish(down_near, back_steps[3])
     in_steps.append(in_ring.step(early=grad_w_in))
     grad_w_in = combine_relative(*grad_w_in, (in_steps[0], in_steps[0])).astype(low)
-    in_steps.append(in_ring.step(early=grad_gate_w))
-    in_steps.append(in_ring.step(early=(grad_w_in, grad_up_w, grad_down_w)))
-    grad_normed = in_ring.total()
+    in_steps.append(in_ring.step(early=(grad_gate_w, grad_up_w)))
+    in_steps.append(in_ring.step(early=grad_w_in))
+    grad_normed = in_ring.total(grad_down_w)
     grad_w_in = after(grad_w_in, in_steps[2]).reshape(size, own_rows, -1)
     grad_w_in = lax.all_to_all(grad_w_in, "fsdp", split_axis=0, concat_axis=0, tiled=True)
     sums = jnp.sum(grad_w_in[:, :, 3 * part :].astype(f32), axis=0)

time: 676 us -> 668 us (0.988)
  Pallas kernels: 273 us -> 265 us
    ppermute x35, waiting for transfers between devices: 67.7 us -> 57 us  [backward(): return lax.ppermute(values, 'fsdp', self.down)]
    ppermute x36, waiting for transfers between devices: 80.2 us -> 88.2 us  [forward(): return lax.ppermute(values, 'fsdp', self.up)]
    all_to_all x1, waiting for transfers between devices: 8.49 us -> 16.1 us  [per_device(): lax.all_to_all(grad_w_in, 'fsdp', split_axis=0, concat_axis=0, tiled=True)]
    unnamed x174 -> x186, local copies, waits for them, and re-layouts: 20.2 us -> 15.4 us
  transfers between devices with their start and end apart: 102 -> 102, of which waited for: 50 -> 55; matrix products, arithmetic and copies ran while one was open for 9% -> 8% of each run, Pallas kernels for 31% -> 31%
where the time goes in v4:
time: 668 us; the launch traced here: 658 us
  Pallas kernels  265 us (40%)
  waiting for transfers between devices  187 us (28%)
  starting transfers between devices  120 us (18%)
  other arithmetic  34.1 us (5%)
  local copies, waits for them, and re-layouts  32.9 us (5%)
  between operations  15.7 us (2%)
    ppermute x36, waiting for transfers between devices, forward(): return lax.ppermute(values, 'fsdp', self.up)  88.2 us
    ppermute x35, waiting for transfers between devices, backward(): return lax.ppermute(values, 'fsdp', self.down)  57 us
    ppermute x35, starting transfers between devices, backward(): return lax.ppermute(values, 'fsdp', self.down)  48.9 us
    ppermute x36, starting transfers between devices, forward(): return lax.ppermute(values, 'fsdp', self.up)  39.9 us
    pallas_call x1, Pallas kernels, expert_hidden(): pl.pallas_call(functools.partial(expert_hidden_kernel, ring.pieces, parts...  32.8 us
    pallas_call x12, Pallas kernels, add_pair(): pl.pallas_call(add_pair_kernel, out_shape=[shape, shape], name='add_pair')  30.7 us
    pallas_call x3, Pallas kernels, weight_near(): pl.pallas_call(weight_near_kernel, grid_spec=pltpu.PrefetchScalarGridSpec...  30.4 us
    pallas_call x1, Pallas kernels, expert_inputs(): pl.pallas_call(functools.partial(expert_inputs_kernel, ring.pieces, parts...  26.3 us
  transfers between devices with their start and end apart: 102, of which 55 were waited for; matrix products, arithmetic and copies ran while one was open for 8% of the time, Pallas kernels for 31%

profile of v4, /device:TPU:0, one launch (start us, length us, event | category | flops | bytes accessed | tf_op | source)
XLA Modules:
  0.0 658.4 jit_solution(17870066498923511469)
XLA Ops:
  9.5 3.0 collective-permute-start
  13.8 6.2 all-to-all-start
  31.5 2.5 collective-permute-done.9
  34.0 4.5 collective-permute-start.10
  38.5 5.1 collective-permute-start.12
  53.6 4.1 collective-permute-done.15
  57.7 5.1 collective-permute-start.2
  62.8 4.4 collective-permute-start.19
  67.8 7.3 %collective-permute-done.2.refs_2_ = bf16[128,2048]{1,0:T(8,128)(2,1)} collective-permute-done((bf16[128,2048]{1,0:T(8,128)(2,1)S(1)}, bf16[128,2048]{1,0:T(8,128)(2,1)}, u32[]{:S(2)}, u32[]{:S(2)}) %collective-permute-start.2) | collective-permute-done | bytes 524320 | tf_op jit(solution)/shard_map/ppermute | solution.py:436
  86.4 5.7 collective-permute-done.3.refs_3_
  95.6 5.5 collective-permute-done.16.refs_4_
  104.5 2.7 collective-permute-done.24.refs_10_.refs_14_
  109.0 13.3 %project.1 = (bf16[1024,2048]{1,0:T(8,128)(2,1)}, f32[1024,768]{1,0:T(8,128)}, f32[1024,1]{1,0:T(8,128)}, f32[8,1024]{1,0:T(8,128)}, bf16[1024,2048]{1,0:T(8,128)(2,1)}) custom-call(s32[9]{0:T(128)} %pad_add_fusion.scalars, bf16[128,2048]{1,0:T(8,128)(2,1)} %tokens.1, bf16[128,2048]{1,0:T(8,128)(2,1)} %copy-done.37, ...), custom_call_target="tpu_custom_call" | custom-call | tf_op jit(solution)/shard_map/project/pallas_call | solution.py:694
  122.5 4.1 collective-permute-done.26
  131.3 3.3 collective-permute-start.28
  139.6 18.7 %attend.1 = (bf16[1024,256]{1,0:T(8,128)(2,1)}, bf16[1024,256]{1,0:T(8,128)(2,1)}, bf16[1024,256]{1,0:T(8,128)(2,1)}, f32[1024,256]{1,0:T(8,128)}, f32[2,1024,1]...) custom-call(s32[9]{0:T(128)} %pad_add_fusion.scalars, ...), custom_call_target="tpu_custom_call" | custom-call | tf_op jit(solution)/shard_map/attend/pallas_call | solution.py:801
  160.5 4.6 collective-permute-done.31.rising
  173.9 11.0 %collective-permute-done.33.rising = bf16[128,2048]{1,0:T(8,128)(2,1)S(1)} collective-permute-done((bf16[128,2048]{1,0:T(8,128)(2,1)}, bf16[128,2048]{1,0:T(8,128)(2,1)S(1)}, u32[]{:S(2)}, u32[]{:S(2)}) %collective-permute-start.33) | collective-permute-done | bytes 524320 | tf_op jit(solution)/shard_map/ppermute | solution.py:433
  187.5 2.7 add_pair.13
  199.7 5.4 collective-permute-done.37.rising
  207.4 2.6 add_pair.14
  214.7 6.6 %collective-permute-done.41.rising = bf16[128,2048]{1,0:T(8,128)(2,1)S(1)} collective-permute-done((bf16[128,2048]{1,0:T(8,128)(2,1)}, bf16[128,2048]{1,0:T(8,128)(2,1)S(1)}, u32[]{:S(2)}, u32[]{:S(2)}) %collective-permute-start.41) | collective-permute-done | bytes 524320 | tf_op jit(solution)/shard_map/ppermute | solution.py:433
  223.5 3.5 middle.1
  229.1 13.6 %collective-permute-done.43.refs_1_ = bf16[128,2176]{1,0:T(8,128)(2,1)S(1)} collective-permute-done((bf16[128,2176]{1,0:T(8,128)(2,1)}, bf16[128,2176]{1,0:T(8,128)(2,1)S(1)}, u32[]{:S(2)}, u32[]{:S(2)}) %collective-permute-start.43) | collective-permute-done | bytes 557088 | tf_op jit(solution)/shard_map/ppermute | solution.py:436
  244.8 16.2 %expert_first.1 = (f32[2,1024,1024]{2,1,0:T(8,128)}, bf16[2048,1024]{1,0:T(8,128)(2,1)}) custom-call(s32[9]{0:T(128)} %pad_add_fusion.scalars, bf16[128,2048]{1,0:T(8,128)(2,1)} %cotangent.1, bf16[128,2048]{1,0:T(8,128)(2,1)} %collective-permute-done.22.refs_1_, bf16[128,2048]{1,0:T(8,128)(2,1)} %copy-done.39, bf16[128,2048]{1,0:T(8,128)(2,1)} %copy-done.23, ...), custom_call_target="tpu_custom_call" | custom-call | tf_op jit(solution)/shard_map/expert_first/pallas_call | solution.py:1194
  263.2 7.5 %collective-permute-done.48.refs_6_ = bf16[128,2176]{1,0:T(8,128)(2,1)S(1)} collective-permute-done((bf16[128,2176]{1,0:T(8,128)(2,1)S(1)}, bf16[128,2176]{1,0:T(8,128)(2,1)S(1)}, u32[]{:S(2)}, u32[]{:S(2)}) %collective-permute-start.48) | collective-permute-done | bytes 557088 | tf_op jit(solution)/shard_map/ppermute | solution.py:433
  273.1 4.3 collective-permute-done.49.refs_4_
  279.4 32.8 %expert_hidden.1 = (bf16[1024,2048]{1,0:T(8,128)(2,1)}, bf16[1024,2048]{1,0:T(8,128)(2,1)}, bf16[1024,2048]{1,0:T(8,128)(2,1)}, bf16[1024,2048]{1,0:T(8,128)(2,1...) custom-call(s32[9]{0:T(128)} %pad_add_fusion.scalars, ...), custom_call_target="tpu_custom_call" | custom-call | tf_op jit(solution)/shard_map/expert_hidden/pallas_call | solution.py:1290
  312.2 26.3 %expert_inputs.1 = (bf16[128,2304]{1,0:T(8,128)(2,1)}, bf16[128,2304]{1,0:T(8,128)(2,1)}, bf16[128,2304]{1,0:T(8,128)(2,1)}, bf16[128,2304]{1,0:T(8,128)(2,1)}, ...) custom-call(s32[9]{0:T(128)} %pad_add_fusion.scalars, ...), custom_call_target="tpu_custom_call" | custom-call | tf_op jit(solution)/shard_map/expert_inputs/pallas_call | solution.py:1381
  340.5 8.4 %weight_far.3 = bf16[2048,1024]{1,0:T(8,128)(2,1)} custom-call(bf16[2048,1024]{1,0:T(8,128)(2,1)} %get-tuple-element.302.left, bf16[1024,2048]{1,0:T(8,128)(2,1)} %get-tuple-element.272.refs_0_.right), custom_call_target="tpu_custom_call" | custom-call | tf_op jit(solution)/shard_map/weight_far/pallas_call | solution.py:1455
  354.3 8.3 %weight_far.4 = bf16[2048,1024]{1,0:T(8,128)(2,1)} custom-call(bf16[2048,1024]{1,0:T(8,128)(2,1)} %get-tuple-element.302.left, bf16[1024,2048]{1,0:T(8,128)(2,1)} %get-tuple-element.273.refs_1_.right), custom_call_target="tpu_custom_call" | custom-call | tf_op jit(solution)/shard_map/weight_far/pallas_call | solution.py:1455
  362.6 4.8 collective-permute-done.53.rising
  368.5 2.7 add_pair.16
  373.3 9.9 %weight_near.3 = bf16[4,2048,256]{2,1,0:T(8,128)(2,1)} custom-call(s32[9]{0:T(128)} %pad_add_fusion.scalars, bf16[2048,1024]{1,0:T(8,128)(2,1)} %get-tuple-element.302.left, bf16[1024,2048]{1,0:T(8,128)(2,1)} %get-tuple-element.272.refs_0_.right, bf16[2048,1024]{1,0:T(8,128)(2,1)} %collective-permute-done.55.arrived), custom_call_target="tpu_custom_call" | custom-call | tf_op jit(solution)/shard_map/weight_near/pallas_call | solution.py:1485
  383.2 3.2 collective-permute-done.56.rising
  388.1 2.7 add_pair.17
  393.9 10.5 %weight_near.4 = bf16[4,2048,256]{2,1,0:T(8,128)(2,1)} custom-call(s32[9]{0:T(128)} %pad_add_fusion.scalars, bf16[2048,1024]{1,0:T(8,128)(2,1)} %get-tuple-element.302.left, bf16[1024,2048]{1,0:T(8,128)(2,1)} %get-tuple-element.273.refs_1_.right, bf16[2048,1024]{1,0:T(8,128)(2,1)} %collective-permute-done.58.arrived), custom_call_target="tpu_custom_call" | custom-call | tf_op jit(solution)/shard_map/weight_near/pallas_call | solution.py:1485
  407.0 4.7 middle_back.1
  414.9 8.6 %weight_far.5 = bf16[2048,1024]{1,0:T(8,128)(2,1)} custom-call(bf16[2048,1024]{1,0:T(8,128)(2,1)} %get-tuple-element.329.left, bf16[1024,2048]{1,0:T(8,128)(2,1)} %get-tuple-element.323.right), custom_call_target="tpu_custom_call" | custom-call | tf_op jit(solution)/shard_map/weight_far/pallas_call | solution.py:1455
  427.1 15.3 %expert_outputs.1 = (bf16[128,2048]{1,0:T(8,128)(2,1)}, bf16[128,2048]{1,0:T(8,128)(2,1)}, bf16[128,2048]{1,0:T(8,128)(2,1)}, bf16[128,2048]{1,0:T(8,128)(2,1)},...) custom-call(s32[9]{0:T(128)} %pad_add_fusion.scalars, ...), custom_call_target="tpu_custom_call" | custom-call | tf_op jit(solution)/shard_map/expert_outputs/pallas_call | solution.py:1427
  444.5 10.0 %weight_near.5 = bf16[4,2048,256]{2,1,0:T(8,128)(2,1)} custom-call(s32[9]{0:T(128)} %pad_add_fusion.scalars, bf16[2048,1024]{1,0:T(8,128)(2,1)} %get-tuple-element.329.left, bf16[1024,2048]{1,0:T(8,128)(2,1)} %get-tuple-element.323.right, bf16[2048,1024]{1,0:T(8,128)(2,1)} %collective-permute-done.65.arrived), custom_call_target="tpu_custom_call" | custom-call | tf_op jit(solution)/shard_map/weight_near/pallas_call | solution.py:1485
  459.1 5.0 collective-permute-done.68.refs_20_
  467.6 4.3 collective-permute-done.70.rising
  478.7 12.1 %attend_back.2 = (f32[1024,128]{1,0:T(8,128)}, f32[1024,128]{1,0:T(8,128)}, bf16[1024,128]{1,0:T(8,128)(2,1)}, f32[8,1024]{1,0:T(8,128)}, f32[1,128]{1,0:T(1,128...) custom-call(s32[9]{0:T(128)} %pad_add_fusion.scalars, bf16[1024,256]{1,0:T(8,128)(2,1)} %get-tuple-element.338.refs_0_, ...), custom_call_target="tpu_custom_call" | custom-call | tf_op jit(solution)/shard_map/attend_back/pallas_call | solution.py:899
  491.8 2.5 add_pair.19
  496.6 11.7 %attend_back.3 = (f32[1024,128]{1,0:T(8,128)}, f32[1024,128]{1,0:T(8,128)}, bf16[1024,128]{1,0:T(8,128)(2,1)}, f32[8,1024]{1,0:T(8,128)}, f32[1,128]{1,0:T(1,128)}, /*index=5*/f32[1,128]{1,0:T(1,128)}) custom-call(s32[9]{0:T(128)} %pad_add_fusion.scalars, bf16[1024,256]{1,0:T(8,128)(2,1)} %get-tuple-element.338.refs_0_, ...), custom_call_target="tpu_custom_call" | custom-call | tf_op jit(solution)/shard_map/attend_back/pallas_call | solution.py:899
  510.7 3.5 fusion.9
  514.8 3.6 collective-permute-done.76
  519.3 2.5 add_pair.20
  529.8 14.2 %project_back.1 = (bf16[1024,768]{1,0:T(8,128)(2,1)}, f32[1,2048]{1,0:T(1,128)}, bf16[128,2048]{1,0:T(8,128)(2,1)}, bf16[128,2048]{1,0:T(8,128)(2,1)}, bf16[128,...) custom-call(s32[9]{0:T(128)} %pad_add_fusion.scalars, ...), custom_call_target="tpu_custom_call" | custom-call | tf_op jit(solution)/shard_map/project_back/pallas_call | solution.py:990
  549.9 9.7 %weight_rows.1 = (bf16[2,512,896]{2,1,0:T(8,128)(2,1)}, f32[2,512,896]{2,1,0:T(8,128)}) custom-call(s32[9]{0:T(128)} %pad_add_fusion.scalars, bf16[1024,2048]{1,0:T(8,128)(2,1)} %get-tuple-element.390.left, bf16[1024,768]{1,0:T(8,128)(2,1)} %get-tuple-element.391.right, f32[24,2048]{1,0:T(8,128)} %concatenate.95.sums), custom_call_target="tpu_custom_call" | custom-call | tf_op jit(solution)/shard_map/weight_rows/pallas_call | solution.py:1527
  559.7 4.0 collective-permute-done.89
  563.7 2.6 fusion.5
  571.0 3.9 convert_element_type.146
  574.9 3.9 convert_element_type.147
  578.9 4.0 collective-permute-done.85.rising
  589.1 3.0 fusion
  592.1 8.2 %collective-permute-done.87.rising = bf16[128,2048]{1,0:T(8,128)(2,1)} collective-permute-done((bf16[128,2048]{1,0:T(8,128)(2,1)}, bf16[128,2048]{1,0:T(8,128)(2,1)}, u32[]{:S(2)}, u32[]{:S(2)}) %collective-permute-start.87) | collective-permute-done | bytes 524320 | tf_op jit(solution)/shard_map/ppermute | solution.py:433
  601.1 3.9 all-to-all-start.1
  605.0 3.8 collective-permute-start.93
  608.9 2.6 add_pair.23
  618.2 16.1 %all-to-all-done.1 = bf16[8,64,896]{2,1,0:T(8,128)(2,1)S(1)} async-done(((bf16[8,64,896]{2,1,0:T(8,128)(2,1)}), bf16[8,64,896]{2,1,0:T(8,128)(2,1)S(1)}, u32[]{:S(2)}, u32[]{:S(2)}) %all-to-all-start.1) | async-done | bytes 917536 | tf_op jit(solution)/shard_map/all_to_all | solution.py:1762
  638.5 4.0 convert_element_type.154
  642.5 6.5 collective-permute-done.92
  (441 shorter events, 185.1 us)
Async XLA Ops:
  7.3 237.5 %all-gather.4.cloned.1.call-start = ((), (), s32[]{:S(2)}) async-start(), calls=%async_computation.5 | async-start | bytes 10485760 | tf_op jit(solution)/shard_map/all_gather | solution.py:1627
  8.0 265.0 %all-gather.6.cloned.1.call-start = ((), (), s32[]{:S(2)}) async-start(), calls=%async_computation.6 | async-start | bytes 10485760 | tf_op jit(solution)/shard_map/all_gather | solution.py:1628
  8.8 264.3 %all-gather.8.cloned.1.call-start = ((), (), s32[]{:S(2)}) async-start(), calls=%async_computation.7 | async-start | bytes 10485760 | tf_op jit(solution)/shard_map/all_gather | solution.py:1629
  9.5 36.5 %collective-permute-start = (bf16[128,2048]{1,0:T(8,128)(2,1)S(1)}, bf16[128,2048]{1,0:T(8,128)(2,1)S(1)}, u32[]{:S(2)}, u32[]{:S(2)}) collective-permute-start(bf16[128,2048]{1,0:T(8,128)(2,1)S(1)} %copy-done.2), channel_id=1, source_target_pairs={{0,1},{2,0},{4,2},{6,4},{7,6},{5,7},{3,5},{1,3},{8,9},{10,8},{12,1... | collective-permute-start | bytes 1572872 | tf_op jit(solution)/shard_map/ppermute | solution.py:436
  12.5 33.5 %collective-permute-start.1 = (bf16[128,2048]{1,0:T(8,128)(2,1)S(1)}, bf16[128,2048]{1,0:T(8,128)(2,1)}, u32[]{:S(2)}, u32[]{:S(2)}) collective-permute-start(bf16[128,2048]{1,0:T(8,128)(2,1)S(1)} %copy-done.2), channel_id=1, source_target_pairs={{0,2},{2,4},{4,6},{6,7},{7,5},{5,3},{3,1},{1,0},{8,10},{10,12},{12... | collective-permute-start | bytes 1572872 | tf_op jit(solution)/shard_map/ppermute | solution.py:433
  12.7 12.6 %collective-permute-start.7 = (bf16[1,20,64]{2,1,0:T(8,128)(2,1)S(1)}, bf16[1,20,64]{2,1,0:T(8,128)(2,1)S(1)}, u32[]{:S(2)}, u32[]{:S(2)}) collective-permute-start(bf16[1,20,64]{2,1,0:T(8,128)(2,1)S(1)} %bitcast.102), channel_id=1, source_target_pairs={{0,8},{8,0},{16,24},{24,16},{1,9},{9,1},{17,25},{25,17},{2,10},{10... | collective-permute-start | bytes 7688 | tf_op jit(solution)/shard_map/ppermute | solution.py:535
  13.8 43.8 %all-to-all-start = ((bf16[8,64,768]{2,1,0:T(8,128)(2,1)}), bf16[8,64,768]{2,1,0:T(8,128)(2,1)S(1)}, u32[]{:S(2)}, u32[]{:S(2)}) async-start(bf16[8,64,768]{2,1,0:T(8,128)(2,1)} %maximum_bitcast_fusion), calls=%async_computation | async-start | bytes 1572864 | tf_op jit(solution)/shard_map/all_to_all | solution.py:1593
  20.1 550.9 %reduce-scatter.4.cloned.1.call-start = ((), (), s32[]{:S(2)}) async-start(), calls=%async_computation.8 | async-start | bytes 6291456 | tf_op jit(solution)/shard_map/reduce_scatter | solution.py:1677
  48.6 37.8 %collective-permute-start.6 = (bf16[64,2048]{1,0:T(8,128)(2,1)}, bf16[64,2048]{1,0:T(8,128)(2,1)S(1)}, u32[]{:S(2)}, u32[]{:S(2)}) collective-permute-start(bf16[64,2048]{1,0:T(8,128)(2,1)} %param.24), channel_id=1, source_target_pairs={{0,0},{1,8},{2,16},{3,24},{4,1},{5,9},{6,17},{7,25},{8,2},{9,10},{... | collective-permute-start | bytes 786440 | tf_op jit(solution)/shard_map/ppermute | solution.py:1617
  57.7 17.4 %collective-permute-start.2 = (bf16[128,2048]{1,0:T(8,128)(2,1)S(1)}, bf16[128,2048]{1,0:T(8,128)(2,1)}, u32[]{:S(2)}, u32[]{:S(2)}) collective-permute-start(bf16[128,2048]{1,0:T(8,128)(2,1)S(1)} %collective-permute-done.refs_1_), channel_id=1, source_target_pairs={{0,1},{2,0},{4,2},{6,4},{7,6},{5,7},{3,5},{1,3},{8,9},{10,8},{12,1... | collective-permute-start | bytes 1572872 | tf_op jit(solution)/shard_map/ppermute | solution.py:436
  62.7 14.7 %collective-permute-start.4 = (bf16[128,2048]{1,0:T(8,128)(2,1)}, bf16[128,2048]{1,0:T(8,128)(2,1)}, u32[]{:S(2)}, u32[]{:S(2)}) collective-permute-start(bf16[128,2048]{1,0:T(8,128)(2,1)} %collective-permute-done.1.refs_8_), channel_id=1, source_target_pairs={{0,2},{2,4},{4,6},{6,7},{7,5},{5,3},{3,1},{1,0},{8,10},{10,12},{12... | collective-permute-start | bytes 1572872 | tf_op jit(solution)/shard_map/ppermute | solution.py:433
  62.8 32.7 %collective-permute-start.19 = (bf16[512,768]{1,0:T(8,128)(2,1)S(1)}, bf16[512,768]{1,0:T(8,128)(2,1)S(1)}, u32[]{:S(2)}, u32[]{:S(2)}) collective-permute-start(bf16[512,768]{1,0:T(8,128)(2,1)S(1)} %bitcast.88), channel_id=1, source_target_pairs={{0,16},{8,24},{16,0},{24,8},{1,17},{9,25},{17,1},{25,9},{2,18},{10... | collective-permute-start | bytes 2359304 | tf_op jit(solution)/shard_map/ppermute | solution.py:553
  75.0 17.1 %collective-permute-start.3 = (bf16[128,2048]{1,0:T(8,128)(2,1)}, bf16[128,2048]{1,0:T(8,128)(2,1)S(1)}, u32[]{:S(2)}, u32[]{:S(2)}) collective-permute-start(bf16[128,2048]{1,0:T(8,128)(2,1)} %collective-permute-done.2.refs_2_), channel_id=1, source_target_pairs={{0,1},{2,0},{4,2},{6,4},{7,6},{5,7},{3,5},{1,3},{8,9},{10,8},{12,1... | collective-permute-start | bytes 1572872 | tf_op jit(solution)/shard_map/ppermute | solution.py:436
  77.4 14.8 %collective-permute-start.5 = (bf16[128,2048]{1,0:T(8,128)(2,1)}, bf16[128,2048]{1,0:T(8,128)(2,1)}, u32[]{:S(2)}, u32[]{:S(2)}) collective-permute-start(bf16[128,2048]{1,0:T(8,128)(2,1)} %collective-permute-done.4.refs_7_), channel_id=1, source_target_pairs={{0,2},{2,4},{4,6},{6,7},{7,5},{5,3},{3,1},{1,0},{8,10},{10,12},{12... | collective-permute-start | bytes 1572872 | tf_op jit(solution)/shard_map/ppermute | solution.py:433
  79.8 27.4 %collective-permute-start.18 = (bf16[512,768]{1,0:T(8,128)(2,1)S(1)}, bf16[512,768]{1,0:T(8,128)(2,1)S(1)}, u32[]{:S(2)}, u32[]{:S(2)}) collective-permute-start(bf16[512,768]{1,0:T(8,128)(2,1)S(1)} %bitcast.89), channel_id=1, source_target_pairs={{0,8},{8,0},{16,24},{24,16},{1,9},{9,1},{17,25},{25,17},{2,10},{10... | collective-permute-start | bytes 2359304 | tf_op jit(solution)/shard_map/ppermute | solution.py:553
  95.4 13.5 %collective-permute-start.20 = (bf16[512,768]{1,0:T(8,128)(2,1)S(1)}, bf16[512,768]{1,0:T(8,128)(2,1)}, u32[]{:S(2)}, u32[]{:S(2)}) collective-permute-start(bf16[512,768]{1,0:T(8,128)(2,1)S(1)} %collective-permute-done.19.refs_11_.refs_15_), channel_id=1, source_target_pairs={{0,8},{8,0},{16,24},{24,16},{1,9},{9,1},{17,25},{25,17},{2,10},{10... | collective-permute-start | bytes 2359304 | tf_op jit(solution)/shard_map/ppermute | solution.py:553
  102.4 20.0 %collective-permute-start.21 = (bf16[128,2048]{1,0:T(8,128)(2,1)}, bf16[128,2048]{1,0:T(8,128)(2,1)}, u32[]{:S(2)}, u32[]{:S(2)}) collective-permute-start(bf16[128,2048]{1,0:T(8,128)(2,1)} %cotangent.1), channel_id=1, source_target_pairs={{0,2},{2,4},{4,6},{6,7},{7,5},{5,3},{3,1},{1,0},{8,10},{10,12},{12... | collective-permute-start | bytes 1572872 | tf_op jit(solution)/shard_map/ppermute | solution.py:433
  103.7 18.7 %collective-permute-start.22 = (bf16[128,2048]{1,0:T(8,128)(2,1)}, bf16[128,2048]{1,0:T(8,128)(2,1)}, u32[]{:S(2)}, u32[]{:S(2)}) collective-permute-start(bf16[128,2048]{1,0:T(8,128)(2,1)} %cotangent.1), channel_id=1, source_target_pairs={{0,1},{2,0},{4,2},{6,4},{7,6},{5,7},{3,5},{1,3},{8,9},{10,8},{12,1... | collective-permute-start | bytes 1572872 | tf_op jit(solution)/shard_map/ppermute | solution.py:436
  107.2 15.2 %collective-permute-start.23 = (bf16[64,2048]{1,0:T(8,128)(2,1)S(1)}, bf16[64,2048]{1,0:T(8,128)(2,1)S(1)}, u32[]{:S(2)}, u32[]{:S(2)}) collective-permute-start(bf16[64,2048]{1,0:T(8,128)(2,1)S(1)} %collective-permute-done.6.refs_8_.refs_12_), channel_id=1, source_target_pairs={{0,8},{8,0},{16,24},{24,16},{1,9},{9,1},{17,25},{25,17},{2,10},{10... | collective-permute-start | bytes 786440 | tf_op jit(solution)/shard_map/ppermute | solution.py:553
  107.2 15.2 %collective-permute-start.25 = (bf16[64,2048]{1,0:T(8,128)(2,1)S(1)}, bf16[64,2048]{1,0:T(8,128)(2,1)}, u32[]{:S(2)}, u32[]{:S(2)}) collective-permute-start(bf16[64,2048]{1,0:T(8,128)(2,1)S(1)} %collective-permute-done.24.refs_10_.refs_14_), channel_id=1, source_target_pairs={{0,8},{8,0},{16,24},{24,16},{1,9},{9,1},{17,25},{25,17},{2,10},{10... | collective-permute-start | bytes 786440 | tf_op jit(solution)/shard_map/ppermute | solution.py:553
  137.1 21.2 %collective-permute-start.29 = (bf16[128,2048]{1,0:T(8,128)(2,1)}, bf16[128,2048]{1,0:T(8,128)(2,1)S(1)}, u32[]{:S(2)}, u32[]{:S(2)}) collective-permute-start(bf16[128,2048]{1,0:T(8,128)(2,1)} %collective-permute-done.21.refs_8_), channel_id=1, source_target_pairs={{0,2},{2,4},{4,6},{6,7},{7,5},{5,3},{3,1},{1,0},{8,10},{10,12},{12... | collective-permute-start | bytes 1572872 | tf_op jit(solution)/shard_map/ppermute | solution.py:433
  138.8 19.6 %collective-permute-start.30 = (bf16[128,2048]{1,0:T(8,128)(2,1)}, bf16[128,2048]{1,0:T(8,128)(2,1)S(1)}, u32[]{:S(2)}, u32[]{:S(2)}) collective-permute-start(bf16[128,2048]{1,0:T(8,128)(2,1)} %collective-permute-done.22.refs_1_), channel_id=1, source_target_pairs={{0,1},{2,0},{4,2},{6,4},{7,6},{5,7},{3,5},{1,3},{8,9},{10,8},{12,1... | collective-permute-start | bytes 1572872 | tf_op jit(solution)/shard_map/ppermute | solution.py:436
  169.9 15.1 %collective-permute-start.33 = (bf16[128,2048]{1,0:T(8,128)(2,1)}, bf16[128,2048]{1,0:T(8,128)(2,1)S(1)}, u32[]{:S(2)}, u32[]{:S(2)}) collective-permute-start(bf16[128,2048]{1,0:T(8,128)(2,1)} %get-tuple-element.252), channel_id=1, source_target_pairs={{0,2},{2,4},{4,6},{6,7},{7,5},{5,3},{3,1},{1,0},{8,10},{10,12},{12... | collective-permute-start | bytes 1572872 | tf_op jit(solution)/shard_map/ppermute | solution.py:433
  171.7 15.1 %collective-permute-start.34 = (bf16[128,2048]{1,0:T(8,128)(2,1)}, bf16[128,2048]{1,0:T(8,128)(2,1)S(1)}, u32[]{:S(2)}, u32[]{:S(2)}) collective-permute-start(bf16[128,2048]{1,0:T(8,128)(2,1)} %get-tuple-element.254), channel_id=1, source_target_pairs={{0,1},{2,0},{4,2},{6,4},{7,6},{5,7},{3,5},{1,3},{8,9},{10,8},{12,1... | collective-permute-start | bytes 1572872 | tf_op jit(solution)/shard_map/ppermute | solution.py:436
  171.9 20.2 %collective-permute-start.35 = (bf16[128,2048]{1,0:T(8,128)(2,1)S(1)}, bf16[128,2048]{1,0:T(8,128)(2,1)S(1)}, u32[]{:S(2)}, u32[]{:S(2)}) collective-permute-start(bf16[128,2048]{1,0:T(8,128)(2,1)S(1)} %collective-permute-done.29.refs_7_), channel_id=1, source_target_pairs={{0,2},{2,4},{4,6},{6,7},{7,5},{5,3},{3,1},{1,0},{8,10},{10,12},{12... | collective-permute-start | bytes 1572872 | tf_op jit(solution)/shard_map/ppermute | solution.py:433
  173.7 20.5 %collective-permute-start.36 = (bf16[128,2048]{1,0:T(8,128)(2,1)S(1)}, bf16[128,2048]{1,0:T(8,128)(2,1)S(1)}, u32[]{:S(2)}, u32[]{:S(2)}) collective-permute-start(bf16[128,2048]{1,0:T(8,128)(2,1)S(1)} %collective-permute-done.30.refs_2_), channel_id=1, source_target_pairs={{0,1},{2,0},{4,2},{6,4},{7,6},{5,7},{3,5},{1,3},{8,9},{10,8},{12,1... | collective-permute-start | bytes 1572872 | tf_op jit(solution)/shard_map/ppermute | solution.py:436
  197.0 13.0 %collective-permute-start.39 = (bf16[64,2048]{1,0:T(8,128)(2,1)}, bf16[64,2048]{1,0:T(8,128)(2,1)S(1)}, u32[]{:S(2)}, u32[]{:S(2)}) collective-permute-start(bf16[64,2048]{1,0:T(8,128)(2,1)} %slice.151), channel_id=1, source_target_pairs={{0,2},{2,4},{4,6},{6,7},{7,5},{5,3},{3,1},{1,0},{8,10},{10,12},{12... | collective-permute-start | bytes 786440 | tf_op jit(solution)/shard_map/ppermute | solution.py:433
  198.7 13.2 %collective-permute-start.40 = (bf16[64,2048]{1,0:T(8,128)(2,1)}, bf16[64,2048]{1,0:T(8,128)(2,1)}, u32[]{:S(2)}, u32[]{:S(2)}) collective-permute-start(bf16[64,2048]{1,0:T(8,128)(2,1)} %slice.152), channel_id=1, source_target_pairs={{0,1},{2,0},{4,2},{6,4},{7,6},{5,7},{3,5},{1,3},{8,9},{10,8},{12,1... | collective-permute-start | bytes 786440 | tf_op jit(solution)/shard_map/ppermute | solution.py:436
  227.1 15.7 %collective-permute-start.43 = (bf16[128,2176]{1,0:T(8,128)(2,1)}, bf16[128,2176]{1,0:T(8,128)(2,1)S(1)}, u32[]{:S(2)}, u32[]{:S(2)}) collective-permute-start(bf16[128,2176]{1,0:T(8,128)(2,1)} %get-tuple-element.267.refs_0_.block), channel_id=1, source_target_pairs={{0,1},{2,0},{4,2},{6,4},{7,6},{5,7},{3,5},{1,3},{8,9},{10,8},{12,1... | collective-permute-start | bytes 1671176 | tf_op jit(solution)/shard_map/ppermute | solution.py:436
  228.7 15.0 %collective-permute-start.45 = (bf16[128,2176]{1,0:T(8,128)(2,1)}, bf16[128,2176]{1,0:T(8,128)(2,1)S(1)}, u32[]{:S(2)}, u32[]{:S(2)}) collective-permute-start(bf16[128,2176]{1,0:T(8,128)(2,1)} %get-tuple-element.267.refs_0_.block), channel_id=1, source_target_pairs={{0,2},{2,4},{4,6},{6,7},{7,5},{5,3},{3,1},{1,0},{8,10},{10,12},{12... | collective-permute-start | bytes 1671176 | tf_op jit(solution)/shard_map/ppermute | solution.py:433
  242.7 18.3 %collective-permute-start.44 = (bf16[128,2176]{1,0:T(8,128)(2,1)S(1)}, bf16[128,2176]{1,0:T(8,128)(2,1)S(1)}, u32[]{:S(2)}, u32[]{:S(2)}) collective-permute-start(bf16[128,2176]{1,0:T(8,128)(2,1)S(1)} %collective-permute-done.43.refs_1_), channel_id=1, source_target_pairs={{0,1},{2,0},{4,2},{6,4},{7,6},{5,7},{3,5},{1,3},{8,9},{10,8},{12,1... | collective-permute-start | bytes 1671176 | tf_op jit(solution)/shard_map/ppermute | solution.py:436
  243.7 17.4 %collective-permute-start.46 = (bf16[128,2176]{1,0:T(8,128)(2,1)S(1)}, bf16[128,2176]{1,0:T(8,128)(2,1)S(1)}, u32[]{:S(2)}, u32[]{:S(2)}) collective-permute-start(bf16[128,2176]{1,0:T(8,128)(2,1)S(1)} %collective-permute-done.45.refs_8_), channel_id=1, source_target_pairs={{0,2},{2,4},{4,6},{6,7},{7,5},{5,3},{3,1},{1,0},{8,10},{10,12},{12... | collective-permute-start | bytes 1671176 | tf_op jit(solution)/shard_map/ppermute | solution.py:433
  348.9 22.3 %collective-permute-start.55 = (bf16[2048,1024]{1,0:T(8,128)(2,1)}, bf16[2048,1024]{1,0:T(8,128)(2,1)}, u32[]{:S(2)}, u32[]{:S(2)}) collective-permute-start(bf16[2048,1024]{1,0:T(8,128)(2,1)} %weight_far.3), channel_id=1, source_target_pairs={{0,8},{8,0},{16,24},{24,16},{1,9},{9,1},{17,25},{25,17},{2,10},{10... | collective-permute-start | bytes 12582920 | tf_op jit(solution)/shard_map/ppermute | solution.py:1670
  352.3 15.2 %collective-permute-start.53 = (bf16[128,2304]{1,0:T(8,128)(2,1)}, bf16[128,2304]{1,0:T(8,128)(2,1)S(1)}, u32[]{:S(2)}, u32[]{:S(2)}) collective-permute-start(bf16[128,2304]{1,0:T(8,128)(2,1)} %get-tuple-element.288), channel_id=1, source_target_pairs={{0,2},{2,4},{4,6},{6,7},{7,5},{5,3},{3,1},{1,0},{8,10},{10,12},{12... | collective-permute-start | bytes 1769480 | tf_op jit(solution)/shard_map/ppermute | solution.py:433
  352.8 14.9 %collective-permute-start.54 = (bf16[128,2304]{1,0:T(8,128)(2,1)}, bf16[128,2304]{1,0:T(8,128)(2,1)S(1)}, u32[]{:S(2)}, u32[]{:S(2)}) collective-permute-start(bf16[128,2304]{1,0:T(8,128)(2,1)} %get-tuple-element.289), channel_id=1, source_target_pairs={{0,1},{2,0},{4,2},{6,4},{7,6},{5,7},{3,5},{1,3},{8,9},{10,8},{12,1... | collective-permute-start | bytes 1769480 | tf_op jit(solution)/shard_map/ppermute | solution.py:436
  367.7 23.1 %collective-permute-start.58 = (bf16[2048,1024]{1,0:T(8,128)(2,1)}, bf16[2048,1024]{1,0:T(8,128)(2,1)}, u32[]{:S(2)}, u32[]{:S(2)}) collective-permute-start(bf16[2048,1024]{1,0:T(8,128)(2,1)} %weight_far.4), channel_id=1, source_target_pairs={{0,8},{8,0},{16,24},{24,16},{1,9},{9,1},{17,25},{25,17},{2,10},{10... | collective-permute-start | bytes 12582920 | tf_op jit(solution)/shard_map/ppermute | solution.py:1670
  371.3 15.1 %collective-permute-start.56 = (bf16[128,2304]{1,0:T(8,128)(2,1)}, bf16[128,2304]{1,0:T(8,128)(2,1)S(1)}, u32[]{:S(2)}, u32[]{:S(2)}) collective-permute-start(bf16[128,2304]{1,0:T(8,128)(2,1)} %get-tuple-element.294), channel_id=1, source_target_pairs={{0,2},{2,4},{4,6},{6,7},{7,5},{5,3},{3,1},{1,0},{8,10},{10,12},{12... | collective-permute-start | bytes 1769480 | tf_op jit(solution)/shard_map/ppermute | solution.py:433
  371.8 14.8 %collective-permute-start.57 = (bf16[128,2304]{1,0:T(8,128)(2,1)}, bf16[128,2304]{1,0:T(8,128)(2,1)S(1)}, u32[]{:S(2)}, u32[]{:S(2)}) collective-permute-start(bf16[128,2304]{1,0:T(8,128)(2,1)} %get-tuple-element.295), channel_id=1, source_target_pairs={{0,1},{2,0},{4,2},{6,4},{7,6},{5,7},{3,5},{1,3},{8,9},{10,8},{12,1... | collective-permute-start | bytes 1769480 | tf_op jit(solution)/shard_map/ppermute | solution.py:436
  390.9 184.0 %reduce-scatter.6.cloned.1.call-start = ((), (), s32[]{:S(2)}) async-start(), calls=%async_computation.9 | async-start | bytes 6291456 | tf_op jit(solution)/shard_map/reduce_scatter | solution.py:1677
  391.9 14.0 %collective-permute-start.59 = (bf16[128,2304]{1,0:T(8,128)(2,1)S(1)}, bf16[128,2304]{1,0:T(8,128)(2,1)S(1)}, u32[]{:S(2)}, u32[]{:S(2)}) collective-permute-start(bf16[128,2304]{1,0:T(8,128)(2,1)S(1)} %copy-done.85), channel_id=1, source_target_pairs={{0,2},{2,4},{4,6},{6,7},{7,5},{5,3},{3,1},{1,0},{8,10},{10,12},{12... | collective-permute-start | bytes 1769480 | tf_op jit(solution)/shard_map/ppermute | solution.py:433
  392.4 13.8 %collective-permute-start.60 = (bf16[128,2304]{1,0:T(8,128)(2,1)S(1)}, bf16[128,2304]{1,0:T(8,128)(2,1)S(1)}, u32[]{:S(2)}, u32[]{:S(2)}) collective-permute-start(bf16[128,2304]{1,0:T(8,128)(2,1)S(1)} %copy-done.84), channel_id=1, source_target_pairs={{0,1},{2,0},{4,2},{6,4},{7,6},{5,7},{3,5},{1,3},{8,9},{10,8},{12,1... | collective-permute-start | bytes 1769480 | tf_op jit(solution)/shard_map/ppermute | solution.py:436
  411.7 226.8 %reduce-scatter.8.cloned.1.call-start = ((), (), s32[]{:S(2)}) async-start(), calls=%async_computation.10 | async-start | bytes 6291456 | tf_op jit(solution)/shard_map/reduce_scatter | solution.py:1677
  425.0 17.4 %collective-permute-start.65 = (bf16[2048,1024]{1,0:T(8,128)(2,1)}, bf16[2048,1024]{1,0:T(8,128)(2,1)}, u32[]{:S(2)}, u32[]{:S(2)}) collective-permute-start(bf16[2048,1024]{1,0:T(8,128)(2,1)} %weight_far.5), channel_id=1, source_target_pairs={{0,8},{8,0},{16,24},{24,16},{1,9},{9,1},{17,25},{25,17},{2,10},{10... | collective-permute-start | bytes 12582920 | tf_op jit(solution)/shard_map/ppermute | solution.py:1670
  425.0 17.3 %collective-permute-start.63 = (bf16[128,2048]{1,0:T(8,128)(2,1)S(1)}, bf16[128,2048]{1,0:T(8,128)(2,1)S(1)}, u32[]{:S(2)}, u32[]{:S(2)}) collective-permute-start(bf16[128,2048]{1,0:T(8,128)(2,1)S(1)} %collective-permute-done.61.refs_24_), channel_id=1, source_target_pairs={{0,2},{2,4},{4,6},{6,7},{7,5},{5,3},{3,1},{1,0},{8,10},{10,12},{12... | collective-permute-start | bytes 1572872 | tf_op jit(solution)/shard_map/ppermute | solution.py:433
  425.9 16.4 %collective-permute-start.64 = (bf16[128,2048]{1,0:T(8,128)(2,1)S(1)}, bf16[128,2048]{1,0:T(8,128)(2,1)S(1)}, u32[]{:S(2)}, u32[]{:S(2)}) collective-permute-start(bf16[128,2048]{1,0:T(8,128)(2,1)S(1)} %collective-permute-done.62.refs_17_), channel_id=1, source_target_pairs={{0,1},{2,0},{4,2},{6,4},{7,6},{5,7},{3,5},{1,3},{8,9},{10,8},{12,1... | collective-permute-start | bytes 1572872 | tf_op jit(solution)/shard_map/ppermute | solution.py:436
  442.4 13.8 %collective-permute-start.66 = (bf16[128,2048]{1,0:T(8,128)(2,1)S(1)}, bf16[128,2048]{1,0:T(8,128)(2,1)S(1)}, u32[]{:S(2)}, u32[]{:S(2)}) collective-permute-start(bf16[128,2048]{1,0:T(8,128)(2,1)S(1)} %collective-permute-done.63.refs_23_), channel_id=1, source_target_pairs={{0,2},{2,4},{4,6},{6,7},{7,5},{5,3},{3,1},{1,0},{8,10},{10,12},{12... | collective-permute-start | bytes 1572872 | tf_op jit(solution)/shard_map/ppermute | solution.py:433
  443.4 13.5 %collective-permute-start.67 = (bf16[128,2048]{1,0:T(8,128)(2,1)S(1)}, bf16[128,2048]{1,0:T(8,128)(2,1)S(1)}, u32[]{:S(2)}, u32[]{:S(2)}) collective-permute-start(bf16[128,2048]{1,0:T(8,128)(2,1)S(1)} %collective-permute-done.64.refs_18_), channel_id=1, source_target_pairs={{0,1},{2,0},{4,2},{6,4},{7,6},{5,7},{3,5},{1,3},{8,9},{10,8},{12,1... | collective-permute-start | bytes 1572872 | tf_op jit(solution)/shard_map/ppermute | solution.py:436
  476.7 14.1 %collective-permute-start.72 = (bf16[128,2048]{1,0:T(8,128)(2,1)}, bf16[128,2048]{1,0:T(8,128)(2,1)S(1)}, u32[]{:S(2)}, u32[]{:S(2)}) collective-permute-start(bf16[128,2048]{1,0:T(8,128)(2,1)} %get-tuple-element.335), channel_id=1, source_target_pairs={{0,2},{2,4},{4,6},{6,7},{7,5},{5,3},{3,1},{1,0},{8,10},{10,12},{12... | collective-permute-start | bytes 1572872 | tf_op jit(solution)/shard_map/ppermute | solution.py:433
  477.6 13.2 %collective-permute-start.73 = (bf16[128,2048]{1,0:T(8,128)(2,1)}, bf16[128,2048]{1,0:T(8,128)(2,1)S(1)}, u32[]{:S(2)}, u32[]{:S(2)}) collective-permute-start(bf16[128,2048]{1,0:T(8,128)(2,1)} %get-tuple-element.336), channel_id=1, source_target_pairs={{0,1},{2,0},{4,2},{6,4},{7,6},{5,7},{3,5},{1,3},{8,9},{10,8},{12,1... | collective-permute-start | bytes 1572872 | tf_op jit(solution)/shard_map/ppermute | solution.py:436
  494.3 14.8 %collective-permute-start.74 = (bf16[128,2048]{1,0:T(8,128)(2,1)}, bf16[128,2048]{1,0:T(8,128)(2,1)S(1)}, u32[]{:S(2)}, u32[]{:S(2)}) collective-permute-start(bf16[128,2048]{1,0:T(8,128)(2,1)} %get-tuple-element.347), channel_id=1, source_target_pairs={{0,2},{2,4},{4,6},{6,7},{7,5},{5,3},{3,1},{1,0},{8,10},{10,12},{12... | collective-permute-start | bytes 1572872 | tf_op jit(solution)/shard_map/ppermute | solution.py:433
  495.2 13.9 %collective-permute-start.75 = (bf16[128,2048]{1,0:T(8,128)(2,1)}, bf16[128,2048]{1,0:T(8,128)(2,1)S(1)}, u32[]{:S(2)}, u32[]{:S(2)}) collective-permute-start(bf16[128,2048]{1,0:T(8,128)(2,1)} %get-tuple-element.348), channel_id=1, source_target_pairs={{0,1},{2,0},{4,2},{6,4},{7,6},{5,7},{3,5},{1,3},{8,9},{10,8},{12,1... | collective-permute-start | bytes 1572872 | tf_op jit(solution)/shard_map/ppermute | solution.py:436
  524.5 19.4 %collective-permute-start.82 = (bf16[64,2048]{1,0:T(8,128)(2,1)}, bf16[64,2048]{1,0:T(8,128)(2,1)S(1)}, u32[]{:S(2)}, u32[]{:S(2)}) collective-permute-start(bf16[64,2048]{1,0:T(8,128)(2,1)} %fusion.6), channel_id=1, source_target_pairs={{0,16},{8,24},{16,0},{24,8},{1,17},{9,25},{17,1},{25,9},{2,18},{10... | collective-permute-start | bytes 786440 | tf_op jit(solution)/shard_map/ppermute | solution.py:562
  527.7 17.0 %collective-permute-start.79 = (bf16[128,2048]{1,0:T(8,128)(2,1)}, bf16[128,2048]{1,0:T(8,128)(2,1)S(1)}, u32[]{:S(2)}, u32[]{:S(2)}) collective-permute-start(bf16[128,2048]{1,0:T(8,128)(2,1)} %get-tuple-element.359), channel_id=1, source_target_pairs={{0,2},{2,4},{4,6},{6,7},{7,5},{5,3},{3,1},{1,0},{8,10},{10,12},{12... | collective-permute-start | bytes 1572872 | tf_op jit(solution)/shard_map/ppermute | solution.py:433
  528.6 16.1 %collective-permute-start.80 = (bf16[128,2048]{1,0:T(8,128)(2,1)}, bf16[128,2048]{1,0:T(8,128)(2,1)}, u32[]{:S(2)}, u32[]{:S(2)}) collective-permute-start(bf16[128,2048]{1,0:T(8,128)(2,1)} %get-tuple-element.360), channel_id=1, source_target_pairs={{0,1},{2,0},{4,2},{6,4},{7,6},{5,7},{3,5},{1,3},{8,9},{10,8},{12,1... | collective-permute-start | bytes 1572872 | tf_op jit(solution)/shard_map/ppermute | solution.py:436
  544.7 14.8 %collective-permute-start.83 = (bf16[64,2048]{1,0:T(8,128)(2,1)}, bf16[64,2048]{1,0:T(8,128)(2,1)S(1)}, u32[]{:S(2)}, u32[]{:S(2)}) collective-permute-start(bf16[64,2048]{1,0:T(8,128)(2,1)} %get-tuple-element.384), channel_id=1, source_target_pairs={{0,2},{2,4},{4,6},{6,7},{7,5},{5,3},{3,1},{1,0},{8,10},{10,12},{12... | collective-permute-start | bytes 786440 | tf_op jit(solution)/shard_map/ppermute | solution.py:433
  545.8 13.8 %collective-permute-start.84 = (bf16[64,2048]{1,0:T(8,128)(2,1)}, bf16[64,2048]{1,0:T(8,128)(2,1)S(1)}, u32[]{:S(2)}, u32[]{:S(2)}) collective-permute-start(bf16[64,2048]{1,0:T(8,128)(2,1)} %get-tuple-element.385), channel_id=1, source_target_pairs={{0,1},{2,0},{4,2},{6,4},{7,6},{5,7},{3,5},{1,3},{8,9},{10,8},{12,1... | collective-permute-start | bytes 786440 | tf_op jit(solution)/shard_map/ppermute | solution.py:436
  566.2 22.8 %collective-permute-start.90 = (bf16[512,896]{1,0:T(8,128)(2,1)}, bf16[512,896]{1,0:T(8,128)(2,1)}, u32[]{:S(2)}, u32[]{:S(2)}) collective-permute-start(bf16[512,896]{1,0:T(8,128)(2,1)} %fusion.5), channel_id=1, source_target_pairs={{0,16},{8,24},{16,0},{24,8},{1,17},{9,25},{17,1},{25,9},{2,18},{10... | collective-permute-start | bytes 2752520 | tf_op jit(solution)/shard_map/ppermute | solution.py:562
  569.0 13.9 %collective-permute-start.85 = (bf16[128,2048]{1,0:T(8,128)(2,1)}, bf16[128,2048]{1,0:T(8,128)(2,1)S(1)}, u32[]{:S(2)}, u32[]{:S(2)}) collective-permute-start(bf16[128,2048]{1,0:T(8,128)(2,1)} %get-tuple-element.403), channel_id=1, source_target_pairs={{0,2},{2,4},{4,6},{6,7},{7,5},{5,3},{3,1},{1,0},{8,10},{10,12},{12... | collective-permute-start | bytes 1572872 | tf_op jit(solution)/shard_map/ppermute | solution.py:433
  570.1 13.6 %collective-permute-start.86 = (bf16[128,2048]{1,0:T(8,128)(2,1)}, bf16[128,2048]{1,0:T(8,128)(2,1)S(1)}, u32[]{:S(2)}, u32[]{:S(2)}) collective-permute-start(bf16[128,2048]{1,0:T(8,128)(2,1)} %get-tuple-element.404), channel_id=1, source_target_pairs={{0,1},{2,0},{4,2},{6,4},{7,6},{5,7},{3,5},{1,3},{8,9},{10,8},{12,1... | collective-permute-start | bytes 1572872 | tf_op jit(solution)/shard_map/ppermute | solution.py:436
  587.0 13.2 %collective-permute-start.87 = (bf16[128,2048]{1,0:T(8,128)(2,1)}, bf16[128,2048]{1,0:T(8,128)(2,1)}, u32[]{:S(2)}, u32[]{:S(2)}) collective-permute-start(bf16[128,2048]{1,0:T(8,128)(2,1)} %get-tuple-element.409), channel_id=1, source_target_pairs={{0,2},{2,4},{4,6},{6,7},{7,5},{5,3},{3,1},{1,0},{8,10},{10,12},{12... | collective-permute-start | bytes 1572872 | tf_op jit(solution)/shard_map/ppermute | solution.py:433
  588.2 12.9 %collective-permute-start.88 = (bf16[128,2048]{1,0:T(8,128)(2,1)}, bf16[128,2048]{1,0:T(8,128)(2,1)}, u32[]{:S(2)}, u32[]{:S(2)}) collective-permute-start(bf16[128,2048]{1,0:T(8,128)(2,1)} %get-tuple-element.410), channel_id=1, source_target_pairs={{0,1},{2,0},{4,2},{6,4},{7,6},{5,7},{3,5},{1,3},{8,9},{10,8},{12,1... | collective-permute-start | bytes 1572872 | tf_op jit(solution)/shard_map/ppermute | solution.py:436
  601.1 33.3 %all-to-all-start.1 = ((bf16[8,64,896]{2,1,0:T(8,128)(2,1)}), bf16[8,64,896]{2,1,0:T(8,128)(2,1)S(1)}, u32[]{:S(2)}, u32[]{:S(2)}) async-start(bf16[8,64,896]{2,1,0:T(8,128)(2,1)} %bitcast.27), calls=%async_computation.4 | async-start | bytes 1835008 | tf_op jit(solution)/shard_map/all_to_all | solution.py:1762
  611.4 31.1 %collective-permute-start.91 = (bf16[128,2048]{1,0:T(8,128)(2,1)}, bf16[128,2048]{1,0:T(8,128)(2,1)S(1)}, u32[]{:S(2)}, u32[]{:S(2)}) collective-permute-start(bf16[128,2048]{1,0:T(8,128)(2,1)} %get-tuple-element.415), channel_id=1, source_target_pairs={{0,2},{2,4},{4,6},{6,7},{7,5},{5,3},{3,1},{1,0},{8,10},{10,12},{12... | collective-permute-start | bytes 1572872 | tf_op jit(solution)/shard_map/ppermute | solution.py:433
  611.8 37.3 %collective-permute-start.92 = (bf16[128,2048]{1,0:T(8,128)(2,1)}, bf16[128,2048]{1,0:T(8,128)(2,1)S(1)}, u32[]{:S(2)}, u32[]{:S(2)}) collective-permute-start(bf16[128,2048]{1,0:T(8,128)(2,1)} %get-tuple-element.416), channel_id=1, source_target_pairs={{0,1},{2,0},{4,2},{6,4},{7,6},{5,7},{3,5},{1,3},{8,9},{10,8},{12,1... | collective-permute-start | bytes 1572872 | tf_op jit(solution)/shard_map/ppermute | solution.py:436
  (127 other events, 1485.1 us)
Sparse Core Ops, SparseCore 0:
  9.7 68.8 all-gather.3
  80.1 71.9 all-gather.5
  153.7 58.0 all-gather.7
  391.0 52.7 reduce-scatter.3
  446.0 54.2 reduce-scatter.5
  502.5 59.9 reduce-scatter.7

commit v5 on v4

--- a/solution.py
+++ b/solution.py
@@ -572,18 +572,22 @@
     return lax.dot_general(left, right, dims, preferred_element_type=jnp.float32)
 
 
+def low_terms(values, count):
+    terms = []
+    for _ in range(count):
+        terms.append(values.astype(jnp.bfloat16))
+        values = values - terms[-1].astype(jnp.float32)
+    return terms
+
+
 def row_sums(*columns):
     total = None
     for i, values in enumerate(columns):
         place = lax.broadcasted_iota(jnp.int32, (8, values.shape[1]), 0) == i
-        sums = lax.dot_general(
-            place.astype(jnp.float32),
-            values,
-            columns_last,
-            precision=lax.Precision.HIGHEST,
-            preferred_element_type=jnp.float32,
-        )
-        total = sums if total is None else total + sums
+        place = jnp.where(place, 1.0, 0.0).astype(jnp.bfloat16)
+        for term in low_terms(values, 2):
+            sums = dot(place, term, columns_last)
+            total = sums if total is None else total + sums
     return total
 
 
@@ -594,13 +598,8 @@
 def rows_as_columns(rows, columns):
     shape = (rows.shape[0], columns)
     same = lax.broadcasted_iota(jnp.int32, shape, 0) == lax.broadcasted_iota(jnp.int32, shape, 1)
-    return lax.dot_general(
-        rows,
-        same.astype(jnp.float32),
-        rows_first,
-        precision=lax.Precision.HIGHEST,
-        preferred_element_type=jnp.float32,
-    )
+    same = jnp.where(same, 1.0, 0.0).astype(jnp.bfloat16)
+    return sum(dot(term, same, rows_first) for term in low_terms(rows, 3))
 
 
 def whole_block(shape):
@@ -800,7 +799,7 @@
     low = jax.ShapeDtypeStruct((tokens, part), jnp.bfloat16)
     out = pl.pallas_call(
         functools.partial(
-            attend_kernel, ring.pieces, len(weights), min(256, tokens), head_dim ** (-0.5)
+            attend_kernel, ring.pieces, len(weights), min(512, tokens), head_dim ** (-0.5)
         ),
         grid_spec=pltpu.PrefetchScalarGridSpec(
             num_scalar_prefetch=1,

time: 668 us -> 662 us (level)
  no operation moved by 1% of the time
where the time goes in v5:
time: 662 us; the launch traced here: 653 us
  Pallas kernels  259 us (39%)
  waiting for transfers between devices  186 us (28%)
  starting transfers between devices  121 us (18%)
  other arithmetic  34.2 us (5%)
  local copies, waits for them, and re-layouts  33.3 us (5%)
  between operations  15.7 us (2%)
    ppermute x36, waiting for transfers between devices, forward(): return lax.ppermute(values, 'fsdp', self.up)  89 us
    ppermute x35, waiting for transfers between devices, backward(): return lax.ppermute(values, 'fsdp', self.down)  55.8 us
    ppermute x35, starting transfers between devices, backward(): return lax.ppermute(values, 'fsdp', self.down)  50.9 us
    ppermute x36, starting transfers between devices, forward(): return lax.ppermute(values, 'fsdp', self.up)  37.9 us
    pallas_call x1, Pallas kernels, expert_hidden(): pl.pallas_call(functools.partial(expert_hidden_kernel, ring.pieces, parts...  32.7 us
    pallas_call x12, Pallas kernels, add_pair(): pl.pallas_call(add_pair_kernel, out_shape=[shape, shape], name='add_pair')  30.5 us
    pallas_call x3, Pallas kernels, weight_near(): pl.pallas_call(weight_near_kernel, grid_spec=pltpu.PrefetchScalarGridSpec...  30.4 us
    pallas_call x1, Pallas kernels, expert_inputs(): pl.pallas_call(functools.partial(expert_inputs_kernel, ring.pieces, parts...  26.3 us
  transfers between devices with their start and end apart: 102, of which 55 were waited for; matrix products, arithmetic and copies ran while one was open for 8% of the time, Pallas kernels for 31%

profile of v5, /device:TPU:0, one launch (start us, length us, event | category | flops | bytes accessed | tf_op | source)
XLA Modules:
  0.0 653.1 jit_solution(14872364780774286959)
XLA Ops:
  9.5 3.0 collective-permute-start
  13.8 6.2 all-to-all-start
  31.5 2.5 collective-permute-done.9
  34.0 4.5 collective-permute-start.10
  38.5 5.1 collective-permute-start.12
  53.6 4.1 collective-permute-done.15
  57.7 5.1 collective-permute-start.2
  62.8 4.4 collective-permute-start.19
  67.8 7.3 %collective-permute-done.2.refs_2_ = bf16[128,2048]{1,0:T(8,128)(2,1)} collective-permute-done((bf16[128,2048]{1,0:T(8,128)(2,1)S(1)}, bf16[128,2048]{1,0:T(8,128)(2,1)}, u32[]{:S(2)}, u32[]{:S(2)}) %collective-permute-start.2) | collective-permute-done | bytes 524320 | tf_op jit(solution)/shard_map/ppermute | solution.py:436
  86.4 5.7 collective-permute-done.3.refs_3_
  95.6 5.5 collective-permute-done.16.refs_4_
  104.5 2.7 collective-permute-done.24.refs_10_.refs_14_
  109.0 11.4 %project.1 = (bf16[1024,2048]{1,0:T(8,128)(2,1)}, f32[1024,768]{1,0:T(8,128)}, f32[1024,1]{1,0:T(8,128)}, f32[8,1024]{1,0:T(8,128)}, bf16[1024,2048]{1,0:T(8,128)(2,1)}) custom-call(s32[9]{0:T(128)} %pad_add_fusion.scalars, bf16[128,2048]{1,0:T(8,128)(2,1)} %tokens.1, bf16[128,2048]{1,0:T(8,128)(2,1)} %copy-done.37, ...), custom_call_target="tpu_custom_call" | custom-call | tf_op jit(solution)/shard_map/project/pallas_call | solution.py:693
  120.5 4.1 collective-permute-done.26
  129.3 3.3 collective-permute-start.28
  137.6 17.1 %attend.1 = (bf16[1024,256]{1,0:T(8,128)(2,1)}, bf16[1024,256]{1,0:T(8,128)(2,1)}, bf16[1024,256]{1,0:T(8,128)(2,1)}, f32[1024,256]{1,0:T(8,128)}, f32[2,1024,1]...) custom-call(s32[9]{0:T(128)} %pad_add_fusion.scalars, ...), custom_call_target="tpu_custom_call" | custom-call | tf_op jit(solution)/shard_map/attend/pallas_call | solution.py:800
  156.8 4.6 collective-permute-done.31.rising
  170.3 11.0 %collective-permute-done.33.rising = bf16[128,2048]{1,0:T(8,128)(2,1)S(1)} collective-permute-done((bf16[128,2048]{1,0:T(8,128)(2,1)}, bf16[128,2048]{1,0:T(8,128)(2,1)S(1)}, u32[]{:S(2)}, u32[]{:S(2)}) %collective-permute-start.33) | collective-permute-done | bytes 524320 | tf_op jit(solution)/shard_map/ppermute | solution.py:433
  183.9 2.6 add_pair.13
  196.4 5.1 collective-permute-done.37.rising
  203.9 2.6 add_pair.14
  211.6 6.6 %collective-permute-done.41.rising = bf16[128,2048]{1,0:T(8,128)(2,1)S(1)} collective-permute-done((bf16[128,2048]{1,0:T(8,128)(2,1)}, bf16[128,2048]{1,0:T(8,128)(2,1)S(1)}, u32[]{:S(2)}, u32[]{:S(2)}) %collective-permute-start.41) | collective-permute-done | bytes 524320 | tf_op jit(solution)/shard_map/ppermute | solution.py:433
  220.2 3.5 middle.1
  226.1 13.2 %collective-permute-done.43.refs_1_ = bf16[128,2176]{1,0:T(8,128)(2,1)S(1)} collective-permute-done((bf16[128,2176]{1,0:T(8,128)(2,1)}, bf16[128,2176]{1,0:T(8,128)(2,1)S(1)}, u32[]{:S(2)}, u32[]{:S(2)}) %collective-permute-start.43) | collective-permute-done | bytes 557088 | tf_op jit(solution)/shard_map/ppermute | solution.py:436
  241.4 16.2 %expert_first.1 = (f32[2,1024,1024]{2,1,0:T(8,128)}, bf16[2048,1024]{1,0:T(8,128)(2,1)}) custom-call(s32[9]{0:T(128)} %pad_add_fusion.scalars, bf16[128,2048]{1,0:T(8,128)(2,1)} %cotangent.1, bf16[128,2048]{1,0:T(8,128)(2,1)} %collective-permute-done.22.refs_1_, bf16[128,2048]{1,0:T(8,128)(2,1)} %copy-done.39, bf16[128,2048]{1,0:T(8,128)(2,1)} %copy-done.23, ...), custom_call_target="tpu_custom_call" | custom-call | tf_op jit(solution)/shard_map/expert_first/pallas_call | solution.py:1193
  259.7 7.9 %collective-permute-done.48.refs_6_ = bf16[128,2176]{1,0:T(8,128)(2,1)S(1)} collective-permute-done((bf16[128,2176]{1,0:T(8,128)(2,1)S(1)}, bf16[128,2176]{1,0:T(8,128)(2,1)S(1)}, u32[]{:S(2)}, u32[]{:S(2)}) %collective-permute-start.48) | collective-permute-done | bytes 557088 | tf_op jit(solution)/shard_map/ppermute | solution.py:433
  269.9 4.3 collective-permute-done.49.refs_4_
  275.9 32.7 %expert_hidden.1 = (bf16[1024,2048]{1,0:T(8,128)(2,1)}, bf16[1024,2048]{1,0:T(8,128)(2,1)}, bf16[1024,2048]{1,0:T(8,128)(2,1)}, bf16[1024,2048]{1,0:T(8,128)(2,1...) custom-call(s32[9]{0:T(128)} %pad_add_fusion.scalars, ...), custom_call_target="tpu_custom_call" | custom-call | tf_op jit(solution)/shard_map/expert_hidden/pallas_call | solution.py:1289
  308.7 26.3 %expert_inputs.1 = (bf16[128,2304]{1,0:T(8,128)(2,1)}, bf16[128,2304]{1,0:T(8,128)(2,1)}, bf16[128,2304]{1,0:T(8,128)(2,1)}, bf16[128,2304]{1,0:T(8,128)(2,1)}, ...) custom-call(s32[9]{0:T(128)} %pad_add_fusion.scalars, ...), custom_call_target="tpu_custom_call" | custom-call | tf_op jit(solution)/shard_map/expert_inputs/pallas_call | solution.py:1380
  337.0 8.4 %weight_far.3 = bf16[2048,1024]{1,0:T(8,128)(2,1)} custom-call(bf16[2048,1024]{1,0:T(8,128)(2,1)} %get-tuple-element.302.left, bf16[1024,2048]{1,0:T(8,128)(2,1)} %get-tuple-element.272.refs_0_.right), custom_call_target="tpu_custom_call" | custom-call | tf_op jit(solution)/shard_map/weight_far/pallas_call | solution.py:1454
  350.8 8.3 %weight_far.4 = bf16[2048,1024]{1,0:T(8,128)(2,1)} custom-call(bf16[2048,1024]{1,0:T(8,128)(2,1)} %get-tuple-element.302.left, bf16[1024,2048]{1,0:T(8,128)(2,1)} %get-tuple-element.273.refs_1_.right), custom_call_target="tpu_custom_call" | custom-call | tf_op jit(solution)/shard_map/weight_far/pallas_call | solution.py:1454
  359.1 4.8 collective-permute-done.53.rising
  365.2 2.7 add_pair.16
  369.9 9.9 %weight_near.3 = bf16[4,2048,256]{2,1,0:T(8,128)(2,1)} custom-call(s32[9]{0:T(128)} %pad_add_fusion.scalars, bf16[2048,1024]{1,0:T(8,128)(2,1)} %get-tuple-element.302.left, bf16[1024,2048]{1,0:T(8,128)(2,1)} %get-tuple-element.272.refs_0_.right, bf16[2048,1024]{1,0:T(8,128)(2,1)} %collective-permute-done.55.arrived), custom_call_target="tpu_custom_call" | custom-call | tf_op jit(solution)/shard_map/weight_near/pallas_call | solution.py:1484
  379.8 3.2 collective-permute-done.56.rising
  384.8 2.7 add_pair.17
  390.6 10.6 %weight_near.4 = bf16[4,2048,256]{2,1,0:T(8,128)(2,1)} custom-call(s32[9]{0:T(128)} %pad_add_fusion.scalars, bf16[2048,1024]{1,0:T(8,128)(2,1)} %get-tuple-element.302.left, bf16[1024,2048]{1,0:T(8,128)(2,1)} %get-tuple-element.273.refs_1_.right, bf16[2048,1024]{1,0:T(8,128)(2,1)} %collective-permute-done.58.arrived), custom_call_target="tpu_custom_call" | custom-call | tf_op jit(solution)/shard_map/weight_near/pallas_call | solution.py:1484
  403.6 4.7 middle_back.1
  411.5 8.6 %weight_far.5 = bf16[2048,1024]{1,0:T(8,128)(2,1)} custom-call(bf16[2048,1024]{1,0:T(8,128)(2,1)} %get-tuple-element.329.left, bf16[1024,2048]{1,0:T(8,128)(2,1)} %get-tuple-element.323.right), custom_call_target="tpu_custom_call" | custom-call | tf_op jit(solution)/shard_map/weight_far/pallas_call | solution.py:1454
  423.8 15.3 %expert_outputs.1 = (bf16[128,2048]{1,0:T(8,128)(2,1)}, bf16[128,2048]{1,0:T(8,128)(2,1)}, bf16[128,2048]{1,0:T(8,128)(2,1)}, bf16[128,2048]{1,0:T(8,128)(2,1)},...) custom-call(s32[9]{0:T(128)} %pad_add_fusion.scalars, ...), custom_call_target="tpu_custom_call" | custom-call | tf_op jit(solution)/shard_map/expert_outputs/pallas_call | solution.py:1426
  441.2 10.0 %weight_near.5 = bf16[4,2048,256]{2,1,0:T(8,128)(2,1)} custom-call(s32[9]{0:T(128)} %pad_add_fusion.scalars, bf16[2048,1024]{1,0:T(8,128)(2,1)} %get-tuple-element.329.left, bf16[1024,2048]{1,0:T(8,128)(2,1)} %get-tuple-element.323.right, bf16[2048,1024]{1,0:T(8,128)(2,1)} %collective-permute-done.65.arrived), custom_call_target="tpu_custom_call" | custom-call | tf_op jit(solution)/shard_map/weight_near/pallas_call | solution.py:1484
  455.9 5.0 collective-permute-done.68.refs_20_
  464.4 4.3 collective-permute-done.70.rising
  475.6 11.3 %attend_back.2 = (f32[1024,128]{1,0:T(8,128)}, f32[1024,128]{1,0:T(8,128)}, bf16[1024,128]{1,0:T(8,128)(2,1)}, f32[8,1024]{1,0:T(8,128)}, f32[1,128]{1,0:T(1,128...) custom-call(s32[9]{0:T(128)} %pad_add_fusion.scalars, bf16[1024,256]{1,0:T(8,128)(2,1)} %get-tuple-element.338.refs_0_, ...), custom_call_target="tpu_custom_call" | custom-call | tf_op jit(solution)/shard_map/attend_back/pallas_call | solution.py:898
  487.9 2.5 add_pair.19
  492.7 11.0 %attend_back.3 = (f32[1024,128]{1,0:T(8,128)}, f32[1024,128]{1,0:T(8,128)}, bf16[1024,128]{1,0:T(8,128)(2,1)}, f32[8,1024]{1,0:T(8,128)}, f32[1,128]{1,0:T(1,128)}, /*index=5*/f32[1,128]{1,0:T(1,128)}) custom-call(s32[9]{0:T(128)} %pad_add_fusion.scalars, bf16[1024,256]{1,0:T(8,128)(2,1)} %get-tuple-element.338.refs_0_, ...), custom_call_target="tpu_custom_call" | custom-call | tf_op jit(solution)/shard_map/attend_back/pallas_call | solution.py:898
  506.2 3.5 fusion.9
  510.7 3.1 collective-permute-done.76
  515.0 2.6 add_pair.20
  525.2 14.1 %project_back.1 = (bf16[1024,768]{1,0:T(8,128)(2,1)}, f32[1,2048]{1,0:T(1,128)}, bf16[128,2048]{1,0:T(8,128)(2,1)}, bf16[128,2048]{1,0:T(8,128)(2,1)}, bf16[128,...) custom-call(s32[9]{0:T(128)} %pad_add_fusion.scalars, ...), custom_call_target="tpu_custom_call" | custom-call | tf_op jit(solution)/shard_map/project_back/pallas_call | solution.py:989
  545.3 9.4 %weight_rows.1 = (bf16[2,512,896]{2,1,0:T(8,128)(2,1)}, f32[2,512,896]{2,1,0:T(8,128)}) custom-call(s32[9]{0:T(128)} %pad_add_fusion.scalars, bf16[1024,2048]{1,0:T(8,128)(2,1)} %get-tuple-element.390.left, bf16[1024,768]{1,0:T(8,128)(2,1)} %get-tuple-element.391.right, f32[24,2048]{1,0:T(8,128)} %concatenate.95.sums), custom_call_target="tpu_custom_call" | custom-call | tf_op jit(solution)/shard_map/weight_rows/pallas_call | solution.py:1526
  554.7 4.0 collective-permute-done.89
  558.7 2.6 fusion.5
  566.8 3.9 convert_element_type.146
  570.7 3.9 convert_element_type.147
  574.6 4.0 collective-permute-done.85.rising
  584.8 3.0 fusion
  587.8 8.2 %collective-permute-done.87.rising = bf16[128,2048]{1,0:T(8,128)(2,1)} collective-permute-done((bf16[128,2048]{1,0:T(8,128)(2,1)}, bf16[128,2048]{1,0:T(8,128)(2,1)}, u32[]{:S(2)}, u32[]{:S(2)}) %collective-permute-start.87) | collective-permute-done | bytes 524320 | tf_op jit(solution)/shard_map/ppermute | solution.py:433
  596.3 3.6 all-to-all-start.1
  599.9 3.6 collective-permute-start.93
  603.5 2.6 add_pair.23
  612.8 16.4 %all-to-all-done.1 = bf16[8,64,896]{2,1,0:T(8,128)(2,1)S(1)} async-done(((bf16[8,64,896]{2,1,0:T(8,128)(2,1)}), bf16[8,64,896]{2,1,0:T(8,128)(2,1)S(1)}, u32[]{:S(2)}, u32[]{:S(2)}) %all-to-all-start.1) | async-done | bytes 917536 | tf_op jit(solution)/shard_map/all_to_all | solution.py:1761
  633.3 4.0 convert_element_type.154
  637.3 6.6 %collective-permute-done.92 = bf16[128,2048]{1,0:T(8,128)(2,1)S(1)} collective-permute-done((bf16[128,2048]{1,0:T(8,128)(2,1)}, bf16[128,2048]{1,0:T(8,128)(2,1)S(1)}, u32[]{:S(2)}, u32[]{:S(2)}) %collective-permute-start.92) | collective-permute-done | bytes 524320 | tf_op jit(solution)/shard_map/ppermute | solution.py:436
  (441 shorter events, 186.5 us)
Async XLA Ops:
  7.3 234.1 %all-gather.4.cloned.1.call-start = ((), (), s32[]{:S(2)}) async-start(), calls=%async_computation.5 | async-start | bytes 10485760 | tf_op jit(solution)/shard_map/all_gather | solution.py:1626
  8.0 261.9 %all-gather.6.cloned.1.call-start = ((), (), s32[]{:S(2)}) async-start(), calls=%async_computation.6 | async-start | bytes 10485760 | tf_op jit(solution)/shard_map/all_gather | solution.py:1627
  8.8 261.2 %all-gather.8.cloned.1.call-start = ((), (), s32[]{:S(2)}) async-start(), calls=%async_computation.7 | async-start | bytes 10485760 | tf_op jit(solution)/shard_map/all_gather | solution.py:1628
  9.5 36.5 %collective-permute-start = (bf16[128,2048]{1,0:T(8,128)(2,1)S(1)}, bf16[128,2048]{1,0:T(8,128)(2,1)S(1)}, u32[]{:S(2)}, u32[]{:S(2)}) collective-permute-start(bf16[128,2048]{1,0:T(8,128)(2,1)S(1)} %copy-done.2), channel_id=1, source_target_pairs={{0,1},{2,0},{4,2},{6,4},{7,6},{5,7},{3,5},{1,3},{8,9},{10,8},{12,1... | collective-permute-start | bytes 1572872 | tf_op jit(solution)/shard_map/ppermute | solution.py:436
  12.5 33.5 %collective-permute-start.1 = (bf16[128,2048]{1,0:T(8,128)(2,1)S(1)}, bf16[128,2048]{1,0:T(8,128)(2,1)}, u32[]{:S(2)}, u32[]{:S(2)}) collective-permute-start(bf16[128,2048]{1,0:T(8,128)(2,1)S(1)} %copy-done.2), channel_id=1, source_target_pairs={{0,2},{2,4},{4,6},{6,7},{7,5},{5,3},{3,1},{1,0},{8,10},{10,12},{12... | collective-permute-start | bytes 1572872 | tf_op jit(solution)/shard_map/ppermute | solution.py:433
  12.7 12.6 %collective-permute-start.7 = (bf16[1,20,64]{2,1,0:T(8,128)(2,1)S(1)}, bf16[1,20,64]{2,1,0:T(8,128)(2,1)S(1)}, u32[]{:S(2)}, u32[]{:S(2)}) collective-permute-start(bf16[1,20,64]{2,1,0:T(8,128)(2,1)S(1)} %bitcast.102), channel_id=1, source_target_pairs={{0,8},{8,0},{16,24},{24,16},{1,9},{9,1},{17,25},{25,17},{2,10},{10... | collective-permute-start | bytes 7688 | tf_op jit(solution)/shard_map/ppermute | solution.py:535
  13.8 43.8 %all-to-all-start = ((bf16[8,64,768]{2,1,0:T(8,128)(2,1)}), bf16[8,64,768]{2,1,0:T(8,128)(2,1)S(1)}, u32[]{:S(2)}, u32[]{:S(2)}) async-start(bf16[8,64,768]{2,1,0:T(8,128)(2,1)} %maximum_bitcast_fusion), calls=%async_computation | async-start | bytes 1572864 | tf_op jit(solution)/shard_map/all_to_all | solution.py:1592
  20.1 546.7 %reduce-scatter.4.cloned.1.call-start = ((), (), s32[]{:S(2)}) async-start(), calls=%async_computation.8 | async-start | bytes 6291456 | tf_op jit(solution)/shard_map/reduce_scatter | solution.py:1676
  48.6 37.8 %collective-permute-start.6 = (bf16[64,2048]{1,0:T(8,128)(2,1)}, bf16[64,2048]{1,0:T(8,128)(2,1)S(1)}, u32[]{:S(2)}, u32[]{:S(2)}) collective-permute-start(bf16[64,2048]{1,0:T(8,128)(2,1)} %param.24), channel_id=1, source_target_pairs={{0,0},{1,8},{2,16},{3,24},{4,1},{5,9},{6,17},{7,25},{8,2},{9,10},{... | collective-permute-start | bytes 786440 | tf_op jit(solution)/shard_map/ppermute | solution.py:1616
  57.7 17.4 %collective-permute-start.2 = (bf16[128,2048]{1,0:T(8,128)(2,1)S(1)}, bf16[128,2048]{1,0:T(8,128)(2,1)}, u32[]{:S(2)}, u32[]{:S(2)}) collective-permute-start(bf16[128,2048]{1,0:T(8,128)(2,1)S(1)} %collective-permute-done.refs_1_), channel_id=1, source_target_pairs={{0,1},{2,0},{4,2},{6,4},{7,6},{5,7},{3,5},{1,3},{8,9},{10,8},{12,1... | collective-permute-start | bytes 1572872 | tf_op jit(solution)/shard_map/ppermute | solution.py:436
  62.7 14.7 %collective-permute-start.4 = (bf16[128,2048]{1,0:T(8,128)(2,1)}, bf16[128,2048]{1,0:T(8,128)(2,1)}, u32[]{:S(2)}, u32[]{:S(2)}) collective-permute-start(bf16[128,2048]{1,0:T(8,128)(2,1)} %collective-permute-done.1.refs_8_), channel_id=1, source_target_pairs={{0,2},{2,4},{4,6},{6,7},{7,5},{5,3},{3,1},{1,0},{8,10},{10,12},{12... | collective-permute-start | bytes 1572872 | tf_op jit(solution)/shard_map/ppermute | solution.py:433
  62.8 32.7 %collective-permute-start.19 = (bf16[512,768]{1,0:T(8,128)(2,1)S(1)}, bf16[512,768]{1,0:T(8,128)(2,1)S(1)}, u32[]{:S(2)}, u32[]{:S(2)}) collective-permute-start(bf16[512,768]{1,0:T(8,128)(2,1)S(1)} %bitcast.88), channel_id=1, source_target_pairs={{0,16},{8,24},{16,0},{24,8},{1,17},{9,25},{17,1},{25,9},{2,18},{10... | collective-permute-start | bytes 2359304 | tf_op jit(solution)/shard_map/ppermute | solution.py:553
  75.0 17.1 %collective-permute-start.3 = (bf16[128,2048]{1,0:T(8,128)(2,1)}, bf16[128,2048]{1,0:T(8,128)(2,1)S(1)}, u32[]{:S(2)}, u32[]{:S(2)}) collective-permute-start(bf16[128,2048]{1,0:T(8,128)(2,1)} %collective-permute-done.2.refs_2_), channel_id=1, source_target_pairs={{0,1},{2,0},{4,2},{6,4},{7,6},{5,7},{3,5},{1,3},{8,9},{10,8},{12,1... | collective-permute-start | bytes 1572872 | tf_op jit(solution)/shard_map/ppermute | solution.py:436
  77.4 14.8 %collective-permute-start.5 = (bf16[128,2048]{1,0:T(8,128)(2,1)}, bf16[128,2048]{1,0:T(8,128)(2,1)}, u32[]{:S(2)}, u32[]{:S(2)}) collective-permute-start(bf16[128,2048]{1,0:T(8,128)(2,1)} %collective-permute-done.4.refs_7_), channel_id=1, source_target_pairs={{0,2},{2,4},{4,6},{6,7},{7,5},{5,3},{3,1},{1,0},{8,10},{10,12},{12... | collective-permute-start | bytes 1572872 | tf_op jit(solution)/shard_map/ppermute | solution.py:433
  79.8 27.4 %collective-permute-start.18 = (bf16[512,768]{1,0:T(8,128)(2,1)S(1)}, bf16[512,768]{1,0:T(8,128)(2,1)S(1)}, u32[]{:S(2)}, u32[]{:S(2)}) collective-permute-start(bf16[512,768]{1,0:T(8,128)(2,1)S(1)} %bitcast.89), channel_id=1, source_target_pairs={{0,8},{8,0},{16,24},{24,16},{1,9},{9,1},{17,25},{25,17},{2,10},{10... | collective-permute-start | bytes 2359304 | tf_op jit(solution)/shard_map/ppermute | solution.py:553
  95.4 13.5 %collective-permute-start.20 = (bf16[512,768]{1,0:T(8,128)(2,1)S(1)}, bf16[512,768]{1,0:T(8,128)(2,1)}, u32[]{:S(2)}, u32[]{:S(2)}) collective-permute-start(bf16[512,768]{1,0:T(8,128)(2,1)S(1)} %collective-permute-done.19.refs_11_.refs_15_), channel_id=1, source_target_pairs={{0,8},{8,0},{16,24},{24,16},{1,9},{9,1},{17,25},{25,17},{2,10},{10... | collective-permute-start | bytes 2359304 | tf_op jit(solution)/shard_map/ppermute | solution.py:553
  102.4 18.0 %collective-permute-start.21 = (bf16[128,2048]{1,0:T(8,128)(2,1)}, bf16[128,2048]{1,0:T(8,128)(2,1)}, u32[]{:S(2)}, u32[]{:S(2)}) collective-permute-start(bf16[128,2048]{1,0:T(8,128)(2,1)} %cotangent.1), channel_id=1, source_target_pairs={{0,2},{2,4},{4,6},{6,7},{7,5},{5,3},{3,1},{1,0},{8,10},{10,12},{12... | collective-permute-start | bytes 1572872 | tf_op jit(solution)/shard_map/ppermute | solution.py:433
  103.7 16.7 %collective-permute-start.22 = (bf16[128,2048]{1,0:T(8,128)(2,1)}, bf16[128,2048]{1,0:T(8,128)(2,1)}, u32[]{:S(2)}, u32[]{:S(2)}) collective-permute-start(bf16[128,2048]{1,0:T(8,128)(2,1)} %cotangent.1), channel_id=1, source_target_pairs={{0,1},{2,0},{4,2},{6,4},{7,6},{5,7},{3,5},{1,3},{8,9},{10,8},{12,1... | collective-permute-start | bytes 1572872 | tf_op jit(solution)/shard_map/ppermute | solution.py:436
  107.2 13.2 %collective-permute-start.23 = (bf16[64,2048]{1,0:T(8,128)(2,1)S(1)}, bf16[64,2048]{1,0:T(8,128)(2,1)S(1)}, u32[]{:S(2)}, u32[]{:S(2)}) collective-permute-start(bf16[64,2048]{1,0:T(8,128)(2,1)S(1)} %collective-permute-done.6.refs_8_.refs_12_), channel_id=1, source_target_pairs={{0,8},{8,0},{16,24},{24,16},{1,9},{9,1},{17,25},{25,17},{2,10},{10... | collective-permute-start | bytes 786440 | tf_op jit(solution)/shard_map/ppermute | solution.py:553
  107.2 13.2 %collective-permute-start.25 = (bf16[64,2048]{1,0:T(8,128)(2,1)S(1)}, bf16[64,2048]{1,0:T(8,128)(2,1)}, u32[]{:S(2)}, u32[]{:S(2)}) collective-permute-start(bf16[64,2048]{1,0:T(8,128)(2,1)S(1)} %collective-permute-done.24.refs_10_.refs_14_), channel_id=1, source_target_pairs={{0,8},{8,0},{16,24},{24,16},{1,9},{9,1},{17,25},{25,17},{2,10},{10... | collective-permute-start | bytes 786440 | tf_op jit(solution)/shard_map/ppermute | solution.py:553
  135.1 19.6 %collective-permute-start.29 = (bf16[128,2048]{1,0:T(8,128)(2,1)}, bf16[128,2048]{1,0:T(8,128)(2,1)S(1)}, u32[]{:S(2)}, u32[]{:S(2)}) collective-permute-start(bf16[128,2048]{1,0:T(8,128)(2,1)} %collective-permute-done.21.refs_8_), channel_id=1, source_target_pairs={{0,2},{2,4},{4,6},{6,7},{7,5},{5,3},{3,1},{1,0},{8,10},{10,12},{12... | collective-permute-start | bytes 1572872 | tf_op jit(solution)/shard_map/ppermute | solution.py:433
  136.8 17.9 %collective-permute-start.30 = (bf16[128,2048]{1,0:T(8,128)(2,1)}, bf16[128,2048]{1,0:T(8,128)(2,1)S(1)}, u32[]{:S(2)}, u32[]{:S(2)}) collective-permute-start(bf16[128,2048]{1,0:T(8,128)(2,1)} %collective-permute-done.22.refs_1_), channel_id=1, source_target_pairs={{0,1},{2,0},{4,2},{6,4},{7,6},{5,7},{3,5},{1,3},{8,9},{10,8},{12,1... | collective-permute-start | bytes 1572872 | tf_op jit(solution)/shard_map/ppermute | solution.py:436
  166.2 15.1 %collective-permute-start.33 = (bf16[128,2048]{1,0:T(8,128)(2,1)}, bf16[128,2048]{1,0:T(8,128)(2,1)S(1)}, u32[]{:S(2)}, u32[]{:S(2)}) collective-permute-start(bf16[128,2048]{1,0:T(8,128)(2,1)} %get-tuple-element.252), channel_id=1, source_target_pairs={{0,2},{2,4},{4,6},{6,7},{7,5},{5,3},{3,1},{1,0},{8,10},{10,12},{12... | collective-permute-start | bytes 1572872 | tf_op jit(solution)/shard_map/ppermute | solution.py:433
  168.0 15.1 %collective-permute-start.34 = (bf16[128,2048]{1,0:T(8,128)(2,1)}, bf16[128,2048]{1,0:T(8,128)(2,1)S(1)}, u32[]{:S(2)}, u32[]{:S(2)}) collective-permute-start(bf16[128,2048]{1,0:T(8,128)(2,1)} %get-tuple-element.254), channel_id=1, source_target_pairs={{0,1},{2,0},{4,2},{6,4},{7,6},{5,7},{3,5},{1,3},{8,9},{10,8},{12,1... | collective-permute-start | bytes 1572872 | tf_op jit(solution)/shard_map/ppermute | solution.py:436
  168.3 20.5 %collective-permute-start.35 = (bf16[128,2048]{1,0:T(8,128)(2,1)S(1)}, bf16[128,2048]{1,0:T(8,128)(2,1)S(1)}, u32[]{:S(2)}, u32[]{:S(2)}) collective-permute-start(bf16[128,2048]{1,0:T(8,128)(2,1)S(1)} %collective-permute-done.29.refs_7_), channel_id=1, source_target_pairs={{0,2},{2,4},{4,6},{6,7},{7,5},{5,3},{3,1},{1,0},{8,10},{10,12},{12... | collective-permute-start | bytes 1572872 | tf_op jit(solution)/shard_map/ppermute | solution.py:433
  170.1 20.9 %collective-permute-start.36 = (bf16[128,2048]{1,0:T(8,128)(2,1)S(1)}, bf16[128,2048]{1,0:T(8,128)(2,1)S(1)}, u32[]{:S(2)}, u32[]{:S(2)}) collective-permute-start(bf16[128,2048]{1,0:T(8,128)(2,1)S(1)} %collective-permute-done.30.refs_2_), channel_id=1, source_target_pairs={{0,1},{2,0},{4,2},{6,4},{7,6},{5,7},{3,5},{1,3},{8,9},{10,8},{12,1... | collective-permute-start | bytes 1572872 | tf_op jit(solution)/shard_map/ppermute | solution.py:436
  193.7 12.9 %collective-permute-start.39 = (bf16[64,2048]{1,0:T(8,128)(2,1)}, bf16[64,2048]{1,0:T(8,128)(2,1)S(1)}, u32[]{:S(2)}, u32[]{:S(2)}) collective-permute-start(bf16[64,2048]{1,0:T(8,128)(2,1)} %slice.151), channel_id=1, source_target_pairs={{0,2},{2,4},{4,6},{6,7},{7,5},{5,3},{3,1},{1,0},{8,10},{10,12},{12... | collective-permute-start | bytes 786440 | tf_op jit(solution)/shard_map/ppermute | solution.py:433
  195.3 13.6 %collective-permute-start.40 = (bf16[64,2048]{1,0:T(8,128)(2,1)}, bf16[64,2048]{1,0:T(8,128)(2,1)}, u32[]{:S(2)}, u32[]{:S(2)}) collective-permute-start(bf16[64,2048]{1,0:T(8,128)(2,1)} %slice.152), channel_id=1, source_target_pairs={{0,1},{2,0},{4,2},{6,4},{7,6},{5,7},{3,5},{1,3},{8,9},{10,8},{12,1... | collective-permute-start | bytes 786440 | tf_op jit(solution)/shard_map/ppermute | solution.py:436
  223.7 15.5 %collective-permute-start.43 = (bf16[128,2176]{1,0:T(8,128)(2,1)}, bf16[128,2176]{1,0:T(8,128)(2,1)S(1)}, u32[]{:S(2)}, u32[]{:S(2)}) collective-permute-start(bf16[128,2176]{1,0:T(8,128)(2,1)} %get-tuple-element.267.refs_0_.block), channel_id=1, source_target_pairs={{0,1},{2,0},{4,2},{6,4},{7,6},{5,7},{3,5},{1,3},{8,9},{10,8},{12,1... | collective-permute-start | bytes 1671176 | tf_op jit(solution)/shard_map/ppermute | solution.py:436
  226.0 14.5 %collective-permute-start.45 = (bf16[128,2176]{1,0:T(8,128)(2,1)}, bf16[128,2176]{1,0:T(8,128)(2,1)S(1)}, u32[]{:S(2)}, u32[]{:S(2)}) collective-permute-start(bf16[128,2176]{1,0:T(8,128)(2,1)} %get-tuple-element.267.refs_0_.block), channel_id=1, source_target_pairs={{0,2},{2,4},{4,6},{6,7},{7,5},{5,3},{3,1},{1,0},{8,10},{10,12},{12... | collective-permute-start | bytes 1671176 | tf_op jit(solution)/shard_map/ppermute | solution.py:433
  239.3 18.3 %collective-permute-start.44 = (bf16[128,2176]{1,0:T(8,128)(2,1)S(1)}, bf16[128,2176]{1,0:T(8,128)(2,1)S(1)}, u32[]{:S(2)}, u32[]{:S(2)}) collective-permute-start(bf16[128,2176]{1,0:T(8,128)(2,1)S(1)} %collective-permute-done.43.refs_1_), channel_id=1, source_target_pairs={{0,1},{2,0},{4,2},{6,4},{7,6},{5,7},{3,5},{1,3},{8,9},{10,8},{12,1... | collective-permute-start | bytes 1671176 | tf_op jit(solution)/shard_map/ppermute | solution.py:436
  240.6 17.0 %collective-permute-start.46 = (bf16[128,2176]{1,0:T(8,128)(2,1)S(1)}, bf16[128,2176]{1,0:T(8,128)(2,1)S(1)}, u32[]{:S(2)}, u32[]{:S(2)}) collective-permute-start(bf16[128,2176]{1,0:T(8,128)(2,1)S(1)} %collective-permute-done.45.refs_8_), channel_id=1, source_target_pairs={{0,2},{2,4},{4,6},{6,7},{7,5},{5,3},{3,1},{1,0},{8,10},{10,12},{12... | collective-permute-start | bytes 1671176 | tf_op jit(solution)/shard_map/ppermute | solution.py:433
  345.4 22.5 %collective-permute-start.55 = (bf16[2048,1024]{1,0:T(8,128)(2,1)}, bf16[2048,1024]{1,0:T(8,128)(2,1)}, u32[]{:S(2)}, u32[]{:S(2)}) collective-permute-start(bf16[2048,1024]{1,0:T(8,128)(2,1)} %weight_far.3), channel_id=1, source_target_pairs={{0,8},{8,0},{16,24},{24,16},{1,9},{9,1},{17,25},{25,17},{2,10},{10... | collective-permute-start | bytes 12582920 | tf_op jit(solution)/shard_map/ppermute | solution.py:1669
  348.8 15.2 %collective-permute-start.53 = (bf16[128,2304]{1,0:T(8,128)(2,1)}, bf16[128,2304]{1,0:T(8,128)(2,1)S(1)}, u32[]{:S(2)}, u32[]{:S(2)}) collective-permute-start(bf16[128,2304]{1,0:T(8,128)(2,1)} %get-tuple-element.288), channel_id=1, source_target_pairs={{0,2},{2,4},{4,6},{6,7},{7,5},{5,3},{3,1},{1,0},{8,10},{10,12},{12... | collective-permute-start | bytes 1769480 | tf_op jit(solution)/shard_map/ppermute | solution.py:433
  349.4 14.9 %collective-permute-start.54 = (bf16[128,2304]{1,0:T(8,128)(2,1)}, bf16[128,2304]{1,0:T(8,128)(2,1)S(1)}, u32[]{:S(2)}, u32[]{:S(2)}) collective-permute-start(bf16[128,2304]{1,0:T(8,128)(2,1)} %get-tuple-element.289), channel_id=1, source_target_pairs={{0,1},{2,0},{4,2},{6,4},{7,6},{5,7},{3,5},{1,3},{8,9},{10,8},{12,1... | collective-permute-start | bytes 1769480 | tf_op jit(solution)/shard_map/ppermute | solution.py:436
  364.4 23.1 %collective-permute-start.58 = (bf16[2048,1024]{1,0:T(8,128)(2,1)}, bf16[2048,1024]{1,0:T(8,128)(2,1)}, u32[]{:S(2)}, u32[]{:S(2)}) collective-permute-start(bf16[2048,1024]{1,0:T(8,128)(2,1)} %weight_far.4), channel_id=1, source_target_pairs={{0,8},{8,0},{16,24},{24,16},{1,9},{9,1},{17,25},{25,17},{2,10},{10... | collective-permute-start | bytes 12582920 | tf_op jit(solution)/shard_map/ppermute | solution.py:1669
  367.9 15.1 %collective-permute-start.56 = (bf16[128,2304]{1,0:T(8,128)(2,1)}, bf16[128,2304]{1,0:T(8,128)(2,1)S(1)}, u32[]{:S(2)}, u32[]{:S(2)}) collective-permute-start(bf16[128,2304]{1,0:T(8,128)(2,1)} %get-tuple-element.294), channel_id=1, source_target_pairs={{0,2},{2,4},{4,6},{6,7},{7,5},{5,3},{3,1},{1,0},{8,10},{10,12},{12... | collective-permute-start | bytes 1769480 | tf_op jit(solution)/shard_map/ppermute | solution.py:433
  368.4 14.9 %collective-permute-start.57 = (bf16[128,2304]{1,0:T(8,128)(2,1)}, bf16[128,2304]{1,0:T(8,128)(2,1)S(1)}, u32[]{:S(2)}, u32[]{:S(2)}) collective-permute-start(bf16[128,2304]{1,0:T(8,128)(2,1)} %get-tuple-element.295), channel_id=1, source_target_pairs={{0,1},{2,0},{4,2},{6,4},{7,6},{5,7},{3,5},{1,3},{8,9},{10,8},{12,1... | collective-permute-start | bytes 1769480 | tf_op jit(solution)/shard_map/ppermute | solution.py:436
  387.5 183.2 %reduce-scatter.6.cloned.1.call-start = ((), (), s32[]{:S(2)}) async-start(), calls=%async_computation.9 | async-start | bytes 6291456 | tf_op jit(solution)/shard_map/reduce_scatter | solution.py:1676
  388.5 14.0 %collective-permute-start.59 = (bf16[128,2304]{1,0:T(8,128)(2,1)S(1)}, bf16[128,2304]{1,0:T(8,128)(2,1)S(1)}, u32[]{:S(2)}, u32[]{:S(2)}) collective-permute-start(bf16[128,2304]{1,0:T(8,128)(2,1)S(1)} %copy-done.85), channel_id=1, source_target_pairs={{0,2},{2,4},{4,6},{6,7},{7,5},{5,3},{3,1},{1,0},{8,10},{10,12},{12... | collective-permute-start | bytes 1769480 | tf_op jit(solution)/shard_map/ppermute | solution.py:433
  389.0 13.8 %collective-permute-start.60 = (bf16[128,2304]{1,0:T(8,128)(2,1)S(1)}, bf16[128,2304]{1,0:T(8,128)(2,1)S(1)}, u32[]{:S(2)}, u32[]{:S(2)}) collective-permute-start(bf16[128,2304]{1,0:T(8,128)(2,1)S(1)} %copy-done.84), channel_id=1, source_target_pairs={{0,1},{2,0},{4,2},{6,4},{7,6},{5,7},{3,5},{1,3},{8,9},{10,8},{12,1... | collective-permute-start | bytes 1769480 | tf_op jit(solution)/shard_map/ppermute | solution.py:436
  408.3 225.0 %reduce-scatter.8.cloned.1.call-start = ((), (), s32[]{:S(2)}) async-start(), calls=%async_computation.10 | async-start | bytes 6291456 | tf_op jit(solution)/shard_map/reduce_scatter | solution.py:1676
  421.7 17.4 %collective-permute-start.65 = (bf16[2048,1024]{1,0:T(8,128)(2,1)}, bf16[2048,1024]{1,0:T(8,128)(2,1)}, u32[]{:S(2)}, u32[]{:S(2)}) collective-permute-start(bf16[2048,1024]{1,0:T(8,128)(2,1)} %weight_far.5), channel_id=1, source_target_pairs={{0,8},{8,0},{16,24},{24,16},{1,9},{9,1},{17,25},{25,17},{2,10},{10... | collective-permute-start | bytes 12582920 | tf_op jit(solution)/shard_map/ppermute | solution.py:1669
  421.7 17.3 %collective-permute-start.63 = (bf16[128,2048]{1,0:T(8,128)(2,1)S(1)}, bf16[128,2048]{1,0:T(8,128)(2,1)S(1)}, u32[]{:S(2)}, u32[]{:S(2)}) collective-permute-start(bf16[128,2048]{1,0:T(8,128)(2,1)S(1)} %collective-permute-done.61.refs_24_), channel_id=1, source_target_pairs={{0,2},{2,4},{4,6},{6,7},{7,5},{5,3},{3,1},{1,0},{8,10},{10,12},{12... | collective-permute-start | bytes 1572872 | tf_op jit(solution)/shard_map/ppermute | solution.py:433
  422.8 16.3 %collective-permute-start.64 = (bf16[128,2048]{1,0:T(8,128)(2,1)S(1)}, bf16[128,2048]{1,0:T(8,128)(2,1)S(1)}, u32[]{:S(2)}, u32[]{:S(2)}) collective-permute-start(bf16[128,2048]{1,0:T(8,128)(2,1)S(1)} %collective-permute-done.62.refs_17_), channel_id=1, source_target_pairs={{0,1},{2,0},{4,2},{6,4},{7,6},{5,7},{3,5},{1,3},{8,9},{10,8},{12,1... | collective-permute-start | bytes 1572872 | tf_op jit(solution)/shard_map/ppermute | solution.py:436
  439.1 13.8 %collective-permute-start.66 = (bf16[128,2048]{1,0:T(8,128)(2,1)S(1)}, bf16[128,2048]{1,0:T(8,128)(2,1)S(1)}, u32[]{:S(2)}, u32[]{:S(2)}) collective-permute-start(bf16[128,2048]{1,0:T(8,128)(2,1)S(1)} %collective-permute-done.63.refs_23_), channel_id=1, source_target_pairs={{0,2},{2,4},{4,6},{6,7},{7,5},{5,3},{3,1},{1,0},{8,10},{10,12},{12... | collective-permute-start | bytes 1572872 | tf_op jit(solution)/shard_map/ppermute | solution.py:433
  440.2 13.5 %collective-permute-start.67 = (bf16[128,2048]{1,0:T(8,128)(2,1)S(1)}, bf16[128,2048]{1,0:T(8,128)(2,1)S(1)}, u32[]{:S(2)}, u32[]{:S(2)}) collective-permute-start(bf16[128,2048]{1,0:T(8,128)(2,1)S(1)} %collective-permute-done.64.refs_18_), channel_id=1, source_target_pairs={{0,1},{2,0},{4,2},{6,4},{7,6},{5,7},{3,5},{1,3},{8,9},{10,8},{12,1... | collective-permute-start | bytes 1572872 | tf_op jit(solution)/shard_map/ppermute | solution.py:436
  473.5 13.4 %collective-permute-start.72 = (bf16[128,2048]{1,0:T(8,128)(2,1)}, bf16[128,2048]{1,0:T(8,128)(2,1)S(1)}, u32[]{:S(2)}, u32[]{:S(2)}) collective-permute-start(bf16[128,2048]{1,0:T(8,128)(2,1)} %get-tuple-element.335), channel_id=1, source_target_pairs={{0,2},{2,4},{4,6},{6,7},{7,5},{5,3},{3,1},{1,0},{8,10},{10,12},{12... | collective-permute-start | bytes 1572872 | tf_op jit(solution)/shard_map/ppermute | solution.py:433
  474.5 12.4 %collective-permute-start.73 = (bf16[128,2048]{1,0:T(8,128)(2,1)}, bf16[128,2048]{1,0:T(8,128)(2,1)S(1)}, u32[]{:S(2)}, u32[]{:S(2)}) collective-permute-start(bf16[128,2048]{1,0:T(8,128)(2,1)} %get-tuple-element.336), channel_id=1, source_target_pairs={{0,1},{2,0},{4,2},{6,4},{7,6},{5,7},{3,5},{1,3},{8,9},{10,8},{12,1... | collective-permute-start | bytes 1572872 | tf_op jit(solution)/shard_map/ppermute | solution.py:436
  490.4 14.1 %collective-permute-start.74 = (bf16[128,2048]{1,0:T(8,128)(2,1)}, bf16[128,2048]{1,0:T(8,128)(2,1)S(1)}, u32[]{:S(2)}, u32[]{:S(2)}) collective-permute-start(bf16[128,2048]{1,0:T(8,128)(2,1)} %get-tuple-element.347), channel_id=1, source_target_pairs={{0,2},{2,4},{4,6},{6,7},{7,5},{5,3},{3,1},{1,0},{8,10},{10,12},{12... | collective-permute-start | bytes 1572872 | tf_op jit(solution)/shard_map/ppermute | solution.py:433
  491.4 13.2 %collective-permute-start.75 = (bf16[128,2048]{1,0:T(8,128)(2,1)}, bf16[128,2048]{1,0:T(8,128)(2,1)S(1)}, u32[]{:S(2)}, u32[]{:S(2)}) collective-permute-start(bf16[128,2048]{1,0:T(8,128)(2,1)} %get-tuple-element.348), channel_id=1, source_target_pairs={{0,1},{2,0},{4,2},{6,4},{7,6},{5,7},{3,5},{1,3},{8,9},{10,8},{12,1... | collective-permute-start | bytes 1572872 | tf_op jit(solution)/shard_map/ppermute | solution.py:436
  520.2 19.1 %collective-permute-start.82 = (bf16[64,2048]{1,0:T(8,128)(2,1)}, bf16[64,2048]{1,0:T(8,128)(2,1)S(1)}, u32[]{:S(2)}, u32[]{:S(2)}) collective-permute-start(bf16[64,2048]{1,0:T(8,128)(2,1)} %fusion.6), channel_id=1, source_target_pairs={{0,16},{8,24},{16,0},{24,8},{1,17},{9,25},{17,1},{25,9},{2,18},{10... | collective-permute-start | bytes 786440 | tf_op jit(solution)/shard_map/ppermute | solution.py:562
  523.2 17.0 %collective-permute-start.79 = (bf16[128,2048]{1,0:T(8,128)(2,1)}, bf16[128,2048]{1,0:T(8,128)(2,1)S(1)}, u32[]{:S(2)}, u32[]{:S(2)}) collective-permute-start(bf16[128,2048]{1,0:T(8,128)(2,1)} %get-tuple-element.359), channel_id=1, source_target_pairs={{0,2},{2,4},{4,6},{6,7},{7,5},{5,3},{3,1},{1,0},{8,10},{10,12},{12... | collective-permute-start | bytes 1572872 | tf_op jit(solution)/shard_map/ppermute | solution.py:433
  524.3 15.8 %collective-permute-start.80 = (bf16[128,2048]{1,0:T(8,128)(2,1)}, bf16[128,2048]{1,0:T(8,128)(2,1)}, u32[]{:S(2)}, u32[]{:S(2)}) collective-permute-start(bf16[128,2048]{1,0:T(8,128)(2,1)} %get-tuple-element.360), channel_id=1, source_target_pairs={{0,1},{2,0},{4,2},{6,4},{7,6},{5,7},{3,5},{1,3},{8,9},{10,8},{12,1... | collective-permute-start | bytes 1572872 | tf_op jit(solution)/shard_map/ppermute | solution.py:436
  540.1 14.5 %collective-permute-start.83 = (bf16[64,2048]{1,0:T(8,128)(2,1)}, bf16[64,2048]{1,0:T(8,128)(2,1)S(1)}, u32[]{:S(2)}, u32[]{:S(2)}) collective-permute-start(bf16[64,2048]{1,0:T(8,128)(2,1)} %get-tuple-element.384), channel_id=1, source_target_pairs={{0,2},{2,4},{4,6},{6,7},{7,5},{5,3},{3,1},{1,0},{8,10},{10,12},{12... | collective-permute-start | bytes 786440 | tf_op jit(solution)/shard_map/ppermute | solution.py:433
  541.2 13.4 %collective-permute-start.84 = (bf16[64,2048]{1,0:T(8,128)(2,1)}, bf16[64,2048]{1,0:T(8,128)(2,1)S(1)}, u32[]{:S(2)}, u32[]{:S(2)}) collective-permute-start(bf16[64,2048]{1,0:T(8,128)(2,1)} %get-tuple-element.385), channel_id=1, source_target_pairs={{0,1},{2,0},{4,2},{6,4},{7,6},{5,7},{3,5},{1,3},{8,9},{10,8},{12,1... | collective-permute-start | bytes 786440 | tf_op jit(solution)/shard_map/ppermute | solution.py:436
  561.3 23.4 %collective-permute-start.90 = (bf16[512,896]{1,0:T(8,128)(2,1)}, bf16[512,896]{1,0:T(8,128)(2,1)}, u32[]{:S(2)}, u32[]{:S(2)}) collective-permute-start(bf16[512,896]{1,0:T(8,128)(2,1)} %fusion.5), channel_id=1, source_target_pairs={{0,16},{8,24},{16,0},{24,8},{1,17},{9,25},{17,1},{25,9},{2,18},{10... | collective-permute-start | bytes 2752520 | tf_op jit(solution)/shard_map/ppermute | solution.py:562
  564.7 13.9 %collective-permute-start.85 = (bf16[128,2048]{1,0:T(8,128)(2,1)}, bf16[128,2048]{1,0:T(8,128)(2,1)S(1)}, u32[]{:S(2)}, u32[]{:S(2)}) collective-permute-start(bf16[128,2048]{1,0:T(8,128)(2,1)} %get-tuple-element.403), channel_id=1, source_target_pairs={{0,2},{2,4},{4,6},{6,7},{7,5},{5,3},{3,1},{1,0},{8,10},{10,12},{12... | collective-permute-start | bytes 1572872 | tf_op jit(solution)/shard_map/ppermute | solution.py:433
  565.3 13.6 %collective-permute-start.86 = (bf16[128,2048]{1,0:T(8,128)(2,1)}, bf16[128,2048]{1,0:T(8,128)(2,1)S(1)}, u32[]{:S(2)}, u32[]{:S(2)}) collective-permute-start(bf16[128,2048]{1,0:T(8,128)(2,1)} %get-tuple-element.404), channel_id=1, source_target_pairs={{0,1},{2,0},{4,2},{6,4},{7,6},{5,7},{3,5},{1,3},{8,9},{10,8},{12,1... | collective-permute-start | bytes 1572872 | tf_op jit(solution)/shard_map/ppermute | solution.py:436
  582.8 13.2 %collective-permute-start.87 = (bf16[128,2048]{1,0:T(8,128)(2,1)}, bf16[128,2048]{1,0:T(8,128)(2,1)}, u32[]{:S(2)}, u32[]{:S(2)}) collective-permute-start(bf16[128,2048]{1,0:T(8,128)(2,1)} %get-tuple-element.409), channel_id=1, source_target_pairs={{0,2},{2,4},{4,6},{6,7},{7,5},{5,3},{3,1},{1,0},{8,10},{10,12},{12... | collective-permute-start | bytes 1572872 | tf_op jit(solution)/shard_map/ppermute | solution.py:433
  583.3 13.0 %collective-permute-start.88 = (bf16[128,2048]{1,0:T(8,128)(2,1)}, bf16[128,2048]{1,0:T(8,128)(2,1)}, u32[]{:S(2)}, u32[]{:S(2)}) collective-permute-start(bf16[128,2048]{1,0:T(8,128)(2,1)} %get-tuple-element.410), channel_id=1, source_target_pairs={{0,1},{2,0},{4,2},{6,4},{7,6},{5,7},{3,5},{1,3},{8,9},{10,8},{12,1... | collective-permute-start | bytes 1572872 | tf_op jit(solution)/shard_map/ppermute | solution.py:436
  596.3 32.9 %all-to-all-start.1 = ((bf16[8,64,896]{2,1,0:T(8,128)(2,1)}), bf16[8,64,896]{2,1,0:T(8,128)(2,1)S(1)}, u32[]{:S(2)}, u32[]{:S(2)}) async-start(bf16[8,64,896]{2,1,0:T(8,128)(2,1)} %bitcast.27), calls=%async_computation.4 | async-start | bytes 1835008 | tf_op jit(solution)/shard_map/all_to_all | solution.py:1761
  606.1 31.3 %collective-permute-start.91 = (bf16[128,2048]{1,0:T(8,128)(2,1)}, bf16[128,2048]{1,0:T(8,128)(2,1)S(1)}, u32[]{:S(2)}, u32[]{:S(2)}) collective-permute-start(bf16[128,2048]{1,0:T(8,128)(2,1)} %get-tuple-element.415), channel_id=1, source_target_pairs={{0,2},{2,4},{4,6},{6,7},{7,5},{5,3},{3,1},{1,0},{8,10},{10,12},{12... | collective-permute-start | bytes 1572872 | tf_op jit(solution)/shard_map/ppermute | solution.py:433
  606.3 37.6 %collective-permute-start.92 = (bf16[128,2048]{1,0:T(8,128)(2,1)}, bf16[128,2048]{1,0:T(8,128)(2,1)S(1)}, u32[]{:S(2)}, u32[]{:S(2)}) collective-permute-start(bf16[128,2048]{1,0:T(8,128)(2,1)} %get-tuple-element.416), channel_id=1, source_target_pairs={{0,1},{2,0},{4,2},{6,4},{7,6},{5,7},{3,5},{1,3},{8,9},{10,8},{12,1... | collective-permute-start | bytes 1572872 | tf_op jit(solution)/shard_map/ppermute | solution.py:436
  (127 other events, 1478.9 us)
Sparse Core Ops, SparseCore 0:
  9.7 68.8 all-gather.3
  80.1 71.9 all-gather.5
  153.7 58.0 all-gather.7
  387.6 52.9 reduce-scatter.3
  442.8 54.3 reduce-scatter.5
  499.3 59.9 reduce-scatter.7

commit v6 on v5

--- a/solution.py
+++ b/solution.py
@@ -1287,7 +1287,7 @@
     column = pl.BlockSpec((None, span, 1), lambda i, s: (i // parts, 0, 0))
     hidden = jax.ShapeDtypeStruct((span, experts * parts * step_hidden), jnp.bfloat16)
     return pl.pallas_call(
-        functools.partial(expert_hidden_kernel, ring.pieces, parts, min(256, span)),
+        functools.partial(expert_hidden_kernel, ring.pieces, parts, min(512, span)),
         grid_spec=pltpu.PrefetchScalarGridSpec(
             num_scalar_prefetch=1,
             grid=(experts * parts,),

time: 662 us -> 662 us (level)
  no operation moved by 1% of the time
where the time goes in v6:
time: 662 us; the launch traced here: 653 us
  Pallas kernels  259 us (39%)
  waiting for transfers between devices  186 us (28%)
  starting transfers between devices  121 us (18%)
  other arithmetic  34.2 us (5%)
  local copies, waits for them, and re-layouts  33.3 us (5%)
  between operations  15.7 us (2%)
    ppermute x36, waiting for transfers between devices, forward(): return lax.ppermute(values, 'fsdp', self.up)  89 us
    ppermute x35, waiting for transfers between devices, backward(): return lax.ppermute(values, 'fsdp', self.down)  55.8 us
    ppermute x35, starting transfers between devices, backward(): return lax.ppermute(values, 'fsdp', self.down)  51.1 us
    ppermute x36, starting transfers between devices, forward(): return lax.ppermute(values, 'fsdp', self.up)  37.7 us
    pallas_call x1, Pallas kernels, expert_hidden(): pl.pallas_call(functools.partial(expert_hidden_kernel, ring.pieces, parts...  32.5 us
    pallas_call x12, Pallas kernels, add_pair(): pl.pallas_call(add_pair_kernel, out_shape=[shape, shape], name='add_pair')  30.5 us
    pallas_call x3, Pallas kernels, weight_near(): pl.pallas_call(weight_near_kernel, grid_spec=pltpu.PrefetchScalarGridSpec...  30.4 us
    pallas_call x1, Pallas kernels, expert_inputs(): pl.pallas_call(functools.partial(expert_inputs_kernel, ring.pieces, parts...  26.3 us
  transfers between devices with their start and end apart: 102, of which 55 were waited for; matrix products, arithmetic and copies ran while one was open for 8% of the time, Pallas kernels for 31%

profile of v6, /device:TPU:0, one launch (start us, length us, event | category | flops | bytes accessed | tf_op | source)
XLA Modules:
  0.0 652.8 jit_solution(13181762539092971676)
XLA Ops:
  9.5 3.0 collective-permute-start
  13.8 6.2 all-to-all-start
  31.5 2.5 collective-permute-done.9
  34.0 4.5 collective-permute-start.10
  38.5 5.1 collective-permute-start.12
  53.6 4.1 collective-permute-done.15
  57.7 5.1 collective-permute-start.2
  62.8 4.4 collective-permute-start.19
  67.8 7.3 %collective-permute-done.2.refs_2_ = bf16[128,2048]{1,0:T(8,128)(2,1)} collective-permute-done((bf16[128,2048]{1,0:T(8,128)(2,1)S(1)}, bf16[128,2048]{1,0:T(8,128)(2,1)}, u32[]{:S(2)}, u32[]{:S(2)}) %collective-permute-start.2) | collective-permute-done | bytes 524320 | tf_op jit(solution)/shard_map/ppermute | solution.py:436
  86.4 5.7 collective-permute-done.3.refs_3_
  95.6 5.5 collective-permute-done.16.refs_4_
  104.5 2.7 collective-permute-done.24.refs_10_.refs_14_
  109.0 11.4 %project.1 = (bf16[1024,2048]{1,0:T(8,128)(2,1)}, f32[1024,768]{1,0:T(8,128)}, f32[1024,1]{1,0:T(8,128)}, f32[8,1024]{1,0:T(8,128)}, bf16[1024,2048]{1,0:T(8,128)(2,1)}) custom-call(s32[9]{0:T(128)} %pad_add_fusion.scalars, bf16[128,2048]{1,0:T(8,128)(2,1)} %tokens.1, bf16[128,2048]{1,0:T(8,128)(2,1)} %copy-done.37, ...), custom_call_target="tpu_custom_call" | custom-call | tf_op jit(solution)/shard_map/project/pallas_call | solution.py:693
  120.5 4.1 collective-permute-done.26
  129.3 3.3 collective-permute-start.28
  137.6 17.1 %attend.1 = (bf16[1024,256]{1,0:T(8,128)(2,1)}, bf16[1024,256]{1,0:T(8,128)(2,1)}, bf16[1024,256]{1,0:T(8,128)(2,1)}, f32[1024,256]{1,0:T(8,128)}, f32[2,1024,1]...) custom-call(s32[9]{0:T(128)} %pad_add_fusion.scalars, ...), custom_call_target="tpu_custom_call" | custom-call | tf_op jit(solution)/shard_map/attend/pallas_call | solution.py:800
  156.8 4.6 collective-permute-done.31.rising
  170.3 11.0 %collective-permute-done.33.rising = bf16[128,2048]{1,0:T(8,128)(2,1)S(1)} collective-permute-done((bf16[128,2048]{1,0:T(8,128)(2,1)}, bf16[128,2048]{1,0:T(8,128)(2,1)S(1)}, u32[]{:S(2)}, u32[]{:S(2)}) %collective-permute-start.33) | collective-permute-done | bytes 524320 | tf_op jit(solution)/shard_map/ppermute | solution.py:433
  183.9 2.6 add_pair.13
  196.4 5.1 collective-permute-done.37.rising
  203.9 2.6 add_pair.14
  211.6 6.6 %collective-permute-done.41.rising = bf16[128,2048]{1,0:T(8,128)(2,1)S(1)} collective-permute-done((bf16[128,2048]{1,0:T(8,128)(2,1)}, bf16[128,2048]{1,0:T(8,128)(2,1)S(1)}, u32[]{:S(2)}, u32[]{:S(2)}) %collective-permute-start.41) | collective-permute-done | bytes 524320 | tf_op jit(solution)/shard_map/ppermute | solution.py:433
  220.2 3.5 middle.1
  226.1 13.2 %collective-permute-done.43.refs_1_ = bf16[128,2176]{1,0:T(8,128)(2,1)S(1)} collective-permute-done((bf16[128,2176]{1,0:T(8,128)(2,1)}, bf16[128,2176]{1,0:T(8,128)(2,1)S(1)}, u32[]{:S(2)}, u32[]{:S(2)}) %collective-permute-start.43) | collective-permute-done | bytes 557088 | tf_op jit(solution)/shard_map/ppermute | solution.py:436
  241.4 16.2 %expert_first.1 = (f32[2,1024,1024]{2,1,0:T(8,128)}, bf16[2048,1024]{1,0:T(8,128)(2,1)}) custom-call(s32[9]{0:T(128)} %pad_add_fusion.scalars, bf16[128,2048]{1,0:T(8,128)(2,1)} %cotangent.1, bf16[128,2048]{1,0:T(8,128)(2,1)} %collective-permute-done.22.refs_1_, bf16[128,2048]{1,0:T(8,128)(2,1)} %copy-done.39, bf16[128,2048]{1,0:T(8,128)(2,1)} %copy-done.23, ...), custom_call_target="tpu_custom_call" | custom-call | tf_op jit(solution)/shard_map/expert_first/pallas_call | solution.py:1193
  259.7 7.9 %collective-permute-done.48.refs_6_ = bf16[128,2176]{1,0:T(8,128)(2,1)S(1)} collective-permute-done((bf16[128,2176]{1,0:T(8,128)(2,1)S(1)}, bf16[128,2176]{1,0:T(8,128)(2,1)S(1)}, u32[]{:S(2)}, u32[]{:S(2)}) %collective-permute-start.48) | collective-permute-done | bytes 557088 | tf_op jit(solution)/shard_map/ppermute | solution.py:433
  269.9 4.3 collective-permute-done.49.refs_4_
  275.9 32.5 %expert_hidden.1 = (bf16[1024,2048]{1,0:T(8,128)(2,1)}, bf16[1024,2048]{1,0:T(8,128)(2,1)}, bf16[1024,2048]{1,0:T(8,128)(2,1)}, bf16[1024,2048]{1,0:T(8,128)(2,1...) custom-call(s32[9]{0:T(128)} %pad_add_fusion.scalars, ...), custom_call_target="tpu_custom_call" | custom-call | tf_op jit(solution)/shard_map/expert_hidden/pallas_call | solution.py:1289
  308.4 26.3 %expert_inputs.1 = (bf16[128,2304]{1,0:T(8,128)(2,1)}, bf16[128,2304]{1,0:T(8,128)(2,1)}, bf16[128,2304]{1,0:T(8,128)(2,1)}, bf16[128,2304]{1,0:T(8,128)(2,1)}, ...) custom-call(s32[9]{0:T(128)} %pad_add_fusion.scalars, ...), custom_call_target="tpu_custom_call" | custom-call | tf_op jit(solution)/shard_map/expert_inputs/pallas_call | solution.py:1380
  336.8 8.4 %weight_far.3 = bf16[2048,1024]{1,0:T(8,128)(2,1)} custom-call(bf16[2048,1024]{1,0:T(8,128)(2,1)} %get-tuple-element.302.left, bf16[1024,2048]{1,0:T(8,128)(2,1)} %get-tuple-element.272.refs_0_.right), custom_call_target="tpu_custom_call" | custom-call | tf_op jit(solution)/shard_map/weight_far/pallas_call | solution.py:1454
  350.5 8.3 %weight_far.4 = bf16[2048,1024]{1,0:T(8,128)(2,1)} custom-call(bf16[2048,1024]{1,0:T(8,128)(2,1)} %get-tuple-element.302.left, bf16[1024,2048]{1,0:T(8,128)(2,1)} %get-tuple-element.273.refs_1_.right), custom_call_target="tpu_custom_call" | custom-call | tf_op jit(solution)/shard_map/weight_far/pallas_call | solution.py:1454
  358.9 4.8 collective-permute-done.53.rising
  364.8 2.7 add_pair.16
  369.6 9.9 %weight_near.3 = bf16[4,2048,256]{2,1,0:T(8,128)(2,1)} custom-call(s32[9]{0:T(128)} %pad_add_fusion.scalars, bf16[2048,1024]{1,0:T(8,128)(2,1)} %get-tuple-element.302.left, bf16[1024,2048]{1,0:T(8,128)(2,1)} %get-tuple-element.272.refs_0_.right, bf16[2048,1024]{1,0:T(8,128)(2,1)} %collective-permute-done.55.arrived), custom_call_target="tpu_custom_call" | custom-call | tf_op jit(solution)/shard_map/weight_near/pallas_call | solution.py:1484
  379.5 3.2 collective-permute-done.56.rising
  384.4 2.7 add_pair.17
  390.2 10.6 %weight_near.4 = bf16[4,2048,256]{2,1,0:T(8,128)(2,1)} custom-call(s32[9]{0:T(128)} %pad_add_fusion.scalars, bf16[2048,1024]{1,0:T(8,128)(2,1)} %get-tuple-element.302.left, bf16[1024,2048]{1,0:T(8,128)(2,1)} %get-tuple-element.273.refs_1_.right, bf16[2048,1024]{1,0:T(8,128)(2,1)} %collective-permute-done.58.arrived), custom_call_target="tpu_custom_call" | custom-call | tf_op jit(solution)/shard_map/weight_near/pallas_call | solution.py:1484
  403.3 4.7 middle_back.1
  411.2 8.6 %weight_far.5 = bf16[2048,1024]{1,0:T(8,128)(2,1)} custom-call(bf16[2048,1024]{1,0:T(8,128)(2,1)} %get-tuple-element.329.left, bf16[1024,2048]{1,0:T(8,128)(2,1)} %get-tuple-element.323.right), custom_call_target="tpu_custom_call" | custom-call | tf_op jit(solution)/shard_map/weight_far/pallas_call | solution.py:1454
  423.5 15.3 %expert_outputs.1 = (bf16[128,2048]{1,0:T(8,128)(2,1)}, bf16[128,2048]{1,0:T(8,128)(2,1)}, bf16[128,2048]{1,0:T(8,128)(2,1)}, bf16[128,2048]{1,0:T(8,128)(2,1)},...) custom-call(s32[9]{0:T(128)} %pad_add_fusion.scalars, ...), custom_call_target="tpu_custom_call" | custom-call | tf_op jit(solution)/shard_map/expert_outputs/pallas_call | solution.py:1426
  440.9 9.9 %weight_near.5 = bf16[4,2048,256]{2,1,0:T(8,128)(2,1)} custom-call(s32[9]{0:T(128)} %pad_add_fusion.scalars, bf16[2048,1024]{1,0:T(8,128)(2,1)} %get-tuple-element.329.left, bf16[1024,2048]{1,0:T(8,128)(2,1)} %get-tuple-element.323.right, bf16[2048,1024]{1,0:T(8,128)(2,1)} %collective-permute-done.65.arrived), custom_call_target="tpu_custom_call" | custom-call | tf_op jit(solution)/shard_map/weight_near/pallas_call | solution.py:1484
  455.6 5.0 collective-permute-done.68.refs_20_
  464.1 4.3 collective-permute-done.70.rising
  475.3 11.3 %attend_back.2 = (f32[1024,128]{1,0:T(8,128)}, f32[1024,128]{1,0:T(8,128)}, bf16[1024,128]{1,0:T(8,128)(2,1)}, f32[8,1024]{1,0:T(8,128)}, f32[1,128]{1,0:T(1,128...) custom-call(s32[9]{0:T(128)} %pad_add_fusion.scalars, bf16[1024,256]{1,0:T(8,128)(2,1)} %get-tuple-element.338.refs_0_, ...), custom_call_target="tpu_custom_call" | custom-call | tf_op jit(solution)/shard_map/attend_back/pallas_call | solution.py:898
  487.6 2.5 add_pair.19
  492.5 11.0 %attend_back.3 = (f32[1024,128]{1,0:T(8,128)}, f32[1024,128]{1,0:T(8,128)}, bf16[1024,128]{1,0:T(8,128)(2,1)}, f32[8,1024]{1,0:T(8,128)}, f32[1,128]{1,0:T(1,128)}, /*index=5*/f32[1,128]{1,0:T(1,128)}) custom-call(s32[9]{0:T(128)} %pad_add_fusion.scalars, bf16[1024,256]{1,0:T(8,128)(2,1)} %get-tuple-element.338.refs_0_, ...), custom_call_target="tpu_custom_call" | custom-call | tf_op jit(solution)/shard_map/attend_back/pallas_call | solution.py:898
  505.9 3.5 fusion.9
  510.4 3.1 collective-permute-done.76
  514.7 2.6 add_pair.20
  524.9 14.1 %project_back.1 = (bf16[1024,768]{1,0:T(8,128)(2,1)}, f32[1,2048]{1,0:T(1,128)}, bf16[128,2048]{1,0:T(8,128)(2,1)}, bf16[128,2048]{1,0:T(8,128)(2,1)}, bf16[128,...) custom-call(s32[9]{0:T(128)} %pad_add_fusion.scalars, ...), custom_call_target="tpu_custom_call" | custom-call | tf_op jit(solution)/shard_map/project_back/pallas_call | solution.py:989
  545.0 9.4 %weight_rows.1 = (bf16[2,512,896]{2,1,0:T(8,128)(2,1)}, f32[2,512,896]{2,1,0:T(8,128)}) custom-call(s32[9]{0:T(128)} %pad_add_fusion.scalars, bf16[1024,2048]{1,0:T(8,128)(2,1)} %get-tuple-element.390.left, bf16[1024,768]{1,0:T(8,128)(2,1)} %get-tuple-element.391.right, f32[24,2048]{1,0:T(8,128)} %concatenate.95.sums), custom_call_target="tpu_custom_call" | custom-call | tf_op jit(solution)/shard_map/weight_rows/pallas_call | solution.py:1526
  554.5 4.0 collective-permute-done.89
  558.4 2.6 fusion.5
  566.4 3.9 convert_element_type.146
  570.4 3.9 convert_element_type.147
  574.3 4.0 collective-permute-done.85.rising
  584.5 3.0 fusion
  587.4 8.2 %collective-permute-done.87.rising = bf16[128,2048]{1,0:T(8,128)(2,1)} collective-permute-done((bf16[128,2048]{1,0:T(8,128)(2,1)}, bf16[128,2048]{1,0:T(8,128)(2,1)}, u32[]{:S(2)}, u32[]{:S(2)}) %collective-permute-start.87) | collective-permute-done | bytes 524320 | tf_op jit(solution)/shard_map/ppermute | solution.py:433
  596.0 3.6 all-to-all-start.1
  599.6 3.6 collective-permute-start.93
  603.2 2.6 add_pair.23
  612.4 16.4 %all-to-all-done.1 = bf16[8,64,896]{2,1,0:T(8,128)(2,1)S(1)} async-done(((bf16[8,64,896]{2,1,0:T(8,128)(2,1)}), bf16[8,64,896]{2,1,0:T(8,128)(2,1)S(1)}, u32[]{:S(2)}, u32[]{:S(2)}) %all-to-all-start.1) | async-done | bytes 917536 | tf_op jit(solution)/shard_map/all_to_all | solution.py:1761
  633.0 4.0 convert_element_type.154
  637.0 6.6 %collective-permute-done.92 = bf16[128,2048]{1,0:T(8,128)(2,1)S(1)} collective-permute-done((bf16[128,2048]{1,0:T(8,128)(2,1)}, bf16[128,2048]{1,0:T(8,128)(2,1)S(1)}, u32[]{:S(2)}, u32[]{:S(2)}) %collective-permute-start.92) | collective-permute-done | bytes 524320 | tf_op jit(solution)/shard_map/ppermute | solution.py:436
  (441 shorter events, 186.5 us)
Async XLA Ops:
  7.3 234.1 %all-gather.4.cloned.1.call-start = ((), (), s32[]{:S(2)}) async-start(), calls=%async_computation.5 | async-start | bytes 10485760 | tf_op jit(solution)/shard_map/all_gather | solution.py:1626
  8.0 261.9 %all-gather.6.cloned.1.call-start = ((), (), s32[]{:S(2)}) async-start(), calls=%async_computation.6 | async-start | bytes 10485760 | tf_op jit(solution)/shard_map/all_gather | solution.py:1627
  8.8 261.2 %all-gather.8.cloned.1.call-start = ((), (), s32[]{:S(2)}) async-start(), calls=%async_computation.7 | async-start | bytes 10485760 | tf_op jit(solution)/shard_map/all_gather | solution.py:1628
  9.5 36.5 %collective-permute-start = (bf16[128,2048]{1,0:T(8,128)(2,1)S(1)}, bf16[128,2048]{1,0:T(8,128)(2,1)S(1)}, u32[]{:S(2)}, u32[]{:S(2)}) collective-permute-start(bf16[128,2048]{1,0:T(8,128)(2,1)S(1)} %copy-done.2), channel_id=1, source_target_pairs={{0,1},{2,0},{4,2},{6,4},{7,6},{5,7},{3,5},{1,3},{8,9},{10,8},{12,1... | collective-permute-start | bytes 1572872 | tf_op jit(solution)/shard_map/ppermute | solution.py:436
  12.5 33.5 %collective-permute-start.1 = (bf16[128,2048]{1,0:T(8,128)(2,1)S(1)}, bf16[128,2048]{1,0:T(8,128)(2,1)}, u32[]{:S(2)}, u32[]{:S(2)}) collective-permute-start(bf16[128,2048]{1,0:T(8,128)(2,1)S(1)} %copy-done.2), channel_id=1, source_target_pairs={{0,2},{2,4},{4,6},{6,7},{7,5},{5,3},{3,1},{1,0},{8,10},{10,12},{12... | collective-permute-start | bytes 1572872 | tf_op jit(solution)/shard_map/ppermute | solution.py:433
  12.7 12.6 %collective-permute-start.7 = (bf16[1,20,64]{2,1,0:T(8,128)(2,1)S(1)}, bf16[1,20,64]{2,1,0:T(8,128)(2,1)S(1)}, u32[]{:S(2)}, u32[]{:S(2)}) collective-permute-start(bf16[1,20,64]{2,1,0:T(8,128)(2,1)S(1)} %bitcast.102), channel_id=1, source_target_pairs={{0,8},{8,0},{16,24},{24,16},{1,9},{9,1},{17,25},{25,17},{2,10},{10... | collective-permute-start | bytes 7688 | tf_op jit(solution)/shard_map/ppermute | solution.py:535
  13.8 43.8 %all-to-all-start = ((bf16[8,64,768]{2,1,0:T(8,128)(2,1)}), bf16[8,64,768]{2,1,0:T(8,128)(2,1)S(1)}, u32[]{:S(2)}, u32[]{:S(2)}) async-start(bf16[8,64,768]{2,1,0:T(8,128)(2,1)} %maximum_bitcast_fusion), calls=%async_computation | async-start | bytes 1572864 | tf_op jit(solution)/shard_map/all_to_all | solution.py:1592
  20.1 546.4 %reduce-scatter.4.cloned.1.call-start = ((), (), s32[]{:S(2)}) async-start(), calls=%async_computation.8 | async-start | bytes 6291456 | tf_op jit(solution)/shard_map/reduce_scatter | solution.py:1676
  48.6 37.8 %collective-permute-start.6 = (bf16[64,2048]{1,0:T(8,128)(2,1)}, bf16[64,2048]{1,0:T(8,128)(2,1)S(1)}, u32[]{:S(2)}, u32[]{:S(2)}) collective-permute-start(bf16[64,2048]{1,0:T(8,128)(2,1)} %param.24), channel_id=1, source_target_pairs={{0,0},{1,8},{2,16},{3,24},{4,1},{5,9},{6,17},{7,25},{8,2},{9,10},{... | collective-permute-start | bytes 786440 | tf_op jit(solution)/shard_map/ppermute | solution.py:1616
  57.7 17.4 %collective-permute-start.2 = (bf16[128,2048]{1,0:T(8,128)(2,1)S(1)}, bf16[128,2048]{1,0:T(8,128)(2,1)}, u32[]{:S(2)}, u32[]{:S(2)}) collective-permute-start(bf16[128,2048]{1,0:T(8,128)(2,1)S(1)} %collective-permute-done.refs_1_), channel_id=1, source_target_pairs={{0,1},{2,0},{4,2},{6,4},{7,6},{5,7},{3,5},{1,3},{8,9},{10,8},{12,1... | collective-permute-start | bytes 1572872 | tf_op jit(solution)/shard_map/ppermute | solution.py:436
  62.7 14.7 %collective-permute-start.4 = (bf16[128,2048]{1,0:T(8,128)(2,1)}, bf16[128,2048]{1,0:T(8,128)(2,1)}, u32[]{:S(2)}, u32[]{:S(2)}) collective-permute-start(bf16[128,2048]{1,0:T(8,128)(2,1)} %collective-permute-done.1.refs_8_), channel_id=1, source_target_pairs={{0,2},{2,4},{4,6},{6,7},{7,5},{5,3},{3,1},{1,0},{8,10},{10,12},{12... | collective-permute-start | bytes 1572872 | tf_op jit(solution)/shard_map/ppermute | solution.py:433
  62.8 32.7 %collective-permute-start.19 = (bf16[512,768]{1,0:T(8,128)(2,1)S(1)}, bf16[512,768]{1,0:T(8,128)(2,1)S(1)}, u32[]{:S(2)}, u32[]{:S(2)}) collective-permute-start(bf16[512,768]{1,0:T(8,128)(2,1)S(1)} %bitcast.88), channel_id=1, source_target_pairs={{0,16},{8,24},{16,0},{24,8},{1,17},{9,25},{17,1},{25,9},{2,18},{10... | collective-permute-start | bytes 2359304 | tf_op jit(solution)/shard_map/ppermute | solution.py:553
  75.0 17.1 %collective-permute-start.3 = (bf16[128,2048]{1,0:T(8,128)(2,1)}, bf16[128,2048]{1,0:T(8,128)(2,1)S(1)}, u32[]{:S(2)}, u32[]{:S(2)}) collective-permute-start(bf16[128,2048]{1,0:T(8,128)(2,1)} %collective-permute-done.2.refs_2_), channel_id=1, source_target_pairs={{0,1},{2,0},{4,2},{6,4},{7,6},{5,7},{3,5},{1,3},{8,9},{10,8},{12,1... | collective-permute-start | bytes 1572872 | tf_op jit(solution)/shard_map/ppermute | solution.py:436
  77.4 14.8 %collective-permute-start.5 = (bf16[128,2048]{1,0:T(8,128)(2,1)}, bf16[128,2048]{1,0:T(8,128)(2,1)}, u32[]{:S(2)}, u32[]{:S(2)}) collective-permute-start(bf16[128,2048]{1,0:T(8,128)(2,1)} %collective-permute-done.4.refs_7_), channel_id=1, source_target_pairs={{0,2},{2,4},{4,6},{6,7},{7,5},{5,3},{3,1},{1,0},{8,10},{10,12},{12... | collective-permute-start | bytes 1572872 | tf_op jit(solution)/shard_map/ppermute | solution.py:433
  79.8 27.4 %collective-permute-start.18 = (bf16[512,768]{1,0:T(8,128)(2,1)S(1)}, bf16[512,768]{1,0:T(8,128)(2,1)S(1)}, u32[]{:S(2)}, u32[]{:S(2)}) collective-permute-start(bf16[512,768]{1,0:T(8,128)(2,1)S(1)} %bitcast.89), channel_id=1, source_target_pairs={{0,8},{8,0},{16,24},{24,16},{1,9},{9,1},{17,25},{25,17},{2,10},{10... | collective-permute-start | bytes 2359304 | tf_op jit(solution)/shard_map/ppermute | solution.py:553
  95.4 13.5 %collective-permute-start.20 = (bf16[512,768]{1,0:T(8,128)(2,1)S(1)}, bf16[512,768]{1,0:T(8,128)(2,1)}, u32[]{:S(2)}, u32[]{:S(2)}) collective-permute-start(bf16[512,768]{1,0:T(8,128)(2,1)S(1)} %collective-permute-done.19.refs_11_.refs_15_), channel_id=1, source_target_pairs={{0,8},{8,0},{16,24},{24,16},{1,9},{9,1},{17,25},{25,17},{2,10},{10... | collective-permute-start | bytes 2359304 | tf_op jit(solution)/shard_map/ppermute | solution.py:553
  102.4 18.0 %collective-permute-start.21 = (bf16[128,2048]{1,0:T(8,128)(2,1)}, bf16[128,2048]{1,0:T(8,128)(2,1)}, u32[]{:S(2)}, u32[]{:S(2)}) collective-permute-start(bf16[128,2048]{1,0:T(8,128)(2,1)} %cotangent.1), channel_id=1, source_target_pairs={{0,2},{2,4},{4,6},{6,7},{7,5},{5,3},{3,1},{1,0},{8,10},{10,12},{12... | collective-permute-start | bytes 1572872 | tf_op jit(solution)/shard_map/ppermute | solution.py:433
  103.7 16.7 %collective-permute-start.22 = (bf16[128,2048]{1,0:T(8,128)(2,1)}, bf16[128,2048]{1,0:T(8,128)(2,1)}, u32[]{:S(2)}, u32[]{:S(2)}) collective-permute-start(bf16[128,2048]{1,0:T(8,128)(2,1)} %cotangent.1), channel_id=1, source_target_pairs={{0,1},{2,0},{4,2},{6,4},{7,6},{5,7},{3,5},{1,3},{8,9},{10,8},{12,1... | collective-permute-start | bytes 1572872 | tf_op jit(solution)/shard_map/ppermute | solution.py:436
  107.2 13.2 %collective-permute-start.23 = (bf16[64,2048]{1,0:T(8,128)(2,1)S(1)}, bf16[64,2048]{1,0:T(8,128)(2,1)S(1)}, u32[]{:S(2)}, u32[]{:S(2)}) collective-permute-start(bf16[64,2048]{1,0:T(8,128)(2,1)S(1)} %collective-permute-done.6.refs_8_.refs_12_), channel_id=1, source_target_pairs={{0,8},{8,0},{16,24},{24,16},{1,9},{9,1},{17,25},{25,17},{2,10},{10... | collective-permute-start | bytes 786440 | tf_op jit(solution)/shard_map/ppermute | solution.py:553
  107.2 13.2 %collective-permute-start.25 = (bf16[64,2048]{1,0:T(8,128)(2,1)S(1)}, bf16[64,2048]{1,0:T(8,128)(2,1)}, u32[]{:S(2)}, u32[]{:S(2)}) collective-permute-start(bf16[64,2048]{1,0:T(8,128)(2,1)S(1)} %collective-permute-done.24.refs_10_.refs_14_), channel_id=1, source_target_pairs={{0,8},{8,0},{16,24},{24,16},{1,9},{9,1},{17,25},{25,17},{2,10},{10... | collective-permute-start | bytes 786440 | tf_op jit(solution)/shard_map/ppermute | solution.py:553
  135.1 19.6 %collective-permute-start.29 = (bf16[128,2048]{1,0:T(8,128)(2,1)}, bf16[128,2048]{1,0:T(8,128)(2,1)S(1)}, u32[]{:S(2)}, u32[]{:S(2)}) collective-permute-start(bf16[128,2048]{1,0:T(8,128)(2,1)} %collective-permute-done.21.refs_8_), channel_id=1, source_target_pairs={{0,2},{2,4},{4,6},{6,7},{7,5},{5,3},{3,1},{1,0},{8,10},{10,12},{12... | collective-permute-start | bytes 1572872 | tf_op jit(solution)/shard_map/ppermute | solution.py:433
  136.8 17.9 %collective-permute-start.30 = (bf16[128,2048]{1,0:T(8,128)(2,1)}, bf16[128,2048]{1,0:T(8,128)(2,1)S(1)}, u32[]{:S(2)}, u32[]{:S(2)}) collective-permute-start(bf16[128,2048]{1,0:T(8,128)(2,1)} %collective-permute-done.22.refs_1_), channel_id=1, source_target_pairs={{0,1},{2,0},{4,2},{6,4},{7,6},{5,7},{3,5},{1,3},{8,9},{10,8},{12,1... | collective-permute-start | bytes 1572872 | tf_op jit(solution)/shard_map/ppermute | solution.py:436
  166.2 15.1 %collective-permute-start.33 = (bf16[128,2048]{1,0:T(8,128)(2,1)}, bf16[128,2048]{1,0:T(8,128)(2,1)S(1)}, u32[]{:S(2)}, u32[]{:S(2)}) collective-permute-start(bf16[128,2048]{1,0:T(8,128)(2,1)} %get-tuple-element.252), channel_id=1, source_target_pairs={{0,2},{2,4},{4,6},{6,7},{7,5},{5,3},{3,1},{1,0},{8,10},{10,12},{12... | collective-permute-start | bytes 1572872 | tf_op jit(solution)/shard_map/ppermute | solution.py:433
  168.0 15.1 %collective-permute-start.34 = (bf16[128,2048]{1,0:T(8,128)(2,1)}, bf16[128,2048]{1,0:T(8,128)(2,1)S(1)}, u32[]{:S(2)}, u32[]{:S(2)}) collective-permute-start(bf16[128,2048]{1,0:T(8,128)(2,1)} %get-tuple-element.254), channel_id=1, source_target_pairs={{0,1},{2,0},{4,2},{6,4},{7,6},{5,7},{3,5},{1,3},{8,9},{10,8},{12,1... | collective-permute-start | bytes 1572872 | tf_op jit(solution)/shard_map/ppermute | solution.py:436
  168.3 20.5 %collective-permute-start.35 = (bf16[128,2048]{1,0:T(8,128)(2,1)S(1)}, bf16[128,2048]{1,0:T(8,128)(2,1)S(1)}, u32[]{:S(2)}, u32[]{:S(2)}) collective-permute-start(bf16[128,2048]{1,0:T(8,128)(2,1)S(1)} %collective-permute-done.29.refs_7_), channel_id=1, source_target_pairs={{0,2},{2,4},{4,6},{6,7},{7,5},{5,3},{3,1},{1,0},{8,10},{10,12},{12... | collective-permute-start | bytes 1572872 | tf_op jit(solution)/shard_map/ppermute | solution.py:433
  170.1 20.9 %collective-permute-start.36 = (bf16[128,2048]{1,0:T(8,128)(2,1)S(1)}, bf16[128,2048]{1,0:T(8,128)(2,1)S(1)}, u32[]{:S(2)}, u32[]{:S(2)}) collective-permute-start(bf16[128,2048]{1,0:T(8,128)(2,1)S(1)} %collective-permute-done.30.refs_2_), channel_id=1, source_target_pairs={{0,1},{2,0},{4,2},{6,4},{7,6},{5,7},{3,5},{1,3},{8,9},{10,8},{12,1... | collective-permute-start | bytes 1572872 | tf_op jit(solution)/shard_map/ppermute | solution.py:436
  193.7 12.9 %collective-permute-start.39 = (bf16[64,2048]{1,0:T(8,128)(2,1)}, bf16[64,2048]{1,0:T(8,128)(2,1)S(1)}, u32[]{:S(2)}, u32[]{:S(2)}) collective-permute-start(bf16[64,2048]{1,0:T(8,128)(2,1)} %slice.151), channel_id=1, source_target_pairs={{0,2},{2,4},{4,6},{6,7},{7,5},{5,3},{3,1},{1,0},{8,10},{10,12},{12... | collective-permute-start | bytes 786440 | tf_op jit(solution)/shard_map/ppermute | solution.py:433
  195.3 13.6 %collective-permute-start.40 = (bf16[64,2048]{1,0:T(8,128)(2,1)}, bf16[64,2048]{1,0:T(8,128)(2,1)}, u32[]{:S(2)}, u32[]{:S(2)}) collective-permute-start(bf16[64,2048]{1,0:T(8,128)(2,1)} %slice.152), channel_id=1, source_target_pairs={{0,1},{2,0},{4,2},{6,4},{7,6},{5,7},{3,5},{1,3},{8,9},{10,8},{12,1... | collective-permute-start | bytes 786440 | tf_op jit(solution)/shard_map/ppermute | solution.py:436
  223.7 15.5 %collective-permute-start.43 = (bf16[128,2176]{1,0:T(8,128)(2,1)}, bf16[128,2176]{1,0:T(8,128)(2,1)S(1)}, u32[]{:S(2)}, u32[]{:S(2)}) collective-permute-start(bf16[128,2176]{1,0:T(8,128)(2,1)} %get-tuple-element.267.refs_0_.block), channel_id=1, source_target_pairs={{0,1},{2,0},{4,2},{6,4},{7,6},{5,7},{3,5},{1,3},{8,9},{10,8},{12,1... | collective-permute-start | bytes 1671176 | tf_op jit(solution)/shard_map/ppermute | solution.py:436
  226.0 14.5 %collective-permute-start.45 = (bf16[128,2176]{1,0:T(8,128)(2,1)}, bf16[128,2176]{1,0:T(8,128)(2,1)S(1)}, u32[]{:S(2)}, u32[]{:S(2)}) collective-permute-start(bf16[128,2176]{1,0:T(8,128)(2,1)} %get-tuple-element.267.refs_0_.block), channel_id=1, source_target_pairs={{0,2},{2,4},{4,6},{6,7},{7,5},{5,3},{3,1},{1,0},{8,10},{10,12},{12... | collective-permute-start | bytes 1671176 | tf_op jit(solution)/shard_map/ppermute | solution.py:433
  239.3 18.3 %collective-permute-start.44 = (bf16[128,2176]{1,0:T(8,128)(2,1)S(1)}, bf16[128,2176]{1,0:T(8,128)(2,1)S(1)}, u32[]{:S(2)}, u32[]{:S(2)}) collective-permute-start(bf16[128,2176]{1,0:T(8,128)(2,1)S(1)} %collective-permute-done.43.refs_1_), channel_id=1, source_target_pairs={{0,1},{2,0},{4,2},{6,4},{7,6},{5,7},{3,5},{1,3},{8,9},{10,8},{12,1... | collective-permute-start | bytes 1671176 | tf_op jit(solution)/shard_map/ppermute | solution.py:436
  240.6 17.0 %collective-permute-start.46 = (bf16[128,2176]{1,0:T(8,128)(2,1)S(1)}, bf16[128,2176]{1,0:T(8,128)(2,1)S(1)}, u32[]{:S(2)}, u32[]{:S(2)}) collective-permute-start(bf16[128,2176]{1,0:T(8,128)(2,1)S(1)} %collective-permute-done.45.refs_8_), channel_id=1, source_target_pairs={{0,2},{2,4},{4,6},{6,7},{7,5},{5,3},{3,1},{1,0},{8,10},{10,12},{12... | collective-permute-start | bytes 1671176 | tf_op jit(solution)/shard_map/ppermute | solution.py:433
  345.2 22.4 %collective-permute-start.55 = (bf16[2048,1024]{1,0:T(8,128)(2,1)}, bf16[2048,1024]{1,0:T(8,128)(2,1)}, u32[]{:S(2)}, u32[]{:S(2)}) collective-permute-start(bf16[2048,1024]{1,0:T(8,128)(2,1)} %weight_far.3), channel_id=1, source_target_pairs={{0,8},{8,0},{16,24},{24,16},{1,9},{9,1},{17,25},{25,17},{2,10},{10... | collective-permute-start | bytes 12582920 | tf_op jit(solution)/shard_map/ppermute | solution.py:1669
  348.5 15.2 %collective-permute-start.53 = (bf16[128,2304]{1,0:T(8,128)(2,1)}, bf16[128,2304]{1,0:T(8,128)(2,1)S(1)}, u32[]{:S(2)}, u32[]{:S(2)}) collective-permute-start(bf16[128,2304]{1,0:T(8,128)(2,1)} %get-tuple-element.288), channel_id=1, source_target_pairs={{0,2},{2,4},{4,6},{6,7},{7,5},{5,3},{3,1},{1,0},{8,10},{10,12},{12... | collective-permute-start | bytes 1769480 | tf_op jit(solution)/shard_map/ppermute | solution.py:433
  349.1 14.9 %collective-permute-start.54 = (bf16[128,2304]{1,0:T(8,128)(2,1)}, bf16[128,2304]{1,0:T(8,128)(2,1)S(1)}, u32[]{:S(2)}, u32[]{:S(2)}) collective-permute-start(bf16[128,2304]{1,0:T(8,128)(2,1)} %get-tuple-element.289), channel_id=1, source_target_pairs={{0,1},{2,0},{4,2},{6,4},{7,6},{5,7},{3,5},{1,3},{8,9},{10,8},{12,1... | collective-permute-start | bytes 1769480 | tf_op jit(solution)/shard_map/ppermute | solution.py:436
  364.0 23.1 %collective-permute-start.58 = (bf16[2048,1024]{1,0:T(8,128)(2,1)}, bf16[2048,1024]{1,0:T(8,128)(2,1)}, u32[]{:S(2)}, u32[]{:S(2)}) collective-permute-start(bf16[2048,1024]{1,0:T(8,128)(2,1)} %weight_far.4), channel_id=1, source_target_pairs={{0,8},{8,0},{16,24},{24,16},{1,9},{9,1},{17,25},{25,17},{2,10},{10... | collective-permute-start | bytes 12582920 | tf_op jit(solution)/shard_map/ppermute | solution.py:1669
  367.6 15.1 %collective-permute-start.56 = (bf16[128,2304]{1,0:T(8,128)(2,1)}, bf16[128,2304]{1,0:T(8,128)(2,1)S(1)}, u32[]{:S(2)}, u32[]{:S(2)}) collective-permute-start(bf16[128,2304]{1,0:T(8,128)(2,1)} %get-tuple-element.294), channel_id=1, source_target_pairs={{0,2},{2,4},{4,6},{6,7},{7,5},{5,3},{3,1},{1,0},{8,10},{10,12},{12... | collective-permute-start | bytes 1769480 | tf_op jit(solution)/shard_map/ppermute | solution.py:433
  368.1 14.9 %collective-permute-start.57 = (bf16[128,2304]{1,0:T(8,128)(2,1)}, bf16[128,2304]{1,0:T(8,128)(2,1)S(1)}, u32[]{:S(2)}, u32[]{:S(2)}) collective-permute-start(bf16[128,2304]{1,0:T(8,128)(2,1)} %get-tuple-element.295), channel_id=1, source_target_pairs={{0,1},{2,0},{4,2},{6,4},{7,6},{5,7},{3,5},{1,3},{8,9},{10,8},{12,1... | collective-permute-start | bytes 1769480 | tf_op jit(solution)/shard_map/ppermute | solution.py:436
  387.2 183.2 %reduce-scatter.6.cloned.1.call-start = ((), (), s32[]{:S(2)}) async-start(), calls=%async_computation.9 | async-start | bytes 6291456 | tf_op jit(solution)/shard_map/reduce_scatter | solution.py:1676
  388.2 14.0 %collective-permute-start.59 = (bf16[128,2304]{1,0:T(8,128)(2,1)S(1)}, bf16[128,2304]{1,0:T(8,128)(2,1)S(1)}, u32[]{:S(2)}, u32[]{:S(2)}) collective-permute-start(bf16[128,2304]{1,0:T(8,128)(2,1)S(1)} %copy-done.85), channel_id=1, source_target_pairs={{0,2},{2,4},{4,6},{6,7},{7,5},{5,3},{3,1},{1,0},{8,10},{10,12},{12... | collective-permute-start | bytes 1769480 | tf_op jit(solution)/shard_map/ppermute | solution.py:433
  388.7 13.8 %collective-permute-start.60 = (bf16[128,2304]{1,0:T(8,128)(2,1)S(1)}, bf16[128,2304]{1,0:T(8,128)(2,1)S(1)}, u32[]{:S(2)}, u32[]{:S(2)}) collective-permute-start(bf16[128,2304]{1,0:T(8,128)(2,1)S(1)} %copy-done.84), channel_id=1, source_target_pairs={{0,1},{2,0},{4,2},{6,4},{7,6},{5,7},{3,5},{1,3},{8,9},{10,8},{12,1... | collective-permute-start | bytes 1769480 | tf_op jit(solution)/shard_map/ppermute | solution.py:436
  408.0 225.0 %reduce-scatter.8.cloned.1.call-start = ((), (), s32[]{:S(2)}) async-start(), calls=%async_computation.10 | async-start | bytes 6291456 | tf_op jit(solution)/shard_map/reduce_scatter | solution.py:1676
  421.4 17.4 %collective-permute-start.65 = (bf16[2048,1024]{1,0:T(8,128)(2,1)}, bf16[2048,1024]{1,0:T(8,128)(2,1)}, u32[]{:S(2)}, u32[]{:S(2)}) collective-permute-start(bf16[2048,1024]{1,0:T(8,128)(2,1)} %weight_far.5), channel_id=1, source_target_pairs={{0,8},{8,0},{16,24},{24,16},{1,9},{9,1},{17,25},{25,17},{2,10},{10... | collective-permute-start | bytes 12582920 | tf_op jit(solution)/shard_map/ppermute | solution.py:1669
  421.4 17.3 %collective-permute-start.63 = (bf16[128,2048]{1,0:T(8,128)(2,1)S(1)}, bf16[128,2048]{1,0:T(8,128)(2,1)S(1)}, u32[]{:S(2)}, u32[]{:S(2)}) collective-permute-start(bf16[128,2048]{1,0:T(8,128)(2,1)S(1)} %collective-permute-done.61.refs_24_), channel_id=1, source_target_pairs={{0,2},{2,4},{4,6},{6,7},{7,5},{5,3},{3,1},{1,0},{8,10},{10,12},{12... | collective-permute-start | bytes 1572872 | tf_op jit(solution)/shard_map/ppermute | solution.py:433
  422.5 16.3 %collective-permute-start.64 = (bf16[128,2048]{1,0:T(8,128)(2,1)S(1)}, bf16[128,2048]{1,0:T(8,128)(2,1)S(1)}, u32[]{:S(2)}, u32[]{:S(2)}) collective-permute-start(bf16[128,2048]{1,0:T(8,128)(2,1)S(1)} %collective-permute-done.62.refs_17_), channel_id=1, source_target_pairs={{0,1},{2,0},{4,2},{6,4},{7,6},{5,7},{3,5},{1,3},{8,9},{10,8},{12,1... | collective-permute-start | bytes 1572872 | tf_op jit(solution)/shard_map/ppermute | solution.py:436
  438.8 13.8 %collective-permute-start.66 = (bf16[128,2048]{1,0:T(8,128)(2,1)S(1)}, bf16[128,2048]{1,0:T(8,128)(2,1)S(1)}, u32[]{:S(2)}, u32[]{:S(2)}) collective-permute-start(bf16[128,2048]{1,0:T(8,128)(2,1)S(1)} %collective-permute-done.63.refs_23_), channel_id=1, source_target_pairs={{0,2},{2,4},{4,6},{6,7},{7,5},{5,3},{3,1},{1,0},{8,10},{10,12},{12... | collective-permute-start | bytes 1572872 | tf_op jit(solution)/shard_map/ppermute | solution.py:433
  439.9 13.5 %collective-permute-start.67 = (bf16[128,2048]{1,0:T(8,128)(2,1)S(1)}, bf16[128,2048]{1,0:T(8,128)(2,1)S(1)}, u32[]{:S(2)}, u32[]{:S(2)}) collective-permute-start(bf16[128,2048]{1,0:T(8,128)(2,1)S(1)} %collective-permute-done.64.refs_18_), channel_id=1, source_target_pairs={{0,1},{2,0},{4,2},{6,4},{7,6},{5,7},{3,5},{1,3},{8,9},{10,8},{12,1... | collective-permute-start | bytes 1572872 | tf_op jit(solution)/shard_map/ppermute | solution.py:436
  473.3 13.4 %collective-permute-start.72 = (bf16[128,2048]{1,0:T(8,128)(2,1)}, bf16[128,2048]{1,0:T(8,128)(2,1)S(1)}, u32[]{:S(2)}, u32[]{:S(2)}) collective-permute-start(bf16[128,2048]{1,0:T(8,128)(2,1)} %get-tuple-element.335), channel_id=1, source_target_pairs={{0,2},{2,4},{4,6},{6,7},{7,5},{5,3},{3,1},{1,0},{8,10},{10,12},{12... | collective-permute-start | bytes 1572872 | tf_op jit(solution)/shard_map/ppermute | solution.py:433
  474.2 12.4 %collective-permute-start.73 = (bf16[128,2048]{1,0:T(8,128)(2,1)}, bf16[128,2048]{1,0:T(8,128)(2,1)S(1)}, u32[]{:S(2)}, u32[]{:S(2)}) collective-permute-start(bf16[128,2048]{1,0:T(8,128)(2,1)} %get-tuple-element.336), channel_id=1, source_target_pairs={{0,1},{2,0},{4,2},{6,4},{7,6},{5,7},{3,5},{1,3},{8,9},{10,8},{12,1... | collective-permute-start | bytes 1572872 | tf_op jit(solution)/shard_map/ppermute | solution.py:436
  490.1 14.1 %collective-permute-start.74 = (bf16[128,2048]{1,0:T(8,128)(2,1)}, bf16[128,2048]{1,0:T(8,128)(2,1)S(1)}, u32[]{:S(2)}, u32[]{:S(2)}) collective-permute-start(bf16[128,2048]{1,0:T(8,128)(2,1)} %get-tuple-element.347), channel_id=1, source_target_pairs={{0,2},{2,4},{4,6},{6,7},{7,5},{5,3},{3,1},{1,0},{8,10},{10,12},{12... | collective-permute-start | bytes 1572872 | tf_op jit(solution)/shard_map/ppermute | solution.py:433
  491.1 13.2 %collective-permute-start.75 = (bf16[128,2048]{1,0:T(8,128)(2,1)}, bf16[128,2048]{1,0:T(8,128)(2,1)S(1)}, u32[]{:S(2)}, u32[]{:S(2)}) collective-permute-start(bf16[128,2048]{1,0:T(8,128)(2,1)} %get-tuple-element.348), channel_id=1, source_target_pairs={{0,1},{2,0},{4,2},{6,4},{7,6},{5,7},{3,5},{1,3},{8,9},{10,8},{12,1... | collective-permute-start | bytes 1572872 | tf_op jit(solution)/shard_map/ppermute | solution.py:436
  519.9 19.1 %collective-permute-start.82 = (bf16[64,2048]{1,0:T(8,128)(2,1)}, bf16[64,2048]{1,0:T(8,128)(2,1)S(1)}, u32[]{:S(2)}, u32[]{:S(2)}) collective-permute-start(bf16[64,2048]{1,0:T(8,128)(2,1)} %fusion.6), channel_id=1, source_target_pairs={{0,16},{8,24},{16,0},{24,8},{1,17},{9,25},{17,1},{25,9},{2,18},{10... | collective-permute-start | bytes 786440 | tf_op jit(solution)/shard_map/ppermute | solution.py:562
  522.9 17.0 %collective-permute-start.79 = (bf16[128,2048]{1,0:T(8,128)(2,1)}, bf16[128,2048]{1,0:T(8,128)(2,1)S(1)}, u32[]{:S(2)}, u32[]{:S(2)}) collective-permute-start(bf16[128,2048]{1,0:T(8,128)(2,1)} %get-tuple-element.359), channel_id=1, source_target_pairs={{0,2},{2,4},{4,6},{6,7},{7,5},{5,3},{3,1},{1,0},{8,10},{10,12},{12... | collective-permute-start | bytes 1572872 | tf_op jit(solution)/shard_map/ppermute | solution.py:433
  524.0 15.8 %collective-permute-start.80 = (bf16[128,2048]{1,0:T(8,128)(2,1)}, bf16[128,2048]{1,0:T(8,128)(2,1)}, u32[]{:S(2)}, u32[]{:S(2)}) collective-permute-start(bf16[128,2048]{1,0:T(8,128)(2,1)} %get-tuple-element.360), channel_id=1, source_target_pairs={{0,1},{2,0},{4,2},{6,4},{7,6},{5,7},{3,5},{1,3},{8,9},{10,8},{12,1... | collective-permute-start | bytes 1572872 | tf_op jit(solution)/shard_map/ppermute | solution.py:436
  539.8 14.5 %collective-permute-start.83 = (bf16[64,2048]{1,0:T(8,128)(2,1)}, bf16[64,2048]{1,0:T(8,128)(2,1)S(1)}, u32[]{:S(2)}, u32[]{:S(2)}) collective-permute-start(bf16[64,2048]{1,0:T(8,128)(2,1)} %get-tuple-element.384), channel_id=1, source_target_pairs={{0,2},{2,4},{4,6},{6,7},{7,5},{5,3},{3,1},{1,0},{8,10},{10,12},{12... | collective-permute-start | bytes 786440 | tf_op jit(solution)/shard_map/ppermute | solution.py:433
  540.9 13.4 %collective-permute-start.84 = (bf16[64,2048]{1,0:T(8,128)(2,1)}, bf16[64,2048]{1,0:T(8,128)(2,1)S(1)}, u32[]{:S(2)}, u32[]{:S(2)}) collective-permute-start(bf16[64,2048]{1,0:T(8,128)(2,1)} %get-tuple-element.385), channel_id=1, source_target_pairs={{0,1},{2,0},{4,2},{6,4},{7,6},{5,7},{3,5},{1,3},{8,9},{10,8},{12,1... | collective-permute-start | bytes 786440 | tf_op jit(solution)/shard_map/ppermute | solution.py:436
  561.1 23.4 %collective-permute-start.90 = (bf16[512,896]{1,0:T(8,128)(2,1)}, bf16[512,896]{1,0:T(8,128)(2,1)}, u32[]{:S(2)}, u32[]{:S(2)}) collective-permute-start(bf16[512,896]{1,0:T(8,128)(2,1)} %fusion.5), channel_id=1, source_target_pairs={{0,16},{8,24},{16,0},{24,8},{1,17},{9,25},{17,1},{25,9},{2,18},{10... | collective-permute-start | bytes 2752520 | tf_op jit(solution)/shard_map/ppermute | solution.py:562
  564.4 13.9 %collective-permute-start.85 = (bf16[128,2048]{1,0:T(8,128)(2,1)}, bf16[128,2048]{1,0:T(8,128)(2,1)S(1)}, u32[]{:S(2)}, u32[]{:S(2)}) collective-permute-start(bf16[128,2048]{1,0:T(8,128)(2,1)} %get-tuple-element.403), channel_id=1, source_target_pairs={{0,2},{2,4},{4,6},{6,7},{7,5},{5,3},{3,1},{1,0},{8,10},{10,12},{12... | collective-permute-start | bytes 1572872 | tf_op jit(solution)/shard_map/ppermute | solution.py:433
  565.0 13.6 %collective-permute-start.86 = (bf16[128,2048]{1,0:T(8,128)(2,1)}, bf16[128,2048]{1,0:T(8,128)(2,1)S(1)}, u32[]{:S(2)}, u32[]{:S(2)}) collective-permute-start(bf16[128,2048]{1,0:T(8,128)(2,1)} %get-tuple-element.404), channel_id=1, source_target_pairs={{0,1},{2,0},{4,2},{6,4},{7,6},{5,7},{3,5},{1,3},{8,9},{10,8},{12,1... | collective-permute-start | bytes 1572872 | tf_op jit(solution)/shard_map/ppermute | solution.py:436
  582.4 13.2 %collective-permute-start.87 = (bf16[128,2048]{1,0:T(8,128)(2,1)}, bf16[128,2048]{1,0:T(8,128)(2,1)}, u32[]{:S(2)}, u32[]{:S(2)}) collective-permute-start(bf16[128,2048]{1,0:T(8,128)(2,1)} %get-tuple-element.409), channel_id=1, source_target_pairs={{0,2},{2,4},{4,6},{6,7},{7,5},{5,3},{3,1},{1,0},{8,10},{10,12},{12... | collective-permute-start | bytes 1572872 | tf_op jit(solution)/shard_map/ppermute | solution.py:433
  583.0 13.0 %collective-permute-start.88 = (bf16[128,2048]{1,0:T(8,128)(2,1)}, bf16[128,2048]{1,0:T(8,128)(2,1)}, u32[]{:S(2)}, u32[]{:S(2)}) collective-permute-start(bf16[128,2048]{1,0:T(8,128)(2,1)} %get-tuple-element.410), channel_id=1, source_target_pairs={{0,1},{2,0},{4,2},{6,4},{7,6},{5,7},{3,5},{1,3},{8,9},{10,8},{12,1... | collective-permute-start | bytes 1572872 | tf_op jit(solution)/shard_map/ppermute | solution.py:436
  596.0 32.9 %all-to-all-start.1 = ((bf16[8,64,896]{2,1,0:T(8,128)(2,1)}), bf16[8,64,896]{2,1,0:T(8,128)(2,1)S(1)}, u32[]{:S(2)}, u32[]{:S(2)}) async-start(bf16[8,64,896]{2,1,0:T(8,128)(2,1)} %bitcast.27), calls=%async_computation.4 | async-start | bytes 1835008 | tf_op jit(solution)/shard_map/all_to_all | solution.py:1761
  605.8 31.3 %collective-permute-start.91 = (bf16[128,2048]{1,0:T(8,128)(2,1)}, bf16[128,2048]{1,0:T(8,128)(2,1)S(1)}, u32[]{:S(2)}, u32[]{:S(2)}) collective-permute-start(bf16[128,2048]{1,0:T(8,128)(2,1)} %get-tuple-element.415), channel_id=1, source_target_pairs={{0,2},{2,4},{4,6},{6,7},{7,5},{5,3},{3,1},{1,0},{8,10},{10,12},{12... | collective-permute-start | bytes 1572872 | tf_op jit(solution)/shard_map/ppermute | solution.py:433
  606.0 37.6 %collective-permute-start.92 = (bf16[128,2048]{1,0:T(8,128)(2,1)}, bf16[128,2048]{1,0:T(8,128)(2,1)S(1)}, u32[]{:S(2)}, u32[]{:S(2)}) collective-permute-start(bf16[128,2048]{1,0:T(8,128)(2,1)} %get-tuple-element.416), channel_id=1, source_target_pairs={{0,1},{2,0},{4,2},{6,4},{7,6},{5,7},{3,5},{1,3},{8,9},{10,8},{12,1... | collective-permute-start | bytes 1572872 | tf_op jit(solution)/shard_map/ppermute | solution.py:436
  (127 other events, 1479.0 us)
Sparse Core Ops, SparseCore 0:
  9.7 68.8 all-gather.3
  80.1 71.9 all-gather.5
  153.7 58.0 all-gather.7
  387.3 52.9 reduce-scatter.3
  442.6 54.3 reduce-scatter.5
  499.0 59.9 reduce-scatter.7
